TPU v7x, 32 devices: a whole 2x2x4 slice. The times are simulated.
32 devices in a mesh: grp: 2 (over core), edge: 4 (over z), gate: 4 (over y, x).
Axes of the slice: x: 2, y: 2, z: 4, core: 2. Of those that a mesh axis runs over, the one named last changes fastest.
Arguments:
- node_feat: bfloat16 [19456, 16], P(('grp', 'edge')), may hold values from -6 to 6
- dist_feat: bfloat16 [39936, 12], P(('grp', 'edge')), may hold values from -6 to 6
- bond: int32 [39936], P(('grp', 'edge')), may hold values from 0 to 3
- source: int32 [39936], P(('grp', 'edge')), may hold values from 0 to 2431, as said below
- target_node: int32 [39936], P(('grp', 'edge')), may hold values from 0 to 2431, as said below
- mol_id: int32 [19456], P(('grp', 'edge')), may hold values from 0 to 127, as said below
- flag: int32 [1024], P(('grp', 'edge')), may hold values 0 or 1
- target: float32 [1024, 12], P(('grp', 'edge')), may hold values from -6 to 6
- embed_weight: float32 [16, 128], P(None, 'gate'), may hold values from -1.5 to 1.5
- edge_first: float32 [17, 128], replicated, may hold values from -1.5 to 1.5
- edge_second: float32 [129, 16384], P(None, 'gate'), may hold values from -0.046875 to 0.046875
- gru_weight: float32 [2, 129, 3, 128], P(None, None, None, 'gate'), may hold values from -0.5 to 0.5
- set_lstm: float32 [385, 512], replicated, may hold values from -0.3125 to 0.3125
- head_weight: float32 [257, 12], replicated, may hold values from -0.375 to 0.375
- mom_embed: float32 [16, 128], P(None, 'gate'), may hold values from -3.8146973e-06 to 3.8146973e-06
- mom_first: float32 [17, 128], replicated, may hold values from -3.8146973e-06 to 3.8146973e-06
- mom_second: float32 [129, 16384], P(None, 'gate'), may hold values from -3.8146973e-06 to 3.8146973e-06
- mom_gru: float32 [2, 129, 3, 128], P(None, None, None, 'gate'), may hold values from -3.8146973e-06 to 3.8146973e-06
- mom_lstm: float32 [385, 512], replicated, may hold values from -3.8146973e-06 to 3.8146973e-06
- mom_head: float32 [257, 12], replicated, may hold values from -3.8146973e-06 to 3.8146973e-06
- var_embed: float32 [16, 128], P(None, 'gate'), may hold values from 4.137299e-14 to 1.6549196e-13
- var_first: float32 [17, 128], replicated, may hold values from 4.137299e-14 to 1.6549196e-13
- var_second: float32 [129, 16384], P(None, 'gate'), may hold values from 4.137299e-14 to 1.6549196e-13
- var_gru: float32 [2, 129, 3, 128], P(None, None, None, 'gate'), may hold values from 4.137299e-14 to 1.6549196e-13
- var_lstm: float32 [385, 512], replicated, may hold values from 4.137299e-14 to 1.6549196e-13
- var_head: float32 [257, 12], replicated, may hold values from 4.137299e-14 to 1.6549196e-13
- step_count: int32 [1], replicated, may hold values from 2 to 20
Outputs:
- loss: float32 [], replicated
- grad_norm: float32 [], replicated
- embed_out: float32 [16, 128], P(None, 'gate')
- first_out: float32 [17, 128], replicated
- second_out: float32 [129, 16384], P(None, 'gate')
- gru_out: float32 [2, 129, 3, 128], P(None, None, None, 'gate')
- lstm_out: float32 [385, 512], replicated
- head_out: float32 [257, 12], replicated
- embed_mom: float32 [16, 128], P(None, 'gate')
- first_mom: float32 [17, 128], replicated
- second_mom: float32 [129, 16384], P(None, 'gate')
- gru_mom: float32 [2, 129, 3, 128], P(None, None, None, 'gate')
- lstm_mom: float32 [385, 512], replicated
- head_mom: float32 [257, 12], replicated
- embed_var: float32 [16, 128], P(None, 'gate')
- first_var: float32 [17, 128], replicated
- second_var: float32 [129, 16384], P(None, 'gate')
- gru_var: float32 [2, 129, 3, 128], P(None, None, None, 'gate')
- lstm_var: float32 [385, 512], replicated
- head_var: float32 [257, 12], replicated
Inputs may be any that keep to these rules, and one draw needn't show every extreme that they name: `mol_id`: within each group of 2432 atoms the molecule ids never fall and every molecule of 0 to 127 has at least one atom. `source`: an atom of the edge's own group. `target_node`: an atom of the same group and molecule as the edge's source.
All inputs are finite; a program needn't handle non-finite values. No bound on the sum of `flag` on one device may be relied on, other than what follows from the above.
Results may differ from a plain program's by a relative error of at most 0.005.
The roundings to bfloat16 on the way count: a program that leaves them out, or rounds other values in their place, can miss the bound.
Values may be sent and summed in bfloat16 or wider, within the bound.
No kernel may reach another device: no remote copies, remote signals or barrier semaphores. Data moves between devices by JAX's collectives and lax.ppermute only.
A program may use at most 256 MiB of HBM per device.

v0:
```python
import functools
import math

import jax
import jax.numpy as jnp
from jax import lax
from jax.experimental import pallas as pl
from jax.experimental.pallas import tpu as pltpu
from jax.sharding import PartitionSpec as P

H = 128
EDGE_HID = 128
NT = 12
BONDS = 4
STEPS = 3
SET_STEPS = 6
EIN = 16
BLK = 256
FEAT = 32
WIN = 768
SLOTS = 14
DEEP = H + 16

CLIP = 0.01
BETA_ONE = 0.9
BETA_TWO = 0.999
EPSILON = 1e-08
DECAY = 0.01
RATES = (0.1, 0.05, 0.005, 0.02, 0.02, 0.02)

F32 = jnp.float32
BF = jnp.bfloat16
VMEM_LIMIT = 60 << 20


def up(value, multiple):
    return -(-value // multiple) * multiple


def dot(left, right):
    return jnp.dot(left, right, preferred_element_type=F32)


def dot_nt(left, right):
    return lax.dot_general(
        left, right, (((1,), (1,)), ((), ())), preferred_element_type=F32
    )


def dot_tn(left, right):
    return lax.dot_general(
        left, right, (((0,), (0,)), ((), ())), preferred_element_type=F32
    )


def split2(value):
    high = value.astype(BF)
    return high, (value - high.astype(F32)).astype(BF)


def split3(value):
    high = value.astype(BF)
    rest = value - high.astype(F32)
    mid = rest.astype(BF)
    return high, mid, (rest - mid.astype(F32)).astype(BF)


def wide(product, left, right):
    lh, ll = split2(left)
    rh, rl = split2(right)
    return product(lh, rh) + (product(lh, rl) + product(ll, rh))


def half_wide(product, left, right):
    lh, lm, ll = split3(left)
    return product(lh, right) + (product(lm, right) + product(ll, right))


def sigmoid(value):
    return jax.nn.sigmoid(value)


def ceil_blocks(value):
    return lax.div(value + (BLK - 1), BLK)


def padded_nodes(nodes):
    return up(nodes, H) + WIN


def start_of(scal, window):
    return pl.multiple_of(scal[0] + window * WIN, H)


def node_hit(row, start):
    ids = lax.broadcasted_iota(jnp.int32, (WIN, row.shape[1]), 0) + start
    return jnp.where(row == ids, 1.0, 0.0).astype(BF)


def at(block):
    return pl.ds(pl.multiple_of(block * BLK, BLK), BLK)


def strip(unit):
    return pl.ds(pl.multiple_of(unit * H, H), H)


def prep_kernel(place, mol, src2d, data, first3, scal, pre, eh_t, eh, feat, idx, comp, *, edges, gates, eblocks):
    mine = place[0]
    mols = lax.broadcasted_iota(jnp.int32, (H, 1), 0)
    row = mol[...]
    size = jnp.sum(jnp.where(row == mols, 1.0, 0.0), axis=1, keepdims=True)
    start = jnp.sum(jnp.where(row < mols, 1.0, 0.0), axis=1, keepdims=True)
    ids = src2d[...]
    ends = (start + size).astype(jnp.int32)
    starts = start.astype(jnp.int32)
    seen = jnp.zeros((H, BLK), F32)
    for block in range(eblocks):
        line = ids[block : block + 1]
        seen = seen + jnp.where(line < ends, 1.0, 0.0) + jnp.where(line < starts, 1.0, 0.0)
    padding = 2.0 * (eblocks * BLK - edges)
    middle = jnp.sum(seen, axis=1, keepdims=True) - padding
    owner = jnp.zeros((H, 1), F32)
    for step in range(1, gates):
        owner = owner + jnp.where(middle * gates >= 2.0 * edges * step, 1.0, 0.0)
    before = jnp.where(owner < mine.astype(F32), 1.0, 0.0)
    until = jnp.where(owner <= mine.astype(F32), 1.0, 0.0)
    node_lo = jnp.sum(size * before).astype(jnp.int32)
    node_hi = jnp.sum(size * until).astype(jnp.int32)
    base = lax.div(node_lo, H) * H
    scal[0] = base
    scal[1] = lax.div(node_hi - base + (WIN - 1), WIN)
    scal[2] = jnp.sum(before).astype(jnp.int32)
    scal[3] = jnp.sum(until).astype(jnp.int32)
    mask = jnp.where((ids >= node_lo) & (ids < node_hi), 1.0, 0.0)
    lower = lax.broadcasted_iota(jnp.int32, (BLK, BLK), 0)
    upper = lax.broadcasted_iota(jnp.int32, (BLK, BLK), 1)
    prefix = dot(mask.astype(BF), jnp.where(lower <= upper, 1.0, 0.0).astype(BF))
    totals = jnp.sum(mask, axis=1, keepdims=True)
    rows = lax.broadcasted_iota(jnp.int32, totals.shape, 0)
    slots = lax.broadcasted_iota(jnp.int32, (BLK, BLK), 0).astype(F32)
    for block in range(eblocks):
        offset = jnp.sum(jnp.where(rows < block, totals, 0.0)).astype(jnp.int32)
        hit = jnp.where(prefix[block : block + 1] - 1.0 == slots, mask[block : block + 1], 0.0)
        comp[pl.ds(offset, BLK), :] = dot(hit.astype(BF), data[block * BLK : (block + 1) * BLK, :])
    count = jnp.sum(totals).astype(jnp.int32)
    comp[pl.ds(count, BLK), :] = jnp.zeros((BLK, H), F32)
    scal[4] = jnp.maximum(count, 1)

    ones = jnp.where(lax.broadcasted_iota(jnp.int32, (DEEP - H, BLK), 0) < 3, 1.0, 0.0).astype(BF)

    def each(block, carry):
        part = comp[at(block), :]
        part_t = part.T
        low = part_t[0:FEAT].astype(BF)
        feat[:, at(block)] = low
        source = 16.0 * part_t[17:18] + part_t[18:19] - 1.0
        target = 16.0 * part_t[19:20] + part_t[20:21] - 1.0
        idx[0:1, at(block)] = source.astype(jnp.int32)
        idx[1:2, at(block)] = target.astype(jnp.int32)
        three = dot(first3[...], low)
        value = three[0:H] + (three[H : 2 * H] + three[2 * H : 3 * H])
        pre[:, at(block)] = value
        hidden = value * sigmoid(value)
        eh_t[0:H, at(block)] = hidden.astype(BF)
        eh_t[H:DEEP, at(block)] = ones
        eh[at(block), :] = hidden.T.astype(BF)
        return carry

    lax.fori_loop(0, ceil_blocks(jnp.maximum(count, 1)), each, 0)


def prep(place, mol, src2d, data, first3, real, gates):
    edges = data.shape[0]
    return pl.pallas_call(
        functools.partial(prep_kernel, edges=real, gates=gates, eblocks=edges // BLK),
        out_shape=(
            jax.ShapeDtypeStruct((8,), jnp.int32),
            jax.ShapeDtypeStruct((H, edges), F32),
            jax.ShapeDtypeStruct((DEEP, edges), BF),
            jax.ShapeDtypeStruct((edges, H), BF),
            jax.ShapeDtypeStruct((FEAT, edges), BF),
            jax.ShapeDtypeStruct((8, edges), jnp.int32),
        ),
        in_specs=[pl.BlockSpec(memory_space=pltpu.SMEM)] + [pl.BlockSpec(memory_space=pltpu.VMEM)] * 4,
        out_specs=[pl.BlockSpec(memory_space=pltpu.SMEM)] + [pl.BlockSpec(memory_space=pltpu.VMEM)] * 5,
        scratch_shapes=[pltpu.VMEM((edges + BLK, H), F32)],
        compiler_params=pltpu.CompilerParams(vmem_limit_bytes=VMEM_LIMIT),
        name="prep",
    )(place, mol, src2d, data, first3)


def piece_index(place, pair, side):
    return (pair ^ place[0]) * 2 + (side ^ place[1])


def load_second(place, parts, bias, second, sems):
    copies = []
    half = second.shape[1] // 2
    for number, part in enumerate(parts):
        pair, side = divmod(number, 2)
        copies.append(
            pltpu.make_async_copy(
                part,
                second.at[pair, pl.ds(side * half, half), pl.ds(0, H)],
                sems.at[number],
            )
        )
    for copy in copies:
        copy.start()
    for number in range(len(parts)):
        pair, side = divmod(number, 2)
        rows = bias[piece_index(place, pair, side)]
        second[pair, side * half : (side + 1) * half, H:DEEP] = rows.astype(F32).T.astype(BF)
    return copies


def matrix_rows(place, pair, width, load):
    for side in range(2):
        begin_row = pl.multiple_of(piece_index(place, pair, side) * width, width)
        yield pl.ds(begin_row, width), [load(side * width + item) for item in range(width)]


class Stream:
    def __init__(self, mats, buffer, sems, count, passes):
        self.mats, self.buffer, self.sems = mats, buffer, sems
        self.gates = mats.shape[1]
        self.chunks = lax.div(count + (H - 1), H) * self.gates
        self.turns = self.chunks * passes

    def copy(self, turn):
        chunk, slot = lax.rem(turn, self.chunks), lax.rem(turn, SLOTS)
        source = self.mats.at[lax.div(chunk, self.gates), lax.rem(chunk, self.gates)]
        return pltpu.make_async_copy(source, self.buffer.at[slot], self.sems.at[slot])

    def begin(self):
        for turn in range(SLOTS - 1):

            @pl.when(turn < self.turns)
            def _():
                self.copy(jnp.int32(turn)).start()

    def run(self, number, use):
        def each(chunk, carry):
            turn = number * self.chunks + chunk

            @pl.when(turn + (SLOTS - 1) < self.turns)
            def _():
                self.copy(turn + (SLOTS - 1)).start()

            self.copy(turn).wait()
            slot = lax.rem(turn, SLOTS)

            def load(item):
                return self.buffer[slot, item * H : (item + 1) * H, :].astype(F32)

            use(lax.div(chunk, self.gates), lax.rem(chunk, self.gates), load)
            return carry

        lax.fori_loop(0, self.chunks, each, 0)


def gather_rows(scal, table, column, blocks, idx, put):
    def each(block, carry):
        row = idx[column : column + 1, at(block)]

        def window(number, acc):
            start = start_of(scal, number)
            return acc + dot(table(pl.ds(start, WIN)), node_hit(row, start))

        put(at(block), lax.fori_loop(0, scal[1], window, jnp.zeros((H, BLK), F32)))
        return carry

    lax.fori_loop(0, blocks, each, 0)


def scatter_rows(scal, values, column, blocks, idx, target):
    def each(block, carry):
        row = idx[column : column + 1, at(block)]
        pair = jnp.concatenate(split2(values[:, at(block)]), axis=0)

        def window(number, carry):
            start = start_of(scal, number)
            both = dot_nt(pair, node_hit(row, start))
            target[:, pl.ds(start, WIN)] += both[0:H] + both[H : 2 * H]
            return carry

        lax.fori_loop(0, scal[1], window, 0)
        return carry

    lax.fori_loop(0, blocks, each, 0)


def gru_parts(gru, gru_bias, message, hidden):
    gate_in = dot(gru[0], message) + gru_bias[0]
    gate_hid = dot(gru[1], hidden) + gru_bias[1]
    reset = sigmoid(gate_in[0:H] + gate_hid[0:H])
    update = sigmoid(gate_in[H : 2 * H] + gate_hid[H : 2 * H])
    last = gate_hid[2 * H : 3 * H]
    fresh = jnp.tanh(gate_in[2 * H : 3 * H] + reset * last)
    return reset, update, fresh, last


def forward_kernel(place, scal, nf_t, embed, bias, gru, gru_bias, eh_t, idx, *refs, gates):
    parts, refs = refs[: 2 * gates], refs[2 * gates :]
    hid, msg, state, near, mats, second, total, part, staged, buffer, sems, out_sems, in_sems = refs
    copies = load_second(place, parts, bias, second, sems)
    width = second.shape[1] // (2 * H)
    windows = scal[1]
    blocks = ceil_blocks(scal[4])
    part[...] = jnp.zeros(part.shape, F32)

    def begin(window, carry):
        nodes = pl.ds(start_of(scal, window), WIN)
        value = dot(embed[...], nf_t[:, nodes])
        state[0, :, nodes] = value
        hid[0, :, nodes] = value.astype(BF)
        return carry

    lax.fori_loop(0, windows, begin, 0)
    for copy in copies:
        copy.wait()

    def gather(step):
        def put(lanes, value):
            near[step, :, lanes] = value.astype(BF)

        gather_rows(scal, lambda nodes: hid[step, :, nodes], 0, blocks, idx, put)

    def message(pair, lanes, rows, load):
        for out_rows, loaded in matrix_rows(place, pair, width, load):
            outs = [jnp.sum(mat * rows, axis=0, keepdims=True) for mat in loaded]
            part[out_rows, lanes] = jnp.concatenate(outs, axis=0)

    def finish(step):
        def clear(window, carry):
            total[:, pl.ds(start_of(scal, window), WIN)] = jnp.zeros((H, WIN), F32)
            return carry

        lax.fori_loop(0, windows, clear, 0)
        scatter_rows(scal, part, 1, blocks, idx, total)

        def cell(window, carry):
            nodes = pl.ds(start_of(scal, window), WIN)
            low = total[:, nodes].astype(BF)
            msg[step, :, nodes] = low
            old = state[step, :, nodes]
            reset, update, fresh, last = gru_parts(gru, gru_bias, low, hid[step, :, nodes])
            new = (1.0 - update) * fresh + update * old
            hid[step + 1, :, nodes] = new.astype(BF)
            state[step + 1, :, nodes] = new
            return carry

        lax.fori_loop(0, windows, cell, 0)

    gather(0)

    def stores(turn):
        slot = lax.rem(turn, 4)
        block, pair = lax.div(turn, gates), lax.rem(turn, gates)
        return [
            pltpu.make_async_copy(
                staged.at[slot, :, pl.ds(side * H, H)], mats.at[block * 2 + side, pair], out_sems.at[slot, side]
            )
            for side in range(2)
        ]

    def make(turn, carry):
        block, pair = lax.div(turn, gates), lax.rem(turn, gates)

        @pl.when(turn >= 4)
        def _():
            for copy in stores(turn - 4):
                copy.wait()

        low = dot(second[pair], eh_t[:, at(block)]).astype(BF)
        staged[lax.rem(turn, 4)] = low
        for copy in stores(turn):
            copy.start()
        rows = near[0, :, at(block)].astype(F32)
        message(pair, at(block), rows, lambda item: low[item * H : (item + 1) * H].astype(F32))
        return carry

    lax.fori_loop(0, blocks * gates, make, 0)
    for turn in range(4, 0, -1):
        for copy in stores(blocks * gates - turn):
            copy.wait()
    matrix_stream = Stream(mats, buffer, in_sems, scal[4], STEPS - 1)
    matrix_stream.begin()
    finish(0)

    def later(step, carry):
        gather(step)

        def use(unit, pair, load):
            message(pair, strip(unit), near[step, :, strip(unit)].astype(F32), load)

        matrix_stream.run(step - 1, use)
        finish(step)
        return carry

    lax.fori_loop(1, STEPS, later, 0)


def forward(place, scal, nf_t, embed, bias, gru, gru_bias, eh_t, idx, second):
    nodes = nf_t.shape[1]
    edges = eh_t.shape[1]
    gates = len(second) // 2
    half = bias.shape[2]
    smem = pl.BlockSpec(memory_space=pltpu.SMEM)
    vmem = pl.BlockSpec(memory_space=pltpu.VMEM)
    hbm = pl.BlockSpec(memory_space=pl.ANY)
    return pl.pallas_call(
        functools.partial(forward_kernel, gates=gates),
        out_shape=(
            jax.ShapeDtypeStruct((STEPS + 1, H, nodes), BF),
            jax.ShapeDtypeStruct((STEPS, H, nodes), BF),
            jax.ShapeDtypeStruct((STEPS + 1, H, nodes), F32),
            jax.ShapeDtypeStruct((STEPS, H, edges), BF),
            jax.ShapeDtypeStruct((edges // H, gates, 2 * half, H), BF),
        ),
        in_specs=[smem] * 2 + [vmem] * 7 + [hbm] * (2 * gates),
        out_specs=[vmem] * 4 + [hbm],
        scratch_shapes=[
            pltpu.VMEM((gates, 2 * half, DEEP), BF),
            pltpu.VMEM((H, nodes), F32),
            pltpu.VMEM((H, edges), F32),
            pltpu.VMEM((4, 2 * half, BLK), BF),
            pltpu.VMEM((SLOTS, 2 * half, H), BF),
            pltpu.SemaphoreType.DMA((2 * gates,)),
            pltpu.SemaphoreType.DMA((4, 2)),
            pltpu.SemaphoreType.DMA((SLOTS,)),
        ],
        compiler_params=pltpu.CompilerParams(vmem_limit_bytes=VMEM_LIMIT),
        cost_estimate=pl.CostEstimate(flops=60_000_000_000, transcendentals=0, bytes_accessed=20_000_000),
        name="forward",
    )(place, scal, nf_t, embed, bias, gru, gru_bias, eh_t, idx, *second)


def readout_kernel(scal, inverse, final, mol, lstm, head, present, target, d_final, d_lstm, d_head, score, weight, slope, before, kept):
    windows = scal[1]
    mols = lax.broadcasted_iota(jnp.int32, (H, 1), 0)
    owned = jnp.where((mols >= scal[2]) & (mols < scal[3]), 1.0, 0.0)
    by_query = lstm[0:H, :] + lstm[2 * H : 3 * H, :]
    by_summary = lstm[H : 2 * H, :]
    lstm_bias = lstm[3 * H : 3 * H + 1, :]
    zero = jnp.zeros((H, H), F32)

    def lstm_round(rounds, carry):
        query, summary, cell = carry
        gates = lstm_bias + wide(dot, query, by_query) + wide(dot, summary, by_summary)
        enter = sigmoid(gates[:, 0:H])
        forget = sigmoid(gates[:, H : 2 * H])
        fresh = jnp.tanh(gates[:, 2 * H : 3 * H])
        leave = sigmoid(gates[:, 3 * H : 4 * H])
        old_cell, old_query, old_summary = cell, query, summary
        cell = forget * cell + enter * fresh
        bent = jnp.tanh(cell)
        query = leave * bent
        stack = jnp.concatenate(split3(query), axis=0)

        def scores(window, peak):
            nodes = pl.ds(start_of(scal, window), WIN)
            three = dot(stack, final[:, nodes])
            value = three[0:H] + (three[H : 2 * H] + three[2 * H : 3 * H])
            value = jnp.where(mol[:, nodes] == mols, value, -1e30)
            score[:, nodes] = value
            return jnp.maximum(peak, jnp.max(value, axis=1, keepdims=True))

        peak = lax.fori_loop(0, windows, scores, jnp.full((H, 1), -1e30, F32))

        def powers(window, sums):
            nodes = pl.ds(start_of(scal, window), WIN)
            value = jnp.where(mol[:, nodes] == mols, jnp.exp(score[:, nodes] - peak), 0.0)
            score[:, nodes] = value
            return sums + jnp.sum(value, axis=1, keepdims=True)

        sums = lax.fori_loop(0, windows, powers, jnp.zeros((H, 1), F32))
        sums = jnp.where(sums > 0.0, sums, 1.0)

        def gather(window, acc):
            nodes = pl.ds(start_of(scal, window), WIN)
            value = score[:, nodes] / sums
            weight[rounds, :, nodes] = value
            three = dot_nt(jnp.concatenate(split3(value), axis=0), final[:, nodes])
            return acc + (three[0:H] + (three[H : 2 * H] + three[2 * H : 3 * H]))

        summary = lax.fori_loop(0, windows, gather, zero)
        for number, value in enumerate((enter, forget, fresh, leave, bent, old_cell, query)):
            kept[rounds, number] = value
        columns = pl.ds(pl.multiple_of(rounds * H, H), H)
        before[0, :, columns] = old_query.T
        before[1, :, columns] = old_summary.T
        return query, summary, cell

    query, summary, cell = lax.fori_loop(0, SET_STEPS, lstm_round, (zero, zero, zero))
    head_query = head[0:H, :]
    head_summary = head[H : 2 * H, :]
    guess = wide(dot, query, head_query) + wide(dot, summary, head_summary) + head[2 * H : 2 * H + 1, :]
    gap = guess - target[...]
    seen = present[...] * owned
    d_head[2 * H + 8 : 2 * H + 16, :] = jnp.broadcast_to(jnp.sum(seen * gap * gap), (8, H)) * inverse[0]
    d_guess = (2.0 * inverse[0]) * seen * gap
    d_head[0:H, :] = wide(dot, query.T, d_guess)
    d_head[H : 2 * H, :] = wide(dot, summary.T, d_guess)
    d_head[2 * H : 2 * H + 8, :] = jnp.broadcast_to(jnp.sum(d_guess, axis=0, keepdims=True), (8, H))
    d_query = wide(dot_nt, d_guess, head_query)
    d_summary = wide(dot_nt, d_guess, head_summary)

    def clear(window, carry):
        nodes = pl.ds(start_of(scal, window), WIN)
        d_final[:, nodes] = jnp.zeros((H, WIN), F32)
        return carry

    lax.fori_loop(0, windows, clear, 0)

    def back_round(number, carry):
        d_query, d_summary, d_cell, d_bias = carry
        rounds = SET_STEPS - 1 - number
        enter, forget, fresh, leave, bent, old_cell, query = [kept[rounds, item] for item in range(7)]
        stack = jnp.concatenate(split3(d_summary), axis=0)

        def products(window, acc):
            nodes = pl.ds(start_of(scal, window), WIN)
            three = dot(stack, final[:, nodes])
            value = three[0:H] + (three[H : 2 * H] + three[2 * H : 3 * H])
            score[:, nodes] = value
            return acc + jnp.sum(value * weight[rounds, :, nodes], axis=1, keepdims=True)

        mean = lax.fori_loop(0, windows, products, jnp.zeros((H, 1), F32))
        query_t = query.T
        d_summary_t = d_summary.T

        def spread(window, acc):
            nodes = pl.ds(start_of(scal, window), WIN)
            share = weight[rounds, :, nodes]
            d_score = share * (score[:, nodes] - mean)
            d_final[:, nodes] += wide(dot, query_t, d_score) + wide(dot, d_summary_t, share)
            three = dot_nt(jnp.concatenate(split3(d_score), axis=0), final[:, nodes])
            return acc + (three[0:H] + (three[H : 2 * H] + three[2 * H : 3 * H]))

        d_query = lax.fori_loop(0, windows, spread, d_query)
        d_leave = d_query * bent
        d_cell = d_cell + d_query * leave * (1.0 - bent * bent)
        d_gates = jnp.concatenate(
            [
                d_cell * fresh * enter * (1.0 - enter),
                d_cell * old_cell * forget * (1.0 - forget),
                d_cell * enter * (1.0 - fresh * fresh),
                d_leave * leave * (1.0 - leave),
            ],
            axis=1,
        )
        d_cell = d_cell * forget
        d_bias = d_bias + jnp.sum(d_gates, axis=0, keepdims=True)
        slope[rounds] = d_gates
        d_query = wide(dot_nt, d_gates, by_query)
        d_summary = wide(dot_nt, d_gates, by_summary)
        return d_query, d_summary, d_cell, d_bias

    start = (d_query, d_summary, zero, jnp.zeros((1, 4 * H), F32))
    d_bias = lax.fori_loop(0, SET_STEPS, back_round, start)[3]
    slopes = slope[...].reshape(SET_STEPS * H, 4 * H)
    d_lstm[0:H, :] = wide(dot, before[0], slopes)
    d_lstm[H : 2 * H, :] = wide(dot, before[1], slopes)
    d_lstm[2 * H : 2 * H + 8, :] = jnp.broadcast_to(d_bias, (8, 4 * H))


def readout(scal, inverse, final, mol, lstm, head, present, target):
    nodes = final.shape[1]
    return pl.pallas_call(
        readout_kernel,
        out_shape=(
            jax.ShapeDtypeStruct((H, nodes), F32),
            jax.ShapeDtypeStruct((2 * H + 8, 4 * H), F32),
            jax.ShapeDtypeStruct((2 * H + 16, H), F32),
        ),
        in_specs=[pl.BlockSpec(memory_space=pltpu.SMEM)] * 2 + [pl.BlockSpec(memory_space=pltpu.VMEM)] * 6,
        out_specs=[pl.BlockSpec(memory_space=pltpu.VMEM)] * 3,
        scratch_shapes=[
            pltpu.VMEM((H, nodes), F32),
            pltpu.VMEM((SET_STEPS, H, nodes), F32),
            pltpu.VMEM((SET_STEPS, H, 4 * H), F32),
            pltpu.VMEM((2, H, SET_STEPS * H), F32),
            pltpu.VMEM((SET_STEPS, 7, H, H), F32),
        ],
        compiler_params=pltpu.CompilerParams(vmem_limit_bytes=VMEM_LIMIT),
        cost_estimate=pl.CostEstimate(flops=30_000_000_000, transcendentals=0, bytes_accessed=5_000_000),
        name="readout",
    )(scal, inverse, final, mol, lstm, head, present, target)


def backward_kernel(place, scal, nf_t, gru, gru_bias, idx, hid, msg, state, near, d_final, mats, far, small, d_gru, d_embed, d_bias, grad, low_msg, part, back, buffer, in_sems):
    gates = mats.shape[1]
    width = mats.shape[2] // (2 * H)
    windows = scal[1]
    blocks = ceil_blocks(scal[4])
    matrix_stream = Stream(mats, buffer, in_sems, scal[4], STEPS)
    matrix_stream.begin()
    d_gru[...] = jnp.zeros(d_gru.shape, F32)
    d_embed[...] = jnp.zeros(d_embed.shape, F32)
    d_bias[...] = jnp.zeros(d_bias.shape, F32)
    back[...] = jnp.zeros(back.shape, F32)
    ones = jnp.where(lax.broadcasted_iota(jnp.int32, (16, WIN), 0) == 0, 1.0, 0.0).astype(BF)

    def begin(window, carry):
        nodes = pl.ds(start_of(scal, window), WIN)
        grad[:, nodes] = d_final[:, nodes]
        return carry

    lax.fori_loop(0, windows, begin, 0)

    def one_step(number, carry):
        step = STEPS - 1 - number

        def cell(window, carry):
            nodes = pl.ds(start_of(scal, window), WIN)
            message = msg[step, :, nodes]
            hidden = hid[step, :, nodes]
            old = state[step, :, nodes]
            reset, update, fresh, last = gru_parts(gru, gru_bias, message, hidden)
            value = grad[:, nodes]
            d_fresh = value * (1.0 - update) * (1.0 - fresh * fresh)
            d_update = value * (old - fresh) * update * (1.0 - update)
            d_reset = d_fresh * last * reset * (1.0 - reset)
            d_in = jnp.concatenate([d_reset, d_update, d_fresh], axis=0).astype(BF)
            d_hid = jnp.concatenate([d_reset, d_update, d_fresh * reset], axis=0).astype(BF)
            d_gru[0] += dot_nt(jnp.concatenate([message, ones], axis=0), d_in)
            d_gru[1] += dot_nt(jnp.concatenate([hidden, ones], axis=0), d_hid)
            low_msg[:, nodes] = dot_tn(gru[0], d_in).astype(BF)
            grad[:, nodes] = value * update + dot_tn(gru[1], d_hid)
            return carry

        lax.fori_loop(0, windows, cell, 0)

        def put(lanes, value):
            low = value.astype(BF)
            part[:, lanes] = value
            far[step, :, lanes] = low
            d_bias[...] += dot_nt(low, near[step, :, lanes])

        gather_rows(scal, lambda nodes: low_msg[:, nodes], 1, blocks, idx, put)

        def use(unit, pair, load):
            lanes = strip(unit)
            acc = jnp.where(pair == 0, 0.0, back[:, lanes])
            for in_rows, loaded in matrix_rows(place, pair, width, load):
                scale = part[in_rows, lanes]
                for item in range(width):
                    acc = acc + loaded[item] * scale[item : item + 1]
            back[:, lanes] = acc

        matrix_stream.run(number, use)
        scatter_rows(scal, back, 0, blocks, idx, grad)
        return carry

    lax.fori_loop(0, STEPS, one_step, 0)

    def finish(window, carry):
        nodes = pl.ds(start_of(scal, window), WIN)
        d_embed[...] += dot_nt(nf_t[:, nodes], grad[:, nodes].astype(BF))
        return carry

    lax.fori_loop(0, windows, finish, 0)
    wide_part = H // gates
    tall = H + 16
    for gate in range(gates):
        columns = slice(gate * wide_part, (gate + 1) * wide_part)
        for side in range(2):
            for kind in range(3):
                begin_column = kind * H + gate * wide_part
                small[gate, side * tall : (side + 1) * tall, kind * wide_part : (kind + 1) * wide_part] = d_gru[
                    side, :, begin_column : begin_column + wide_part
                ]
        small[gate, 0:16, 3 * wide_part : 4 * wide_part] = d_embed[:, columns]
        small[gate, 16 : 2 * tall, 3 * wide_part : 4 * wide_part] = jnp.zeros((2 * tall - 16, wide_part), F32)
        small[gate, 2 * tall : 2 * tall + wide_part, :] = d_bias[columns, :]


def backward(place, scal, nf_t, gru, gru_bias, idx, hid, msg, state, near, d_final, mats):
    nodes = nf_t.shape[1]
    edges = idx.shape[1]
    _, gates, rows, _ = mats.shape
    smem = pl.BlockSpec(memory_space=pltpu.SMEM)
    vmem = pl.BlockSpec(memory_space=pltpu.VMEM)
    return pl.pallas_call(
        backward_kernel,
        out_shape=(
            jax.ShapeDtypeStruct((STEPS, H, edges), BF),
            jax.ShapeDtypeStruct((gates, 2 * (H + 16) + H // gates, H), F32),
        ),
        in_specs=[smem] * 2 + [vmem] * 9 + [pl.BlockSpec(memory_space=pl.ANY)],
        out_specs=[vmem] * 2,
        scratch_shapes=[
            pltpu.VMEM((2, H + 16, 3 * H), F32),
            pltpu.VMEM((16, H), F32),
            pltpu.VMEM((H, H), F32),
            pltpu.VMEM((H, nodes), F32),
            pltpu.VMEM((H, nodes), BF),
            pltpu.VMEM((H, edges), F32),
            pltpu.VMEM((H, edges), F32),
            pltpu.VMEM((SLOTS, rows, H), BF),
            pltpu.SemaphoreType.DMA((SLOTS,)),
        ],
        compiler_params=pltpu.CompilerParams(vmem_limit_bytes=VMEM_LIMIT),
        cost_estimate=pl.CostEstimate(flops=60_000_000_000, transcendentals=0, bytes_accessed=20_000_000),
        name="backward",
    )(place, scal, nf_t, gru, gru_bias, idx, hid, msg, state, near, d_final, mats)


def final_kernel(place, scal, mine, other, first_in, near, far, eh, pre, feat, d_mine, d_other, first_out, acc, near_s, far_s, eh_s, pre_s, feat_s, sems, *, pair, group):
    edge_blocks = ceil_blocks(scal[4])
    half = acc.shape[1]
    width = half // H

    def copies(block, slot):
        moves = (
            (near.at[:, :, at(block)], near_s),
            (far.at[:, :, at(block)], far_s),
            (eh.at[at(block), :], eh_s),
            (pre.at[:, at(block)], pre_s),
            (feat.at[:, at(block)], feat_s),
        )
        return [
            pltpu.make_async_copy(source, target.at[slot], sems.at[slot, number])
            for number, (source, target) in enumerate(moves)
        ]

    for copy in copies(0, 0):
        copy.start()
    acc[...] = jnp.zeros(acc.shape, F32)
    first_out[...] = first_in[...]

    def edge_block(block, carry):
        slot = lax.rem(block, 2)
        for copy in copies(block, slot):
            copy.wait()

        @pl.when(block + 1 < edge_blocks)
        def _():
            for copy in copies(block + 1, 1 - slot):
                copy.start()

        sides = [near_s[slot, step].astype(F32) for step in range(STEPS)]
        low = eh_s[slot]
        d_pre = jnp.zeros((H, BLK), F32)
        for side in range(2):
            second = (mine, other)[side]
            begin_row = pl.multiple_of(piece_index(place, pair, side) * width, width)
            tops = [far_s[slot, step, pl.ds(begin_row, width), :].astype(F32) for step in range(STEPS)]
            for part in range(width // group):
                mats = []
                for item in range(part * group, (part + 1) * group):
                    value = sides[0] * tops[0][item : item + 1]
                    for step in range(1, STEPS):
                        value = value + sides[step] * tops[step][item : item + 1]
                    mats.append(value.astype(BF))
                flat = jnp.concatenate(mats, axis=0)
                rows = slice(part * group * H, (part + 1) * group * H)
                acc[side, rows, :] += dot(flat, low)
                d_pre = d_pre + dot_tn(second[rows, :], flat)
        value = pre_s[slot]
        sig = sigmoid(value)
        slope = d_pre * sig * (1.0 + value * (1.0 - sig))
        total = first_out[...]
        for piece in split3(slope):
            total = total + dot_nt(feat_s[slot], piece)
        first_out[...] = total
        return carry

    lax.fori_loop(0, edge_blocks, edge_block, 0)
    d_mine[...] = acc[0]
    d_other[...] = acc[1]


def edge_grads(place, scal, mine, other, near, far, eh, pre, feat, first_in, pair, half):
    smem = pl.BlockSpec(memory_space=pltpu.SMEM)
    vmem = pl.BlockSpec(memory_space=pltpu.VMEM)
    return pl.pallas_call(
        functools.partial(final_kernel, pair=pair, group=8),
        in_specs=[smem] * 2 + [vmem] * 3 + [pl.BlockSpec(memory_space=pl.ANY)] * 5,
        out_specs=[vmem] * 3,
        out_shape=(
            jax.ShapeDtypeStruct((half, H), F32),
            jax.ShapeDtypeStruct((half, H), F32),
            jax.ShapeDtypeStruct((FEAT, H), F32),
        ),
        scratch_shapes=[
            pltpu.VMEM((2, half, H), F32),
            pltpu.VMEM((2, STEPS, H, BLK), BF),
            pltpu.VMEM((2, STEPS, H, BLK), BF),
            pltpu.VMEM((2, BLK, H), BF),
            pltpu.VMEM((2, H, BLK), F32),
            pltpu.VMEM((2, FEAT, BLK), BF),
            pltpu.SemaphoreType.DMA((2, 5)),
        ],
        compiler_params=pltpu.CompilerParams(vmem_limit_bytes=VMEM_LIMIT),
        cost_estimate=pl.CostEstimate(flops=9_000_000_000, transcendentals=0, bytes_accessed=5_000_000),
        name="edge_grads",
    )(place, scal, mine, other, first_in, near, far, eh, pre, feat)


def exact3(value):
    high = lax.reduce_precision(value, 8, 7)
    mid = lax.reduce_precision(value - high, 8, 7)
    low = lax.reduce_precision(value - high - mid, 8, 7)
    return jnp.stack([high, mid, low]).astype(BF)


def swap(value, axis, size, step):
    return lax.ppermute(value, axis, [(index, index ^ step) for index in range(size)])


def pick(parts, index):
    return lax.dynamic_index_in_dim(parts, index, 0, keepdims=False)


def scatter_sum(value, axis, size, me):
    parts = value.reshape((size, value.shape[0] // size) + value.shape[1:])
    total = pick(parts, me)
    parts = scaled(parts)
    for step in range(1, size):
        total = total + unscaled(swap(pick(parts, me ^ step), axis, size, step))
    return total


def gather_all(value, axis, size, me):
    rows = value.shape[0]
    out = jnp.zeros((size * rows,) + value.shape[1:], value.dtype)
    for step in range(size):
        part = swap(value, axis, size, step) if step else value
        out = lax.dynamic_update_slice_in_dim(out, part, (me ^ step) * rows, 0)
    return out


def tree_sum(value, axis, size):
    values = [value] + [swap(value, axis, size, step) for step in range(1, size)]
    while len(values) > 1:
        values = [left + right for left, right in zip(values[::2], values[1::2])]
    return values[0]


def scaled(value):
    peak = jnp.max(jnp.abs(value))
    power = jnp.floor(14.0 - jnp.log2(jnp.maximum(peak, 1e-30)))
    low = (value * jnp.exp2(power)).astype(jnp.float16)
    return jnp.concatenate([low, jnp.full(value.shape[:-2] + (16, H), power, jnp.float16)], axis=-2)


def unscaled(low):
    power = low[..., -1:, :1].astype(F32)
    return low[..., :-16, :].astype(F32) * jnp.exp2(-power)


def butterfly(value, axis, size):
    step = 1
    while step < size:
        value = value + swap(value, axis, size, step)
        step *= 2
    return value


def flat_rows(array):
    line = array.reshape(-1)
    return jnp.pad(line, (0, up(line.size, H) - line.size)).reshape(-1, H)


def adamw(weight, grad, mom, var, rate, count):
    mom_new = BETA_ONE * mom + (1.0 - BETA_ONE) * grad
    var_new = BETA_TWO * var + (1.0 - BETA_TWO) * grad * grad
    mom_hat = mom_new / (1.0 - BETA_ONE**count)
    var_hat = var_new / (1.0 - BETA_TWO**count)
    return (
        weight - rate * (mom_hat / (jnp.sqrt(var_hat) + EPSILON) + DECAY * weight),
        mom_new,
        var_new,
    )


def on_device(
    node_feat, dist_feat, bond, source, target_node, mol_id, flag, target,
    embed_weight, edge_first, edge_second, gru_weight, set_lstm, head_weight,
    mom_embed, mom_first, mom_second, mom_gru, mom_lstm, mom_head,
    var_embed, var_first, var_second, var_gru, var_lstm, var_head, step_count,
    *, sizes,
):
    width = embed_weight.shape[1]
    gates, groups, cores = sizes["gate"], sizes["edge"], sizes["grp"]
    gate, group, core = lax.axis_index("gate"), lax.axis_index("edge"), lax.axis_index("grp")
    place = jnp.stack([gate, core]).astype(jnp.int32)
    axes = (("grp", cores), ("gate", gates), ("edge", groups))

    wide_rows = edge_second[:EDGE_HID].astype(BF).T
    half = wide_rows.shape[0] // 2
    halves = wide_rows.reshape(2, half, H)
    own = pick(halves, core)
    second = [own, pick(halves, 1 - core)]
    for step in range(1, gates):
        got = swap(own, "gate", gates, step)
        second += [got, swap(got, "grp", cores, 1)]
    small_parts = [
        exact3(edge_second[EDGE_HID]),
        gru_weight[:, :H].astype(BF).transpose(0, 2, 3, 1),
        exact3(gru_weight[:, H]),
        embed_weight.astype(BF).T,
    ]
    lines = [flat_rows(part) for part in small_parts]
    counts = [line.shape[0] for line in lines]
    tail = up(sum(counts), 16)
    lines = jnp.pad(jnp.concatenate(lines, axis=0), ((0, tail - sum(counts)), (0, 0)))
    tails = jnp.stack([lines] + [swap(lines, "gate", gates, step) for step in range(1, gates)])
    order = [jnp.stack([tails[index ^ step] for index in range(gates)]) for step in range(gates)]
    tails = order[0]
    for step in range(1, gates):
        tails = jnp.where(gate == step, order[step], tails)
    begins = [sum(counts[:index]) for index in range(len(counts))]
    pieces = [
        tails[:, begin : begin + count].reshape(gates, -1)[:, : part.size].reshape((gates,) + part.shape)
        for begin, count, part in zip(begins, counts, small_parts)
    ]
    bias = pieces[0].reshape(gates, 3, 2, half).transpose(0, 2, 1, 3).reshape(gates * 2, 3, half)
    bias = jnp.pad(bias, ((0, 0), (0, DEEP - H - 3), (0, 0)))
    gru = pieces[1].transpose(1, 2, 0, 3, 4).reshape(2, 3 * H, H)
    gru_bias = jnp.sum(pieces[2].astype(F32), axis=1).transpose(1, 2, 0, 3).reshape(2, 3 * H, 1)
    embed_t = pieces[3].reshape(H, -1)

    columns = jnp.arange(NT)[None, :]
    present = jnp.maximum(flag[:, None], (columns < NT // 2).astype(jnp.int32)).astype(F32)
    count = jnp.sum(present).reshape(1, 1)
    count = count + swap(count, "grp", cores, 1)

    nodes = node_feat.shape[0]
    edges = source.shape[0]
    mols = target.shape[0]
    wide_nodes = padded_nodes(nodes)
    wide_edges = up(edges, BLK)
    one_hot = (bond[:, None] == jnp.arange(BONDS)[None, :]).astype(BF)
    src_one = source + 1
    tgt_one = target_node + 1
    index = jnp.stack([src_one >> 4, src_one & 15, tgt_one >> 4, tgt_one & 15], axis=1).astype(BF)
    data = jnp.concatenate([one_hot, dist_feat, jnp.ones((edges, 1), BF), index], axis=1)
    data = jnp.pad(data, ((0, wide_edges - edges), (0, H - data.shape[1])))
    src2d = jnp.pad(source, (0, wide_edges - edges), constant_values=-1).reshape(-1, BLK)
    src2d = jnp.pad(src2d, ((0, up(src2d.shape[0], 16) - src2d.shape[0]), (0, 0)), constant_values=-1)
    mol = jnp.pad(mol_id, (0, wide_nodes - nodes), constant_values=1 << 20).reshape(1, wide_nodes)
    nf_t = jnp.pad(node_feat.T, ((0, 0), (0, wide_nodes - nodes)))
    first_t = jnp.pad(edge_first.T, ((0, 0), (0, FEAT - EIN - 1)))
    first3 = exact3(first_t).reshape(3 * H, FEAT)
    lstm = jnp.pad(set_lstm, ((0, 7), (0, 0)))
    head = jnp.pad(head_weight, ((0, 7), (0, H - NT)))

    scal, pre, eh_t, eh, feat, idx = prep(place, mol, src2d, data, first3, edges, gates)
    scal, count = lax.optimization_barrier((scal, count))
    hid, msg, state, near, mats = forward(place, scal, nf_t, embed_t, bias, gru, gru_bias, eh_t, idx, second)
    inverse = (1.0 / tree_sum(count, "edge", groups)).reshape(1)
    d_final, d_lstm, d_head = readout(
        scal, inverse, hid[STEPS], mol, lstm, head,
        jnp.pad(present, ((0, H - mols), (0, H - NT))), jnp.pad(target, ((0, H - mols), (0, H - NT))),
    )
    read = jnp.concatenate([d_lstm.reshape(-1, H), d_head], axis=0)
    read = jnp.pad(read, ((0, up(read.shape[0], 16) - read.shape[0]), (0, 0)))

    def read_chain():
        parts = read.reshape(cores, -1, H)
        (got,) = yield [swap(pick(parts, 1 - core), "grp", cores, 1)]
        value = pick(parts, core) + got
        for axis, size in (("gate", gates), ("edge", groups)):
            step = 1
            while step < size:
                (got,) = yield [swap(value, axis, size, step)]
                value = value + got
                step *= 2
        (got,) = yield [swap(value, "grp", cores, 1)]
        return jnp.where(core == 0, jnp.concatenate([value, got]), jnp.concatenate([got, value]))

    fresh = read_chain()
    chains = [("read", fresh, next(fresh))]
    far, small = backward(
        place, scal, nf_t, gru, gru_bias, idx, hid, msg, state, near, d_final, mats
    )
    (small, far), moved = lax.optimization_barrier(((small, far), [arrays for _, _, arrays in chains]))

    def narrow_chain():
        (got,) = yield [swap(small, "grp", cores, 1)]
        parts = small + got
        moved = yield [swap(pick(parts, gate ^ step), "gate", gates, step) for step in range(1, gates)]
        value = pick(parts, gate)
        for got in moved:
            value = value + got
        step = 1
        while step < groups:
            (got,) = yield [swap(value, "edge", groups, step)]
            value = value + got
            step *= 2
        return value

    def wide_chain(mine, other, step):
        (got,) = yield [swap(other, "grp", cores, 1)]
        part = mine + got
        if step:
            (part,) = yield [swap(part.astype(BF), "gate", gates, step)]
        return part.astype(F32)

    results = {}

    def advance(chains, moved):
        out = []
        for (name, chain, _), values in zip(chains, moved):
            try:
                out.append((name, chain, chain.send(values)))
            except StopIteration as stop:
                results[name] = stop.value
        return out

    first = jnp.zeros((FEAT, H), F32)
    chains = advance(chains, moved)
    fresh = narrow_chain()
    chains.append(("narrow", fresh, next(fresh)))
    for step in reversed(range(gates)):
        mine, other, first = edge_grads(
            place, scal, second[2 * step], second[2 * step + 1], near, far, eh, pre, feat, first, step, half
        )
        first, moved = lax.optimization_barrier((first, [arrays for _, _, arrays in chains]))
        chains = advance(chains, moved)
        fresh = wide_chain(mine, other, step)
        chains.append((step, fresh, next(fresh)))
    while chains:
        chains = advance(chains, [arrays for _, _, arrays in chains])
    read = results["read"]
    head_begin = d_lstm.shape[0] * 4
    by_query = read[: 4 * H].reshape(H, 4 * H)
    by_rest = read[4 * H : 4 * (2 * H + 1)].reshape(H + 1, 4 * H)
    grad_lstm = jnp.concatenate([by_query, by_rest[:H], by_query, by_rest[H:]], axis=0)
    grad_head = read[head_begin : head_begin + 2 * H + 1, :NT]
    loss = read[head_begin + 2 * H + 8, 0]
    small = results["narrow"]
    tall = H + 16
    grad_gru = small[: 2 * tall, : 3 * width].reshape(2, tall, 3, width)[:, : H + 1]
    grad_embed = small[:16, 3 * width :]
    grad_bias = small[2 * tall :].reshape(1, width * H)
    total = results[0]
    for step in range(1, gates):
        total = total + results[step]
    rows = up(half, 16 * groups)
    total = jnp.pad(total, ((0, rows - half), (0, 0)))
    shard = scatter_sum(total, "edge", groups, group)
    for axis, size in axes:
        first = butterfly(first, axis, size)
    grad_first = first[: EIN + 1]
    whole_sq = jnp.sum(grad_lstm * grad_lstm) + jnp.sum(grad_head * grad_head) + jnp.sum(grad_first * grad_first)
    shard = gather_all(scaled(shard), "edge", groups, group)
    shard = gather_all(shard, "grp", cores, core)
    shard = unscaled(shard.reshape(cores, groups, -1, H)).reshape(cores, -1, H)[:, :half].reshape(-1, H)
    squares = (jnp.sum(shard * shard) + jnp.sum(small * small)).reshape(1, 1)
    squares = tree_sum(squares, "gate", gates)
    grad_second = jnp.concatenate([shard.T, grad_bias], axis=0)

    norm = jnp.sqrt(squares[0, 0] + whole_sq)
    factor = jnp.minimum(1.0, CLIP / norm)
    grads = (grad_embed, grad_first, grad_second, grad_gru, grad_lstm, grad_head)
    params = (embed_weight, edge_first, edge_second, gru_weight, set_lstm, head_weight)
    moms = (mom_embed, mom_first, mom_second, mom_gru, mom_lstm, mom_head)
    varis = (var_embed, var_first, var_second, var_gru, var_lstm, var_head)
    stepno = step_count[0].astype(F32)
    results = [
        adamw(params[index], grads[index] * factor, moms[index], varis[index], RATES[index], stepno)
        for index in range(6)
    ]
    return (loss, norm) + tuple(results[index][kind] for kind in range(3) for index in range(6))


def solution(mesh):
    rows = P(("grp", "edge"), None)
    line = P(("grp", "edge"))
    cols = P(None, "gate")
    deep = P(None, None, None, "gate")
    weights = (cols, P(), cols, deep, P(), P())
    return jax.shard_map(
        functools.partial(on_device, sizes=dict(mesh.shape)),
        mesh=mesh,
        in_specs=(rows, rows, line, line, line, line, line, rows) + weights * 3 + (P(),),
        out_specs=(P(), P()) + weights * 3,
        check_vma=False,
    )
```

profile of v0, /device:TPU:0, one launch (start us, length us, event | category | flops | bytes accessed | tf_op | source)
XLA Modules:
  0.0 387.6 jit_solution(6906991512183574089)
XLA Ops:
  0.7 1.7 fusion.1
  4.0 2.9 collective-permute-start.7
  7.0 1.5 collective-permute-start.9
  10.7 2.0 collective-permute-start.6
  14.2 1.9 concatenate.28
  23.3 7.9 %prep.1 = (s32[8]{0:T(128)}, f32[128,5120]{1,0:T(8,128)}, bf16[144,5120]{1,0:T(8,128)(2,1)}, bf16[5120,128]{1,0:T(8,128)(2,1)}, bf16[32,5120]{1,0:T(8,128)(2,1)}, /*index=5*/s32[8,5120]{1,0:T(8,128)}) custom-call(s32[2]{0:T(128)} %pad_add_fusion.place, s32[1,3200]{1,0:T(1,128)} %reshape.178.mol, s32[32,256]{1,0:T(8,128)} %pad.55.src2d, ...), custom_call_target="tpu_custom_call" | custom-call | tf_op jit(solution)/shard_map/prep/pallas_call | solution.py:175
  32.5 2.9 collective-permute-start.1
  36.2 3.9 %collective-permute-start.2 = (f32[1,1]{1,0:T(1,128)}, f32[1,1]{1,0:T(1,128)}, u32[]{:S(2)}, u32[]{:S(2)}) collective-permute-start(f32[1,1]{1,0:T(1,128)} %add.295), channel_id=1, source_target_pairs={{0,8},{4,12},{8,0},{12,4},{1,9},{5,13},{9,1},{13,5},{2,10},{6,14},... | collective-permute-start | bytes 20 | tf_op jit(solution)/shard_map/ppermute | solution.py:811
  40.7 4.9 %collective-permute-start.3 = (f32[1,1]{1,0:T(1,128)}, f32[1,1]{1,0:T(1,128)}, u32[]{:S(2)}, u32[]{:S(2)}) collective-permute-start(f32[1,1]{1,0:T(1,128)} %add.295), channel_id=1, source_target_pairs={{0,12},{4,8},{8,4},{12,0},{1,13},{5,9},{9,5},{13,1},{2,14},{6,10},... | collective-permute-start | bytes 20 | tf_op jit(solution)/shard_map/ppermute | solution.py:811
  46.2 1.5 collective-permute-start.5
  50.6 2.4 collective-permute-done.4
  58.0 58.9 %forward.1 = (bf16[4,128,3200]{2,1,0:T(8,128)(2,1)}, bf16[3,128,3200]{2,1,0:T(8,128)(2,1)}, f32[4,128,3200]{2,1,0:T(8,128)}, bf16[3,128,5120]{2,1,0:T(8,128)(2,1)}, bf16[40,4,4096,128]{3,2,1,0:T(8,128)(2,1)}) custom-call(s32[2]{0:T(128)} %pad_add_fusion.place, s32[8]{0:T(128)} %get-tuple-element.73.scal, bf16[16,3200]{1,0:T(8,128)(2,1)} %pad.58.nf_t, ...), custom_call_target="tpu_custom_call" | custom-call | flops 60000002048 | bytes 20000000 | tf_op jit(solution)/shard_map/forward/pallas_call | solution.py:413
  116.9 2.1 slice_bitcast_fusion.final
  119.0 21.8 %readout.1 = (f32[128,3200]{1,0:T(8,128)}, f32[264,512]{1,0:T(8,128)}, f32[272,128]{1,0:T(8,128)}) custom-call(s32[8]{0:T(128)} %get-tuple-element.73.scal, f32[1]{0:T(128)} %bitcast.8.inverse, bf16[128,3200]{1,0:T(8,128)(2,1)} %slice_bitcast_fusion.final, s32[1,3200]{1,0:T(1,128)} %reshape.178.mol, f32[392,512]{1,0:T(8,128)} %pad.62.lstm, ...), custom_call_target="tpu_custom_call" | custom-call | flops 30000001024 | bytes 5000000 | tf_op jit(solution)/shard_map/readout/pallas_call | solution.py:571
  143.1 54.9 %backward.1 = (bf16[3,128,5120]{2,1,0:T(8,128)(2,1)}, f32[4,320,128]{2,1,0:T(8,128)}) custom-call(s32[2]{0:T(128)} %pad_add_fusion.place, s32[8]{0:T(128)} %get-tuple-element.73.scal, bf16[16,3200]{1,0:T(8,128)(2,1)} %pad.58.nf_t, bf16[2,384,128]{2,1,0:T(8,128)(2,1)} %bitcast.122, f32[2,384,1]{2,1,0:T(8,128)} %reshape.199.gru_bias, ...), custom_call_target="tpu_custom_call" | custom-call | flops 60000002048 | bytes 20000000 | tf_op jit(solution)/shard_map/backward/pallas_call | solution.py:686
  199.8 11.4 %edge_grads.4 = (f32[2048,128]{1,0:T(8,128)}, f32[2048,128]{1,0:T(8,128)}, f32[32,128]{1,0:T(8,128)}) custom-call(s32[2]{0:T(128)} %pad_add_fusion.place, s32[8]{0:T(128)} %get-tuple-element.73.scal, bf16[2048,128]{1,0:T(8,128)(2,1)} %collective-permute-done.11.refs_6_.mine, bf16[2048,128]{1,0:T(8,128)(2,1)} %copy-done.48, ...), custom_call_target="tpu_custom_call" | custom-call | flops 8999999488 | bytes 5000000 | tf_op jit(solution)/shard_map/edge_grads/pallas_call | solution.py:779
  213.3 12.8 %collective-permute-start.16 = (f32[664,128]{0,1:T(8,128)S(1)}, f32[664,128]{0,1:T(8,128)S(1)}, u32[]{:S(2)}, u32[]{:S(2)}) collective-permute-start(f32[664,128]{0,1:T(8,128)S(1)} %add.302), channel_id=1, source_target_pairs={{0,2},{1,3},{2,0},{3,1},{4,6},{5,7},{6,4},{7,5},{8,10},{9,11},{10,... | collective-permute-start | bytes 1019912 | tf_op jit(solution)/shard_map/ppermute | solution.py:811
  227.1 3.3 collective-permute-start.19
  230.4 11.5 %edge_grads.5 = (f32[2048,128]{1,0:T(8,128)}, f32[2048,128]{1,0:T(8,128)}, f32[32,128]{1,0:T(8,128)}) custom-call(s32[2]{0:T(128)} %pad_add_fusion.place, s32[8]{0:T(128)} %get-tuple-element.73.scal, bf16[2048,128]{1,0:T(8,128)(2,1)} %collective-permute-done.9.refs_4_.mine, bf16[2048,128]{1,0:T(8,128)(2,1)} %copy-done.47, ...), custom_call_target="tpu_custom_call" | custom-call | flops 8999999488 | bytes 5000000 | tf_op jit(solution)/shard_map/edge_grads/pallas_call | solution.py:779
  246.5 1.8 collective-permute-start.23
  248.3 11.3 %edge_grads.6 = (f32[2048,128]{1,0:T(8,128)}, f32[2048,128]{1,0:T(8,128)}, f32[32,128]{1,0:T(8,128)}) custom-call(s32[2]{0:T(128)} %pad_add_fusion.place, s32[8]{0:T(128)} %get-tuple-element.73.scal, bf16[2048,128]{1,0:T(8,128)(2,1)} %collective-permute-done.7.refs_2_.mine, bf16[2048,128]{1,0:T(8,128)(2,1)} %copy-done.46, ...), custom_call_target="tpu_custom_call" | custom-call | flops 8999999488 | bytes 5000000 | tf_op jit(solution)/shard_map/edge_grads/pallas_call | solution.py:779
  262.1 2.4 collective-permute-start.25
  267.0 11.4 %edge_grads.7 = (f32[2048,128]{1,0:T(8,128)}, f32[2048,128]{1,0:T(8,128)}, f32[32,128]{1,0:T(8,128)}) custom-call(s32[2]{0:T(128)} %pad_add_fusion.place, s32[8]{0:T(128)} %get-tuple-element.73.scal, bf16[2048,128]{1,0:T(8,128)(2,1)} %copy-done.20, bf16[2048,128]{1,0:T(8,128)(2,1)} %get-tuple-element.211.refs_1_.other, ...), custom_call_target="tpu_custom_call" | custom-call | flops 8999999488 | bytes 5000000 | tf_op jit(solution)/shard_map/edge_grads/pallas_call | solution.py:779
  278.5 11.0 %collective-permute-done.26 = f32[320,128]{1,0:T(8,128)} collective-permute-done((f32[320,128]{1,0:T(8,128)S(1)}, f32[320,128]{1,0:T(8,128)}, u32[]{:S(2)}, u32[]{:S(2)}) %collective-permute-start.26) | collective-permute-done | bytes 163872 | tf_op jit(solution)/shard_map/ppermute | solution.py:811
  290.3 1.3 add_convert_fusion
  294.9 10.0 %collective-permute-done.43 = f32[32,128]{1,0:T(8,128)S(1)} collective-permute-done((f32[32,128]{1,0:T(8,128)S(1)}, f32[32,128]{1,0:T(8,128)S(1)}, u32[]{:S(2)}, u32[]{:S(2)}) %collective-permute-start.43) | collective-permute-done | bytes 16416 | tf_op jit(solution)/shard_map/ppermute | solution.py:811
  304.9 3.7 collective-permute-done.44
  308.7 1.7 collective-permute-start.45
  311.1 1.4 collective-permute-done.45
  313.2 3.1 collective-permute-start.46
  317.2 2.2 abs_reduce_fusion
  320.4 1.5 collective-permute-start.34
  321.9 2.0 collective-permute-start.33
  324.9 2.2 multiply_reduce_fusion.2
  329.8 1.3 multiply_reduce_fusion.4
  339.1 2.6 collective-permute-start.37
  341.7 2.2 collective-permute-done.35
  344.0 6.9 %collective-permute-done.36 = f16[528,128]{1,0:T(8,128)(2,1)S(1)} collective-permute-done((f16[528,128]{1,0:T(8,128)(2,1)S(1)}, f16[528,128]{1,0:T(8,128)(2,1)S(1)}, u32[]{:S(2)}, u32[]{:S(2)}) %collective-permute-start.36) | collective-permute-done | bytes 135200 | tf_op jit(solution)/shard_map/ppermute | solution.py:811
  359.9 1.9 collective-permute-start.39
  361.8 1.6 collective-permute-start.40
  363.4 4.0 %collective-permute-start.41 = (f32[1,1]{1,0:T(1,128)}, f32[1,1]{1,0:T(1,128)}, u32[]{:S(2)}, u32[]{:S(2)}) collective-permute-start(f32[1,1]{1,0:T(1,128)} %bitcast.48), channel_id=1, source_target_pairs={{0,3},{1,2},{2,1},{3,0},{4,7},{5,6},{6,5},{7,4},{8,11},{9,10},{10,... | collective-permute-start | bytes 20 | tf_op jit(solution)/shard_map/ppermute | solution.py:811
  367.4 1.8 copy.166
  371.2 1.5 multiply_subtract_fusion.5
  372.7 3.4 multiply_subtract_fusion.1
  376.1 1.5 multiply_subtract_fusion.3
  377.5 1.9 multiply_subtract_fusion.2
  379.5 5.7 %multiply_subtract_fusion = (f32[129,4096]{1,0:T(8,128)}, f32[129,4096]{1,0:T(8,128)}, f32[129,4096]{1,0:T(8,128)}) fusion(f32[129,4096]{1,0:T(8,128)S(1)} %copy-done.1, f32[]{:T(128)} %bitcast.52, f32[]{:T(128)} %bitcast.51, f32[]{:T(128)S(6)} %min.3, f32[1,4096]{1,0:T(1,128)S(1)} %bitcast.128, f32[128,4096]{1,0:T(8,128)S(1)} %bitcast.106, ...), kind=kLoop, calls=%fused_computation.3 | loop fusion | flops 8982528 | bytes 14794764 | tf_op jit(solution)/shard_map/sub | solution.py:874
  385.2 1.3 multiply_subtract_fusion.4
  (285 shorter events, 57.2 us)
Async XLA Ops:
  4.0 45.8 %collective-permute-start.7 = (bf16[2048,128]{1,0:T(8,128)(2,1)S(1)}, bf16[2048,128]{1,0:T(8,128)(2,1)}, u32[]{:S(2)}, u32[]{:S(2)}) collective-permute-start(bf16[2048,128]{1,0:T(8,128)(2,1)S(1)} %get-tuple-element.212.refs_0_.mine), channel_id=1, source_target_pairs={{0,1},{1,0},{2,3},{3,2},{4,5},{5,4},{6,7},{7,6},{8,9},{9,8},{10,11... | collective-permute-start | bytes 1572872 | tf_op jit(solution)/shard_map/ppermute | solution.py:811
  7.0 43.0 %collective-permute-start.9 = (bf16[2048,128]{1,0:T(8,128)(2,1)S(1)}, bf16[2048,128]{1,0:T(8,128)(2,1)}, u32[]{:S(2)}, u32[]{:S(2)}) collective-permute-start(bf16[2048,128]{1,0:T(8,128)(2,1)S(1)} %get-tuple-element.212.refs_0_.mine), channel_id=1, source_target_pairs={{0,2},{1,3},{2,0},{3,1},{4,6},{5,7},{6,4},{7,5},{8,10},{9,11},{10,... | collective-permute-start | bytes 1572872 | tf_op jit(solution)/shard_map/ppermute | solution.py:811
  8.5 41.9 %collective-permute-start.11 = (bf16[2048,128]{1,0:T(8,128)(2,1)S(1)}, bf16[2048,128]{1,0:T(8,128)(2,1)}, u32[]{:S(2)}, u32[]{:S(2)}) collective-permute-start(bf16[2048,128]{1,0:T(8,128)(2,1)S(1)} %get-tuple-element.212.refs_0_.mine), channel_id=1, source_target_pairs={{0,3},{1,2},{2,1},{3,0},{4,7},{5,6},{6,5},{7,4},{8,11},{9,10},{10,... | collective-permute-start | bytes 1572872 | tf_op jit(solution)/shard_map/ppermute | solution.py:811
  9.2 22.0 %collective-permute-start = (f32[1,1]{1,0:T(1,128)}, f32[1,1]{1,0:T(1,128)}, u32[]{:S(2)}, u32[]{:S(2)}) collective-permute-start(f32[1,1]{1,0:T(1,128)} %bitcast.7), channel_id=1, source_target_pairs={{0,16},{16,0},{1,17},{17,1},{2,18},{18,2},{3,19},{19,3},{4,20},{20... | collective-permute-start | bytes 20 | tf_op jit(solution)/shard_map/ppermute | solution.py:811
  10.7 36.9 %collective-permute-start.6 = (bf16[304,128]{1,0:T(8,128)(2,1)S(1)}, bf16[304,128]{1,0:T(8,128)(2,1)S(1)}, u32[]{:S(2)}, u32[]{:S(2)}) collective-permute-start(bf16[304,128]{1,0:T(8,128)(2,1)S(1)} %fusion.18), channel_id=1, source_target_pairs={{0,1},{1,0},{2,3},{3,2},{4,5},{5,4},{6,7},{7,6},{8,9},{9,8},{10,11... | collective-permute-start | bytes 233480 | tf_op jit(solution)/shard_map/ppermute | solution.py:811
  32.5 3.7 collective-permute-start.1
  36.2 4.5 %collective-permute-start.2 = (f32[1,1]{1,0:T(1,128)}, f32[1,1]{1,0:T(1,128)}, u32[]{:S(2)}, u32[]{:S(2)}) collective-permute-start(f32[1,1]{1,0:T(1,128)} %add.295), channel_id=1, source_target_pairs={{0,8},{4,12},{8,0},{12,4},{1,9},{5,13},{9,1},{13,5},{2,10},{6,14},... | collective-permute-start | bytes 20 | tf_op jit(solution)/shard_map/ppermute | solution.py:811
  40.7 5.4 %collective-permute-start.3 = (f32[1,1]{1,0:T(1,128)}, f32[1,1]{1,0:T(1,128)}, u32[]{:S(2)}, u32[]{:S(2)}) collective-permute-start(f32[1,1]{1,0:T(1,128)} %add.295), channel_id=1, source_target_pairs={{0,12},{4,8},{8,4},{12,0},{1,13},{5,9},{9,5},{13,1},{2,14},{6,10},... | collective-permute-start | bytes 20 | tf_op jit(solution)/shard_map/ppermute | solution.py:811
  46.2 4.4 %collective-permute-start.5 = (bf16[304,128]{1,0:T(8,128)(2,1)S(1)}, bf16[304,128]{1,0:T(8,128)(2,1)S(1)}, u32[]{:S(2)}, u32[]{:S(2)}) collective-permute-start(bf16[304,128]{1,0:T(8,128)(2,1)S(1)} %fusion.18), channel_id=1, source_target_pairs={{0,2},{1,3},{2,0},{3,1},{4,6},{5,7},{6,4},{7,5},{8,10},{9,11},{10,... | collective-permute-start | bytes 233480 | tf_op jit(solution)/shard_map/ppermute | solution.py:811
  47.7 5.3 %collective-permute-start.4 = (bf16[304,128]{1,0:T(8,128)(2,1)S(1)}, bf16[304,128]{1,0:T(8,128)(2,1)S(1)}, u32[]{:S(2)}, u32[]{:S(2)}) collective-permute-start(bf16[304,128]{1,0:T(8,128)(2,1)S(1)} %fusion.18), channel_id=1, source_target_pairs={{0,3},{1,2},{2,1},{3,0},{4,7},{5,6},{6,5},{7,4},{8,11},{9,10},{10,... | collective-permute-start | bytes 233480 | tf_op jit(solution)/shard_map/ppermute | solution.py:811
  49.8 7.0 %collective-permute-start.8 = (bf16[2048,128]{1,0:T(8,128)(2,1)}, bf16[2048,128]{1,0:T(8,128)(2,1)S(1)}, u32[]{:S(2)}, u32[]{:S(2)}) collective-permute-start(bf16[2048,128]{1,0:T(8,128)(2,1)} %collective-permute-done.7.refs_2_.mine), channel_id=1, source_target_pairs={{0,16},{16,0},{1,17},{17,1},{2,18},{18,2},{3,19},{19,3},{4,20},{20... | collective-permute-start | bytes 1572872 | tf_op jit(solution)/shard_map/ppermute | solution.py:811
  49.9 6.9 %collective-permute-start.10 = (bf16[2048,128]{1,0:T(8,128)(2,1)}, bf16[2048,128]{1,0:T(8,128)(2,1)S(1)}, u32[]{:S(2)}, u32[]{:S(2)}) collective-permute-start(bf16[2048,128]{1,0:T(8,128)(2,1)} %collective-permute-done.9.refs_4_.mine), channel_id=1, source_target_pairs={{0,16},{16,0},{1,17},{17,1},{2,18},{18,2},{3,19},{19,3},{4,20},{20... | collective-permute-start | bytes 1572872 | tf_op jit(solution)/shard_map/ppermute | solution.py:811
  50.4 6.4 %collective-permute-start.12 = (bf16[2048,128]{1,0:T(8,128)(2,1)}, bf16[2048,128]{1,0:T(8,128)(2,1)S(1)}, u32[]{:S(2)}, u32[]{:S(2)}) collective-permute-start(bf16[2048,128]{1,0:T(8,128)(2,1)} %collective-permute-done.11.refs_6_.mine), channel_id=1, source_target_pairs={{0,16},{16,0},{1,17},{17,1},{2,18},{18,2},{3,19},{19,3},{4,20},{20... | collective-permute-start | bytes 1572872 | tf_op jit(solution)/shard_map/ppermute | solution.py:811
  143.1 55.2 %collective-permute-start.13 = (f32[664,128]{0,1:T(8,128)S(1)}, f32[664,128]{0,1:T(8,128)S(1)}, u32[]{:S(2)}, u32[]{:S(2)}) collective-permute-start(f32[664,128]{0,1:T(8,128)S(1)} %bitcast.118), channel_id=1, source_target_pairs={{0,16},{16,0},{1,17},{17,1},{2,18},{18,2},{3,19},{19,3},{4,20},{20... | collective-permute-start | bytes 1019912 | tf_op jit(solution)/shard_map/ppermute | solution.py:811
  198.3 13.3 %collective-permute-start.14 = (f32[664,128]{0,1:T(8,128)S(1)}, f32[664,128]{0,1:T(8,128)S(1)}, u32[]{:S(2)}, u32[]{:S(2)}) collective-permute-start(f32[664,128]{0,1:T(8,128)S(1)} %bitcast_add_fusion), channel_id=1, source_target_pairs={{0,1},{1,0},{2,3},{3,2},{4,5},{5,4},{6,7},{7,6},{8,9},{9,8},{10,11... | collective-permute-start | bytes 1019912 | tf_op jit(solution)/shard_map/ppermute | solution.py:811
  198.9 12.6 %collective-permute-start.15 = (f32[4,320,128]{2,1,0:T(8,128)}, f32[4,320,128]{2,1,0:T(8,128)S(1)}, u32[]{:S(2)}, u32[]{:S(2)}) collective-permute-start(f32[4,320,128]{2,1,0:T(8,128)} %get-tuple-element.93), channel_id=1, source_target_pairs={{0,16},{16,0},{1,17},{17,1},{2,18},{18,2},{3,19},{19,3},{4,20},{20... | collective-permute-start | bytes 1966088 | tf_op jit(solution)/shard_map/ppermute | solution.py:811
  211.2 31.3 %collective-permute-start.20 = (f32[2048,128]{1,0:T(8,128)}, f32[2048,128]{1,0:T(8,128)S(1)}, u32[]{:S(2)}, u32[]{:S(2)}) collective-permute-start(f32[2048,128]{1,0:T(8,128)} %get-tuple-element.98), channel_id=1, source_target_pairs={{0,16},{16,0},{1,17},{17,1},{2,18},{18,2},{3,19},{19,3},{4,20},{20... | collective-permute-start | bytes 3145736 | tf_op jit(solution)/shard_map/ppermute | solution.py:811
  213.3 29.1 %collective-permute-start.16 = (f32[664,128]{0,1:T(8,128)S(1)}, f32[664,128]{0,1:T(8,128)S(1)}, u32[]{:S(2)}, u32[]{:S(2)}) collective-permute-start(f32[664,128]{0,1:T(8,128)S(1)} %add.302), channel_id=1, source_target_pairs={{0,2},{1,3},{2,0},{3,1},{4,6},{5,7},{6,4},{7,5},{8,10},{9,11},{10,... | collective-permute-start | bytes 1019912 | tf_op jit(solution)/shard_map/ppermute | solution.py:811
  226.9 15.0 %collective-permute-start.17 = (f32[320,128]{1,0:T(8,128)S(1)}, f32[320,128]{1,0:T(8,128)S(1)}, u32[]{:S(2)}, u32[]{:S(2)}) collective-permute-start(f32[320,128]{1,0:T(8,128)S(1)} %get-tuple-element.219), channel_id=1, source_target_pairs={{0,1},{1,0},{2,3},{3,2},{4,5},{5,4},{6,7},{7,6},{8,9},{9,8},{10,11... | collective-permute-start | bytes 491528 | tf_op jit(solution)/shard_map/ppermute | solution.py:811
  227.1 15.4 %collective-permute-start.18 = (f32[320,128]{1,0:T(8,128)}, f32[320,128]{1,0:T(8,128)S(1)}, u32[]{:S(2)}, u32[]{:S(2)}) collective-permute-start(f32[320,128]{1,0:T(8,128)} %get-tuple-element.218), channel_id=1, source_target_pairs={{0,2},{1,3},{2,0},{3,1},{4,6},{5,7},{6,4},{7,5},{8,10},{9,11},{10,... | collective-permute-start | bytes 491528 | tf_op jit(solution)/shard_map/ppermute | solution.py:811
  227.1 15.3 %collective-permute-start.19 = (f32[320,128]{1,0:T(8,128)}, f32[320,128]{1,0:T(8,128)S(1)}, u32[]{:S(2)}, u32[]{:S(2)}) collective-permute-start(f32[320,128]{1,0:T(8,128)} %get-tuple-element.217), channel_id=1, source_target_pairs={{0,3},{1,2},{2,1},{3,0},{4,7},{5,6},{6,5},{7,4},{8,11},{9,10},{10,... | collective-permute-start | bytes 491528 | tf_op jit(solution)/shard_map/ppermute | solution.py:811
  242.0 18.9 %collective-permute-start.24 = (f32[2048,128]{1,0:T(8,128)}, f32[2048,128]{1,0:T(8,128)S(1)}, u32[]{:S(2)}, u32[]{:S(2)}) collective-permute-start(f32[2048,128]{1,0:T(8,128)} %get-tuple-element.107), channel_id=1, source_target_pairs={{0,16},{16,0},{1,17},{17,1},{2,18},{18,2},{3,19},{19,3},{4,20},{20... | collective-permute-start | bytes 3145736 | tf_op jit(solution)/shard_map/ppermute | solution.py:811
  244.2 15.6 %collective-permute-start.21 = (f32[664,128]{0,1:T(8,128)S(1)}, f32[664,128]{0,1:T(8,128)}, u32[]{:S(2)}, u32[]{:S(2)}) collective-permute-start(f32[664,128]{0,1:T(8,128)S(1)} %add.307), channel_id=1, source_target_pairs={{0,4},{4,0},{8,12},{12,8},{1,5},{5,1},{9,13},{13,9},{2,6},{6,2},{1... | collective-permute-start | bytes 1019912 | tf_op jit(solution)/shard_map/ppermute | solution.py:811
  245.3 14.5 %collective-permute-start.22 = (f32[320,128]{1,0:T(8,128)S(1)}, f32[320,128]{1,0:T(8,128)S(1)}, u32[]{:S(2)}, u32[]{:S(2)}) collective-permute-start(f32[320,128]{1,0:T(8,128)S(1)} %fusion.7), channel_id=1, source_target_pairs={{0,4},{4,0},{8,12},{12,8},{1,5},{5,1},{9,13},{13,9},{2,6},{6,2},{1... | collective-permute-start | bytes 491528 | tf_op jit(solution)/shard_map/ppermute | solution.py:811
  246.5 14.4 %collective-permute-start.23 = (bf16[2048,128]{1,0:T(8,128)(2,1)S(1)}, bf16[2048,128]{1,0:T(8,128)(2,1)S(1)}, u32[]{:S(2)}, u32[]{:S(2)}) collective-permute-start(bf16[2048,128]{1,0:T(8,128)(2,1)S(1)} %add_convert_fusion.2), channel_id=1, source_target_pairs={{0,3},{1,2},{2,1},{3,0},{4,7},{5,6},{6,5},{7,4},{8,11},{9,10},{10,... | collective-permute-start | bytes 1572872 | tf_op jit(solution)/shard_map/ppermute | solution.py:811
  259.7 29.9 %collective-permute-start.28 = (f32[2048,128]{1,0:T(8,128)}, f32[2048,128]{1,0:T(8,128)}, u32[]{:S(2)}, u32[]{:S(2)}) collective-permute-start(f32[2048,128]{1,0:T(8,128)} %get-tuple-element.114), channel_id=1, source_target_pairs={{0,16},{16,0},{1,17},{17,1},{2,18},{18,2},{3,19},{19,3},{4,20},{20... | collective-permute-start | bytes 3145736 | tf_op jit(solution)/shard_map/ppermute | solution.py:811
  262.1 27.4 %collective-permute-start.25 = (f32[664,128]{0,1:T(8,128)S(1)}, f32[664,128]{0,1:T(8,128)S(1)}, u32[]{:S(2)}, u32[]{:S(2)}) collective-permute-start(f32[664,128]{0,1:T(8,128)S(1)} %add.313), channel_id=1, source_target_pairs={{0,8},{4,12},{8,0},{12,4},{1,9},{5,13},{9,1},{13,5},{2,10},{6,14},... | collective-permute-start | bytes 1019912 | tf_op jit(solution)/shard_map/ppermute | solution.py:811
  264.5 25.0 %collective-permute-start.26 = (f32[320,128]{1,0:T(8,128)S(1)}, f32[320,128]{1,0:T(8,128)}, u32[]{:S(2)}, u32[]{:S(2)}) collective-permute-start(f32[320,128]{1,0:T(8,128)S(1)} %add.314), channel_id=1, source_target_pairs={{0,8},{4,12},{8,0},{12,4},{1,9},{5,13},{9,1},{13,5},{2,10},{6,14},... | collective-permute-start | bytes 491528 | tf_op jit(solution)/shard_map/ppermute | solution.py:811
  266.1 23.4 %collective-permute-start.27 = (bf16[2048,128]{1,0:T(8,128)(2,1)}, bf16[2048,128]{1,0:T(8,128)(2,1)}, u32[]{:S(2)}, u32[]{:S(2)}) collective-permute-start(bf16[2048,128]{1,0:T(8,128)(2,1)} %add_convert_fusion.1), channel_id=1, source_target_pairs={{0,2},{1,3},{2,0},{3,1},{4,6},{5,7},{6,4},{7,5},{8,10},{9,11},{10,... | collective-permute-start | bytes 1572872 | tf_op jit(solution)/shard_map/ppermute | solution.py:811
  278.4 38.7 %copy-start.8 = (f32[2048,128]{1,0:T(8,128)S(1)}, f32[2048,128]{1,0:T(8,128)}, u32[]{:S(2)}) copy-start(f32[2048,128]{1,0:T(8,128)} %get-tuple-element.116) | copy-start | bytes 3145732
  278.4 37.9 %collective-permute-start.30 = (f32[2048,128]{1,0:T(8,128)}, f32[2048,128]{1,0:T(8,128)S(1)}, u32[]{:S(2)}, u32[]{:S(2)}) collective-permute-start(f32[2048,128]{1,0:T(8,128)} %get-tuple-element.117), channel_id=1, source_target_pairs={{0,16},{16,0},{1,17},{17,1},{2,18},{18,2},{3,19},{19,3},{4,20},{20... | collective-permute-start | bytes 3145736 | tf_op jit(solution)/shard_map/ppermute | solution.py:811
  291.6 24.7 %collective-permute-start.31 = (bf16[2048,128]{1,0:T(8,128)(2,1)S(1)}, bf16[2048,128]{1,0:T(8,128)(2,1)S(1)}, u32[]{:S(2)}, u32[]{:S(2)}) collective-permute-start(bf16[2048,128]{1,0:T(8,128)(2,1)S(1)} %add_convert_fusion), channel_id=1, source_target_pairs={{0,1},{1,0},{2,3},{3,2},{4,5},{5,4},{6,7},{7,6},{8,9},{9,8},{10,11... | collective-permute-start | bytes 1572872 | tf_op jit(solution)/shard_map/ppermute | solution.py:811
  292.7 1.2 collective-permute-start.42
  293.9 11.0 %collective-permute-start.43 = (f32[32,128]{1,0:T(8,128)S(1)}, f32[32,128]{1,0:T(8,128)S(1)}, u32[]{:S(2)}, u32[]{:S(2)}) collective-permute-start(f32[32,128]{1,0:T(8,128)S(1)} %add.341), channel_id=1, source_target_pairs={{0,1},{1,0},{2,3},{3,2},{4,5},{5,4},{6,7},{7,6},{8,9},{9,8},{10,11... | collective-permute-start | bytes 49160 | tf_op jit(solution)/shard_map/ppermute | solution.py:811
  304.9 3.7 collective-permute-start.44
  308.7 3.8 collective-permute-start.45
  313.2 16.6 %collective-permute-start.46 = (f32[32,128]{1,0:T(8,128)S(1)}, f32[32,128]{1,0:T(8,128)}, u32[]{:S(2)}, u32[]{:S(2)}) collective-permute-start(f32[32,128]{1,0:T(8,128)S(1)} %add.344), channel_id=1, source_target_pairs={{0,8},{4,12},{8,0},{12,4},{1,9},{5,13},{9,1},{13,5},{2,10},{6,14},... | collective-permute-start | bytes 49160 | tf_op jit(solution)/shard_map/ppermute | solution.py:811
  320.4 10.8 %collective-permute-start.34 = (f16[528,128]{1,0:T(8,128)(2,1)S(1)}, f16[528,128]{1,0:T(8,128)(2,1)S(1)}, u32[]{:S(2)}, u32[]{:S(2)}) collective-permute-start(f16[528,128]{1,0:T(8,128)(2,1)S(1)} %get-tuple-element.222), channel_id=1, source_target_pairs={{0,12},{4,8},{8,4},{12,0},{1,13},{5,9},{9,5},{13,1},{2,14},{6,10},... | collective-permute-start | bytes 405512 | tf_op jit(solution)/shard_map/ppermute | solution.py:811
  321.9 10.8 %collective-permute-start.33 = (f16[528,128]{1,0:T(8,128)(2,1)S(1)}, f16[528,128]{1,0:T(8,128)(2,1)S(1)}, u32[]{:S(2)}, u32[]{:S(2)}) collective-permute-start(f16[528,128]{1,0:T(8,128)(2,1)S(1)} %get-tuple-element.221), channel_id=1, source_target_pairs={{0,8},{4,12},{8,0},{12,4},{1,9},{5,13},{9,1},{13,5},{2,10},{6,14},... | collective-permute-start | bytes 405512 | tf_op jit(solution)/shard_map/ppermute | solution.py:811
  324.0 10.0 %collective-permute-start.32 = (f16[528,128]{1,0:T(8,128)(2,1)S(1)}, f16[528,128]{1,0:T(8,128)(2,1)S(1)}, u32[]{:S(2)}, u32[]{:S(2)}) collective-permute-start(f16[528,128]{1,0:T(8,128)(2,1)S(1)} %get-tuple-element.220), channel_id=1, source_target_pairs={{0,4},{4,0},{8,12},{12,8},{1,5},{5,1},{9,13},{13,9},{2,6},{6,2},{1... | collective-permute-start | bytes 405512 | tf_op jit(solution)/shard_map/ppermute | solution.py:811
  328.8 10.1 %collective-permute-start.29 = (f32[664,128]{0,1:T(8,128)S(1)}, f32[664,128]{0,1:T(8,128)S(1)}, u32[]{:S(2)}, u32[]{:S(2)}) collective-permute-start(f32[664,128]{0,1:T(8,128)S(1)} %add.316), channel_id=1, source_target_pairs={{0,16},{16,0},{1,17},{17,1},{2,18},{18,2},{3,19},{19,3},{4,20},{20... | collective-permute-start | bytes 1019912 | tf_op jit(solution)/shard_map/ppermute | solution.py:811
  336.9 7.0 %collective-permute-start.35 = (f16[528,128]{1,0:T(8,128)(2,1)S(1)}, f16[528,128]{1,0:T(8,128)(2,1)S(1)}, u32[]{:S(2)}, u32[]{:S(2)}) collective-permute-start(f16[528,128]{1,0:T(8,128)(2,1)S(1)} %get-tuple-element.223), channel_id=1, source_target_pairs={{0,4},{4,0},{8,12},{12,8},{1,5},{5,1},{9,13},{13,9},{2,6},{6,2},{1... | collective-permute-start | bytes 405512 | tf_op jit(solution)/shard_map/ppermute | solution.py:811
  337.7 13.1 %collective-permute-start.36 = (f16[528,128]{1,0:T(8,128)(2,1)S(1)}, f16[528,128]{1,0:T(8,128)(2,1)S(1)}, u32[]{:S(2)}, u32[]{:S(2)}) collective-permute-start(f16[528,128]{1,0:T(8,128)(2,1)S(1)} %get-tuple-element.223), channel_id=1, source_target_pairs={{0,8},{4,12},{8,0},{12,4},{1,9},{5,13},{9,1},{13,5},{2,10},{6,14},... | collective-permute-start | bytes 405512 | tf_op jit(solution)/shard_map/ppermute | solution.py:811
  339.1 11.8 %collective-permute-start.37 = (f16[528,128]{1,0:T(8,128)(2,1)S(1)}, f16[528,128]{1,0:T(8,128)(2,1)S(1)}, u32[]{:S(2)}, u32[]{:S(2)}) collective-permute-start(f16[528,128]{1,0:T(8,128)(2,1)S(1)} %get-tuple-element.223), channel_id=1, source_target_pairs={{0,12},{4,8},{8,4},{12,0},{1,13},{5,9},{9,5},{13,1},{2,14},{6,10},... | collective-permute-start | bytes 405512 | tf_op jit(solution)/shard_map/ppermute | solution.py:811
  350.9 4.9 %collective-permute-start.38 = (f16[2112,128]{1,0:T(8,128)(2,1)S(1)}, f16[2112,128]{1,0:T(8,128)(2,1)}, u32[]{:S(2)}, u32[]{:S(2)}) collective-permute-start(f16[2112,128]{1,0:T(8,128)(2,1)S(1)} %constant_dynamic-update-slice_fusion.2), channel_id=1, source_target_pairs={{0,16},{16,0},{1,17},{17,1},{2,18},{18,2},{3,19},{19,3},{4,20},{20... | collective-permute-start | bytes 1622024 | tf_op jit(solution)/shard_map/ppermute | solution.py:811
  359.9 9.3 %collective-permute-start.39 = (f32[1,1]{1,0:T(1,128)}, f32[1,1]{1,0:T(1,128)}, u32[]{:S(2)}, u32[]{:S(2)}) collective-permute-start(f32[1,1]{1,0:T(1,128)} %bitcast.48), channel_id=1, source_target_pairs={{0,1},{1,0},{2,3},{3,2},{4,5},{5,4},{6,7},{7,6},{8,9},{9,8},{10,11... | collective-permute-start | bytes 20 | tf_op jit(solution)/shard_map/ppermute | solution.py:811
  361.8 7.9 %collective-permute-start.40 = (f32[1,1]{1,0:T(1,128)}, f32[1,1]{1,0:T(1,128)}, u32[]{:S(2)}, u32[]{:S(2)}) collective-permute-start(f32[1,1]{1,0:T(1,128)} %bitcast.48), channel_id=1, source_target_pairs={{0,2},{1,3},{2,0},{3,1},{4,6},{5,7},{6,4},{7,5},{8,10},{9,11},{10,... | collective-permute-start | bytes 20 | tf_op jit(solution)/shard_map/ppermute | solution.py:811
  363.4 6.4 %collective-permute-start.41 = (f32[1,1]{1,0:T(1,128)}, f32[1,1]{1,0:T(1,128)}, u32[]{:S(2)}, u32[]{:S(2)}) collective-permute-start(f32[1,1]{1,0:T(1,128)} %bitcast.48), channel_id=1, source_target_pairs={{0,3},{1,2},{2,1},{3,0},{4,7},{5,6},{6,5},{7,4},{8,11},{9,10},{10,... | collective-permute-start | bytes 20 | tf_op jit(solution)/shard_map/ppermute | solution.py:811
  (49 other events, 390.9 us)
where the time goes:
time: 389 us; the launch traced here: 388 us
  Pallas kernels  189 us (49%)
  starting transfers between devices  69.8 us (18%)
  waiting for transfers between devices  42.8 us (11%)
  local copies, waits for them, and re-layouts  35.3 us (9%)
  other arithmetic  35.1 us (9%)
  between operations  15.6 us (4%)
    ppermute x47, starting transfers between devices, swap(): lax.ppermute(value, axis, [(index, index ^ step) for index in range(size)])  69.8 us
    pallas_call x1, Pallas kernels, forward(): pl.pallas_call(functools.partial(forward_kernel, gates=gates), out_shape=...  58.9 us
    pallas_call x1, Pallas kernels, backward(): pl.pallas_call(backward_kernel, out_shape=(jax.ShapeDtypeStruct((STEPS, H...  54.9 us
    pallas_call x4, Pallas kernels, edge_grads(): pl.pallas_call(functools.partial(final_kernel, pair=pair, group=8), in_sp...  45.6 us
    ppermute x47, waiting for transfers between devices, swap(): lax.ppermute(value, axis, [(index, index ^ step) for index in range(size)])  42.8 us
    pallas_call x1, Pallas kernels, readout(): pl.pallas_call(readout_kernel, out_shape=(jax.ShapeDtypeStruct((H, nodes)...  21.8 us
    sub x6, other arithmetic, adamw(): weight - rate * (mom_hat / (jnp.sqrt(var_hat) + EPSILON) + DECAY * weight)  15.2 us
    pallas_call x1, Pallas kernels, prep(): pl.pallas_call(functools.partial(prep_kernel, edges=real, gates=gates, eb...  7.9 us
  transfers between devices with their start and end apart: 47, of which 14 were waited for; matrix products, arithmetic and copies ran while one was open for 10% of the time, Pallas kernels for 28%

commit v1 on v0

--- a/solution.py
+++ b/solution.py
@@ -437,8 +437,11 @@
     )(place, scal, nf_t, embed, bias, gru, gru_bias, eh_t, idx, *second)
 
 
-def readout_kernel(scal, inverse, final, mol, lstm, head, present, target, d_final, d_lstm, d_head, score, weight, slope, before, kept):
+def readout_kernel(scal, inverse, mol, lstm, head, present, target, hid, d_final, read, score, weight, slope, before, kept):
     windows = scal[1]
+    final = hid.at[STEPS]
+    tall = 2 * H + 8
+    d_head = read.at[pl.ds(4 * tall, 2 * H + 16)]
     mols = lax.broadcasted_iota(jnp.int32, (H, 1), 0)
     owned = jnp.where((mols >= scal[2]) & (mols < scal[3]), 1.0, 0.0)
     by_query = lstm[0:H, :] + lstm[2 * H : 3 * H, :]
@@ -561,22 +564,25 @@
     start = (d_query, d_summary, zero, jnp.zeros((1, 4 * H), F32))
     d_bias = lax.fori_loop(0, SET_STEPS, back_round, start)[3]
     slopes = slope[...].reshape(SET_STEPS * H, 4 * H)
-    d_lstm[0:H, :] = wide(dot, before[0], slopes)
-    d_lstm[H : 2 * H, :] = wide(dot, before[1], slopes)
-    d_lstm[2 * H : 2 * H + 8, :] = jnp.broadcast_to(d_bias, (8, 4 * H))
-
-
-def readout(scal, inverse, final, mol, lstm, head, present, target):
-    nodes = final.shape[1]
+    d_by_query = wide(dot, before[0], slopes)
+    d_by_summary = wide(dot, before[1], slopes)
+    for part in range(4):
+        columns = slice(part * H, (part + 1) * H)
+        read[part * tall : part * tall + H, :] = d_by_query[:, columns]
+        read[part * tall + H : part * tall + 2 * H, :] = d_by_summary[:, columns]
+        read[part * tall + 2 * H : (part + 1) * tall, :] = jnp.broadcast_to(d_bias[:, columns], (8, H))
+
+
+def readout(scal, inverse, hid, mol, lstm, head, present, target):
+    nodes = hid.shape[2]
     return pl.pallas_call(
         readout_kernel,
         out_shape=(
             jax.ShapeDtypeStruct((H, nodes), F32),
-            jax.ShapeDtypeStruct((2 * H + 8, 4 * H), F32),
-            jax.ShapeDtypeStruct((2 * H + 16, H), F32),
+            jax.ShapeDtypeStruct((4 * (2 * H + 8) + 2 * H + 16, H), F32),
         ),
         in_specs=[pl.BlockSpec(memory_space=pltpu.SMEM)] * 2 + [pl.BlockSpec(memory_space=pltpu.VMEM)] * 6,
-        out_specs=[pl.BlockSpec(memory_space=pltpu.VMEM)] * 3,
+        out_specs=[pl.BlockSpec(memory_space=pltpu.VMEM)] * 2,
         scratch_shapes=[
             pltpu.VMEM((H, nodes), F32),
             pltpu.VMEM((SET_STEPS, H, nodes), F32),
@@ -587,7 +593,7 @@
         compiler_params=pltpu.CompilerParams(vmem_limit_bytes=VMEM_LIMIT),
         cost_estimate=pl.CostEstimate(flops=30_000_000_000, transcendentals=0, bytes_accessed=5_000_000),
         name="readout",
-    )(scal, inverse, final, mol, lstm, head, present, target)
+    )(scal, inverse, mol, lstm, head, present, target, hid)
 
 
 def backward_kernel(place, scal, nf_t, gru, gru_bias, idx, hid, msg, state, near, d_final, mats, far, small, d_gru, d_embed, d_bias, grad, low_msg, part, back, buffer, in_sems):
@@ -815,24 +821,6 @@
     return lax.dynamic_index_in_dim(parts, index, 0, keepdims=False)
 
 
-def scatter_sum(value, axis, size, me):
-    parts = value.reshape((size, value.shape[0] // size) + value.shape[1:])
-    total = pick(parts, me)
-    parts = scaled(parts)
-    for step in range(1, size):
-        total = total + unscaled(swap(pick(parts, me ^ step), axis, size, step))
-    return total
-
-
-def gather_all(value, axis, size, me):
-    rows = value.shape[0]
-    out = jnp.zeros((size * rows,) + value.shape[1:], value.dtype)
-    for step in range(size):
-        part = swap(value, axis, size, step) if step else value
-        out = lax.dynamic_update_slice_in_dim(out, part, (me ^ step) * rows, 0)
-    return out
-
-
 def tree_sum(value, axis, size):
     values = [value] + [swap(value, axis, size, step) for step in range(1, size)]
     while len(values) > 1:
@@ -850,14 +838,6 @@
 def unscaled(low):
     power = low[..., -1:, :1].astype(F32)
     return low[..., :-16, :].astype(F32) * jnp.exp2(-power)
-
-
-def butterfly(value, axis, size):
-    step = 1
-    while step < size:
-        value = value + swap(value, axis, size, step)
-        step *= 2
-    return value
 
 
 def flat_rows(array):
@@ -875,6 +855,42 @@
         mom_new,
         var_new,
     )
+
+
+def wide_adamw_kernel(scale, grad, bias, weight, mom, var, weight_out, mom_out, var_out, *, rate):
+    def update(rows, value):
+        mom_new = BETA_ONE * mom[rows, :] + (1.0 - BETA_ONE) * value
+        var_new = BETA_TWO * var[rows, :] + (1.0 - BETA_TWO) * value * value
+        mom_out[rows, :] = mom_new
+        var_out[rows, :] = var_new
+        old = weight[rows, :]
+        step = (mom_new / scale[1]) / (jnp.sqrt(var_new / scale[2]) + EPSILON)
+        weight_out[rows, :] = old - rate * (step + DECAY * old)
+
+    update(slice(0, H), grad[...].T * scale[0])
+    update(slice(H, H + 1), bias[...] * scale[0])
+
+
+def wide_adamw(scale, grad, bias, weight, mom, var, rate):
+    rows, columns = weight.shape
+    block = 1024
+    tall = pl.BlockSpec((rows, block), lambda index: (0, index))
+    return pl.pallas_call(
+        functools.partial(wide_adamw_kernel, rate=rate),
+        grid=(columns // block,),
+        in_specs=[
+            pl.BlockSpec(memory_space=pltpu.SMEM),
+            pl.BlockSpec((block, H), lambda index: (index, 0)),
+            pl.BlockSpec((1, block), lambda index: (0, index)),
+            tall,
+            tall,
+            tall,
+        ],
+        out_specs=[tall] * 3,
+        out_shape=[jax.ShapeDtypeStruct(weight.shape, F32)] * 3,
+        compiler_params=pltpu.CompilerParams(vmem_limit_bytes=VMEM_LIMIT),
+        name="wide_adamw",
+    )(scale, grad, bias, weight, mom, var)
 
 
 def on_device(
@@ -890,14 +906,6 @@
     place = jnp.stack([gate, core]).astype(jnp.int32)
     axes = (("grp", cores), ("gate", gates), ("edge", groups))
 
-    wide_rows = edge_second[:EDGE_HID].astype(BF).T
-    half = wide_rows.shape[0] // 2
-    halves = wide_rows.reshape(2, half, H)
-    own = pick(halves, core)
-    second = [own, pick(halves, 1 - core)]
-    for step in range(1, gates):
-        got = swap(own, "gate", gates, step)
-        second += [got, swap(got, "grp", cores, 1)]
     small_parts = [
         exact3(edge_second[EDGE_HID]),
         gru_weight[:, :H].astype(BF).transpose(0, 2, 3, 1),
@@ -908,7 +916,16 @@
     counts = [line.shape[0] for line in lines]
     tail = up(sum(counts), 16)
     lines = jnp.pad(jnp.concatenate(lines, axis=0), ((0, tail - sum(counts)), (0, 0)))
+    wide_rows = edge_second[:EDGE_HID].astype(BF).T
+    half = wide_rows.shape[0] // 2
+    halves = wide_rows.reshape(2, half, H)
+    own = pick(halves, core)
+    lines, own = lax.optimization_barrier((lines, own))
     tails = jnp.stack([lines] + [swap(lines, "gate", gates, step) for step in range(1, gates)])
+    second = [own, pick(halves, 1 - core)]
+    for step in range(1, gates):
+        got = swap(own, "gate", gates, step)
+        second += [got, swap(got, "grp", cores, 1)]
     order = [jnp.stack([tails[index ^ step] for index in range(gates)]) for step in range(gates)]
     tails = order[0]
     for step in range(1, gates):
@@ -950,16 +967,13 @@
     head = jnp.pad(head_weight, ((0, 7), (0, H - NT)))
 
     scal, pre, eh_t, eh, feat, idx = prep(place, mol, src2d, data, first3, edges, gates)
-    scal, count = lax.optimization_barrier((scal, count))
+    second, count = lax.optimization_barrier((second, count))
     hid, msg, state, near, mats = forward(place, scal, nf_t, embed_t, bias, gru, gru_bias, eh_t, idx, second)
     inverse = (1.0 / tree_sum(count, "edge", groups)).reshape(1)
-    d_final, d_lstm, d_head = readout(
-        scal, inverse, hid[STEPS], mol, lstm, head,
+    d_final, read = readout(
+        scal, inverse, hid, mol, lstm, head,
         jnp.pad(present, ((0, H - mols), (0, H - NT))), jnp.pad(target, ((0, H - mols), (0, H - NT))),
     )
-    read = jnp.concatenate([d_lstm.reshape(-1, H), d_head], axis=0)
-    read = jnp.pad(read, ((0, up(read.shape[0], 16) - read.shape[0]), (0, 0)))
-
     def read_chain():
         parts = read.reshape(cores, -1, H)
         (got,) = yield [swap(pick(parts, 1 - core), "grp", cores, 1)]
@@ -996,10 +1010,45 @@
 
     def wide_chain(mine, other, step):
         (got,) = yield [swap(other, "grp", cores, 1)]
-        part = mine + got
-        if step:
-            (part,) = yield [swap(part.astype(BF), "gate", gates, step)]
+        (part,) = yield [swap((mine + got).astype(BF), "gate", gates, step)]
         return part.astype(F32)
+
+    def last_chain(mine, other):
+        (got,) = yield [swap(other, "grp", cores, 1)]
+        total = mine + got
+        for step in range(1, gates):
+            total = total + results[step]
+        rows = up(half, 16 * groups)
+        total = jnp.pad(total, ((0, rows - half), (0, 0))).reshape(groups, rows // groups, H)
+        parts = scaled(total)
+        moved = yield [swap(pick(parts, group ^ step), "edge", groups, step) for step in range(1, groups)]
+        shard = pick(total, group)
+        for got in moved:
+            shard = shard + unscaled(got)
+        shard = scaled(shard)
+        moved = yield [swap(shard, "edge", groups, step) for step in range(1, groups)]
+        tall = shard.shape[0]
+        full = jnp.zeros((groups * tall, H), shard.dtype)
+        for step, part in enumerate([shard] + moved):
+            full = lax.dynamic_update_slice_in_dim(full, part, (group ^ step) * tall, 0)
+        (got,) = yield [swap(full, "grp", cores, 1)]
+        full = jnp.where(core == 0, jnp.stack([full, got]), jnp.stack([got, full]))
+        grads = unscaled(full.reshape(cores, groups, tall, H)).reshape(cores, rows, H)[:, :half].reshape(-1, H)
+        narrow = results["narrow"]
+        values = [(jnp.sum(grads * grads) + jnp.sum(narrow * narrow)).reshape(1, 1)]
+        values += yield [swap(values[0], "gate", gates, step) for step in range(1, gates)]
+        while len(values) > 1:
+            values = [left + right for left, right in zip(values[::2], values[1::2])]
+        return grads, values[0][0, 0]
+
+    def first_chain(first):
+        for axis, size in axes:
+            step = 1
+            while step < size:
+                (got,) = yield [swap(first, axis, size, step)]
+                first = first + got
+                step *= 2
+        return first
 
     results = {}
 
@@ -1022,15 +1071,18 @@
         )
         first, moved = lax.optimization_barrier((first, [arrays for _, _, arrays in chains]))
         chains = advance(chains, moved)
-        fresh = wide_chain(mine, other, step)
-        chains.append((step, fresh, next(fresh)))
+        fresh = wide_chain(mine, other, step) if step else last_chain(mine, other)
+        arrays = next(fresh)
+        chains.append((step, fresh, arrays))
+    fresh = first_chain(first)
+    chains.append(("first", fresh, next(fresh)))
     while chains:
-        chains = advance(chains, [arrays for _, _, arrays in chains])
+        chains = advance(chains, lax.optimization_barrier([arrays for _, _, arrays in chains]))
     read = results["read"]
-    head_begin = d_lstm.shape[0] * 4
-    by_query = read[: 4 * H].reshape(H, 4 * H)
-    by_rest = read[4 * H : 4 * (2 * H + 1)].reshape(H + 1, 4 * H)
-    grad_lstm = jnp.concatenate([by_query, by_rest[:H], by_query, by_rest[H:]], axis=0)
+    head_begin = 4 * (2 * H + 8)
+    by_part = read[:head_begin].reshape(4, 2 * H + 8, H)
+    by_row = jnp.concatenate([by_part[part] for part in range(4)], axis=1)
+    grad_lstm = jnp.concatenate([by_row[: 2 * H], by_row[:H], by_row[2 * H : 2 * H + 1]], axis=0)
     grad_head = read[head_begin : head_begin + 2 * H + 1, :NT]
     loss = read[head_begin + 2 * H + 8, 0]
     small = results["narrow"]
@@ -1038,32 +1090,22 @@
     grad_gru = small[: 2 * tall, : 3 * width].reshape(2, tall, 3, width)[:, : H + 1]
     grad_embed = small[:16, 3 * width :]
     grad_bias = small[2 * tall :].reshape(1, width * H)
-    total = results[0]
-    for step in range(1, gates):
-        total = total + results[step]
-    rows = up(half, 16 * groups)
-    total = jnp.pad(total, ((0, rows - half), (0, 0)))
-    shard = scatter_sum(total, "edge", groups, group)
-    for axis, size in axes:
-        first = butterfly(first, axis, size)
-    grad_first = first[: EIN + 1]
+    grad_first = results["first"][: EIN + 1]
+    grads, squares = results[0]
     whole_sq = jnp.sum(grad_lstm * grad_lstm) + jnp.sum(grad_head * grad_head) + jnp.sum(grad_first * grad_first)
-    shard = gather_all(scaled(shard), "edge", groups, group)
-    shard = gather_all(shard, "grp", cores, core)
-    shard = unscaled(shard.reshape(cores, groups, -1, H)).reshape(cores, -1, H)[:, :half].reshape(-1, H)
-    squares = (jnp.sum(shard * shard) + jnp.sum(small * small)).reshape(1, 1)
-    squares = tree_sum(squares, "gate", gates)
-    grad_second = jnp.concatenate([shard.T, grad_bias], axis=0)
-
-    norm = jnp.sqrt(squares[0, 0] + whole_sq)
+
+    norm = jnp.sqrt(squares + whole_sq)
     factor = jnp.minimum(1.0, CLIP / norm)
-    grads = (grad_embed, grad_first, grad_second, grad_gru, grad_lstm, grad_head)
     params = (embed_weight, edge_first, edge_second, gru_weight, set_lstm, head_weight)
     moms = (mom_embed, mom_first, mom_second, mom_gru, mom_lstm, mom_head)
     varis = (var_embed, var_first, var_second, var_gru, var_lstm, var_head)
     stepno = step_count[0].astype(F32)
+    narrow = (grad_embed, grad_first, None, grad_gru, grad_lstm, grad_head)
+    scale = jnp.stack([factor, 1.0 - BETA_ONE**stepno, 1.0 - BETA_TWO**stepno])
     results = [
-        adamw(params[index], grads[index] * factor, moms[index], varis[index], RATES[index], stepno)
+        adamw(params[index], narrow[index] * factor, moms[index], varis[index], RATES[index], stepno)
+        if narrow[index] is not None
+        else wide_adamw(scale, grads, grad_bias, params[index], moms[index], varis[index], RATES[index])
         for index in range(6)
     ]
     return (loss, norm) + tuple(results[index][kind] for kind in range(3) for index in range(6))

time: 389 us -> 625 us (1.61)
  local copies, waits for them, and re-layouts: 35.3 us -> 168 us
  other arithmetic: 35.1 us -> 127 us
  Pallas kernels: 189 us -> 197 us
    another operation x1 -> x2, local copies, waits for them, and re-layouts: 1.8 us -> 85.4 us  [last_chain(): full = jnp.where(core == 0, jnp.stack([full, got]), jnp.stack([got, full]))]
    mul x2, other arithmetic: 1.31 us -> 73.9 us  [unscaled(): return low[..., :-16, :].astype(F32) * jnp.exp2(-power)]
    mul x0 -> x1, local copies, waits for them, and re-layouts: none -> 54 us  [unscaled(): return low[..., :-16, :].astype(F32) * jnp.exp2(-power)]
    select_n x0 -> x1, other arithmetic: none -> 23.8 us  [last_chain(): full = jnp.where(core == 0, jnp.stack([full, got]), jnp.stack([got, full]))]
    sub x6 -> x5, other arithmetic: 15.2 us -> 6.38 us  [adamw(): weight - rate * (mom_hat / (jnp.sqrt(var_hat) + EPSILON) + DECAY * weight)]
    pallas_call x0 -> x1, Pallas kernels: none -> 7.2 us  [wide_adamw(): pl.pallas_call(functools.partial(wide_adamw_kernel, rate=rate), grid=(col...]
  transfers between devices with their start and end apart: 47 -> 47, of which waited for: 14 -> 8; matrix products, arithmetic and copies ran while one was open for 10% -> 44% of each run, Pallas kernels for 28% -> 27%
where the time goes in v1:
time: 625 us; the launch traced here: 622 us
  Pallas kernels  197 us (32%)
  local copies, waits for them, and re-layouts  168 us (27%)
  other arithmetic  127 us (20%)
  starting transfers between devices  67.1 us (11%)
  waiting for transfers between devices  47.1 us (8%)
  between operations  16 us (3%)
    another operation x2, local copies, waits for them, and re-layouts, last_chain(): full = jnp.where(core == 0, jnp.stack([full, got]), jnp.stack([got, full]))  85.4 us
    mul x2, other arithmetic, unscaled(): return low[..., :-16, :].astype(F32) * jnp.exp2(-power)  73.9 us
    ppermute x47, starting transfers between devices, swap(): lax.ppermute(value, axis, [(index, index ^ step) for index in range(size)])  67.1 us
    pallas_call x1, Pallas kernels, forward(): pl.pallas_call(functools.partial(forward_kernel, gates=gates), out_shape=...  58.9 us
    pallas_call x1, Pallas kernels, backward(): pl.pallas_call(backward_kernel, out_shape=(jax.ShapeDtypeStruct((STEPS, H...  54.9 us
    mul x1, local copies, waits for them, and re-layouts, unscaled(): return low[..., :-16, :].astype(F32) * jnp.exp2(-power)  54 us
    ppermute x47, waiting for transfers between devices, swap(): lax.ppermute(value, axis, [(index, index ^ step) for index in range(size)])  47.1 us
    pallas_call x4, Pallas kernels, edge_grads(): pl.pallas_call(functools.partial(final_kernel, pair=pair, group=8), in_sp...  45.6 us
  transfers between devices with their start and end apart: 47, of which 8 were waited for; matrix products, arithmetic and copies ran while one was open for 44% of the time, Pallas kernels for 27%

profile of v1, /device:TPU:0, one launch (start us, length us, event | category | flops | bytes accessed | tf_op | source)
XLA Modules:
  0.0 622.3 jit_solution(14726598385831999414)
XLA Ops:
  0.7 1.8 fusion
  6.5 3.0 collective-permute-start
  11.7 2.9 collective-permute-start.10
  15.7 1.9 concatenate.27
  25.2 10.5 %collective-permute-done.10 = bf16[304,128]{1,0:T(8,128)(2,1)S(1)} collective-permute-done((bf16[304,128]{1,0:T(8,128)(2,1)S(1)}, bf16[304,128]{1,0:T(8,128)(2,1)S(1)}, u32[]{:S(2)}, u32[]{:S(2)}) %collective-permute-start.10) | collective-permute-done | bytes 77856 | tf_op jit(solution)/shard_map/ppermute | solution.py:817
  37.7 7.9 %prep.1 = (s32[8]{0:T(128)}, f32[128,5120]{1,0:T(8,128)}, bf16[144,5120]{1,0:T(8,128)(2,1)}, bf16[5120,128]{1,0:T(8,128)(2,1)}, bf16[32,5120]{1,0:T(8,128)(2,1)}, /*index=5*/s32[8,5120]{1,0:T(8,128)}) custom-call(s32[2]{0:T(128)} %pad_add_fusion.place, s32[1,3200]{1,0:T(1,128)} %reshape.186.mol, s32[32,256]{1,0:T(8,128)} %pad.55.src2d, ...), custom_call_target="tpu_custom_call" | custom-call | tf_op jit(solution)/shard_map/prep/pallas_call | solution.py:175
  51.5 3.9 collective-permute-start.8
  55.5 2.7 collective-permute-start.9
  59.6 58.9 %forward.1 = (bf16[4,128,3200]{2,1,0:T(8,128)(2,1)}, bf16[3,128,3200]{2,1,0:T(8,128)(2,1)}, f32[4,128,3200]{2,1,0:T(8,128)}, bf16[3,128,5120]{2,1,0:T(8,128)(2,1)}, bf16[40,4,4096,128]{3,2,1,0:T(8,128)(2,1)}) custom-call(s32[2]{0:T(128)} %pad_add_fusion.place, s32[8]{0:T(128)} %get-tuple-element.101.scal, bf16[16,3200]{1,0:T(8,128)(2,1)} %pad.64.nf_t, ...), custom_call_target="tpu_custom_call" | custom-call | flops 60000002048 | bytes 20000000 | tf_op jit(solution)/shard_map/forward/pallas_call | solution.py:413
  120.6 22.6 %readout.1 = (f32[128,3200]{1,0:T(8,128)}, f32[1328,128]{1,0:T(8,128)}) custom-call(s32[8]{0:T(128)} %get-tuple-element.101.scal, f32[1]{0:T(128)} %bitcast.17.inverse, s32[1,3200]{1,0:T(1,128)} %reshape.186.mol, f32[392,512]{1,0:T(8,128)} %pad.60.lstm, f32[264,128]{1,0:T(8,128)} %pad.61.head, f32[128,128]{1,0:T(8,128)} %pad.62.present, ...), custom_call_target="tpu_custom_call" | custom-call | flops 30000001024 | bytes 5000000 | tf_op jit(solution)/shard_map/readout/pallas_call | solution.py:578
  144.3 54.9 %backward.1 = (bf16[3,128,5120]{2,1,0:T(8,128)(2,1)}, f32[4,320,128]{2,1,0:T(8,128)}) custom-call(s32[2]{0:T(128)} %pad_add_fusion.place, s32[8]{0:T(128)} %get-tuple-element.101.scal, bf16[16,3200]{1,0:T(8,128)(2,1)} %pad.64.nf_t, bf16[2,384,128]{2,1,0:T(8,128)(2,1)} %bitcast.125, f32[2,384,1]{2,1,0:T(8,128)} %reshape.204.gru_bias, ...), custom_call_target="tpu_custom_call" | custom-call | flops 60000002048 | bytes 20000000 | tf_op jit(solution)/shard_map/backward/pallas_call | solution.py:692
  199.3 6.0 collective-permute-start.14
  205.3 5.0 collective-permute-start.15
  211.0 11.4 %edge_grads.4 = (f32[2048,128]{1,0:T(8,128)}, f32[2048,128]{1,0:T(8,128)}, f32[32,128]{1,0:T(8,128)}) custom-call(s32[2]{0:T(128)} %pad_add_fusion.place, s32[8]{0:T(128)} %get-tuple-element.101.scal, bf16[2048,128]{1,0:T(8,128)(2,1)} %collective-permute-done.4.refs_6_.mine, bf16[2048,128]{1,0:T(8,128)(2,1)} %copy-done.48, ...), custom_call_target="tpu_custom_call" | custom-call | flops 8999999488 | bytes 5000000 | tf_op jit(solution)/shard_map/edge_grads/pallas_call | solution.py:785
  223.4 1.9 collective-permute-start.17
  225.3 1.6 collective-permute-start.19
  227.4 11.4 %edge_grads.5 = (f32[2048,128]{1,0:T(8,128)}, f32[2048,128]{1,0:T(8,128)}, f32[32,128]{1,0:T(8,128)}) custom-call(s32[2]{0:T(128)} %pad_add_fusion.place, s32[8]{0:T(128)} %get-tuple-element.101.scal, bf16[2048,128]{1,0:T(8,128)(2,1)} %collective-permute-done.2.refs_4_.mine, bf16[2048,128]{1,0:T(8,128)(2,1)} %copy-done.47, ...), custom_call_target="tpu_custom_call" | custom-call | flops 8999999488 | bytes 5000000 | tf_op jit(solution)/shard_map/edge_grads/pallas_call | solution.py:785
  238.9 3.2 collective-permute-done.16
  244.2 2.1 collective-permute-start.21
  246.3 11.3 %edge_grads.6 = (f32[2048,128]{1,0:T(8,128)}, f32[2048,128]{1,0:T(8,128)}, f32[32,128]{1,0:T(8,128)}) custom-call(s32[2]{0:T(128)} %pad_add_fusion.place, s32[8]{0:T(128)} %get-tuple-element.101.scal, bf16[2048,128]{1,0:T(8,128)(2,1)} %collective-permute-done.refs_2_.mine, bf16[2048,128]{1,0:T(8,128)(2,1)} %copy-done.46, ...), custom_call_target="tpu_custom_call" | custom-call | flops 8999999488 | bytes 5000000 | tf_op jit(solution)/shard_map/edge_grads/pallas_call | solution.py:785
  257.8 2.4 add_convert_fusion.1
  261.5 6.6 %collective-permute-start.26 = (f32[320,128]{1,0:T(8,128)S(1)}, f32[320,128]{1,0:T(8,128)}, u32[]{:S(2)}, u32[]{:S(2)}) collective-permute-start(f32[320,128]{1,0:T(8,128)S(1)} %add.293), channel_id=1, source_target_pairs={{0,8},{4,12},{8,0},{12,4},{1,9},{5,13},{9,1},{13,5},{2,10},{6,14},... | collective-permute-start | bytes 491528 | tf_op jit(solution)/shard_map/ppermute | solution.py:817
  268.2 11.4 %edge_grads.7 = (f32[2048,128]{1,0:T(8,128)}, f32[2048,128]{1,0:T(8,128)}, f32[32,128]{1,0:T(8,128)}) custom-call(s32[2]{0:T(128)} %pad_add_fusion.place, s32[8]{0:T(128)} %get-tuple-element.101.scal, bf16[2048,128]{1,0:T(8,128)(2,1)} %copy-done.20, bf16[2048,128]{1,0:T(8,128)(2,1)} %get-tuple-element.108.refs_1_.other, ...), custom_call_target="tpu_custom_call" | custom-call | flops 8999999488 | bytes 5000000 | tf_op jit(solution)/shard_map/edge_grads/pallas_call | solution.py:785
  279.8 2.8 collective-permute-done.26
  282.6 7.1 %collective-permute-done.25 = f32[664,128]{1,0:T(8,128)S(1)} collective-permute-done((f32[664,128]{1,0:T(8,128)S(1)}, f32[664,128]{1,0:T(8,128)S(1)}, u32[]{:S(2)}, u32[]{:S(2)}) %collective-permute-start.25) | collective-permute-done | bytes 340000 | tf_op jit(solution)/shard_map/ppermute | solution.py:817
  289.8 2.2 add_convert_fusion
  295.4 10.7 %collective-permute-done.30 = bf16[2048,128]{1,0:T(8,128)(2,1)S(1)} collective-permute-done((bf16[2048,128]{1,0:T(8,128)(2,1)}, bf16[2048,128]{1,0:T(8,128)(2,1)S(1)}, u32[]{:S(2)}, u32[]{:S(2)}) %collective-permute-start.30) | collective-permute-done | bytes 524320 | tf_op jit(solution)/shard_map/ppermute | solution.py:817
  307.0 2.3 abs_reduce_fusion
  311.3 3.4 collective-permute-start.34
  314.8 1.6 multiply_reduce_fusion.2
  317.9 6.4 %collective-permute-done.34 = f16[528,128]{1,0:T(8,128)(2,1)S(1)} collective-permute-done((f16[528,128]{1,0:T(8,128)(2,1)S(1)}, f16[528,128]{1,0:T(8,128)(2,1)S(1)}, u32[]{:S(2)}, u32[]{:S(2)}) %collective-permute-start.34) | collective-permute-done | bytes 135200 | tf_op jit(solution)/shard_map/ppermute | solution.py:817
  329.7 2.1 collective-permute-start.37
  337.2 1.5 collective-permute-done.40
  338.7 4.7 collective-permute-done.38
  343.8 1.6 multiply_reduce_fusion.1
  345.5 2.4 collective-permute-start.42
  351.0 1.8 collective-permute-start.46
  352.7 1.8 pad_maximum_fusion.1
  354.5 42.7 %copy.204 = f16[2,4,528,128]{1,0,3,2:T(2,128)(2,1)} copy(f16[2,4,528,128]{3,2,1,0:T(8,128)(2,1)S(1)} %get-tuple-element.329) | data formatting | bytes 2162688 | tf_op jit(solution)/shard_map/stack | solution.py:1035
  397.2 42.7 %copy.205 = f16[2,4,528,128]{1,0,3,2:T(2,128)(2,1)} copy(f16[2,4,528,128]{3,2,1,0:T(8,128)(2,1)S(1)} %get-tuple-element.328) | data formatting | bytes 2162688 | tf_op jit(solution)/shard_map/stack | solution.py:1035
  440.0 23.8 %broadcast_select_fusion = f16[8,4,528,32]{1,0,3,2:T(8,128)(2,1)} fusion(f16[8,4,528,32]{1,0,3,2:T(8,128)(2,1)} %bitcast.106, f16[8,4,528,32]{1,0,3,2:T(8,128)(2,1)} %bitcast.107, pred[]{:T(512)S(6)} %eq.26), kind=kLoop, calls=%fused_computation | loop fusion | flops 540672 | bytes 3244033 | tf_op jit(solution)/shard_map/jit(_where)/select_n | solution.py:1035
  464.5 73.2 %convert_multiply_fusion = (f32[2,4,512,128]{1,0,3,2:T(2,128)}, f32[]{:T(128)}) fusion(f16[2,4,528,128]{1,0,3,2:T(2,128)(2,1)} %bitcast.109, f32[2,4]{1,0:T(2,128)S(1)} %exponential_bitcast_fusion), kind=kLoop, calls=%fused_computation.2 | loop fusion | flops 2097151 | bytes 3145764 | tf_op jit(solution)/shard_map/mul | solution.py:840
  539.0 1.9 collective-permute-start.43
  540.9 2.4 collective-permute-start.44
  543.2 3.2 collective-permute-start.45
  546.6 54.0 %copy.206 = f32[2,4,512,128]{3,2,1,0:T(8,128)} copy(f32[2,4,512,128]{1,0,3,2:T(2,128)} %get-tuple-element.323) | data formatting | bytes 4194304 | tf_op jit(solution)/shard_map/mul | solution.py:840
  609.7 3.3 multiply_subtract_fusion
  613.9 7.2 %wide_adamw.1 = (f32[129,4096]{1,0:T(8,128)}, f32[129,4096]{1,0:T(8,128)}, f32[129,4096]{1,0:T(8,128)}) custom-call(f32[3]{0:T(128)} %pad_maximum_fusion.6.scale, f32[4096,128]{1,0:T(8,128)} %bitcast.110, f32[1,4096]{1,0:T(1,128)} %bitcast.131, f32[129,4096]{1,0:T(8,128)} %weight.1, f32[129,4096]{1,0:T(8,128)} %mom.1, f32[129,4096]{1,0:T(8,128)} %var.1), custom_call_target="tpu_custom_call" | custom-call | tf_op jit(solution)/shard_map/wide_adamw/pallas_call | solution.py:878
  (281 shorter events, 54.3 us)
Async XLA Ops:
  6.5 40.4 %collective-permute-start = (bf16[2048,128]{1,0:T(8,128)(2,1)S(1)}, bf16[2048,128]{1,0:T(8,128)(2,1)}, u32[]{:S(2)}, u32[]{:S(2)}) collective-permute-start(bf16[2048,128]{1,0:T(8,128)(2,1)S(1)} %get-tuple-element.107.refs_0_.mine), channel_id=1, source_target_pairs={{0,1},{1,0},{2,3},{3,2},{4,5},{5,4},{6,7},{7,6},{8,9},{9,8},{10,11... | collective-permute-start | bytes 1572872 | tf_op jit(solution)/shard_map/ppermute | solution.py:817
  9.5 37.5 %collective-permute-start.2 = (bf16[2048,128]{1,0:T(8,128)(2,1)S(1)}, bf16[2048,128]{1,0:T(8,128)(2,1)}, u32[]{:S(2)}, u32[]{:S(2)}) collective-permute-start(bf16[2048,128]{1,0:T(8,128)(2,1)S(1)} %get-tuple-element.107.refs_0_.mine), channel_id=1, source_target_pairs={{0,2},{1,3},{2,0},{3,1},{4,6},{5,7},{6,4},{7,5},{8,10},{9,11},{10,... | collective-permute-start | bytes 1572872 | tf_op jit(solution)/shard_map/ppermute | solution.py:817
  11.0 36.5 %collective-permute-start.4 = (bf16[2048,128]{1,0:T(8,128)(2,1)S(1)}, bf16[2048,128]{1,0:T(8,128)(2,1)}, u32[]{:S(2)}, u32[]{:S(2)}) collective-permute-start(bf16[2048,128]{1,0:T(8,128)(2,1)S(1)} %get-tuple-element.107.refs_0_.mine), channel_id=1, source_target_pairs={{0,3},{1,2},{2,1},{3,0},{4,7},{5,6},{6,5},{7,4},{8,11},{9,10},{10,... | collective-permute-start | bytes 1572872 | tf_op jit(solution)/shard_map/ppermute | solution.py:817
  11.7 12.9 %collective-permute-start.6 = (f32[1,1]{1,0:T(1,128)}, f32[1,1]{1,0:T(1,128)}, u32[]{:S(2)}, u32[]{:S(2)}) collective-permute-start(f32[1,1]{1,0:T(1,128)} %bitcast.16), channel_id=1, source_target_pairs={{0,16},{16,0},{1,17},{17,1},{2,18},{18,2},{3,19},{19,3},{4,20},{20... | collective-permute-start | bytes 20 | tf_op jit(solution)/shard_map/ppermute | solution.py:817
  11.7 23.9 %collective-permute-start.10 = (bf16[304,128]{1,0:T(8,128)(2,1)S(1)}, bf16[304,128]{1,0:T(8,128)(2,1)S(1)}, u32[]{:S(2)}, u32[]{:S(2)}) collective-permute-start(bf16[304,128]{1,0:T(8,128)(2,1)S(1)} %fusion.19), channel_id=1, source_target_pairs={{0,3},{1,2},{2,1},{3,0},{4,7},{5,6},{6,5},{7,4},{8,11},{9,10},{10,... | collective-permute-start | bytes 233480 | tf_op jit(solution)/shard_map/ppermute | solution.py:817
  24.7 22.9 %collective-permute-start.11 = (bf16[304,128]{1,0:T(8,128)(2,1)S(1)}, bf16[304,128]{1,0:T(8,128)(2,1)S(1)}, u32[]{:S(2)}, u32[]{:S(2)}) collective-permute-start(bf16[304,128]{1,0:T(8,128)(2,1)S(1)} %fusion.19), channel_id=1, source_target_pairs={{0,2},{1,3},{2,0},{3,1},{4,6},{5,7},{6,4},{7,5},{8,10},{9,11},{10,... | collective-permute-start | bytes 233480 | tf_op jit(solution)/shard_map/ppermute | solution.py:817
  35.6 12.0 %collective-permute-start.12 = (bf16[304,128]{1,0:T(8,128)(2,1)S(1)}, bf16[304,128]{1,0:T(8,128)(2,1)S(1)}, u32[]{:S(2)}, u32[]{:S(2)}) collective-permute-start(bf16[304,128]{1,0:T(8,128)(2,1)S(1)} %fusion.19), channel_id=1, source_target_pairs={{0,1},{1,0},{2,3},{3,2},{4,5},{5,4},{6,7},{7,6},{8,9},{9,8},{10,11... | collective-permute-start | bytes 233480 | tf_op jit(solution)/shard_map/ppermute | solution.py:817
  46.9 4.5 collective-permute-start.1
  47.0 4.5 collective-permute-start.3
  47.5 4.0 collective-permute-start.5
  51.5 67.8 %collective-permute-start.8 = (f32[1,1]{1,0:T(1,128)}, f32[1,1]{1,0:T(1,128)}, u32[]{:S(2)}, u32[]{:S(2)}) collective-permute-start(f32[1,1]{1,0:T(1,128)} %add.276), channel_id=1, source_target_pairs={{0,8},{4,12},{8,0},{12,4},{1,9},{5,13},{9,1},{13,5},{2,10},{6,14},... | collective-permute-start | bytes 20 | tf_op jit(solution)/shard_map/ppermute | solution.py:817
  55.5 63.8 %collective-permute-start.9 = (f32[1,1]{1,0:T(1,128)}, f32[1,1]{1,0:T(1,128)}, u32[]{:S(2)}, u32[]{:S(2)}) collective-permute-start(f32[1,1]{1,0:T(1,128)} %add.276), channel_id=1, source_target_pairs={{0,12},{4,8},{8,4},{12,0},{1,13},{5,9},{9,5},{13,1},{2,14},{6,10},... | collective-permute-start | bytes 20 | tf_op jit(solution)/shard_map/ppermute | solution.py:817
  58.1 60.4 %collective-permute-start.7 = (f32[1,1]{1,0:T(1,128)}, f32[1,1]{1,0:T(1,128)}, u32[]{:S(2)}, u32[]{:S(2)}) collective-permute-start(f32[1,1]{1,0:T(1,128)} %add.276), channel_id=1, source_target_pairs={{0,4},{4,0},{8,12},{12,8},{1,5},{5,1},{9,13},{13,9},{2,6},{6,2},{1... | collective-permute-start | bytes 20 | tf_op jit(solution)/shard_map/ppermute | solution.py:817
  144.2 55.0 %collective-permute-start.13 = (f32[664,128]{1,0:T(8,128)S(1)}, f32[664,128]{1,0:T(8,128)S(1)}, u32[]{:S(2)}, u32[]{:S(2)}) collective-permute-start(f32[664,128]{1,0:T(8,128)S(1)} %dynamic-slice_bitcast_fusion.2), channel_id=1, source_target_pairs={{0,16},{16,0},{1,17},{17,1},{2,18},{18,2},{3,19},{19,3},{4,20},{20... | collective-permute-start | bytes 1019912 | tf_op jit(solution)/shard_map/ppermute | solution.py:817
  199.3 23.2 %collective-permute-start.14 = (f32[664,128]{1,0:T(8,128)S(1)}, f32[664,128]{1,0:T(8,128)S(1)}, u32[]{:S(2)}, u32[]{:S(2)}) collective-permute-start(f32[664,128]{1,0:T(8,128)S(1)} %bitcast_add_fusion), channel_id=1, source_target_pairs={{0,1},{1,0},{2,3},{3,2},{4,5},{5,4},{6,7},{7,6},{8,9},{9,8},{10,11... | collective-permute-start | bytes 1019912 | tf_op jit(solution)/shard_map/ppermute | solution.py:817
  205.3 17.2 %collective-permute-start.15 = (f32[4,320,128]{2,1,0:T(8,128)}, f32[4,320,128]{2,1,0:T(8,128)S(1)}, u32[]{:S(2)}, u32[]{:S(2)}) collective-permute-start(f32[4,320,128]{2,1,0:T(8,128)} %get-tuple-element.130), channel_id=1, source_target_pairs={{0,16},{16,0},{1,17},{17,1},{2,18},{18,2},{3,19},{19,3},{4,20},{20... | collective-permute-start | bytes 1966088 | tf_op jit(solution)/shard_map/ppermute | solution.py:817
  222.4 19.8 %collective-permute-start.20 = (f32[2048,128]{1,0:T(8,128)}, f32[2048,128]{1,0:T(8,128)S(1)}, u32[]{:S(2)}, u32[]{:S(2)}) collective-permute-start(f32[2048,128]{1,0:T(8,128)} %get-tuple-element.135), channel_id=1, source_target_pairs={{0,16},{16,0},{1,17},{17,1},{2,18},{18,2},{3,19},{19,3},{4,20},{20... | collective-permute-start | bytes 3145736 | tf_op jit(solution)/shard_map/ppermute | solution.py:817
  223.4 15.4 %collective-permute-start.17 = (f32[320,128]{1,0:T(8,128)}, f32[320,128]{1,0:T(8,128)S(1)}, u32[]{:S(2)}, u32[]{:S(2)}) collective-permute-start(f32[320,128]{1,0:T(8,128)} %get-tuple-element.338), channel_id=1, source_target_pairs={{0,1},{1,0},{2,3},{3,2},{4,5},{5,4},{6,7},{7,6},{8,9},{9,8},{10,11... | collective-permute-start | bytes 491528 | tf_op jit(solution)/shard_map/ppermute | solution.py:817
  225.3 13.6 %collective-permute-start.18 = (f32[320,128]{1,0:T(8,128)}, f32[320,128]{1,0:T(8,128)S(1)}, u32[]{:S(2)}, u32[]{:S(2)}) collective-permute-start(f32[320,128]{1,0:T(8,128)} %get-tuple-element.337), channel_id=1, source_target_pairs={{0,2},{1,3},{2,0},{3,1},{4,6},{5,7},{6,4},{7,5},{8,10},{9,11},{10,... | collective-permute-start | bytes 491528 | tf_op jit(solution)/shard_map/ppermute | solution.py:817
  225.3 13.7 %collective-permute-start.19 = (f32[320,128]{1,0:T(8,128)}, f32[320,128]{1,0:T(8,128)}, u32[]{:S(2)}, u32[]{:S(2)}) collective-permute-start(f32[320,128]{1,0:T(8,128)} %get-tuple-element.336), channel_id=1, source_target_pairs={{0,3},{1,2},{2,1},{3,0},{4,7},{5,6},{6,5},{7,4},{8,11},{9,10},{10,... | collective-permute-start | bytes 491528 | tf_op jit(solution)/shard_map/ppermute | solution.py:817
  226.9 15.2 %collective-permute-start.16 = (f32[664,128]{1,0:T(8,128)S(1)}, f32[664,128]{1,0:T(8,128)S(1)}, u32[]{:S(2)}, u32[]{:S(2)}) collective-permute-start(f32[664,128]{1,0:T(8,128)S(1)} %add.281), channel_id=1, source_target_pairs={{0,2},{1,3},{2,0},{3,1},{4,6},{5,7},{6,4},{7,5},{8,10},{9,11},{10,... | collective-permute-start | bytes 1019912 | tf_op jit(solution)/shard_map/ppermute | solution.py:817
  238.8 18.9 %collective-permute-start.24 = (f32[2048,128]{1,0:T(8,128)}, f32[2048,128]{1,0:T(8,128)}, u32[]{:S(2)}, u32[]{:S(2)}) collective-permute-start(f32[2048,128]{1,0:T(8,128)} %get-tuple-element.144), channel_id=1, source_target_pairs={{0,16},{16,0},{1,17},{17,1},{2,18},{18,2},{3,19},{19,3},{4,20},{20... | collective-permute-start | bytes 3145736 | tf_op jit(solution)/shard_map/ppermute | solution.py:817
  242.3 15.4 %collective-permute-start.23 = (bf16[2048,128]{1,0:T(8,128)(2,1)S(1)}, bf16[2048,128]{1,0:T(8,128)(2,1)S(1)}, u32[]{:S(2)}, u32[]{:S(2)}) collective-permute-start(bf16[2048,128]{1,0:T(8,128)(2,1)S(1)} %add_convert_fusion.2), channel_id=1, source_target_pairs={{0,3},{1,2},{2,1},{3,0},{4,7},{5,6},{6,5},{7,4},{8,11},{9,10},{10,... | collective-permute-start | bytes 1572872 | tf_op jit(solution)/shard_map/ppermute | solution.py:817
  244.0 13.7 %collective-permute-start.22 = (f32[320,128]{1,0:T(8,128)S(1)}, f32[320,128]{1,0:T(8,128)S(1)}, u32[]{:S(2)}, u32[]{:S(2)}) collective-permute-start(f32[320,128]{1,0:T(8,128)S(1)} %fusion.7), channel_id=1, source_target_pairs={{0,4},{4,0},{8,12},{12,8},{1,5},{5,1},{9,13},{13,9},{2,6},{6,2},{1... | collective-permute-start | bytes 491528 | tf_op jit(solution)/shard_map/ppermute | solution.py:817
  244.2 13.5 %collective-permute-start.21 = (f32[664,128]{1,0:T(8,128)S(1)}, f32[664,128]{1,0:T(8,128)S(1)}, u32[]{:S(2)}, u32[]{:S(2)}) collective-permute-start(f32[664,128]{1,0:T(8,128)S(1)} %add.286), channel_id=1, source_target_pairs={{0,4},{4,0},{8,12},{12,8},{1,5},{5,1},{9,13},{13,9},{2,6},{6,2},{1... | collective-permute-start | bytes 1019912 | tf_op jit(solution)/shard_map/ppermute | solution.py:817
  257.6 32.1 %collective-permute-start.28 = (f32[2048,128]{1,0:T(8,128)}, f32[2048,128]{1,0:T(8,128)}, u32[]{:S(2)}, u32[]{:S(2)}) collective-permute-start(f32[2048,128]{1,0:T(8,128)} %get-tuple-element.151), channel_id=1, source_target_pairs={{0,16},{16,0},{1,17},{17,1},{2,18},{18,2},{3,19},{19,3},{4,20},{20... | collective-permute-start | bytes 3145736 | tf_op jit(solution)/shard_map/ppermute | solution.py:817
  260.1 29.6 %collective-permute-start.27 = (bf16[2048,128]{1,0:T(8,128)(2,1)}, bf16[2048,128]{1,0:T(8,128)(2,1)}, u32[]{:S(2)}, u32[]{:S(2)}) collective-permute-start(bf16[2048,128]{1,0:T(8,128)(2,1)} %add_convert_fusion.1), channel_id=1, source_target_pairs={{0,2},{1,3},{2,0},{3,1},{4,6},{5,7},{6,4},{7,5},{8,10},{9,11},{10,... | collective-permute-start | bytes 1572872 | tf_op jit(solution)/shard_map/ppermute | solution.py:817
  261.5 21.1 %collective-permute-start.26 = (f32[320,128]{1,0:T(8,128)S(1)}, f32[320,128]{1,0:T(8,128)}, u32[]{:S(2)}, u32[]{:S(2)}) collective-permute-start(f32[320,128]{1,0:T(8,128)S(1)} %add.293), channel_id=1, source_target_pairs={{0,8},{4,12},{8,0},{12,4},{1,9},{5,13},{9,1},{13,5},{2,10},{6,14},... | collective-permute-start | bytes 491528 | tf_op jit(solution)/shard_map/ppermute | solution.py:817
  268.1 21.7 %collective-permute-start.25 = (f32[664,128]{1,0:T(8,128)S(1)}, f32[664,128]{1,0:T(8,128)S(1)}, u32[]{:S(2)}, u32[]{:S(2)}) collective-permute-start(f32[664,128]{1,0:T(8,128)S(1)} %add.292), channel_id=1, source_target_pairs={{0,8},{4,12},{8,0},{12,4},{1,9},{5,13},{9,1},{13,5},{2,10},{6,14},... | collective-permute-start | bytes 1019912 | tf_op jit(solution)/shard_map/ppermute | solution.py:817
  279.7 26.4 %collective-permute-start.31 = (f32[2048,128]{1,0:T(8,128)}, f32[2048,128]{1,0:T(8,128)S(1)}, u32[]{:S(2)}, u32[]{:S(2)}) collective-permute-start(f32[2048,128]{1,0:T(8,128)} %get-tuple-element.155), channel_id=1, source_target_pairs={{0,16},{16,0},{1,17},{17,1},{2,18},{18,2},{3,19},{19,3},{4,20},{20... | collective-permute-start | bytes 3145736 | tf_op jit(solution)/shard_map/ppermute | solution.py:817
  291.9 14.1 %collective-permute-start.30 = (bf16[2048,128]{1,0:T(8,128)(2,1)}, bf16[2048,128]{1,0:T(8,128)(2,1)S(1)}, u32[]{:S(2)}, u32[]{:S(2)}) collective-permute-start(bf16[2048,128]{1,0:T(8,128)(2,1)} %add_convert_fusion), channel_id=1, source_target_pairs={{0,1},{1,0},{2,3},{3,2},{4,5},{5,4},{6,7},{7,6},{8,9},{9,8},{10,11... | collective-permute-start | bytes 1572872 | tf_op jit(solution)/shard_map/ppermute | solution.py:817
  292.5 2.9 collective-permute-start.29
  292.6 2.8 collective-permute-start.32
  306.7 11.2 %collective-permute-start.36 = (f32[32,128]{1,0:T(8,128)}, f32[32,128]{1,0:T(8,128)}, u32[]{:S(2)}, u32[]{:S(2)}) collective-permute-start(f32[32,128]{1,0:T(8,128)} %add.305), channel_id=1, source_target_pairs={{0,1},{1,0},{2,3},{3,2},{4,5},{5,4},{6,7},{7,6},{8,9},{9,8},{10,11... | collective-permute-start | bytes 49160 | tf_op jit(solution)/shard_map/ppermute | solution.py:817
  310.3 7.6 %collective-permute-start.33 = (f16[528,128]{1,0:T(8,128)(2,1)S(1)}, f16[528,128]{1,0:T(8,128)(2,1)S(1)}, u32[]{:S(2)}, u32[]{:S(2)}) collective-permute-start(f16[528,128]{1,0:T(8,128)(2,1)S(1)} %get-tuple-element.341), channel_id=1, source_target_pairs={{0,4},{4,0},{8,12},{12,8},{1,5},{5,1},{9,13},{13,9},{2,6},{6,2},{1... | collective-permute-start | bytes 405512 | tf_op jit(solution)/shard_map/ppermute | solution.py:817
  311.3 13.0 %collective-permute-start.34 = (f16[528,128]{1,0:T(8,128)(2,1)S(1)}, f16[528,128]{1,0:T(8,128)(2,1)S(1)}, u32[]{:S(2)}, u32[]{:S(2)}) collective-permute-start(f16[528,128]{1,0:T(8,128)(2,1)S(1)} %get-tuple-element.340), channel_id=1, source_target_pairs={{0,8},{4,12},{8,0},{12,4},{1,9},{5,13},{9,1},{13,5},{2,10},{6,14},... | collective-permute-start | bytes 405512 | tf_op jit(solution)/shard_map/ppermute | solution.py:817
  314.7 9.7 %collective-permute-start.35 = (f16[528,128]{1,0:T(8,128)(2,1)S(1)}, f16[528,128]{1,0:T(8,128)(2,1)S(1)}, u32[]{:S(2)}, u32[]{:S(2)}) collective-permute-start(f16[528,128]{1,0:T(8,128)(2,1)S(1)} %get-tuple-element.339), channel_id=1, source_target_pairs={{0,12},{4,8},{8,4},{12,0},{1,13},{5,9},{9,5},{13,1},{2,14},{6,10},... | collective-permute-start | bytes 405512 | tf_op jit(solution)/shard_map/ppermute | solution.py:817
  329.7 9.0 %collective-permute-start.37 = (f16[528,128]{1,0:T(8,128)(2,1)S(1)}, f16[528,128]{1,0:T(8,128)(2,1)S(1)}, u32[]{:S(2)}, u32[]{:S(2)}) collective-permute-start(f16[528,128]{1,0:T(8,128)(2,1)S(1)} %get-tuple-element.342), channel_id=1, source_target_pairs={{0,4},{4,0},{8,12},{12,8},{1,5},{5,1},{9,13},{13,9},{2,6},{6,2},{1... | collective-permute-start | bytes 405512 | tf_op jit(solution)/shard_map/ppermute | solution.py:817
  331.8 11.7 %collective-permute-start.38 = (f16[528,128]{1,0:T(8,128)(2,1)S(1)}, f16[528,128]{1,0:T(8,128)(2,1)S(1)}, u32[]{:S(2)}, u32[]{:S(2)}) collective-permute-start(f16[528,128]{1,0:T(8,128)(2,1)S(1)} %get-tuple-element.342), channel_id=1, source_target_pairs={{0,8},{4,12},{8,0},{12,4},{1,9},{5,13},{9,1},{13,5},{2,10},{6,14},... | collective-permute-start | bytes 405512 | tf_op jit(solution)/shard_map/ppermute | solution.py:817
  332.8 10.6 %collective-permute-start.39 = (f16[528,128]{1,0:T(8,128)(2,1)S(1)}, f16[528,128]{1,0:T(8,128)(2,1)S(1)}, u32[]{:S(2)}, u32[]{:S(2)}) collective-permute-start(f16[528,128]{1,0:T(8,128)(2,1)S(1)} %get-tuple-element.342), channel_id=1, source_target_pairs={{0,12},{4,8},{8,4},{12,0},{1,13},{5,9},{9,5},{13,1},{2,14},{6,10},... | collective-permute-start | bytes 405512 | tf_op jit(solution)/shard_map/ppermute | solution.py:817
  335.0 3.7 collective-permute-start.40
  343.6 6.7 %collective-permute-start.41 = (f16[2112,128]{1,0:T(8,128)(2,1)S(1)}, f16[2112,128]{1,0:T(8,128)(2,1)S(1)}, u32[]{:S(2)}, u32[]{:S(2)}) collective-permute-start(f16[2112,128]{1,0:T(8,128)(2,1)S(1)} %constant_dynamic-update-slice_fusion), channel_id=1, source_target_pairs={{0,16},{16,0},{1,17},{17,1},{2,18},{18,2},{3,19},{19,3},{4,20},{20... | collective-permute-start | bytes 1622024 | tf_op jit(solution)/shard_map/ppermute | solution.py:817
  345.5 4.8 collective-permute-start.42
  351.0 249.5 %collective-permute-start.46 = (f32[32,128]{1,0:T(8,128)}, f32[32,128]{1,0:T(8,128)}, u32[]{:S(2)}, u32[]{:S(2)}) collective-permute-start(f32[32,128]{1,0:T(8,128)} %add.317), channel_id=1, source_target_pairs={{0,8},{4,12},{8,0},{12,4},{1,9},{5,13},{9,1},{13,5},{2,10},{6,14},... | collective-permute-start | bytes 49160 | tf_op jit(solution)/shard_map/ppermute | solution.py:817
  539.0 61.5 %collective-permute-start.43 = (f32[1,1]{1,0:T(1,128)}, f32[1,1]{1,0:T(1,128)}, u32[]{:S(2)}, u32[]{:S(2)}) collective-permute-start(f32[1,1]{1,0:T(1,128)} %bitcast.48), channel_id=1, source_target_pairs={{0,1},{1,0},{2,3},{3,2},{4,5},{5,4},{6,7},{7,6},{8,9},{9,8},{10,11... | collective-permute-start | bytes 20 | tf_op jit(solution)/shard_map/ppermute | solution.py:817
  540.9 59.6 %collective-permute-start.44 = (f32[1,1]{1,0:T(1,128)}, f32[1,1]{1,0:T(1,128)}, u32[]{:S(2)}, u32[]{:S(2)}) collective-permute-start(f32[1,1]{1,0:T(1,128)} %bitcast.48), channel_id=1, source_target_pairs={{0,2},{1,3},{2,0},{3,1},{4,6},{5,7},{6,4},{7,5},{8,10},{9,11},{10,... | collective-permute-start | bytes 20 | tf_op jit(solution)/shard_map/ppermute | solution.py:817
  543.2 57.3 %collective-permute-start.45 = (f32[1,1]{1,0:T(1,128)}, f32[1,1]{1,0:T(1,128)}, u32[]{:S(2)}, u32[]{:S(2)}) collective-permute-start(f32[1,1]{1,0:T(1,128)} %bitcast.48), channel_id=1, source_target_pairs={{0,3},{1,2},{2,1},{3,0},{4,7},{5,6},{6,5},{7,4},{8,11},{9,10},{10,... | collective-permute-start | bytes 20 | tf_op jit(solution)/shard_map/ppermute | solution.py:817
  546.5 63.1 %copy-start.1 = (f32[385,512]{1,0:T(8,128)S(1)}, f32[385,512]{1,0:T(8,128)}, u32[]{:S(2)}) copy-start(f32[385,512]{1,0:T(8,128)} %param.39) | copy-start | bytes 2365444
  (49 other events, 1025.0 us)

commit v2 on v1

--- a/solution.py
+++ b/solution.py
@@ -201,7 +201,7 @@
         pair, side = divmod(number, 2)
         copies.append(
             pltpu.make_async_copy(
-                part,
+                part.at[pl.ds(0, half)],
                 second.at[pair, pl.ds(side * half, half), pl.ds(0, H)],
                 sems.at[number],
             )
@@ -714,7 +714,11 @@
     )(place, scal, nf_t, gru, gru_bias, idx, hid, msg, state, near, d_final, mats)
 
 
-def final_kernel(place, scal, mine, other, first_in, near, far, eh, pre, feat, d_mine, d_other, first_out, acc, near_s, far_s, eh_s, pre_s, feat_s, sems, *, pair, group):
+def final_kernel(place, scal, first_in, *refs, pair, sides, group):
+    seconds, refs = refs[: len(sides)], refs[len(sides) :]
+    (near, far, eh, pre, feat), refs = refs[:5], refs[5:]
+    outs, refs = refs[: len(sides)], refs[len(sides) :]
+    first_out, acc, near_s, far_s, eh_s, pre_s, feat_s, sems = refs
     edge_blocks = ceil_blocks(scal[4])
     half = acc.shape[1]
     width = half // H
@@ -747,23 +751,23 @@
             for copy in copies(block + 1, 1 - slot):
                 copy.start()
 
-        sides = [near_s[slot, step].astype(F32) for step in range(STEPS)]
+        lefts = [near_s[slot, step].astype(F32) for step in range(STEPS)]
         low = eh_s[slot]
         d_pre = jnp.zeros((H, BLK), F32)
-        for side in range(2):
-            second = (mine, other)[side]
+        for number, side in enumerate(sides):
+            second = seconds[number]
             begin_row = pl.multiple_of(piece_index(place, pair, side) * width, width)
             tops = [far_s[slot, step, pl.ds(begin_row, width), :].astype(F32) for step in range(STEPS)]
             for part in range(width // group):
                 mats = []
                 for item in range(part * group, (part + 1) * group):
-                    value = sides[0] * tops[0][item : item + 1]
+                    value = lefts[0] * tops[0][item : item + 1]
                     for step in range(1, STEPS):
-                        value = value + sides[step] * tops[step][item : item + 1]
+                        value = value + lefts[step] * tops[step][item : item + 1]
                     mats.append(value.astype(BF))
                 flat = jnp.concatenate(mats, axis=0)
                 rows = slice(part * group * H, (part + 1) * group * H)
-                acc[side, rows, :] += dot(flat, low)
+                acc[number, rows, :] += dot(flat, low)
                 d_pre = d_pre + dot_tn(second[rows, :], flat)
         value = pre_s[slot]
         sig = sigmoid(value)
@@ -775,24 +779,21 @@
         return carry
 
     lax.fori_loop(0, edge_blocks, edge_block, 0)
-    d_mine[...] = acc[0]
-    d_other[...] = acc[1]
-
-
-def edge_grads(place, scal, mine, other, near, far, eh, pre, feat, first_in, pair, half):
+    for number, out in enumerate(outs):
+        out[...] = acc[number]
+
+
+def edge_grads(place, scal, seconds, near, far, eh, pre, feat, first_in, pair, sides, half):
     smem = pl.BlockSpec(memory_space=pltpu.SMEM)
     vmem = pl.BlockSpec(memory_space=pltpu.VMEM)
+    size = len(sides)
     return pl.pallas_call(
-        functools.partial(final_kernel, pair=pair, group=8),
-        in_specs=[smem] * 2 + [vmem] * 3 + [pl.BlockSpec(memory_space=pl.ANY)] * 5,
-        out_specs=[vmem] * 3,
-        out_shape=(
-            jax.ShapeDtypeStruct((half, H), F32),
-            jax.ShapeDtypeStruct((half, H), F32),
-            jax.ShapeDtypeStruct((FEAT, H), F32),
-        ),
+        functools.partial(final_kernel, pair=pair, sides=sides, group=8),
+        in_specs=[smem] * 2 + [vmem] * (1 + size) + [pl.BlockSpec(memory_space=pl.ANY)] * 5,
+        out_specs=[vmem] * (size + 1),
+        out_shape=[jax.ShapeDtypeStruct((half, H), F32)] * size + [jax.ShapeDtypeStruct((FEAT, H), F32)],
         scratch_shapes=[
-            pltpu.VMEM((2, half, H), F32),
+            pltpu.VMEM((size, half, H), F32),
             pltpu.VMEM((2, STEPS, H, BLK), BF),
             pltpu.VMEM((2, STEPS, H, BLK), BF),
             pltpu.VMEM((2, BLK, H), BF),
@@ -803,7 +804,7 @@
         compiler_params=pltpu.CompilerParams(vmem_limit_bytes=VMEM_LIMIT),
         cost_estimate=pl.CostEstimate(flops=9_000_000_000, transcendentals=0, bytes_accessed=5_000_000),
         name="edge_grads",
-    )(place, scal, mine, other, first_in, near, far, eh, pre, feat)
+    )(place, scal, first_in, *seconds, near, far, eh, pre, feat)
 
 
 def exact3(value):
@@ -819,13 +820,6 @@
 
 def pick(parts, index):
     return lax.dynamic_index_in_dim(parts, index, 0, keepdims=False)
-
-
-def tree_sum(value, axis, size):
-    values = [value] + [swap(value, axis, size, step) for step in range(1, size)]
-    while len(values) > 1:
-        values = [left + right for left, right in zip(values[::2], values[1::2])]
-    return values[0]
 
 
 def scaled(value):
@@ -904,7 +898,6 @@
     gates, groups, cores = sizes["gate"], sizes["edge"], sizes["grp"]
     gate, group, core = lax.axis_index("gate"), lax.axis_index("edge"), lax.axis_index("grp")
     place = jnp.stack([gate, core]).astype(jnp.int32)
-    axes = (("grp", cores), ("gate", gates), ("edge", groups))
 
     small_parts = [
         exact3(edge_second[EDGE_HID]),
@@ -919,13 +912,12 @@
     wide_rows = edge_second[:EDGE_HID].astype(BF).T
     half = wide_rows.shape[0] // 2
     halves = wide_rows.reshape(2, half, H)
-    own = pick(halves, core)
-    lines, own = lax.optimization_barrier((lines, own))
-    tails = jnp.stack([lines] + [swap(lines, "gate", gates, step) for step in range(1, gates)])
+    own = jnp.concatenate([pick(halves, core), lines], axis=0)
     second = [own, pick(halves, 1 - core)]
     for step in range(1, gates):
         got = swap(own, "gate", gates, step)
         second += [got, swap(got, "grp", cores, 1)]
+    tails = jnp.stack([part[half:] for part in second[::2]])
     order = [jnp.stack([tails[index ^ step] for index in range(gates)]) for step in range(gates)]
     tails = order[0]
     for step in range(1, gates):
@@ -944,7 +936,12 @@
     columns = jnp.arange(NT)[None, :]
     present = jnp.maximum(flag[:, None], (columns < NT // 2).astype(jnp.int32)).astype(F32)
     count = jnp.sum(present).reshape(1, 1)
-    count = count + swap(count, "grp", cores, 1)
+    for axis, size in (("grp", cores), ("edge", groups)):
+        step = 1
+        while step < size:
+            count = count + swap(count, axis, size, step)
+            step *= 2
+    inverse = (1.0 / count).reshape(1)
 
     nodes = node_feat.shape[0]
     edges = source.shape[0]
@@ -966,10 +963,9 @@
     lstm = jnp.pad(set_lstm, ((0, 7), (0, 0)))
     head = jnp.pad(head_weight, ((0, 7), (0, H - NT)))
 
+    data, inverse = lax.optimization_barrier((data, inverse))
     scal, pre, eh_t, eh, feat, idx = prep(place, mol, src2d, data, first3, edges, gates)
-    second, count = lax.optimization_barrier((second, count))
     hid, msg, state, near, mats = forward(place, scal, nf_t, embed_t, bias, gru, gru_bias, eh_t, idx, second)
-    inverse = (1.0 / tree_sum(count, "edge", groups)).reshape(1)
     d_final, read = readout(
         scal, inverse, hid, mol, lstm, head,
         jnp.pad(present, ((0, H - mols), (0, H - NT))), jnp.pad(target, ((0, H - mols), (0, H - NT))),
@@ -1013,7 +1009,7 @@
         (part,) = yield [swap((mine + got).astype(BF), "gate", gates, step)]
         return part.astype(F32)
 
-    def last_chain(mine, other):
+    def last_chain(other):
         (got,) = yield [swap(other, "grp", cores, 1)]
         total = mine + got
         for step in range(1, gates):
@@ -1028,12 +1024,17 @@
         shard = scaled(shard)
         moved = yield [swap(shard, "edge", groups, step) for step in range(1, groups)]
         tall = shard.shape[0]
-        full = jnp.zeros((groups * tall, H), shard.dtype)
-        for step, part in enumerate([shard] + moved):
-            full = lax.dynamic_update_slice_in_dim(full, part, (group ^ step) * tall, 0)
+
+        def joined(parts, me, total):
+            out = jnp.zeros((total, H), parts[0].dtype)
+            for step, part in enumerate(parts):
+                out = lax.dynamic_update_slice_in_dim(out, part, (me ^ step) * part.shape[0], 0)
+            return out
+
+        full = joined([shard] + moved, group, groups * tall)
         (got,) = yield [swap(full, "grp", cores, 1)]
-        full = jnp.where(core == 0, jnp.stack([full, got]), jnp.stack([got, full]))
-        grads = unscaled(full.reshape(cores, groups, tall, H)).reshape(cores, rows, H)[:, :half].reshape(-1, H)
+        full = joined([full, got], core, cores * groups * tall)
+        grads = unscaled(full.reshape(cores * groups, tall, H)).reshape(cores, rows, H)[:, :half].reshape(-1, H)
         narrow = results["narrow"]
         values = [(jnp.sum(grads * grads) + jnp.sum(narrow * narrow)).reshape(1, 1)]
         values += yield [swap(values[0], "gate", gates, step) for step in range(1, gates)]
@@ -1042,13 +1043,17 @@
         return grads, values[0][0, 0]
 
     def first_chain(first):
-        for axis, size in axes:
-            step = 1
-            while step < size:
-                (got,) = yield [swap(first, axis, size, step)]
-                first = first + got
-                step *= 2
-        return first
+        (got,) = yield [swap(first, "grp", cores, 1)]
+        values = [first + got]
+        values += yield [swap(values[0], "gate", gates, step) for step in range(1, gates)]
+        while len(values) > 1:
+            values = [left + right for left, right in zip(values[::2], values[1::2])]
+        step = 1
+        while step < groups:
+            (got,) = yield [swap(values[0], "edge", groups, step)]
+            values = [values[0] + got]
+            step *= 2
+        return values[0]
 
     results = {}
 
@@ -1066,14 +1071,19 @@
     fresh = narrow_chain()
     chains.append(("narrow", fresh, next(fresh)))
     for step in reversed(range(gates)):
-        mine, other, first = edge_grads(
-            place, scal, second[2 * step], second[2 * step + 1], near, far, eh, pre, feat, first, step, half
-        )
+        pieces = second[2 * step : 2 * step + 2]
+        edge_args = (near, far, eh, pre, feat)
+        if step:
+            mine, other, first = edge_grads(place, scal, pieces, *edge_args, first, step, (0, 1), half)
+        else:
+            other, first = edge_grads(place, scal, pieces[1:], *edge_args, first, step, (1,), half)
         first, moved = lax.optimization_barrier((first, [arrays for _, _, arrays in chains]))
         chains = advance(chains, moved)
-        fresh = wide_chain(mine, other, step) if step else last_chain(mine, other)
-        arrays = next(fresh)
-        chains.append((step, fresh, arrays))
+        fresh = wide_chain(mine, other, step) if step else last_chain(other)
+        chains.append((step, fresh, next(fresh)))
+    mine, first = edge_grads(place, scal, second[:1], *edge_args, first, 0, (0,), half)
+    first, moved = lax.optimization_barrier((first, [arrays for _, _, arrays in chains]))
+    chains = advance(chains, moved)
     fresh = first_chain(first)
     chains.append(("first", fresh, next(fresh)))
     while chains:

time: 625 us -> 380 us (0.61)
  local copies, waits for them, and re-layouts: 168 us -> 35.8 us
  other arithmetic: 127 us -> 27.5 us
  waiting for transfers between devices: 47.1 us -> 27.1 us
  Pallas kernels: 197 us -> 204 us
    another operation x2 -> x3, local copies, waits for them, and re-layouts: 85.4 us -> 2.67 us  [on_device(): tails = jnp.stack([part[half:] for part in second[::2]])]
    mul x2, other arithmetic: 73.9 us -> 2.19 us  [unscaled(): return low[..., :-16, :].astype(F32) * jnp.exp2(-power)]
    mul x1 -> x0, local copies, waits for them, and re-layouts: 54 us -> none  [unscaled(): return low[..., :-16, :].astype(F32) * jnp.exp2(-power)]
    select_n x1 -> x0, other arithmetic: 23.8 us -> none  [last_chain(): full = jnp.where(core == 0, jnp.stack([full, got]), jnp.stack([got, full]))]
    ppermute x47 -> x44, waiting for transfers between devices: 47.1 us -> 27.1 us  [swap(): lax.ppermute(value, axis, [(index, index ^ step) for index in range(size)])]
    pallas_call x4 -> x5, Pallas kernels: 45.6 us -> 52.7 us  [edge_grads(): pl.pallas_call(functools.partial(final_kernel, pair=pair, sides=sides, gr...]
    ppermute x47 -> x44, starting transfers between devices: 67.1 us -> 69.9 us  [swap(): lax.ppermute(value, axis, [(index, index ^ step) for index in range(size)])]
  transfers between devices with their start and end apart: 47 -> 44, of which waited for: 8 -> 12; matrix products, arithmetic and copies ran while one was open for 44% -> 10% of each run, Pallas kernels for 27% -> 30%
where the time goes in v2:
time: 380 us
  Pallas kernels  204 us (54%)
  starting transfers between devices  69.9 us (18%)
  local copies, waits for them, and re-layouts  35.8 us (9%)
  other arithmetic  27.5 us (7%)
  waiting for transfers between devices  27.1 us (7%)
  between operations  15 us (4%)
    ppermute x44, starting transfers between devices, swap(): lax.ppermute(value, axis, [(index, index ^ step) for index in range(size)])  69.9 us
    pallas_call x1, Pallas kernels, forward(): pl.pallas_call(functools.partial(forward_kernel, gates=gates), out_shape=...  58.9 us
    pallas_call x1, Pallas kernels, backward(): pl.pallas_call(backward_kernel, out_shape=(jax.ShapeDtypeStruct((STEPS, H...  54.9 us
    pallas_call x5, Pallas kernels, edge_grads(): pl.pallas_call(functools.partial(final_kernel, pair=pair, sides=sides, gr...  52.7 us
    ppermute x44, waiting for transfers between devices, swap(): lax.ppermute(value, axis, [(index, index ^ step) for index in range(size)])  27.1 us
    pallas_call x1, Pallas kernels, readout(): pl.pallas_call(readout_kernel, out_shape=(jax.ShapeDtypeStruct((H, nodes)...  22.6 us
    sub x5, other arithmetic, adamw(): weight - rate * (mom_hat / (jnp.sqrt(var_hat) + EPSILON) + DECAY * weight)  8.49 us
    pallas_call x1, Pallas kernels, prep(): pl.pallas_call(functools.partial(prep_kernel, edges=real, gates=gates, eb...  7.91 us
  transfers between devices with their start and end apart: 44, of which 12 were waited for; matrix products, arithmetic and copies ran while one was open for 10% of the time, Pallas kernels for 30%

profile of v2, /device:TPU:0, one launch (start us, length us, event | category | flops | bytes accessed | tf_op | source)
XLA Modules:
  0.0 379.6 jit_solution(1565921207582012829)
XLA Ops:
  0.7 1.8 fusion
  5.7 3.0 collective-permute-start.5
  11.9 1.9 concatenate.28
  22.9 3.4 collective-permute-start.1
  27.1 4.4 %collective-permute-start.2 = (f32[1,1]{1,0:T(1,128)}, f32[1,1]{1,0:T(1,128)}, u32[]{:S(2)}, u32[]{:S(2)}) collective-permute-start(f32[1,1]{1,0:T(1,128)} %add.281), channel_id=1, source_target_pairs={{0,8},{4,12},{8,0},{12,4},{1,9},{5,13},{9,1},{13,5},{2,10},{6,14},... | collective-permute-start | bytes 20 | tf_op jit(solution)/shard_map/ppermute | solution.py:818
  32.3 7.9 %prep.1 = (s32[8]{0:T(128)}, f32[128,5120]{1,0:T(8,128)}, bf16[144,5120]{1,0:T(8,128)(2,1)}, bf16[5120,128]{1,0:T(8,128)(2,1)}, bf16[32,5120]{1,0:T(8,128)(2,1)}, /*index=5*/s32[8,5120]{1,0:T(8,128)}) custom-call(s32[2]{0:T(128)} %pad_add_fusion.place, s32[1,3200]{1,0:T(1,128)} %reshape.180.mol, s32[32,256]{1,0:T(8,128)} %pad.55.src2d, ...), custom_call_target="tpu_custom_call" | custom-call | tf_op jit(solution)/shard_map/prep/pallas_call | solution.py:175
  48.8 58.9 %forward.1 = (bf16[4,128,3200]{2,1,0:T(8,128)(2,1)}, bf16[3,128,3200]{2,1,0:T(8,128)(2,1)}, f32[4,128,3200]{2,1,0:T(8,128)}, bf16[3,128,5120]{2,1,0:T(8,128)(2,1)}, bf16[40,4,4096,128]{3,2,1,0:T(8,128)(2,1)}) custom-call(s32[2]{0:T(128)} %pad_add_fusion.place, s32[8]{0:T(128)} %get-tuple-element.96.scal, bf16[16,3200]{1,0:T(8,128)(2,1)} %pad.62.nf_t, ...), custom_call_target="tpu_custom_call" | custom-call | flops 60000002048 | bytes 20000000 | tf_op jit(solution)/shard_map/forward/pallas_call | solution.py:413
  107.8 22.6 %readout.1 = (f32[128,3200]{1,0:T(8,128)}, f32[1328,128]{1,0:T(8,128)}) custom-call(s32[8]{0:T(128)} %get-tuple-element.96.scal, f32[1]{0:T(128)} %bitcast.3.inverse, s32[1,3200]{1,0:T(1,128)} %reshape.180.mol, f32[392,512]{1,0:T(8,128)} %pad.58.lstm, f32[264,128]{1,0:T(8,128)} %pad.59.head, f32[128,128]{1,0:T(8,128)} %pad.60.present, ...), custom_call_target="tpu_custom_call" | custom-call | flops 30000001024 | bytes 5000000 | tf_op jit(solution)/shard_map/readout/pallas_call | solution.py:578
  131.8 54.9 %backward.1 = (bf16[3,128,5120]{2,1,0:T(8,128)(2,1)}, f32[4,320,128]{2,1,0:T(8,128)}) custom-call(s32[2]{0:T(128)} %pad_add_fusion.place, s32[8]{0:T(128)} %get-tuple-element.96.scal, bf16[16,3200]{1,0:T(8,128)(2,1)} %pad.62.nf_t, bf16[2,384,128]{2,1,0:T(8,128)(2,1)} %bitcast.122, f32[2,384,1]{2,1,0:T(8,128)} %reshape.199.gru_bias, ...), custom_call_target="tpu_custom_call" | custom-call | flops 60000002048 | bytes 20000000 | tf_op jit(solution)/shard_map/backward/pallas_call | solution.py:692
  186.9 8.9 %collective-permute-start.10 = (f32[664,128]{1,0:T(8,128)S(1)}, f32[664,128]{1,0:T(8,128)S(1)}, u32[]{:S(2)}, u32[]{:S(2)}) collective-permute-start(f32[664,128]{1,0:T(8,128)S(1)} %bitcast_add_fusion), channel_id=1, source_target_pairs={{0,1},{1,0},{2,3},{3,2},{4,5},{5,4},{6,7},{7,6},{8,9},{9,8},{10,11... | collective-permute-start | bytes 1019912 | tf_op jit(solution)/shard_map/ppermute | solution.py:818
  195.8 5.0 %collective-permute-start.11 = (f32[4,320,128]{2,1,0:T(8,128)}, f32[4,320,128]{2,1,0:T(8,128)S(1)}, u32[]{:S(2)}, u32[]{:S(2)}) collective-permute-start(f32[4,320,128]{2,1,0:T(8,128)} %get-tuple-element.115), channel_id=1, source_target_pairs={{0,16},{16,0},{1,17},{17,1},{2,18},{18,2},{3,19},{19,3},{4,20},{20... | collective-permute-start | bytes 1966088 | tf_op jit(solution)/shard_map/ppermute | solution.py:818
  201.5 11.5 %edge_grads.5 = (f32[2048,128]{1,0:T(8,128)}, f32[2048,128]{1,0:T(8,128)}, f32[32,128]{1,0:T(8,128)}) custom-call(s32[2]{0:T(128)} %pad_add_fusion.place, s32[8]{0:T(128)} %get-tuple-element.96.scal, f32[32,128]{1,0:T(8,128)} %broadcast_in_dim.9.first_in, bf16[2352,128]{1,0:T(8,128)(2,1)} %collective-permute-done.3.refs_6_.refs_0_, ...), custom_call_target="tpu_custom_call" | custom-call | flops 8999999488 | bytes 5000000 | tf_op jit(solution)/shard_map/edge_grads/pallas_call | solution.py:790
  216.2 1.9 collective-permute-start.13
  219.8 1.9 collective-permute-start.12
  221.7 11.4 %edge_grads.6 = (f32[2048,128]{1,0:T(8,128)}, f32[2048,128]{1,0:T(8,128)}, f32[32,128]{1,0:T(8,128)}) custom-call(s32[2]{0:T(128)} %pad_add_fusion.place, s32[8]{0:T(128)} %get-tuple-element.96.scal, f32[32,128]{1,0:T(8,128)} %get-tuple-element.117.first_in, bf16[2352,128]{1,0:T(8,128)(2,1)} %collective-permute-done.4.refs_4_.refs_0_, ...), custom_call_target="tpu_custom_call" | custom-call | flops 8999999488 | bytes 5000000 | tf_op jit(solution)/shard_map/edge_grads/pallas_call | solution.py:790
  233.3 1.7 collective-permute-done.12
  235.2 1.9 collective-permute-start.19
  238.6 1.6 collective-permute-start.17
  240.2 11.4 %edge_grads.7 = (f32[2048,128]{1,0:T(8,128)}, f32[2048,128]{1,0:T(8,128)}, f32[32,128]{1,0:T(8,128)}) custom-call(s32[2]{0:T(128)} %pad_add_fusion.place, s32[8]{0:T(128)} %get-tuple-element.96.scal, f32[32,128]{1,0:T(8,128)} %get-tuple-element.122.first_in, bf16[2352,128]{1,0:T(8,128)(2,1)} %collective-permute-done.5.refs_2_.refs_0_, ...), custom_call_target="tpu_custom_call" | custom-call | flops 8999999488 | bytes 5000000 | tf_op jit(solution)/shard_map/edge_grads/pallas_call | solution.py:790
  251.8 2.4 add_convert_fusion.1
  254.2 1.8 collective-permute-start.23
  256.0 3.7 collective-permute-start.22
  259.9 8.9 %edge_grads.8 = (f32[2048,128]{1,0:T(8,128)}, f32[32,128]{1,0:T(8,128)}) custom-call(s32[2]{0:T(128)} %pad_add_fusion.place, s32[8]{0:T(128)} %get-tuple-element.96.scal, f32[32,128]{1,0:T(8,128)} %get-tuple-element.131.first_in, bf16[2048,128]{1,0:T(8,128)(2,1)} %get-tuple-element.296.refs_1_.refs_0_, ...), custom_call_target="tpu_custom_call" | custom-call | flops 8999999488 | bytes 5000000 | tf_op jit(solution)/shard_map/edge_grads/pallas_call | solution.py:790
  268.9 4.6 %collective-permute-done.22 = f32[320,128]{1,0:T(8,128)S(1)} collective-permute-done((f32[320,128]{1,0:T(8,128)S(1)}, f32[320,128]{1,0:T(8,128)S(1)}, u32[]{:S(2)}, u32[]{:S(2)}) %collective-permute-start.22) | collective-permute-done | bytes 163872 | tf_op jit(solution)/shard_map/ppermute | solution.py:818
  273.5 7.2 %collective-permute-done.21 = f32[664,128]{1,0:T(8,128)S(1)} collective-permute-done((f32[664,128]{1,0:T(8,128)S(1)}, f32[664,128]{1,0:T(8,128)S(1)}, u32[]{:S(2)}, u32[]{:S(2)}) %collective-permute-start.21) | collective-permute-done | bytes 340000 | tf_op jit(solution)/shard_map/ppermute | solution.py:818
  280.7 2.4 add_convert_fusion
  284.7 9.4 %edge_grads.9 = (f32[2048,128]{1,0:T(8,128)}, f32[32,128]{1,0:T(8,128)}) custom-call(s32[2]{0:T(128)} %pad_add_fusion.place, s32[8]{0:T(128)} %get-tuple-element.96.scal, f32[32,128]{1,0:T(8,128)} %get-tuple-element.138.first_in, bf16[2352,128]{1,0:T(8,128)(2,1)} %copy-done.15, bf16[3,128,5120]{2,1,0:T(8,128)(2,1)} %get-tuple-element.104.near.refs_2_.refs_1_, ...), custom_call_target="tpu_custom_call" | custom-call | flops 8999999488 | bytes 5000000 | tf_op jit(solution)/shard_map/edge_grads/pallas_call | solution.py:790
  298.0 2.6 abs_reduce_fusion
  301.6 2.0 collective-permute-start.29
  303.6 2.4 collective-permute-start.30
  309.2 5.7 %collective-permute-done.29 = f16[528,128]{1,0:T(8,128)(2,1)S(1)} collective-permute-done((f16[528,128]{1,0:T(8,128)(2,1)S(1)}, f16[528,128]{1,0:T(8,128)(2,1)S(1)}, u32[]{:S(2)}, u32[]{:S(2)}) %collective-permute-start.29) | collective-permute-done | bytes 135200 | tf_op jit(solution)/shard_map/ppermute | solution.py:818
  320.2 3.0 collective-permute-start.32
  323.3 2.3 collective-permute-start.34
  325.6 1.8 collective-permute-start.35
  327.4 1.9 multiply_reduce_fusion.1
  329.4 1.7 collective-permute-start.37
  334.0 1.7 collective-permute-done.33
  335.9 2.5 collective-permute-start.39
  340.1 2.2 collective-permute-start.43
  342.6 2.2 convert_multiply_fusion
  346.2 3.3 collective-permute-start.40
  349.5 1.8 collective-permute-start.41
  351.2 2.4 collective-permute-start.42
  353.6 2.2 collective-permute-done.42
  359.0 1.8 multiply_subtract_fusion.2
  360.7 1.6 copy.186
  367.2 3.1 multiply_subtract_fusion
  371.2 7.2 %wide_adamw.1 = (f32[129,4096]{1,0:T(8,128)}, f32[129,4096]{1,0:T(8,128)}, f32[129,4096]{1,0:T(8,128)}) custom-call(f32[3]{0:T(128)} %pad_maximum_fusion.5.scale, f32[4096,128]{1,0:T(8,128)} %bitcast.106, f32[1,4096]{1,0:T(1,128)} %bitcast.124, f32[129,4096]{1,0:T(8,128)} %weight.1, f32[129,4096]{1,0:T(8,128)} %mom.1, f32[129,4096]{1,0:T(8,128)} %var.1), custom_call_target="tpu_custom_call" | custom-call | tf_op jit(solution)/shard_map/wide_adamw/pallas_call | solution.py:872
  (270 shorter events, 52.9 us)
Async XLA Ops:
  5.7 34.5 %collective-permute-start.5 = (bf16[2352,128]{1,0:T(8,128)(2,1)S(1)}, bf16[2352,128]{1,0:T(8,128)(2,1)}, u32[]{:S(2)}, u32[]{:S(2)}) collective-permute-start(bf16[2352,128]{1,0:T(8,128)(2,1)S(1)} %pad_maximum_fusion.refs_0_), channel_id=1, source_target_pairs={{0,1},{1,0},{2,3},{3,2},{4,5},{5,4},{6,7},{7,6},{8,9},{9,8},{10,11... | collective-permute-start | bytes 1806344 | tf_op jit(solution)/shard_map/ppermute | solution.py:818
  8.7 31.6 %collective-permute-start.4 = (bf16[2352,128]{1,0:T(8,128)(2,1)S(1)}, bf16[2352,128]{1,0:T(8,128)(2,1)}, u32[]{:S(2)}, u32[]{:S(2)}) collective-permute-start(bf16[2352,128]{1,0:T(8,128)(2,1)S(1)} %pad_maximum_fusion.refs_0_), channel_id=1, source_target_pairs={{0,2},{1,3},{2,0},{3,1},{4,6},{5,7},{6,4},{7,5},{8,10},{9,11},{10,... | collective-permute-start | bytes 1806344 | tf_op jit(solution)/shard_map/ppermute | solution.py:818
  10.2 32.4 %collective-permute-start.3 = (bf16[2352,128]{1,0:T(8,128)(2,1)S(1)}, bf16[2352,128]{1,0:T(8,128)(2,1)}, u32[]{:S(2)}, u32[]{:S(2)}) collective-permute-start(bf16[2352,128]{1,0:T(8,128)(2,1)S(1)} %pad_maximum_fusion.refs_0_), channel_id=1, source_target_pairs={{0,3},{1,2},{2,1},{3,0},{4,7},{5,6},{6,5},{7,4},{8,11},{9,10},{10,... | collective-permute-start | bytes 1806344 | tf_op jit(solution)/shard_map/ppermute | solution.py:818
  11.0 10.6 %collective-permute-start = (f32[1,1]{1,0:T(1,128)}, f32[1,1]{1,0:T(1,128)}, u32[]{:S(2)}, u32[]{:S(2)}) collective-permute-start(f32[1,1]{1,0:T(1,128)} %bitcast.2), channel_id=1, source_target_pairs={{0,16},{16,0},{1,17},{17,1},{2,18},{18,2},{3,19},{19,3},{4,20},{20... | collective-permute-start | bytes 20 | tf_op jit(solution)/shard_map/ppermute | solution.py:818
  18.5 25.1 %copy-start.5 = (f32[257,12]{1,0:T(8,128)}, f32[257,12]{1,0:T(8,128)S(1)}, u32[]{:S(2)}) copy-start(f32[257,12]{1,0:T(8,128)S(1)} %copy.167) | copy-start | bytes 37012
  22.9 3.6 collective-permute-start.1
  27.1 4.6 %collective-permute-start.2 = (f32[1,1]{1,0:T(1,128)}, f32[1,1]{1,0:T(1,128)}, u32[]{:S(2)}, u32[]{:S(2)}) collective-permute-start(f32[1,1]{1,0:T(1,128)} %add.281), channel_id=1, source_target_pairs={{0,8},{4,12},{8,0},{12,4},{1,9},{5,13},{9,1},{13,5},{2,10},{6,14},... | collective-permute-start | bytes 20 | tf_op jit(solution)/shard_map/ppermute | solution.py:818
  40.3 7.3 %collective-permute-start.6 = (bf16[2352,128]{1,0:T(8,128)(2,1)}, bf16[2352,128]{1,0:T(8,128)(2,1)S(1)}, u32[]{:S(2)}, u32[]{:S(2)}) collective-permute-start(bf16[2352,128]{1,0:T(8,128)(2,1)} %collective-permute-done.5.refs_2_.refs_0_), channel_id=1, source_target_pairs={{0,16},{16,0},{1,17},{17,1},{2,18},{18,2},{3,19},{19,3},{4,20},{20... | collective-permute-start | bytes 1806344 | tf_op jit(solution)/shard_map/ppermute | solution.py:818
  40.3 7.2 %collective-permute-start.7 = (bf16[2352,128]{1,0:T(8,128)(2,1)}, bf16[2352,128]{1,0:T(8,128)(2,1)S(1)}, u32[]{:S(2)}, u32[]{:S(2)}) collective-permute-start(bf16[2352,128]{1,0:T(8,128)(2,1)} %collective-permute-done.4.refs_4_.refs_0_), channel_id=1, source_target_pairs={{0,16},{16,0},{1,17},{17,1},{2,18},{18,2},{3,19},{19,3},{4,20},{20... | collective-permute-start | bytes 1806344 | tf_op jit(solution)/shard_map/ppermute | solution.py:818
  42.6 4.9 %collective-permute-start.8 = (bf16[2352,128]{1,0:T(8,128)(2,1)}, bf16[2352,128]{1,0:T(8,128)(2,1)S(1)}, u32[]{:S(2)}, u32[]{:S(2)}) collective-permute-start(bf16[2352,128]{1,0:T(8,128)(2,1)} %collective-permute-done.3.refs_6_.refs_0_), channel_id=1, source_target_pairs={{0,16},{16,0},{1,17},{17,1},{2,18},{18,2},{3,19},{19,3},{4,20},{20... | collective-permute-start | bytes 1806344 | tf_op jit(solution)/shard_map/ppermute | solution.py:818
  131.4 55.5 %collective-permute-start.9 = (f32[664,128]{1,0:T(8,128)S(1)}, f32[664,128]{1,0:T(8,128)S(1)}, u32[]{:S(2)}, u32[]{:S(2)}) collective-permute-start(f32[664,128]{1,0:T(8,128)S(1)} %dynamic-slice_bitcast_fusion.2), channel_id=1, source_target_pairs={{0,16},{16,0},{1,17},{17,1},{2,18},{18,2},{3,19},{19,3},{4,20},{20... | collective-permute-start | bytes 1019912 | tf_op jit(solution)/shard_map/ppermute | solution.py:818
  131.8 55.0 %copy-start.13 = (f32[1328,128]{1,0:T(8,128)S(1)}, f32[1328,128]{1,0:T(8,128)}, u32[]{:S(2)}) copy-start(f32[1328,128]{1,0:T(8,128)} %get-tuple-element.101) | copy-start | bytes 2039812
  186.9 28.5 %collective-permute-start.10 = (f32[664,128]{1,0:T(8,128)S(1)}, f32[664,128]{1,0:T(8,128)S(1)}, u32[]{:S(2)}, u32[]{:S(2)}) collective-permute-start(f32[664,128]{1,0:T(8,128)S(1)} %bitcast_add_fusion), channel_id=1, source_target_pairs={{0,1},{1,0},{2,3},{3,2},{4,5},{5,4},{6,7},{7,6},{8,9},{9,8},{10,11... | collective-permute-start | bytes 1019912 | tf_op jit(solution)/shard_map/ppermute | solution.py:818
  195.8 19.6 %collective-permute-start.11 = (f32[4,320,128]{2,1,0:T(8,128)}, f32[4,320,128]{2,1,0:T(8,128)S(1)}, u32[]{:S(2)}, u32[]{:S(2)}) collective-permute-start(f32[4,320,128]{2,1,0:T(8,128)} %get-tuple-element.115), channel_id=1, source_target_pairs={{0,16},{16,0},{1,17},{17,1},{2,18},{18,2},{3,19},{19,3},{4,20},{20... | collective-permute-start | bytes 1966088 | tf_op jit(solution)/shard_map/ppermute | solution.py:818
  212.9 22.1 %collective-permute-start.16 = (f32[2048,128]{1,0:T(8,128)}, f32[2048,128]{1,0:T(8,128)S(1)}, u32[]{:S(2)}, u32[]{:S(2)}) collective-permute-start(f32[2048,128]{1,0:T(8,128)} %get-tuple-element.120), channel_id=1, source_target_pairs={{0,16},{16,0},{1,17},{17,1},{2,18},{18,2},{3,19},{19,3},{4,20},{20... | collective-permute-start | bytes 3145736 | tf_op jit(solution)/shard_map/ppermute | solution.py:818
  216.2 16.9 %collective-permute-start.13 = (f32[320,128]{1,0:T(8,128)}, f32[320,128]{1,0:T(8,128)S(1)}, u32[]{:S(2)}, u32[]{:S(2)}) collective-permute-start(f32[320,128]{1,0:T(8,128)} %get-tuple-element.304), channel_id=1, source_target_pairs={{0,1},{1,0},{2,3},{3,2},{4,5},{5,4},{6,7},{7,6},{8,9},{9,8},{10,11... | collective-permute-start | bytes 491528 | tf_op jit(solution)/shard_map/ppermute | solution.py:818
  218.1 15.1 %collective-permute-start.14 = (f32[320,128]{1,0:T(8,128)}, f32[320,128]{1,0:T(8,128)S(1)}, u32[]{:S(2)}, u32[]{:S(2)}) collective-permute-start(f32[320,128]{1,0:T(8,128)} %get-tuple-element.303), channel_id=1, source_target_pairs={{0,2},{1,3},{2,0},{3,1},{4,6},{5,7},{6,4},{7,5},{8,10},{9,11},{10,... | collective-permute-start | bytes 491528 | tf_op jit(solution)/shard_map/ppermute | solution.py:818
  219.0 14.3 %collective-permute-start.15 = (f32[320,128]{1,0:T(8,128)}, f32[320,128]{1,0:T(8,128)}, u32[]{:S(2)}, u32[]{:S(2)}) collective-permute-start(f32[320,128]{1,0:T(8,128)} %get-tuple-element.302), channel_id=1, source_target_pairs={{0,3},{1,2},{2,1},{3,0},{4,7},{5,6},{6,5},{7,4},{8,11},{9,10},{10,... | collective-permute-start | bytes 491528 | tf_op jit(solution)/shard_map/ppermute | solution.py:818
  219.8 15.2 %collective-permute-start.12 = (f32[664,128]{1,0:T(8,128)S(1)}, f32[664,128]{1,0:T(8,128)S(1)}, u32[]{:S(2)}, u32[]{:S(2)}) collective-permute-start(f32[664,128]{1,0:T(8,128)S(1)} %add.286), channel_id=1, source_target_pairs={{0,2},{1,3},{2,0},{3,1},{4,6},{5,7},{6,4},{7,5},{8,10},{9,11},{10,... | collective-permute-start | bytes 1019912 | tf_op jit(solution)/shard_map/ppermute | solution.py:818
  233.2 18.6 %collective-permute-start.20 = (f32[2048,128]{1,0:T(8,128)}, f32[2048,128]{1,0:T(8,128)}, u32[]{:S(2)}, u32[]{:S(2)}) collective-permute-start(f32[2048,128]{1,0:T(8,128)} %get-tuple-element.129), channel_id=1, source_target_pairs={{0,16},{16,0},{1,17},{17,1},{2,18},{18,2},{3,19},{19,3},{4,20},{20... | collective-permute-start | bytes 3145736 | tf_op jit(solution)/shard_map/ppermute | solution.py:818
  235.2 16.6 %collective-permute-start.19 = (bf16[2048,128]{1,0:T(8,128)(2,1)S(1)}, bf16[2048,128]{1,0:T(8,128)(2,1)S(1)}, u32[]{:S(2)}, u32[]{:S(2)}) collective-permute-start(bf16[2048,128]{1,0:T(8,128)(2,1)S(1)} %add_convert_fusion.2), channel_id=1, source_target_pairs={{0,3},{1,2},{2,1},{3,0},{4,7},{5,6},{6,5},{7,4},{8,11},{9,10},{10,... | collective-permute-start | bytes 1572872 | tf_op jit(solution)/shard_map/ppermute | solution.py:818
  238.0 13.7 %collective-permute-start.18 = (f32[320,128]{1,0:T(8,128)S(1)}, f32[320,128]{1,0:T(8,128)S(1)}, u32[]{:S(2)}, u32[]{:S(2)}) collective-permute-start(f32[320,128]{1,0:T(8,128)S(1)} %fusion.7), channel_id=1, source_target_pairs={{0,4},{4,0},{8,12},{12,8},{1,5},{5,1},{9,13},{13,9},{2,6},{6,2},{1... | collective-permute-start | bytes 491528 | tf_op jit(solution)/shard_map/ppermute | solution.py:818
  238.6 13.1 %collective-permute-start.17 = (f32[664,128]{1,0:T(8,128)S(1)}, f32[664,128]{1,0:T(8,128)S(1)}, u32[]{:S(2)}, u32[]{:S(2)}) collective-permute-start(f32[664,128]{1,0:T(8,128)S(1)} %add.291), channel_id=1, source_target_pairs={{0,4},{4,0},{8,12},{12,8},{1,5},{5,1},{9,13},{13,9},{2,6},{6,2},{1... | collective-permute-start | bytes 1019912 | tf_op jit(solution)/shard_map/ppermute | solution.py:818
  251.7 29.1 %collective-permute-start.24 = (f32[2048,128]{1,0:T(8,128)}, f32[2048,128]{1,0:T(8,128)}, u32[]{:S(2)}, u32[]{:S(2)}) collective-permute-start(f32[2048,128]{1,0:T(8,128)} %get-tuple-element.136), channel_id=1, source_target_pairs={{0,16},{16,0},{1,17},{17,1},{2,18},{18,2},{3,19},{19,3},{4,20},{20... | collective-permute-start | bytes 3145736 | tf_op jit(solution)/shard_map/ppermute | solution.py:818
  254.2 26.6 %collective-permute-start.23 = (bf16[2048,128]{1,0:T(8,128)(2,1)}, bf16[2048,128]{1,0:T(8,128)(2,1)S(1)}, u32[]{:S(2)}, u32[]{:S(2)}) collective-permute-start(bf16[2048,128]{1,0:T(8,128)(2,1)} %add_convert_fusion.1), channel_id=1, source_target_pairs={{0,2},{1,3},{2,0},{3,1},{4,6},{5,7},{6,4},{7,5},{8,10},{9,11},{10,... | collective-permute-start | bytes 1572872 | tf_op jit(solution)/shard_map/ppermute | solution.py:818
  256.0 17.4 %collective-permute-start.22 = (f32[320,128]{1,0:T(8,128)S(1)}, f32[320,128]{1,0:T(8,128)S(1)}, u32[]{:S(2)}, u32[]{:S(2)}) collective-permute-start(f32[320,128]{1,0:T(8,128)S(1)} %add.298), channel_id=1, source_target_pairs={{0,8},{4,12},{8,0},{12,4},{1,9},{5,13},{9,1},{13,5},{2,10},{6,14},... | collective-permute-start | bytes 491528 | tf_op jit(solution)/shard_map/ppermute | solution.py:818
  259.8 20.9 %collective-permute-start.21 = (f32[664,128]{1,0:T(8,128)S(1)}, f32[664,128]{1,0:T(8,128)S(1)}, u32[]{:S(2)}, u32[]{:S(2)}) collective-permute-start(f32[664,128]{1,0:T(8,128)S(1)} %add.297), channel_id=1, source_target_pairs={{0,8},{4,12},{8,0},{12,4},{1,9},{5,13},{9,1},{13,5},{2,10},{6,14},... | collective-permute-start | bytes 1019912 | tf_op jit(solution)/shard_map/ppermute | solution.py:818
  268.8 28.5 %collective-permute-start.27 = (f32[2048,128]{1,0:T(8,128)}, f32[2048,128]{1,0:T(8,128)S(1)}, u32[]{:S(2)}, u32[]{:S(2)}) collective-permute-start(f32[2048,128]{1,0:T(8,128)} %get-tuple-element.142), channel_id=1, source_target_pairs={{0,16},{16,0},{1,17},{17,1},{2,18},{18,2},{3,19},{19,3},{4,20},{20... | collective-permute-start | bytes 3145736 | tf_op jit(solution)/shard_map/ppermute | solution.py:818
  283.1 14.1 %collective-permute-start.26 = (bf16[2048,128]{1,0:T(8,128)(2,1)}, bf16[2048,128]{1,0:T(8,128)(2,1)S(1)}, u32[]{:S(2)}, u32[]{:S(2)}) collective-permute-start(bf16[2048,128]{1,0:T(8,128)(2,1)} %add_convert_fusion), channel_id=1, source_target_pairs={{0,1},{1,0},{2,3},{3,2},{4,5},{5,4},{6,7},{7,6},{8,9},{9,8},{10,11... | collective-permute-start | bytes 1572872 | tf_op jit(solution)/shard_map/ppermute | solution.py:818
  284.7 12.4 %collective-permute-start.25 = (f32[664,128]{1,0:T(8,128)S(1)}, f32[664,128]{1,0:T(8,128)S(1)}, u32[]{:S(2)}, u32[]{:S(2)}) collective-permute-start(f32[664,128]{1,0:T(8,128)S(1)} %add.300), channel_id=1, source_target_pairs={{0,16},{16,0},{1,17},{17,1},{2,18},{18,2},{3,19},{19,3},{4,20},{20... | collective-permute-start | bytes 1019912 | tf_op jit(solution)/shard_map/ppermute | solution.py:818
  301.6 7.6 %collective-permute-start.28 = (f16[528,128]{1,0:T(8,128)(2,1)S(1)}, f16[528,128]{1,0:T(8,128)(2,1)S(1)}, u32[]{:S(2)}, u32[]{:S(2)}) collective-permute-start(f16[528,128]{1,0:T(8,128)(2,1)S(1)} %get-tuple-element.307), channel_id=1, source_target_pairs={{0,4},{4,0},{8,12},{12,8},{1,5},{5,1},{9,13},{13,9},{2,6},{6,2},{1... | collective-permute-start | bytes 405512 | tf_op jit(solution)/shard_map/ppermute | solution.py:818
  301.6 13.2 %collective-permute-start.29 = (f16[528,128]{1,0:T(8,128)(2,1)S(1)}, f16[528,128]{1,0:T(8,128)(2,1)S(1)}, u32[]{:S(2)}, u32[]{:S(2)}) collective-permute-start(f16[528,128]{1,0:T(8,128)(2,1)S(1)} %get-tuple-element.306), channel_id=1, source_target_pairs={{0,8},{4,12},{8,0},{12,4},{1,9},{5,13},{9,1},{13,5},{2,10},{6,14},... | collective-permute-start | bytes 405512 | tf_op jit(solution)/shard_map/ppermute | solution.py:818
  303.6 11.2 %collective-permute-start.30 = (f16[528,128]{1,0:T(8,128)(2,1)S(1)}, f16[528,128]{1,0:T(8,128)(2,1)S(1)}, u32[]{:S(2)}, u32[]{:S(2)}) collective-permute-start(f16[528,128]{1,0:T(8,128)(2,1)S(1)} %get-tuple-element.305), channel_id=1, source_target_pairs={{0,12},{4,8},{8,4},{12,0},{1,13},{5,9},{9,5},{13,1},{2,14},{6,10},... | collective-permute-start | bytes 405512 | tf_op jit(solution)/shard_map/ppermute | solution.py:818
  306.0 1.7 collective-permute-start.31
  320.2 13.8 %collective-permute-start.32 = (f16[528,128]{1,0:T(8,128)(2,1)S(1)}, f16[528,128]{1,0:T(8,128)(2,1)S(1)}, u32[]{:S(2)}, u32[]{:S(2)}) collective-permute-start(f16[528,128]{1,0:T(8,128)(2,1)S(1)} %get-tuple-element.308), channel_id=1, source_target_pairs={{0,4},{4,0},{8,12},{12,8},{1,5},{5,1},{9,13},{13,9},{2,6},{6,2},{1... | collective-permute-start | bytes 405512 | tf_op jit(solution)/shard_map/ppermute | solution.py:818
  323.2 12.5 %collective-permute-start.33 = (f16[528,128]{1,0:T(8,128)(2,1)S(1)}, f16[528,128]{1,0:T(8,128)(2,1)S(1)}, u32[]{:S(2)}, u32[]{:S(2)}) collective-permute-start(f16[528,128]{1,0:T(8,128)(2,1)S(1)} %get-tuple-element.308), channel_id=1, source_target_pairs={{0,8},{4,12},{8,0},{12,4},{1,9},{5,13},{9,1},{13,5},{2,10},{6,14},... | collective-permute-start | bytes 405512 | tf_op jit(solution)/shard_map/ppermute | solution.py:818
  323.3 12.4 %collective-permute-start.34 = (f16[528,128]{1,0:T(8,128)(2,1)S(1)}, f16[528,128]{1,0:T(8,128)(2,1)S(1)}, u32[]{:S(2)}, u32[]{:S(2)}) collective-permute-start(f16[528,128]{1,0:T(8,128)(2,1)S(1)} %get-tuple-element.308), channel_id=1, source_target_pairs={{0,12},{4,8},{8,4},{12,0},{1,13},{5,9},{9,5},{13,1},{2,14},{6,10},... | collective-permute-start | bytes 405512 | tf_op jit(solution)/shard_map/ppermute | solution.py:818
  325.6 3.7 collective-permute-start.35
  329.4 4.1 %collective-permute-start.36 = (f32[32,128]{1,0:T(8,128)S(1)}, f32[32,128]{1,0:T(8,128)S(1)}, u32[]{:S(2)}, u32[]{:S(2)}) collective-permute-start(f32[32,128]{1,0:T(8,128)S(1)} %add.314), channel_id=1, source_target_pairs={{0,2},{1,3},{2,0},{3,1},{4,6},{5,7},{6,4},{7,5},{8,10},{9,11},{10,... | collective-permute-start | bytes 49160 | tf_op jit(solution)/shard_map/ppermute | solution.py:818
  329.4 4.6 %collective-permute-start.37 = (f32[32,128]{1,0:T(8,128)S(1)}, f32[32,128]{1,0:T(8,128)S(1)}, u32[]{:S(2)}, u32[]{:S(2)}) collective-permute-start(f32[32,128]{1,0:T(8,128)S(1)} %add.314), channel_id=1, source_target_pairs={{0,3},{1,2},{2,1},{3,0},{4,7},{5,6},{6,5},{7,4},{8,11},{9,10},{10,... | collective-permute-start | bytes 49160 | tf_op jit(solution)/shard_map/ppermute | solution.py:818
  335.8 4.3 %collective-permute-start.38 = (f16[2112,128]{1,0:T(8,128)(2,1)S(1)}, f16[2112,128]{1,0:T(8,128)(2,1)S(1)}, u32[]{:S(2)}, u32[]{:S(2)}) collective-permute-start(f16[2112,128]{1,0:T(8,128)(2,1)S(1)} %constant_dynamic-update-slice_fusion.2), channel_id=1, source_target_pairs={{0,16},{16,0},{1,17},{17,1},{2,18},{18,2},{3,19},{19,3},{4,20},{20... | collective-permute-start | bytes 1622024 | tf_op jit(solution)/shard_map/ppermute | solution.py:818
  335.9 4.2 %collective-permute-start.39 = (f32[32,128]{1,0:T(8,128)S(1)}, f32[32,128]{1,0:T(8,128)S(1)}, u32[]{:S(2)}, u32[]{:S(2)}) collective-permute-start(f32[32,128]{1,0:T(8,128)S(1)} %add_add_fusion), channel_id=1, source_target_pairs={{0,4},{4,0},{8,12},{12,8},{1,5},{5,1},{9,13},{13,9},{2,6},{6,2},{1... | collective-permute-start | bytes 49160 | tf_op jit(solution)/shard_map/ppermute | solution.py:818
  340.1 15.6 %collective-permute-start.43 = (f32[32,128]{1,0:T(8,128)S(1)}, f32[32,128]{1,0:T(8,128)S(1)}, u32[]{:S(2)}, u32[]{:S(2)}) collective-permute-start(f32[32,128]{1,0:T(8,128)S(1)} %add.325), channel_id=1, source_target_pairs={{0,8},{4,12},{8,0},{12,4},{1,9},{5,13},{9,1},{13,5},{2,10},{6,14},... | collective-permute-start | bytes 49160 | tf_op jit(solution)/shard_map/ppermute | solution.py:818
  342.6 23.2 %copy-start.31 = (f32[16,32]{1,0:T(8,128)S(1)}, f32[16,32]{1,0:T(8,128)}, u32[]{:S(2)}) copy-start(f32[16,32]{1,0:T(8,128)} %param.35) | copy-start | bytes 6148
  342.6 24.6 %copy-start.1 = (f32[385,512]{1,0:T(8,128)S(1)}, f32[385,512]{1,0:T(8,128)}, u32[]{:S(2)}) copy-start(f32[385,512]{1,0:T(8,128)} %param.39) | copy-start | bytes 2365444
  346.2 7.4 %collective-permute-start.40 = (f32[1,1]{1,0:T(1,128)}, f32[1,1]{1,0:T(1,128)}, u32[]{:S(2)}, u32[]{:S(2)}) collective-permute-start(f32[1,1]{1,0:T(1,128)} %bitcast.47), channel_id=1, source_target_pairs={{0,1},{1,0},{2,3},{3,2},{4,5},{5,4},{6,7},{7,6},{8,9},{9,8},{10,11... | collective-permute-start | bytes 20 | tf_op jit(solution)/shard_map/ppermute | solution.py:818
  349.5 4.1 %collective-permute-start.41 = (f32[1,1]{1,0:T(1,128)}, f32[1,1]{1,0:T(1,128)}, u32[]{:S(2)}, u32[]{:S(2)}) collective-permute-start(f32[1,1]{1,0:T(1,128)} %bitcast.47), channel_id=1, source_target_pairs={{0,2},{1,3},{2,0},{3,1},{4,6},{5,7},{6,4},{7,5},{8,10},{9,11},{10,... | collective-permute-start | bytes 20 | tf_op jit(solution)/shard_map/ppermute | solution.py:818
  351.2 4.5 %collective-permute-start.42 = (f32[1,1]{1,0:T(1,128)}, f32[1,1]{1,0:T(1,128)}, u32[]{:S(2)}, u32[]{:S(2)}) collective-permute-start(f32[1,1]{1,0:T(1,128)} %bitcast.47), channel_id=1, source_target_pairs={{0,3},{1,2},{2,1},{3,0},{4,7},{5,6},{6,5},{7,4},{8,11},{9,10},{10,... | collective-permute-start | bytes 20 | tf_op jit(solution)/shard_map/ppermute | solution.py:818
  (41 other events, 309.2 us)

commit v3 on v2

--- a/solution.py
+++ b/solution.py
@@ -19,6 +19,7 @@
 FEAT = 32
 WIN = 768
 SLOTS = 14
+AHEAD = 6
 DEEP = H + 16
 
 CLIP = 0.01
@@ -153,15 +154,16 @@
         part = comp[at(block), :]
         part_t = part.T
         low = part_t[0:FEAT].astype(BF)
-        feat[:, at(block)] = low
+        feat[block] = low
         source = 16.0 * part_t[17:18] + part_t[18:19] - 1.0
         target = 16.0 * part_t[19:20] + part_t[20:21] - 1.0
         idx[0:1, at(block)] = source.astype(jnp.int32)
         idx[1:2, at(block)] = target.astype(jnp.int32)
         three = dot(first3[...], low)
         value = three[0:H] + (three[H : 2 * H] + three[2 * H : 3 * H])
-        pre[:, at(block)] = value
-        hidden = value * sigmoid(value)
+        sig = sigmoid(value)
+        pre[block] = sig * (1.0 + value * (1.0 - sig))
+        hidden = value * sig
         eh_t[0:H, at(block)] = hidden.astype(BF)
         eh_t[H:DEEP, at(block)] = ones
         eh[at(block), :] = hidden.T.astype(BF)
@@ -176,10 +178,10 @@
         functools.partial(prep_kernel, edges=real, gates=gates, eblocks=edges // BLK),
         out_shape=(
             jax.ShapeDtypeStruct((8,), jnp.int32),
-            jax.ShapeDtypeStruct((H, edges), F32),
+            jax.ShapeDtypeStruct((edges // BLK, H, BLK), F32),
             jax.ShapeDtypeStruct((DEEP, edges), BF),
             jax.ShapeDtypeStruct((edges, H), BF),
-            jax.ShapeDtypeStruct((FEAT, edges), BF),
+            jax.ShapeDtypeStruct((edges // BLK, FEAT, BLK), BF),
             jax.ShapeDtypeStruct((8, edges), jnp.int32),
         ),
         in_specs=[pl.BlockSpec(memory_space=pltpu.SMEM)] + [pl.BlockSpec(memory_space=pltpu.VMEM)] * 4,
@@ -268,7 +270,7 @@
             start = start_of(scal, number)
             return acc + dot(table(pl.ds(start, WIN)), node_hit(row, start))
 
-        put(at(block), lax.fori_loop(0, scal[1], window, jnp.zeros((H, BLK), F32)))
+        put(block, lax.fori_loop(0, scal[1], window, jnp.zeros((H, BLK), F32)))
         return carry
 
     lax.fori_loop(0, blocks, each, 0)
@@ -322,8 +324,8 @@
         copy.wait()
 
     def gather(step):
-        def put(lanes, value):
-            near[step, :, lanes] = value.astype(BF)
+        def put(block, value):
+            near[block, step] = value.astype(BF)
 
         gather_rows(scal, lambda nodes: hid[step, :, nodes], 0, blocks, idx, put)
 
@@ -377,7 +379,7 @@
         staged[lax.rem(turn, 4)] = low
         for copy in stores(turn):
             copy.start()
-        rows = near[0, :, at(block)].astype(F32)
+        rows = near[block, 0].astype(F32)
         message(pair, at(block), rows, lambda item: low[item * H : (item + 1) * H].astype(F32))
         return carry
 
@@ -393,7 +395,8 @@
         gather(step)
 
         def use(unit, pair, load):
-            message(pair, strip(unit), near[step, :, strip(unit)].astype(F32), load)
+            rows = near[lax.div(unit, 2), step, :, strip(lax.rem(unit, 2))].astype(F32)
+            message(pair, strip(unit), rows, load)
 
         matrix_stream.run(step - 1, use)
         finish(step)
@@ -416,7 +419,7 @@
             jax.ShapeDtypeStruct((STEPS + 1, H, nodes), BF),
             jax.ShapeDtypeStruct((STEPS, H, nodes), BF),
             jax.ShapeDtypeStruct((STEPS + 1, H, nodes), F32),
-            jax.ShapeDtypeStruct((STEPS, H, edges), BF),
+            jax.ShapeDtypeStruct((edges // BLK, STEPS, H, BLK), BF),
             jax.ShapeDtypeStruct((edges // H, gates, 2 * half, H), BF),
         ),
         in_specs=[smem] * 2 + [vmem] * 7 + [hbm] * (2 * gates),
@@ -437,7 +440,7 @@
     )(place, scal, nf_t, embed, bias, gru, gru_bias, eh_t, idx, *second)
 
 
-def readout_kernel(scal, inverse, mol, lstm, head, present, target, hid, d_final, read, score, weight, slope, before, kept):
+def readout_kernel(scal, mol, lstm, head, present, target, hid, d_final, read, score, weight, slope, before, kept):
     windows = scal[1]
     final = hid.at[STEPS]
     tall = 2 * H + 8
@@ -502,8 +505,8 @@
     guess = wide(dot, query, head_query) + wide(dot, summary, head_summary) + head[2 * H : 2 * H + 1, :]
     gap = guess - target[...]
     seen = present[...] * owned
-    d_head[2 * H + 8 : 2 * H + 16, :] = jnp.broadcast_to(jnp.sum(seen * gap * gap), (8, H)) * inverse[0]
-    d_guess = (2.0 * inverse[0]) * seen * gap
+    d_head[2 * H + 8 : 2 * H + 16, :] = jnp.broadcast_to(jnp.sum(seen * gap * gap), (8, H))
+    d_guess = 2.0 * seen * gap
     d_head[0:H, :] = wide(dot, query.T, d_guess)
     d_head[H : 2 * H, :] = wide(dot, summary.T, d_guess)
     d_head[2 * H : 2 * H + 8, :] = jnp.broadcast_to(jnp.sum(d_guess, axis=0, keepdims=True), (8, H))
@@ -573,7 +576,7 @@
         read[part * tall + 2 * H : (part + 1) * tall, :] = jnp.broadcast_to(d_bias[:, columns], (8, H))
 
 
-def readout(scal, inverse, hid, mol, lstm, head, present, target):
+def readout(scal, hid, mol, lstm, head, present, target):
     nodes = hid.shape[2]
     return pl.pallas_call(
         readout_kernel,
@@ -581,7 +584,7 @@
             jax.ShapeDtypeStruct((H, nodes), F32),
             jax.ShapeDtypeStruct((4 * (2 * H + 8) + 2 * H + 16, H), F32),
         ),
-        in_specs=[pl.BlockSpec(memory_space=pltpu.SMEM)] * 2 + [pl.BlockSpec(memory_space=pltpu.VMEM)] * 6,
+        in_specs=[pl.BlockSpec(memory_space=pltpu.SMEM)] + [pl.BlockSpec(memory_space=pltpu.VMEM)] * 6,
         out_specs=[pl.BlockSpec(memory_space=pltpu.VMEM)] * 2,
         scratch_shapes=[
             pltpu.VMEM((H, nodes), F32),
@@ -593,10 +596,10 @@
         compiler_params=pltpu.CompilerParams(vmem_limit_bytes=VMEM_LIMIT),
         cost_estimate=pl.CostEstimate(flops=30_000_000_000, transcendentals=0, bytes_accessed=5_000_000),
         name="readout",
-    )(scal, inverse, mol, lstm, head, present, target, hid)
-
-
-def backward_kernel(place, scal, nf_t, gru, gru_bias, idx, hid, msg, state, near, d_final, mats, far, small, d_gru, d_embed, d_bias, grad, low_msg, part, back, buffer, in_sems):
+    )(scal, mol, lstm, head, present, target, hid)
+
+
+def backward_kernel(place, scal, inverse, nf_t, gru, gru_bias, idx, hid, msg, state, near, d_final, mats, far, small, d_gru, d_embed, d_bias, grad, low_msg, part, back, buffer, in_sems):
     gates = mats.shape[1]
     width = mats.shape[2] // (2 * H)
     windows = scal[1]
@@ -611,7 +614,7 @@
 
     def begin(window, carry):
         nodes = pl.ds(start_of(scal, window), WIN)
-        grad[:, nodes] = d_final[:, nodes]
+        grad[:, nodes] = d_final[:, nodes] * inverse[0]
         return carry
 
     lax.fori_loop(0, windows, begin, 0)
@@ -639,11 +642,11 @@
 
         lax.fori_loop(0, windows, cell, 0)
 
-        def put(lanes, value):
+        def put(block, value):
             low = value.astype(BF)
-            part[:, lanes] = value
-            far[step, :, lanes] = low
-            d_bias[...] += dot_nt(low, near[step, :, lanes])
+            part[:, at(block)] = value
+            far[block, step] = low
+            d_bias[...] += dot_nt(low, near[block, step])
 
         gather_rows(scal, lambda nodes: low_msg[:, nodes], 1, blocks, idx, put)
 
@@ -683,7 +686,7 @@
         small[gate, 2 * tall : 2 * tall + wide_part, :] = d_bias[columns, :]
 
 
-def backward(place, scal, nf_t, gru, gru_bias, idx, hid, msg, state, near, d_final, mats):
+def backward(place, scal, inverse, nf_t, gru, gru_bias, idx, hid, msg, state, near, d_final, mats):
     nodes = nf_t.shape[1]
     edges = idx.shape[1]
     _, gates, rows, _ = mats.shape
@@ -692,10 +695,10 @@
     return pl.pallas_call(
         backward_kernel,
         out_shape=(
-            jax.ShapeDtypeStruct((STEPS, H, edges), BF),
+            jax.ShapeDtypeStruct((edges // BLK, STEPS, H, BLK), BF),
             jax.ShapeDtypeStruct((gates, 2 * (H + 16) + H // gates, H), F32),
         ),
-        in_specs=[smem] * 2 + [vmem] * 9 + [pl.BlockSpec(memory_space=pl.ANY)],
+        in_specs=[smem] * 3 + [vmem] * 9 + [pl.BlockSpec(memory_space=pl.ANY)],
         out_specs=[vmem] * 2,
         scratch_shapes=[
             pltpu.VMEM((2, H + 16, 3 * H), F32),
@@ -711,52 +714,59 @@
         compiler_params=pltpu.CompilerParams(vmem_limit_bytes=VMEM_LIMIT),
         cost_estimate=pl.CostEstimate(flops=60_000_000_000, transcendentals=0, bytes_accessed=20_000_000),
         name="backward",
-    )(place, scal, nf_t, gru, gru_bias, idx, hid, msg, state, near, d_final, mats)
+    )(place, scal, inverse, nf_t, gru, gru_bias, idx, hid, msg, state, near, d_final, mats)
 
 
 def final_kernel(place, scal, first_in, *refs, pair, sides, group):
     seconds, refs = refs[: len(sides)], refs[len(sides) :]
     (near, far, eh, pre, feat), refs = refs[:5], refs[5:]
     outs, refs = refs[: len(sides)], refs[len(sides) :]
-    first_out, acc, near_s, far_s, eh_s, pre_s, feat_s, sems = refs
+    first_out, near_s, far_s, eh_s, pre_s, feat_s, sems = refs
     edge_blocks = ceil_blocks(scal[4])
-    half = acc.shape[1]
+    half = outs[0].shape[0]
     width = half // H
 
     def copies(block, slot):
         moves = (
-            (near.at[:, :, at(block)], near_s),
-            (far.at[:, :, at(block)], far_s),
+            (near.at[block], near_s),
+            (far.at[block, :, pl.ds(pl.multiple_of((pair ^ place[0]) * 2 * width, 2 * width), 2 * width)], far_s),
             (eh.at[at(block), :], eh_s),
-            (pre.at[:, at(block)], pre_s),
-            (feat.at[:, at(block)], feat_s),
+            (pre.at[block], pre_s),
+            (feat.at[block], feat_s),
         )
         return [
             pltpu.make_async_copy(source, target.at[slot], sems.at[slot, number])
             for number, (source, target) in enumerate(moves)
         ]
 
-    for copy in copies(0, 0):
-        copy.start()
-    acc[...] = jnp.zeros(acc.shape, F32)
+    for block in range(AHEAD - 1):
+
+        @pl.when(block < edge_blocks)
+        def _():
+            for copy in copies(jnp.int32(block), block):
+                copy.start()
+
+    for out in outs:
+        out[...] = jnp.zeros(out.shape, F32)
     first_out[...] = first_in[...]
 
     def edge_block(block, carry):
-        slot = lax.rem(block, 2)
+        slot = lax.rem(block, AHEAD)
+
+        @pl.when(block + (AHEAD - 1) < edge_blocks)
+        def _():
+            for copy in copies(block + (AHEAD - 1), lax.rem(block + (AHEAD - 1), AHEAD)):
+                copy.start()
+
         for copy in copies(block, slot):
             copy.wait()
-
-        @pl.when(block + 1 < edge_blocks)
-        def _():
-            for copy in copies(block + 1, 1 - slot):
-                copy.start()
 
         lefts = [near_s[slot, step].astype(F32) for step in range(STEPS)]
         low = eh_s[slot]
         d_pre = jnp.zeros((H, BLK), F32)
         for number, side in enumerate(sides):
             second = seconds[number]
-            begin_row = pl.multiple_of(piece_index(place, pair, side) * width, width)
+            begin_row = pl.multiple_of((side ^ place[1]) * width, width)
             tops = [far_s[slot, step, pl.ds(begin_row, width), :].astype(F32) for step in range(STEPS)]
             for part in range(width // group):
                 mats = []
@@ -767,20 +777,14 @@
                     mats.append(value.astype(BF))
                 flat = jnp.concatenate(mats, axis=0)
                 rows = slice(part * group * H, (part + 1) * group * H)
-                acc[number, rows, :] += dot(flat, low)
+                outs[number][rows, :] += dot(flat, low)
                 d_pre = d_pre + dot_tn(second[rows, :], flat)
-        value = pre_s[slot]
-        sig = sigmoid(value)
-        slope = d_pre * sig * (1.0 + value * (1.0 - sig))
-        total = first_out[...]
-        for piece in split3(slope):
-            total = total + dot_nt(feat_s[slot], piece)
+        both = dot_nt(feat_s[slot], jnp.concatenate(split2(d_pre * pre_s[slot]), axis=0))
+        total = first_out[...] + (both[:, 0:H] + both[:, H : 2 * H])
         first_out[...] = total
         return carry
 
     lax.fori_loop(0, edge_blocks, edge_block, 0)
-    for number, out in enumerate(outs):
-        out[...] = acc[number]
 
 
 def edge_grads(place, scal, seconds, near, far, eh, pre, feat, first_in, pair, sides, half):
@@ -788,18 +792,17 @@
     vmem = pl.BlockSpec(memory_space=pltpu.VMEM)
     size = len(sides)
     return pl.pallas_call(
-        functools.partial(final_kernel, pair=pair, sides=sides, group=8),
+        functools.partial(final_kernel, pair=pair, sides=sides, group=4),
         in_specs=[smem] * 2 + [vmem] * (1 + size) + [pl.BlockSpec(memory_space=pl.ANY)] * 5,
         out_specs=[vmem] * (size + 1),
         out_shape=[jax.ShapeDtypeStruct((half, H), F32)] * size + [jax.ShapeDtypeStruct((FEAT, H), F32)],
         scratch_shapes=[
-            pltpu.VMEM((size, half, H), F32),
-            pltpu.VMEM((2, STEPS, H, BLK), BF),
-            pltpu.VMEM((2, STEPS, H, BLK), BF),
-            pltpu.VMEM((2, BLK, H), BF),
-            pltpu.VMEM((2, H, BLK), F32),
-            pltpu.VMEM((2, FEAT, BLK), BF),
-            pltpu.SemaphoreType.DMA((2, 5)),
+            pltpu.VMEM((AHEAD, STEPS, H, BLK), BF),
+            pltpu.VMEM((AHEAD, STEPS, 2 * half // H, BLK), BF),
+            pltpu.VMEM((AHEAD, BLK, H), BF),
+            pltpu.VMEM((AHEAD, H, BLK), F32),
+            pltpu.VMEM((AHEAD, FEAT, BLK), BF),
+            pltpu.SemaphoreType.DMA((AHEAD, 5)),
         ],
         compiler_params=pltpu.CompilerParams(vmem_limit_bytes=VMEM_LIMIT),
         cost_estimate=pl.CostEstimate(flops=9_000_000_000, transcendentals=0, bytes_accessed=5_000_000),
@@ -936,12 +939,7 @@
     columns = jnp.arange(NT)[None, :]
     present = jnp.maximum(flag[:, None], (columns < NT // 2).astype(jnp.int32)).astype(F32)
     count = jnp.sum(present).reshape(1, 1)
-    for axis, size in (("grp", cores), ("edge", groups)):
-        step = 1
-        while step < size:
-            count = count + swap(count, axis, size, step)
-            step *= 2
-    inverse = (1.0 / count).reshape(1)
+    count = count + swap(count, "grp", cores, 1)
 
     nodes = node_feat.shape[0]
     edges = source.shape[0]
@@ -963,30 +961,49 @@
     lstm = jnp.pad(set_lstm, ((0, 7), (0, 0)))
     head = jnp.pad(head_weight, ((0, 7), (0, H - NT)))
 
-    data, inverse = lax.optimization_barrier((data, inverse))
     scal, pre, eh_t, eh, feat, idx = prep(place, mol, src2d, data, first3, edges, gates)
+    scal, count = lax.optimization_barrier((scal, count))
+    moved = swap(count, "edge", groups, 1) if groups > 1 else None
     hid, msg, state, near, mats = forward(place, scal, nf_t, embed_t, bias, gru, gru_bias, eh_t, idx, second)
+    if groups > 1:
+        hid, moved = lax.optimization_barrier((hid, moved))
+        count = count + moved
+    step = 2
+    moved = []
+    if step < groups:
+        moved = [swap(count, "edge", groups, step)]
     d_final, read = readout(
-        scal, inverse, hid, mol, lstm, head,
+        scal, hid, mol, lstm, head,
         jnp.pad(present, ((0, H - mols), (0, H - NT))), jnp.pad(target, ((0, H - mols), (0, H - NT))),
     )
+    d_final, moved = lax.optimization_barrier((d_final, moved))
+    while step < groups:
+        count = count + (moved.pop() if moved else swap(count, "edge", groups, step))
+        step *= 2
+    inverse = (1.0 / count).reshape(1)
+
     def read_chain():
-        parts = read.reshape(cores, -1, H)
+        value = read
+        if groups > 1:
+            (got,) = yield [swap(value, "edge", groups, groups // 2)]
+            value = value + got
+        parts = value.reshape(cores, -1, H)
         (got,) = yield [swap(pick(parts, 1 - core), "grp", cores, 1)]
         value = pick(parts, core) + got
-        for axis, size in (("gate", gates), ("edge", groups)):
+        for axis, size in (("gate", gates), ("edge", groups // 2)):
             step = 1
             while step < size:
-                (got,) = yield [swap(value, axis, size, step)]
+                (got,) = yield [swap(value, axis, sizes[axis], step)]
                 value = value + got
                 step *= 2
         (got,) = yield [swap(value, "grp", cores, 1)]
-        return jnp.where(core == 0, jnp.concatenate([value, got]), jnp.concatenate([got, value]))
+        value = jnp.where(core == 0, jnp.concatenate([value, got]), jnp.concatenate([got, value]))
+        return value * inverse
 
     fresh = read_chain()
     chains = [("read", fresh, next(fresh))]
     far, small = backward(
-        place, scal, nf_t, gru, gru_bias, idx, hid, msg, state, near, d_final, mats
+        place, scal, inverse, nf_t, gru, gru_bias, idx, hid, msg, state, near, d_final, mats
     )
     (small, far), moved = lax.optimization_barrier(((small, far), [arrays for _, _, arrays in chains]))
 

time: 380 us -> 369 us (0.971)
  Pallas kernels: 204 us -> 198 us
  waiting for transfers between devices: 27.1 us -> 22.5 us
    pallas_call x5, Pallas kernels: 52.7 us -> 46.6 us  [edge_grads(): pl.pallas_call(functools.partial(final_kernel, pair=pair, sides=sides, gr...]
    ppermute x44, waiting for transfers between devices: 27.1 us -> 22.5 us  [swap(): lax.ppermute(value, axis, [(index, index ^ step) for index in range(size)])]
    unnamed x98 -> x92, local copies, waits for them, and re-layouts: 7.79 us -> 8.63 us
  transfers between devices with their start and end apart: 44 -> 44, of which waited for: 12 -> 10; matrix products, arithmetic and copies ran while one was open for 10% -> 10% of each run, Pallas kernels for 30% -> 52%
where the time goes in v3:
time: 369 us
  Pallas kernels  198 us (54%)
  starting transfers between devices  69.1 us (19%)
  local copies, waits for them, and re-layouts  35.6 us (10%)
  other arithmetic  28.3 us (8%)
  waiting for transfers between devices  22.5 us (6%)
  between operations  15.1 us (4%)
    ppermute x44, starting transfers between devices, swap(): lax.ppermute(value, axis, [(index, index ^ step) for index in range(size)])  69.1 us
    pallas_call x1, Pallas kernels, forward(): pl.pallas_call(functools.partial(forward_kernel, gates=gates), out_shape=...  58.7 us
    pallas_call x1, Pallas kernels, backward(): pl.pallas_call(backward_kernel, out_shape=(jax.ShapeDtypeStruct((edges //...  54.8 us
    pallas_call x5, Pallas kernels, edge_grads(): pl.pallas_call(functools.partial(final_kernel, pair=pair, sides=sides, gr...  46.6 us
    pallas_call x1, Pallas kernels, readout(): pl.pallas_call(readout_kernel, out_shape=(jax.ShapeDtypeStruct((H, nodes)...  22.6 us
    ppermute x44, waiting for transfers between devices, swap(): lax.ppermute(value, axis, [(index, index ^ step) for index in range(size)])  22.5 us
    unnamed x92, local copies, waits for them, and re-layouts  8.63 us
    sub x5, other arithmetic, adamw(): weight - rate * (mom_hat / (jnp.sqrt(var_hat) + EPSILON) + DECAY * weight)  8.49 us
  transfers between devices with their start and end apart: 44, of which 10 were waited for; matrix products, arithmetic and copies ran while one was open for 10% of the time, Pallas kernels for 52%

profile of v3, /device:TPU:0, one launch (start us, length us, event | category | flops | bytes accessed | tf_op | source)
XLA Modules:
  0.0 368.5 jit_solution(11613361034372968400)
XLA Ops:
  0.7 1.8 fusion
  5.7 3.0 collective-permute-start.3
  8.7 1.5 collective-permute-start.2
  12.6 1.9 concatenate.28
  23.8 8.0 %prep.1 = (s32[8]{0:T(128)}, f32[20,128,256]{2,1,0:T(8,128)}, bf16[144,5120]{1,0:T(8,128)(2,1)}, bf16[5120,128]{1,0:T(8,128)(2,1)}, bf16[20,32,256]{2,1,0:T(8,128)(2,1)}, /*index=5*/s32[8,5120]{1,0:T(8,128)}) custom-call(s32[2]{0:T(128)} %pad_add_fusion.place, s32[1,3200]{1,0:T(1,128)} %reshape.180.mol, s32[32,256]{1,0:T(8,128)} %pad.55.src2d, ...), custom_call_target="tpu_custom_call" | custom-call | tf_op jit(solution)/shard_map/prep/pallas_call | solution.py:177
  33.1 3.4 collective-permute-start.7
  45.2 58.7 %forward.1 = (bf16[4,128,3200]{2,1,0:T(8,128)(2,1)}, bf16[3,128,3200]{2,1,0:T(8,128)(2,1)}, f32[4,128,3200]{2,1,0:T(8,128)}, bf16[20,3,128,256]{3,2,1,0:T(8,128)(2,1)}, bf16[40,4,4096,128]{3,2,1,0:T(8,128)(2,1)}) custom-call(s32[2]{0:T(128)} %pad_add_fusion.place, s32[8]{0:T(128)} %get-tuple-element.100.scal, bf16[16,3200]{1,0:T(8,128)(2,1)} %pad.62.nf_t, ...), custom_call_target="tpu_custom_call" | custom-call | flops 60000002048 | bytes 20000000 | tf_op jit(solution)/shard_map/forward/pallas_call | solution.py:416
  104.5 3.9 %collective-permute-start.8 = (f32[1,1]{1,0:T(1,128)}, f32[1,1]{1,0:T(1,128)}, u32[]{:S(2)}, u32[]{:S(2)}) collective-permute-start(f32[1,1]{1,0:T(1,128)} %add.283), channel_id=1, source_target_pairs={{0,8},{4,12},{8,0},{12,4},{1,9},{5,13},{9,1},{13,5},{2,10},{6,14},... | collective-permute-start | bytes 20 | tf_op jit(solution)/shard_map/ppermute | solution.py:821
  108.5 22.6 %readout.1 = (f32[128,3200]{1,0:T(8,128)}, f32[1328,128]{1,0:T(8,128)}) custom-call(s32[8]{0:T(128)} %get-tuple-element.100.scal, s32[1,3200]{1,0:T(1,128)} %reshape.180.mol, f32[392,512]{1,0:T(8,128)} %pad.58.lstm, f32[264,128]{1,0:T(8,128)} %pad.59.head, f32[128,128]{1,0:T(8,128)} %pad.60.present, f32[128,128]{1,0:T(8,128)} %pad.61.target, ...), custom_call_target="tpu_custom_call" | custom-call | flops 30000001024 | bytes 5000000 | tf_op jit(solution)/shard_map/readout/pallas_call | solution.py:581
  132.1 54.8 %backward.1 = (bf16[20,3,128,256]{3,2,1,0:T(8,128)(2,1)}, f32[4,320,128]{2,1,0:T(8,128)}) custom-call(s32[2]{0:T(128)} %pad_add_fusion.place, s32[8]{0:T(128)} %get-tuple-element.100.scal, f32[1]{0:T(128)} %bitcast.28.inverse, bf16[16,3200]{1,0:T(8,128)(2,1)} %pad.62.nf_t, bf16[2,384,128]{2,1,0:T(8,128)(2,1)} %bitcast.123, f32[2,384,1]{2,1,0:T(8,128)} %reshape.199.gru_bias, ...), custom_call_target="tpu_custom_call" | custom-call | flops 60000002048 | bytes 20000000 | tf_op jit(solution)/shard_map/backward/pallas_call | solution.py:695
  188.6 10.6 %edge_grads.5 = (f32[2048,128]{1,0:T(8,128)}, f32[2048,128]{1,0:T(8,128)}, f32[32,128]{1,0:T(8,128)}) custom-call(s32[2]{0:T(128)} %pad_add_fusion.place, s32[8]{0:T(128)} %get-tuple-element.100.scal, f32[32,128]{1,0:T(8,128)} %broadcast_in_dim.9.first_in, bf16[2352,128]{1,0:T(8,128)(2,1)} %collective-permute-done.1.refs_6_.refs_0_, ...), custom_call_target="tpu_custom_call" | custom-call | flops 8999999488 | bytes 5000000 | tf_op jit(solution)/shard_map/edge_grads/pallas_call | solution.py:794
  200.7 1.4 collective-permute-start.13
  202.1 12.4 %collective-permute-start.14 = (f32[320,128]{1,0:T(8,128)}, f32[320,128]{1,0:T(8,128)}, u32[]{:S(2)}, u32[]{:S(2)}) collective-permute-start(f32[320,128]{1,0:T(8,128)} %get-tuple-element.311), channel_id=1, source_target_pairs={{0,2},{1,3},{2,0},{3,1},{4,6},{5,7},{6,4},{7,5},{8,10},{9,11},{10,... | collective-permute-start | bytes 491528 | tf_op jit(solution)/shard_map/ppermute | solution.py:821
  214.5 1.5 collective-permute-start.15
  216.7 10.6 %edge_grads.6 = (f32[2048,128]{1,0:T(8,128)}, f32[2048,128]{1,0:T(8,128)}, f32[32,128]{1,0:T(8,128)}) custom-call(s32[2]{0:T(128)} %pad_add_fusion.place, s32[8]{0:T(128)} %get-tuple-element.100.scal, f32[32,128]{1,0:T(8,128)} %get-tuple-element.125.first_in, bf16[2352,128]{1,0:T(8,128)(2,1)} %collective-permute-done.2.refs_4_.refs_0_, ...), custom_call_target="tpu_custom_call" | custom-call | flops 8999999488 | bytes 5000000 | tf_op jit(solution)/shard_map/edge_grads/pallas_call | solution.py:794
  228.8 3.5 collective-permute-start.19
  233.4 1.3 collective-permute-start.18
  235.1 10.6 %edge_grads.7 = (f32[2048,128]{1,0:T(8,128)}, f32[2048,128]{1,0:T(8,128)}, f32[32,128]{1,0:T(8,128)}) custom-call(s32[2]{0:T(128)} %pad_add_fusion.place, s32[8]{0:T(128)} %get-tuple-element.100.scal, f32[32,128]{1,0:T(8,128)} %get-tuple-element.130.first_in, bf16[2352,128]{1,0:T(8,128)(2,1)} %collective-permute-done.3.refs_2_.refs_0_, ...), custom_call_target="tpu_custom_call" | custom-call | flops 8999999488 | bytes 5000000 | tf_op jit(solution)/shard_map/edge_grads/pallas_call | solution.py:794
  245.9 5.6 %collective-permute-done.17 = f32[664,128]{1,0:T(8,128)S(1)} collective-permute-done((f32[664,128]{1,0:T(8,128)S(1)}, f32[664,128]{1,0:T(8,128)S(1)}, u32[]{:S(2)}, u32[]{:S(2)}) %collective-permute-start.17) | collective-permute-done | bytes 340000 | tf_op jit(solution)/shard_map/ppermute | solution.py:821
  251.5 2.4 add_convert_fusion.1
  253.9 2.5 collective-permute-start.23
  256.5 6.0 %collective-permute-start.21 = (f32[664,128]{1,0:T(8,128)S(1)}, f32[664,128]{1,0:T(8,128)S(1)}, u32[]{:S(2)}, u32[]{:S(2)}) collective-permute-start(f32[664,128]{1,0:T(8,128)S(1)} %add.297), channel_id=1, source_target_pairs={{0,4},{4,0},{8,12},{12,8},{1,5},{5,1},{9,13},{13,9},{2,6},{6,2},{1... | collective-permute-start | bytes 1019912 | tf_op jit(solution)/shard_map/ppermute | solution.py:821
  262.6 7.4 %edge_grads.8 = (f32[2048,128]{1,0:T(8,128)}, f32[32,128]{1,0:T(8,128)}) custom-call(s32[2]{0:T(128)} %pad_add_fusion.place, s32[8]{0:T(128)} %get-tuple-element.100.scal, f32[32,128]{1,0:T(8,128)} %get-tuple-element.139.first_in, bf16[2048,128]{1,0:T(8,128)(2,1)} %get-tuple-element.304.refs_1_.refs_0_, ...), custom_call_target="tpu_custom_call" | custom-call | flops 8999999488 | bytes 5000000 | tf_op jit(solution)/shard_map/edge_grads/pallas_call | solution.py:794
  270.8 2.2 add_convert_fusion
  273.7 7.4 %edge_grads.9 = (f32[2048,128]{1,0:T(8,128)}, f32[32,128]{1,0:T(8,128)}) custom-call(s32[2]{0:T(128)} %pad_add_fusion.place, s32[8]{0:T(128)} %get-tuple-element.100.scal, f32[32,128]{1,0:T(8,128)} %get-tuple-element.146.first_in, bf16[2352,128]{1,0:T(8,128)(2,1)} %copy-done.15, bf16[20,3,128,256]{3,2,1,0:T(8,128)(2,1)} %get-tuple-element.112.near.refs_2_.refs_1_, ...), custom_call_target="tpu_custom_call" | custom-call | flops 8999999488 | bytes 5000000 | tf_op jit(solution)/shard_map/edge_grads/pallas_call | solution.py:794
  284.0 2.8 collective-permute-done.26
  287.6 2.6 abs_reduce_fusion
  291.3 4.3 %collective-permute-start.29 = (f16[528,128]{1,0:T(8,128)(2,1)S(1)}, f16[528,128]{1,0:T(8,128)(2,1)S(1)}, u32[]{:S(2)}, u32[]{:S(2)}) collective-permute-start(f16[528,128]{1,0:T(8,128)(2,1)S(1)} %get-tuple-element.314), channel_id=1, source_target_pairs={{0,8},{4,12},{8,0},{12,4},{1,9},{5,13},{9,1},{13,5},{2,10},{6,14},... | collective-permute-start | bytes 405512 | tf_op jit(solution)/shard_map/ppermute | solution.py:821
  297.3 7.2 %collective-permute-done.29 = f16[528,128]{1,0:T(8,128)(2,1)S(1)} collective-permute-done((f16[528,128]{1,0:T(8,128)(2,1)S(1)}, f16[528,128]{1,0:T(8,128)(2,1)S(1)}, u32[]{:S(2)}, u32[]{:S(2)}) %collective-permute-start.29) | collective-permute-done | bytes 135200 | tf_op jit(solution)/shard_map/ppermute | solution.py:821
  309.9 2.1 collective-permute-start.32
  313.2 1.4 collective-permute-start.34
  314.6 1.3 collective-permute-start.35
  315.9 1.9 multiply_reduce_fusion.1
  318.6 1.3 collective-permute-start.37
  324.3 2.1 collective-permute-start.39
  326.7 1.4 collective-permute-done.39
  328.1 3.1 collective-permute-start.43
  331.5 2.2 convert_multiply_fusion
  335.0 3.0 collective-permute-start.40
  338.1 2.1 collective-permute-start.41
  340.1 2.3 collective-permute-start.42
  342.5 2.2 collective-permute-done.42
  348.0 1.8 multiply_subtract_fusion.2
  349.7 1.6 copy.186
  353.4 1.4 multiply_subtract_fusion.3
  354.7 1.4 multiply_subtract_fusion.4
  356.2 3.1 multiply_subtract_fusion
  360.2 7.2 %wide_adamw.1 = (f32[129,4096]{1,0:T(8,128)}, f32[129,4096]{1,0:T(8,128)}, f32[129,4096]{1,0:T(8,128)}) custom-call(f32[3]{0:T(128)} %pad_maximum_fusion.5.scale, f32[4096,128]{1,0:T(8,128)} %bitcast.107, f32[1,4096]{1,0:T(1,128)} %bitcast.125, f32[129,4096]{1,0:T(8,128)} %weight.1, f32[129,4096]{1,0:T(8,128)} %mom.1, f32[129,4096]{1,0:T(8,128)} %var.1), custom_call_target="tpu_custom_call" | custom-call | tf_op jit(solution)/shard_map/wide_adamw/pallas_call | solution.py:875
  (264 shorter events, 48.7 us)
Async XLA Ops:
  5.7 30.8 %collective-permute-start.3 = (bf16[2352,128]{1,0:T(8,128)(2,1)S(1)}, bf16[2352,128]{1,0:T(8,128)(2,1)}, u32[]{:S(2)}, u32[]{:S(2)}) collective-permute-start(bf16[2352,128]{1,0:T(8,128)(2,1)S(1)} %pad_maximum_fusion.refs_0_), channel_id=1, source_target_pairs={{0,1},{1,0},{2,3},{3,2},{4,5},{5,4},{6,7},{7,6},{8,9},{9,8},{10,11... | collective-permute-start | bytes 1806344 | tf_op jit(solution)/shard_map/ppermute | solution.py:821
  8.7 28.1 %collective-permute-start.2 = (bf16[2352,128]{1,0:T(8,128)(2,1)S(1)}, bf16[2352,128]{1,0:T(8,128)(2,1)}, u32[]{:S(2)}, u32[]{:S(2)}) collective-permute-start(bf16[2352,128]{1,0:T(8,128)(2,1)S(1)} %pad_maximum_fusion.refs_0_), channel_id=1, source_target_pairs={{0,2},{1,3},{2,0},{3,1},{4,6},{5,7},{6,4},{7,5},{8,10},{9,11},{10,... | collective-permute-start | bytes 1806344 | tf_op jit(solution)/shard_map/ppermute | solution.py:821
  10.2 28.6 %collective-permute-start.1 = (bf16[2352,128]{1,0:T(8,128)(2,1)S(1)}, bf16[2352,128]{1,0:T(8,128)(2,1)}, u32[]{:S(2)}, u32[]{:S(2)}) collective-permute-start(bf16[2352,128]{1,0:T(8,128)(2,1)S(1)} %pad_maximum_fusion.refs_0_), channel_id=1, source_target_pairs={{0,3},{1,2},{2,1},{3,0},{4,7},{5,6},{6,5},{7,4},{8,11},{9,10},{10,... | collective-permute-start | bytes 1806344 | tf_op jit(solution)/shard_map/ppermute | solution.py:821
  11.0 20.9 %collective-permute-start = (f32[1,1]{1,0:T(1,128)}, f32[1,1]{1,0:T(1,128)}, u32[]{:S(2)}, u32[]{:S(2)}) collective-permute-start(f32[1,1]{1,0:T(1,128)} %bitcast.7), channel_id=1, source_target_pairs={{0,16},{16,0},{1,17},{17,1},{2,18},{18,2},{3,19},{19,3},{4,20},{20... | collective-permute-start | bytes 20 | tf_op jit(solution)/shard_map/ppermute | solution.py:821
  33.1 70.7 %collective-permute-start.7 = (f32[1,1]{1,0:T(1,128)}, f32[1,1]{1,0:T(1,128)}, u32[]{:S(2)}, u32[]{:S(2)}) collective-permute-start(f32[1,1]{1,0:T(1,128)} %add.280), channel_id=1, source_target_pairs={{0,4},{4,0},{8,12},{12,8},{1,5},{5,1},{9,13},{13,9},{2,6},{6,2},{1... | collective-permute-start | bytes 20 | tf_op jit(solution)/shard_map/ppermute | solution.py:821
  36.5 7.3 %collective-permute-start.4 = (bf16[2352,128]{1,0:T(8,128)(2,1)}, bf16[2352,128]{1,0:T(8,128)(2,1)S(1)}, u32[]{:S(2)}, u32[]{:S(2)}) collective-permute-start(bf16[2352,128]{1,0:T(8,128)(2,1)} %collective-permute-done.3.refs_2_.refs_0_), channel_id=1, source_target_pairs={{0,16},{16,0},{1,17},{17,1},{2,18},{18,2},{3,19},{19,3},{4,20},{20... | collective-permute-start | bytes 1806344 | tf_op jit(solution)/shard_map/ppermute | solution.py:821
  36.8 7.1 %collective-permute-start.5 = (bf16[2352,128]{1,0:T(8,128)(2,1)}, bf16[2352,128]{1,0:T(8,128)(2,1)S(1)}, u32[]{:S(2)}, u32[]{:S(2)}) collective-permute-start(bf16[2352,128]{1,0:T(8,128)(2,1)} %collective-permute-done.2.refs_4_.refs_0_), channel_id=1, source_target_pairs={{0,16},{16,0},{1,17},{17,1},{2,18},{18,2},{3,19},{19,3},{4,20},{20... | collective-permute-start | bytes 1806344 | tf_op jit(solution)/shard_map/ppermute | solution.py:821
  38.9 5.1 %collective-permute-start.6 = (bf16[2352,128]{1,0:T(8,128)(2,1)}, bf16[2352,128]{1,0:T(8,128)(2,1)S(1)}, u32[]{:S(2)}, u32[]{:S(2)}) collective-permute-start(bf16[2352,128]{1,0:T(8,128)(2,1)} %collective-permute-done.1.refs_6_.refs_0_), channel_id=1, source_target_pairs={{0,16},{16,0},{1,17},{17,1},{2,18},{18,2},{3,19},{19,3},{4,20},{20... | collective-permute-start | bytes 1806344 | tf_op jit(solution)/shard_map/ppermute | solution.py:821
  104.5 26.9 %collective-permute-start.8 = (f32[1,1]{1,0:T(1,128)}, f32[1,1]{1,0:T(1,128)}, u32[]{:S(2)}, u32[]{:S(2)}) collective-permute-start(f32[1,1]{1,0:T(1,128)} %add.283), channel_id=1, source_target_pairs={{0,8},{4,12},{8,0},{12,4},{1,9},{5,13},{9,1},{13,5},{2,10},{6,14},... | collective-permute-start | bytes 20 | tf_op jit(solution)/shard_map/ppermute | solution.py:821
  131.0 55.9 %collective-permute-start.9 = (f32[1328,128]{1,0:T(8,128)}, f32[1328,128]{1,0:T(8,128)S(1)}, u32[]{:S(2)}, u32[]{:S(2)}) collective-permute-start(f32[1328,128]{1,0:T(8,128)} %get-tuple-element.106), channel_id=1, source_target_pairs={{0,8},{4,12},{8,0},{12,4},{1,9},{5,13},{9,1},{13,5},{2,10},{6,14},... | collective-permute-start | bytes 2039816 | tf_op jit(solution)/shard_map/ppermute | solution.py:821
  132.0 54.9 %copy-start.13 = (f32[1328,128]{1,0:T(8,128)S(1)}, f32[1328,128]{1,0:T(8,128)}, u32[]{:S(2)}) copy-start(f32[1328,128]{1,0:T(8,128)} %get-tuple-element.106) | copy-start | bytes 2039812
  187.1 12.7 %collective-permute-start.10 = (f32[664,128]{1,0:T(8,128)S(1)}, f32[664,128]{1,0:T(8,128)S(1)}, u32[]{:S(2)}, u32[]{:S(2)}) collective-permute-start(f32[664,128]{1,0:T(8,128)S(1)} %dynamic-slice_bitcast_fusion.2), channel_id=1, source_target_pairs={{0,16},{16,0},{1,17},{17,1},{2,18},{18,2},{3,19},{19,3},{4,20},{20... | collective-permute-start | bytes 1019912 | tf_op jit(solution)/shard_map/ppermute | solution.py:821
  188.0 11.8 %collective-permute-start.11 = (f32[4,320,128]{2,1,0:T(8,128)S(1)}, f32[4,320,128]{2,1,0:T(8,128)S(1)}, u32[]{:S(2)}, u32[]{:S(2)}) collective-permute-start(f32[4,320,128]{2,1,0:T(8,128)S(1)} %copy-done.14), channel_id=1, source_target_pairs={{0,16},{16,0},{1,17},{17,1},{2,18},{18,2},{3,19},{19,3},{4,20},{20... | collective-permute-start | bytes 1966088 | tf_op jit(solution)/shard_map/ppermute | solution.py:821
  199.2 28.7 %collective-permute-start.16 = (f32[2048,128]{1,0:T(8,128)}, f32[2048,128]{1,0:T(8,128)S(1)}, u32[]{:S(2)}, u32[]{:S(2)}) collective-permute-start(f32[2048,128]{1,0:T(8,128)} %get-tuple-element.128), channel_id=1, source_target_pairs={{0,16},{16,0},{1,17},{17,1},{2,18},{18,2},{3,19},{19,3},{4,20},{20... | collective-permute-start | bytes 3145736 | tf_op jit(solution)/shard_map/ppermute | solution.py:821
  200.7 26.6 %collective-permute-start.13 = (f32[320,128]{1,0:T(8,128)}, f32[320,128]{1,0:T(8,128)}, u32[]{:S(2)}, u32[]{:S(2)}) collective-permute-start(f32[320,128]{1,0:T(8,128)} %get-tuple-element.312), channel_id=1, source_target_pairs={{0,1},{1,0},{2,3},{3,2},{4,5},{5,4},{6,7},{7,6},{8,9},{9,8},{10,11... | collective-permute-start | bytes 491528 | tf_op jit(solution)/shard_map/ppermute | solution.py:821
  202.1 25.3 %collective-permute-start.14 = (f32[320,128]{1,0:T(8,128)}, f32[320,128]{1,0:T(8,128)}, u32[]{:S(2)}, u32[]{:S(2)}) collective-permute-start(f32[320,128]{1,0:T(8,128)} %get-tuple-element.311), channel_id=1, source_target_pairs={{0,2},{1,3},{2,0},{3,1},{4,6},{5,7},{6,4},{7,5},{8,10},{9,11},{10,... | collective-permute-start | bytes 491528 | tf_op jit(solution)/shard_map/ppermute | solution.py:821
  214.5 12.9 %collective-permute-start.15 = (f32[320,128]{1,0:T(8,128)}, f32[320,128]{1,0:T(8,128)}, u32[]{:S(2)}, u32[]{:S(2)}) collective-permute-start(f32[320,128]{1,0:T(8,128)} %get-tuple-element.310), channel_id=1, source_target_pairs={{0,3},{1,2},{2,1},{3,0},{4,7},{5,6},{6,5},{7,4},{8,11},{9,10},{10,... | collective-permute-start | bytes 491528 | tf_op jit(solution)/shard_map/ppermute | solution.py:821
  216.0 11.9 %collective-permute-start.12 = (f32[664,128]{1,0:T(8,128)S(1)}, f32[664,128]{1,0:T(8,128)S(1)}, u32[]{:S(2)}, u32[]{:S(2)}) collective-permute-start(f32[664,128]{1,0:T(8,128)S(1)} %bitcast_add_fusion), channel_id=1, source_target_pairs={{0,1},{1,0},{2,3},{3,2},{4,5},{5,4},{6,7},{7,6},{8,9},{9,8},{10,11... | collective-permute-start | bytes 1019912 | tf_op jit(solution)/shard_map/ppermute | solution.py:821
  227.3 24.2 %collective-permute-start.20 = (f32[2048,128]{1,0:T(8,128)}, f32[2048,128]{1,0:T(8,128)}, u32[]{:S(2)}, u32[]{:S(2)}) collective-permute-start(f32[2048,128]{1,0:T(8,128)} %get-tuple-element.137), channel_id=1, source_target_pairs={{0,16},{16,0},{1,17},{17,1},{2,18},{18,2},{3,19},{19,3},{4,20},{20... | collective-permute-start | bytes 3145736 | tf_op jit(solution)/shard_map/ppermute | solution.py:821
  228.8 22.7 %collective-permute-start.19 = (bf16[2048,128]{1,0:T(8,128)(2,1)}, bf16[2048,128]{1,0:T(8,128)(2,1)S(1)}, u32[]{:S(2)}, u32[]{:S(2)}) collective-permute-start(bf16[2048,128]{1,0:T(8,128)(2,1)} %add_convert_fusion.2), channel_id=1, source_target_pairs={{0,3},{1,2},{2,1},{3,0},{4,7},{5,6},{6,5},{7,4},{8,11},{9,10},{10,... | collective-permute-start | bytes 1572872 | tf_op jit(solution)/shard_map/ppermute | solution.py:821
  233.4 12.4 %collective-permute-start.18 = (f32[320,128]{1,0:T(8,128)S(1)}, f32[320,128]{1,0:T(8,128)S(1)}, u32[]{:S(2)}, u32[]{:S(2)}) collective-permute-start(f32[320,128]{1,0:T(8,128)S(1)} %fusion.8), channel_id=1, source_target_pairs={{0,4},{4,0},{8,12},{12,8},{1,5},{5,1},{9,13},{13,9},{2,6},{6,2},{1... | collective-permute-start | bytes 491528 | tf_op jit(solution)/shard_map/ppermute | solution.py:821
  234.8 16.7 %collective-permute-start.17 = (f32[664,128]{1,0:T(8,128)S(1)}, f32[664,128]{1,0:T(8,128)S(1)}, u32[]{:S(2)}, u32[]{:S(2)}) collective-permute-start(f32[664,128]{1,0:T(8,128)S(1)} %add.291), channel_id=1, source_target_pairs={{0,2},{1,3},{2,0},{3,1},{4,6},{5,7},{6,4},{7,5},{8,10},{9,11},{10,... | collective-permute-start | bytes 1019912 | tf_op jit(solution)/shard_map/ppermute | solution.py:821
  245.8 25.0 %collective-permute-start.24 = (f32[2048,128]{1,0:T(8,128)}, f32[2048,128]{1,0:T(8,128)}, u32[]{:S(2)}, u32[]{:S(2)}) collective-permute-start(f32[2048,128]{1,0:T(8,128)} %get-tuple-element.144), channel_id=1, source_target_pairs={{0,16},{16,0},{1,17},{17,1},{2,18},{18,2},{3,19},{19,3},{4,20},{20... | collective-permute-start | bytes 3145736 | tf_op jit(solution)/shard_map/ppermute | solution.py:821
  253.9 16.9 %collective-permute-start.23 = (bf16[2048,128]{1,0:T(8,128)(2,1)}, bf16[2048,128]{1,0:T(8,128)(2,1)}, u32[]{:S(2)}, u32[]{:S(2)}) collective-permute-start(bf16[2048,128]{1,0:T(8,128)(2,1)} %add_convert_fusion.1), channel_id=1, source_target_pairs={{0,2},{1,3},{2,0},{3,1},{4,6},{5,7},{6,4},{7,5},{8,10},{9,11},{10,... | collective-permute-start | bytes 1572872 | tf_op jit(solution)/shard_map/ppermute | solution.py:821
  256.4 13.6 %collective-permute-start.22 = (f32[320,128]{1,0:T(8,128)S(1)}, f32[320,128]{1,0:T(8,128)S(1)}, u32[]{:S(2)}, u32[]{:S(2)}) collective-permute-start(f32[320,128]{1,0:T(8,128)S(1)} %add.298), channel_id=1, source_target_pairs={{0,8},{4,12},{8,0},{12,4},{1,9},{5,13},{9,1},{13,5},{2,10},{6,14},... | collective-permute-start | bytes 491528 | tf_op jit(solution)/shard_map/ppermute | solution.py:821
  256.5 14.3 %collective-permute-start.21 = (f32[664,128]{1,0:T(8,128)S(1)}, f32[664,128]{1,0:T(8,128)S(1)}, u32[]{:S(2)}, u32[]{:S(2)}) collective-permute-start(f32[664,128]{1,0:T(8,128)S(1)} %add.297), channel_id=1, source_target_pairs={{0,4},{4,0},{8,12},{12,8},{1,5},{5,1},{9,13},{13,9},{2,6},{6,2},{1... | collective-permute-start | bytes 1019912 | tf_op jit(solution)/shard_map/ppermute | solution.py:821
  270.0 16.8 %collective-permute-start.27 = (f32[2048,128]{1,0:T(8,128)}, f32[2048,128]{1,0:T(8,128)S(1)}, u32[]{:S(2)}, u32[]{:S(2)}) collective-permute-start(f32[2048,128]{1,0:T(8,128)} %get-tuple-element.150), channel_id=1, source_target_pairs={{0,16},{16,0},{1,17},{17,1},{2,18},{18,2},{3,19},{19,3},{4,20},{20... | collective-permute-start | bytes 3145736 | tf_op jit(solution)/shard_map/ppermute | solution.py:821
  273.0 13.8 %collective-permute-start.26 = (bf16[2048,128]{1,0:T(8,128)(2,1)}, bf16[2048,128]{1,0:T(8,128)(2,1)S(1)}, u32[]{:S(2)}, u32[]{:S(2)}) collective-permute-start(bf16[2048,128]{1,0:T(8,128)(2,1)} %add_convert_fusion), channel_id=1, source_target_pairs={{0,1},{1,0},{2,3},{3,2},{4,5},{5,4},{6,7},{7,6},{8,9},{9,8},{10,11... | collective-permute-start | bytes 1572872 | tf_op jit(solution)/shard_map/ppermute | solution.py:821
  273.6 10.4 %collective-permute-start.25 = (f32[664,128]{1,0:T(8,128)S(1)}, f32[664,128]{1,0:T(8,128)S(1)}, u32[]{:S(2)}, u32[]{:S(2)}) collective-permute-start(f32[664,128]{1,0:T(8,128)S(1)} %add.300), channel_id=1, source_target_pairs={{0,16},{16,0},{1,17},{17,1},{2,18},{18,2},{3,19},{19,3},{4,20},{20... | collective-permute-start | bytes 1019912 | tf_op jit(solution)/shard_map/ppermute | solution.py:821
  291.1 6.2 %collective-permute-start.28 = (f16[528,128]{1,0:T(8,128)(2,1)S(1)}, f16[528,128]{1,0:T(8,128)(2,1)S(1)}, u32[]{:S(2)}, u32[]{:S(2)}) collective-permute-start(f16[528,128]{1,0:T(8,128)(2,1)S(1)} %get-tuple-element.315), channel_id=1, source_target_pairs={{0,4},{4,0},{8,12},{12,8},{1,5},{5,1},{9,13},{13,9},{2,6},{6,2},{1... | collective-permute-start | bytes 405512 | tf_op jit(solution)/shard_map/ppermute | solution.py:821
  291.3 13.3 %collective-permute-start.29 = (f16[528,128]{1,0:T(8,128)(2,1)S(1)}, f16[528,128]{1,0:T(8,128)(2,1)S(1)}, u32[]{:S(2)}, u32[]{:S(2)}) collective-permute-start(f16[528,128]{1,0:T(8,128)(2,1)S(1)} %get-tuple-element.314), channel_id=1, source_target_pairs={{0,8},{4,12},{8,0},{12,4},{1,9},{5,13},{9,1},{13,5},{2,10},{6,14},... | collective-permute-start | bytes 405512 | tf_op jit(solution)/shard_map/ppermute | solution.py:821
  295.6 9.0 %collective-permute-start.30 = (f16[528,128]{1,0:T(8,128)(2,1)S(1)}, f16[528,128]{1,0:T(8,128)(2,1)S(1)}, u32[]{:S(2)}, u32[]{:S(2)}) collective-permute-start(f16[528,128]{1,0:T(8,128)(2,1)S(1)} %get-tuple-element.313), channel_id=1, source_target_pairs={{0,12},{4,8},{8,4},{12,0},{1,13},{5,9},{9,5},{13,1},{2,14},{6,10},... | collective-permute-start | bytes 405512 | tf_op jit(solution)/shard_map/ppermute | solution.py:821
  295.6 1.7 collective-permute-start.31
  309.9 13.3 %collective-permute-start.32 = (f16[528,128]{1,0:T(8,128)(2,1)S(1)}, f16[528,128]{1,0:T(8,128)(2,1)S(1)}, u32[]{:S(2)}, u32[]{:S(2)}) collective-permute-start(f16[528,128]{1,0:T(8,128)(2,1)S(1)} %get-tuple-element.316), channel_id=1, source_target_pairs={{0,4},{4,0},{8,12},{12,8},{1,5},{5,1},{9,13},{13,9},{2,6},{6,2},{1... | collective-permute-start | bytes 405512 | tf_op jit(solution)/shard_map/ppermute | solution.py:821
  312.0 12.0 %collective-permute-start.33 = (f16[528,128]{1,0:T(8,128)(2,1)S(1)}, f16[528,128]{1,0:T(8,128)(2,1)S(1)}, u32[]{:S(2)}, u32[]{:S(2)}) collective-permute-start(f16[528,128]{1,0:T(8,128)(2,1)S(1)} %get-tuple-element.316), channel_id=1, source_target_pairs={{0,8},{4,12},{8,0},{12,4},{1,9},{5,13},{9,1},{13,5},{2,10},{6,14},... | collective-permute-start | bytes 405512 | tf_op jit(solution)/shard_map/ppermute | solution.py:821
  313.2 10.9 %collective-permute-start.34 = (f16[528,128]{1,0:T(8,128)(2,1)S(1)}, f16[528,128]{1,0:T(8,128)(2,1)S(1)}, u32[]{:S(2)}, u32[]{:S(2)}) collective-permute-start(f16[528,128]{1,0:T(8,128)(2,1)S(1)} %get-tuple-element.316), channel_id=1, source_target_pairs={{0,12},{4,8},{8,4},{12,0},{1,13},{5,9},{9,5},{13,1},{2,14},{6,10},... | collective-permute-start | bytes 405512 | tf_op jit(solution)/shard_map/ppermute | solution.py:821
  314.6 4.1 %collective-permute-start.35 = (f32[32,128]{1,0:T(8,128)S(1)}, f32[32,128]{1,0:T(8,128)S(1)}, u32[]{:S(2)}, u32[]{:S(2)}) collective-permute-start(f32[32,128]{1,0:T(8,128)S(1)} %add.314), channel_id=1, source_target_pairs={{0,1},{1,0},{2,3},{3,2},{4,5},{5,4},{6,7},{7,6},{8,9},{9,8},{10,11... | collective-permute-start | bytes 49160 | tf_op jit(solution)/shard_map/ppermute | solution.py:821
  317.8 4.6 %collective-permute-start.36 = (f32[32,128]{1,0:T(8,128)S(1)}, f32[32,128]{1,0:T(8,128)S(1)}, u32[]{:S(2)}, u32[]{:S(2)}) collective-permute-start(f32[32,128]{1,0:T(8,128)S(1)} %add.314), channel_id=1, source_target_pairs={{0,2},{1,3},{2,0},{3,1},{4,6},{5,7},{6,4},{7,5},{8,10},{9,11},{10,... | collective-permute-start | bytes 49160 | tf_op jit(solution)/shard_map/ppermute | solution.py:821
  318.6 4.6 %collective-permute-start.37 = (f32[32,128]{1,0:T(8,128)S(1)}, f32[32,128]{1,0:T(8,128)S(1)}, u32[]{:S(2)}, u32[]{:S(2)}) collective-permute-start(f32[32,128]{1,0:T(8,128)S(1)} %add.314), channel_id=1, source_target_pairs={{0,3},{1,2},{2,1},{3,0},{4,7},{5,6},{6,5},{7,4},{8,11},{9,10},{10,... | collective-permute-start | bytes 49160 | tf_op jit(solution)/shard_map/ppermute | solution.py:821
  324.2 3.9 %collective-permute-start.38 = (f16[2112,128]{1,0:T(8,128)(2,1)S(1)}, f16[2112,128]{1,0:T(8,128)(2,1)S(1)}, u32[]{:S(2)}, u32[]{:S(2)}) collective-permute-start(f16[2112,128]{1,0:T(8,128)(2,1)S(1)} %constant_dynamic-update-slice_fusion.2), channel_id=1, source_target_pairs={{0,16},{16,0},{1,17},{17,1},{2,18},{18,2},{3,19},{19,3},{4,20},{20... | collective-permute-start | bytes 1622024 | tf_op jit(solution)/shard_map/ppermute | solution.py:821
  324.3 3.8 %collective-permute-start.39 = (f32[32,128]{1,0:T(8,128)S(1)}, f32[32,128]{1,0:T(8,128)S(1)}, u32[]{:S(2)}, u32[]{:S(2)}) collective-permute-start(f32[32,128]{1,0:T(8,128)S(1)} %add_add_fusion), channel_id=1, source_target_pairs={{0,4},{4,0},{8,12},{12,8},{1,5},{5,1},{9,13},{13,9},{2,6},{6,2},{1... | collective-permute-start | bytes 49160 | tf_op jit(solution)/shard_map/ppermute | solution.py:821
  328.1 16.6 %collective-permute-start.43 = (f32[32,128]{1,0:T(8,128)S(1)}, f32[32,128]{1,0:T(8,128)S(1)}, u32[]{:S(2)}, u32[]{:S(2)}) collective-permute-start(f32[32,128]{1,0:T(8,128)S(1)} %add.325), channel_id=1, source_target_pairs={{0,8},{4,12},{8,0},{12,4},{1,9},{5,13},{9,1},{13,5},{2,10},{6,14},... | collective-permute-start | bytes 49160 | tf_op jit(solution)/shard_map/ppermute | solution.py:821
  331.4 23.3 %copy-start.28 = (f32[16,32]{1,0:T(8,128)S(1)}, f32[16,32]{1,0:T(8,128)}, u32[]{:S(2)}) copy-start(f32[16,32]{1,0:T(8,128)} %param.35) | copy-start | bytes 6148
  331.5 24.7 %copy-start.1 = (f32[385,512]{1,0:T(8,128)S(1)}, f32[385,512]{1,0:T(8,128)}, u32[]{:S(2)}) copy-start(f32[385,512]{1,0:T(8,128)} %param.39) | copy-start | bytes 2365444
  333.7 22.5 %copy-start.10 = (f32[385,512]{1,0:T(8,128)S(1)}, f32[385,512]{1,0:T(8,128)}, u32[]{:S(2)}) copy-start(f32[385,512]{1,0:T(8,128)} %param.51) | copy-start | bytes 2365444
  335.0 7.4 %collective-permute-start.40 = (f32[1,1]{1,0:T(1,128)}, f32[1,1]{1,0:T(1,128)}, u32[]{:S(2)}, u32[]{:S(2)}) collective-permute-start(f32[1,1]{1,0:T(1,128)} %bitcast.48), channel_id=1, source_target_pairs={{0,1},{1,0},{2,3},{3,2},{4,5},{5,4},{6,7},{7,6},{8,9},{9,8},{10,11... | collective-permute-start | bytes 20 | tf_op jit(solution)/shard_map/ppermute | solution.py:821
  338.1 4.4 %collective-permute-start.41 = (f32[1,1]{1,0:T(1,128)}, f32[1,1]{1,0:T(1,128)}, u32[]{:S(2)}, u32[]{:S(2)}) collective-permute-start(f32[1,1]{1,0:T(1,128)} %bitcast.48), channel_id=1, source_target_pairs={{0,2},{1,3},{2,0},{3,1},{4,6},{5,7},{6,4},{7,5},{8,10},{9,11},{10,... | collective-permute-start | bytes 20 | tf_op jit(solution)/shard_map/ppermute | solution.py:821
  340.1 4.5 %collective-permute-start.42 = (f32[1,1]{1,0:T(1,128)}, f32[1,1]{1,0:T(1,128)}, u32[]{:S(2)}, u32[]{:S(2)}) collective-permute-start(f32[1,1]{1,0:T(1,128)} %bitcast.48), channel_id=1, source_target_pairs={{0,3},{1,2},{2,1},{3,0},{4,7},{5,6},{6,5},{7,4},{8,11},{9,10},{10,... | collective-permute-start | bytes 20 | tf_op jit(solution)/shard_map/ppermute | solution.py:821
  (38 other events, 282.1 us)

commit v4 on v3

--- a/solution.py
+++ b/solution.py
@@ -833,7 +833,7 @@
 
 
 def unscaled(low):
-    power = low[..., -1:, :1].astype(F32)
+    power = low[..., -1:, :].astype(F32)
     return low[..., :-16, :].astype(F32) * jnp.exp2(-power)
 
 
@@ -854,40 +854,81 @@
     )
 
 
-def wide_adamw_kernel(scale, grad, bias, weight, mom, var, weight_out, mom_out, var_out, *, rate):
-    def update(rows, value):
-        mom_new = BETA_ONE * mom[rows, :] + (1.0 - BETA_ONE) * value
-        var_new = BETA_TWO * var[rows, :] + (1.0 - BETA_TWO) * value * value
-        mom_out[rows, :] = mom_new
-        var_out[rows, :] = var_new
-        old = weight[rows, :]
-        step = (mom_new / scale[1]) / (jnp.sqrt(var_new / scale[2]) + EPSILON)
-        weight_out[rows, :] = old - rate * (step + DECAY * old)
-
-    update(slice(0, H), grad[...].T * scale[0])
-    update(slice(H, H + 1), bias[...] * scale[0])
-
-
-def wide_adamw(scale, grad, bias, weight, mom, var, rate):
-    rows, columns = weight.shape
+def update_rows(scale, refs, index, value, rate):
+    weight, mom, var, weight_out, mom_out, var_out = refs
+    value = value * scale[0]
+    mom_new = BETA_ONE * mom[index] + (1.0 - BETA_ONE) * value
+    var_new = BETA_TWO * var[index] + (1.0 - BETA_TWO) * value * value
+    mom_out[index] = mom_new
+    var_out[index] = var_new
+    old = weight[index]
+    step = (mom_new / scale[1]) / (jnp.sqrt(var_new / scale[2]) + EPSILON)
+    weight_out[index] = old - rate * (step + DECAY * old)
+
+
+def adamw_kernel(scale, wide, bias, read, small, first, *refs):
+    ins, outs = refs[:15], refs[15:]
+    embed, edge_first, second, lstm, head = [
+        ins[3 * item : 3 * item + 3] + outs[3 * item : 3 * item + 3] for item in range(5)
+    ]
+    every = slice(None)
+    update_rows(scale, second, (slice(0, H), every), wide[...].T, RATES[2])
+    update_rows(scale, second, (slice(H, H + 1), every), bias[...], RATES[2])
+
+    @pl.when(pl.program_id(0) == 0)
+    def _():
+        width = embed[0].shape[1]
+        update_rows(scale, embed, (every, every), small[0:16, H - width :], RATES[0])
+        update_rows(scale, edge_first, (every, every), first[0 : EIN + 1, :], RATES[1])
+        tall = 2 * H + 8
+        for part in range(4):
+            columns = slice(part * H, (part + 1) * H)
+            by_query = read[part * tall : part * tall + H, :]
+            for begin, value in (
+                (0, by_query),
+                (H, read[part * tall + H : part * tall + 2 * H, :]),
+                (2 * H, by_query),
+                (3 * H, read[part * tall + 2 * H : part * tall + 2 * H + 1, :]),
+            ):
+                update_rows(scale, lstm, (slice(begin, begin + value.shape[0]), columns), value, RATES[4])
+        for part in range(2):
+            value = read[4 * tall + part * H : 4 * tall + (part + 1) * H, :].T[0:NT]
+            update_rows(scale, head, (every, slice(part * H, (part + 1) * H)), value, RATES[5])
+        value = read[4 * tall + 2 * H : 4 * tall + 2 * H + 8, :].T[0:NT, 0:1]
+        update_rows(scale, head, (every, slice(2 * H, 2 * H + 1)), value, RATES[5])
+
+
+def adamw_step(scale, wide, bias, read, small, first, groups):
     block = 1024
-    tall = pl.BlockSpec((rows, block), lambda index: (0, index))
+    columns = groups[2][0].shape[1]
+
+    def whole(array):
+        return pl.BlockSpec(array.shape, lambda index: (0, 0))
+
+    def specs(number, array):
+        if number == 2:
+            return pl.BlockSpec((array.shape[0], block), lambda index: (0, index))
+        return whole(array)
+
+    weights = [array for group in groups for array in group]
+    weight_specs = [specs(number, array) for number, group in enumerate(groups) for array in group]
     return pl.pallas_call(
-        functools.partial(wide_adamw_kernel, rate=rate),
+        adamw_kernel,
         grid=(columns // block,),
         in_specs=[
             pl.BlockSpec(memory_space=pltpu.SMEM),
             pl.BlockSpec((block, H), lambda index: (index, 0)),
             pl.BlockSpec((1, block), lambda index: (0, index)),
-            tall,
-            tall,
-            tall,
-        ],
-        out_specs=[tall] * 3,
-        out_shape=[jax.ShapeDtypeStruct(weight.shape, F32)] * 3,
+            whole(read),
+            whole(small),
+            whole(first),
+        ]
+        + weight_specs,
+        out_specs=weight_specs,
+        out_shape=[jax.ShapeDtypeStruct(array.shape, F32) for array in weights],
         compiler_params=pltpu.CompilerParams(vmem_limit_bytes=VMEM_LIMIT),
-        name="wide_adamw",
-    )(scale, grad, bias, weight, mom, var)
+        name="adamw_step",
+    )(scale, wide, bias, read, small, first, *weights)
 
 
 def on_device(
@@ -1085,6 +1126,10 @@
 
     first = jnp.zeros((FEAT, H), F32)
     chains = advance(chains, moved)
+    if groups > 1:
+        name, chain, arrays = chains[0]
+        first, arrays = lax.optimization_barrier((first, arrays))
+        chains[0] = (name, chain, chain.send(arrays))
     fresh = narrow_chain()
     chains.append(("narrow", fresh, next(fresh)))
     for step in reversed(range(gates)):
@@ -1107,19 +1152,17 @@
         chains = advance(chains, lax.optimization_barrier([arrays for _, _, arrays in chains]))
     read = results["read"]
     head_begin = 4 * (2 * H + 8)
-    by_part = read[:head_begin].reshape(4, 2 * H + 8, H)
-    by_row = jnp.concatenate([by_part[part] for part in range(4)], axis=1)
-    grad_lstm = jnp.concatenate([by_row[: 2 * H], by_row[:H], by_row[2 * H : 2 * H + 1]], axis=0)
-    grad_head = read[head_begin : head_begin + 2 * H + 1, :NT]
     loss = read[head_begin + 2 * H + 8, 0]
+    row = jnp.arange(read.shape[0])[:, None]
+    within = jnp.where(row < head_begin, row % (2 * H + 8), row - head_begin)
+    times = jnp.where(within <= 2 * H, jnp.where((row < head_begin) & (within < H), 2.0, 1.0), 0.0)
     small = results["narrow"]
     tall = H + 16
     grad_gru = small[: 2 * tall, : 3 * width].reshape(2, tall, 3, width)[:, : H + 1]
-    grad_embed = small[:16, 3 * width :]
     grad_bias = small[2 * tall :].reshape(1, width * H)
-    grad_first = results["first"][: EIN + 1]
+    first = results["first"]
     grads, squares = results[0]
-    whole_sq = jnp.sum(grad_lstm * grad_lstm) + jnp.sum(grad_head * grad_head) + jnp.sum(grad_first * grad_first)
+    whole_sq = jnp.sum(read * read * times) + jnp.sum(first[: EIN + 1] * first[: EIN + 1])
 
     norm = jnp.sqrt(squares + whole_sq)
     factor = jnp.minimum(1.0, CLIP / norm)
@@ -1127,14 +1170,13 @@
     moms = (mom_embed, mom_first, mom_second, mom_gru, mom_lstm, mom_head)
     varis = (var_embed, var_first, var_second, var_gru, var_lstm, var_head)
     stepno = step_count[0].astype(F32)
-    narrow = (grad_embed, grad_first, None, grad_gru, grad_lstm, grad_head)
     scale = jnp.stack([factor, 1.0 - BETA_ONE**stepno, 1.0 - BETA_TWO**stepno])
-    results = [
-        adamw(params[index], narrow[index] * factor, moms[index], varis[index], RATES[index], stepno)
-        if narrow[index] is not None
-        else wide_adamw(scale, grads, grad_bias, params[index], moms[index], varis[index], RATES[index])
-        for index in range(6)
-    ]
+    trees = [[params[index], moms[index], varis[index]] for index in (0, 1, 2, 4)]
+    trees.append([head_weight.T, mom_head.T, var_head.T])
+    updated = adamw_step(scale, grads, grad_bias, read, small, first, trees)
+    results = {index: updated[3 * turn : 3 * turn + 3] for turn, index in enumerate((0, 1, 2, 4, 5))}
+    results[5] = [array.T for array in results[5]]
+    results[3] = adamw(params[3], grad_gru * factor, moms[3], varis[3], RATES[3], stepno)
     return (loss, norm) + tuple(results[index][kind] for kind in range(3) for index in range(6))
 
 

time: 369 us -> 356 us (0.965)
  local copies, waits for them, and re-layouts: 35.6 us -> 24.8 us
  other arithmetic: 28.3 us -> 19.8 us
  waiting for transfers between devices: 22.5 us -> 29 us
    sub x5 -> x1, other arithmetic: 8.49 us -> 0.89 us  [adamw(): weight - rate * (mom_hat / (jnp.sqrt(var_hat) + EPSILON) + DECAY * weight)]
    unnamed x92 -> x68, local copies, waits for them, and re-layouts: 8.63 us -> 1.62 us
    ppermute x44, waiting for transfers between devices: 22.5 us -> 29 us  [swap(): lax.ppermute(value, axis, [(index, index ^ step) for index in range(size)])]
  transfers between devices with their start and end apart: 44 -> 44, of which waited for: 10 -> 10; matrix products, arithmetic and copies ran while one was open for 10% -> 9% of each run, Pallas kernels for 52% -> 54%
where the time goes in v4:
time: 356 us; the launch traced here: 355 us
  Pallas kernels  201 us (56%)
  starting transfers between devices  67.9 us (19%)
  waiting for transfers between devices  29 us (8%)
  local copies, waits for them, and re-layouts  24.8 us (7%)
  other arithmetic  19.8 us (6%)
  between operations  12.1 us (3%)
    ppermute x44, starting transfers between devices, swap(): lax.ppermute(value, axis, [(index, index ^ step) for index in range(size)])  67.9 us
    pallas_call x1, Pallas kernels, forward(): pl.pallas_call(functools.partial(forward_kernel, gates=gates), out_shape=...  58.7 us
    pallas_call x1, Pallas kernels, backward(): pl.pallas_call(backward_kernel, out_shape=(jax.ShapeDtypeStruct((edges //...  54.8 us
    pallas_call x5, Pallas kernels, edge_grads(): pl.pallas_call(functools.partial(final_kernel, pair=pair, sides=sides, gr...  46.7 us
    ppermute x44, waiting for transfers between devices, swap(): lax.ppermute(value, axis, [(index, index ^ step) for index in range(size)])  29 us
    pallas_call x1, Pallas kernels, readout(): pl.pallas_call(readout_kernel, out_shape=(jax.ShapeDtypeStruct((H, nodes)...  22.6 us
    pallas_call x1, Pallas kernels, adamw_step(): pl.pallas_call(adamw_kernel, grid=(columns // block,), in_specs=[pl.Block...  10.2 us
    pallas_call x1, Pallas kernels, prep(): pl.pallas_call(functools.partial(prep_kernel, edges=real, gates=gates, eb...  8 us
  transfers between devices with their start and end apart: 44, of which 10 were waited for; matrix products, arithmetic and copies ran while one was open for 9% of the time, Pallas kernels for 54%

profile of v4, /device:TPU:0, one launch (start us, length us, event | category | flops | bytes accessed | tf_op | source)
XLA Modules:
  0.0 354.6 jit_solution(6802223996410687308)
XLA Ops:
  0.7 1.8 fusion
  5.7 3.0 collective-permute-start.3
  8.7 1.5 collective-permute-start.2
  12.6 1.9 concatenate.22
  16.4 1.3 pad.56.data
  21.5 8.0 %prep.1 = (s32[8]{0:T(128)}, f32[20,128,256]{2,1,0:T(8,128)}, bf16[144,5120]{1,0:T(8,128)(2,1)}, bf16[5120,128]{1,0:T(8,128)(2,1)}, bf16[20,32,256]{2,1,0:T(8,128)(2,1)}, /*index=5*/s32[8,5120]{1,0:T(8,128)}) custom-call(s32[2]{0:T(128)} %pad_add_fusion.place, s32[1,3200]{1,0:T(1,128)} %reshape.206.mol, s32[32,256]{1,0:T(8,128)} %pad.55.src2d, ...), custom_call_target="tpu_custom_call" | custom-call | tf_op jit(solution)/shard_map/prep/pallas_call | solution.py:177
  30.8 3.8 %collective-permute-start.7 = (f32[1,1]{1,0:T(1,128)}, f32[1,1]{1,0:T(1,128)}, u32[]{:S(2)}, u32[]{:S(2)}) collective-permute-start(f32[1,1]{1,0:T(1,128)} %add.234), channel_id=1, source_target_pairs={{0,4},{4,0},{8,12},{12,8},{1,5},{5,1},{9,13},{13,9},{2,6},{6,2},{1... | collective-permute-start | bytes 20 | tf_op jit(solution)/shard_map/ppermute | solution.py:821
  34.6 2.2 collective-permute-done.2.refs_4_.refs_0_
  45.2 58.7 %forward.1 = (bf16[4,128,3200]{2,1,0:T(8,128)(2,1)}, bf16[3,128,3200]{2,1,0:T(8,128)(2,1)}, f32[4,128,3200]{2,1,0:T(8,128)}, bf16[20,3,128,256]{3,2,1,0:T(8,128)(2,1)}, bf16[40,4,4096,128]{3,2,1,0:T(8,128)(2,1)}) custom-call(s32[2]{0:T(128)} %pad_add_fusion.place, s32[8]{0:T(128)} %get-tuple-element.113.scal, bf16[16,3200]{1,0:T(8,128)(2,1)} %pad.62.nf_t, ...), custom_call_target="tpu_custom_call" | custom-call | flops 60000002048 | bytes 20000000 | tf_op jit(solution)/shard_map/forward/pallas_call | solution.py:416
  104.4 3.9 %collective-permute-start.8 = (f32[1,1]{1,0:T(1,128)}, f32[1,1]{1,0:T(1,128)}, u32[]{:S(2)}, u32[]{:S(2)}) collective-permute-start(f32[1,1]{1,0:T(1,128)} %add.237), channel_id=1, source_target_pairs={{0,8},{4,12},{8,0},{12,4},{1,9},{5,13},{9,1},{13,5},{2,10},{6,14},... | collective-permute-start | bytes 20 | tf_op jit(solution)/shard_map/ppermute | solution.py:821
  108.4 22.6 %readout.1 = (f32[128,3200]{1,0:T(8,128)}, f32[1328,128]{1,0:T(8,128)}) custom-call(s32[8]{0:T(128)} %get-tuple-element.113.scal, s32[1,3200]{1,0:T(1,128)} %reshape.206.mol, f32[392,512]{1,0:T(8,128)} %pad.58.lstm, f32[264,128]{1,0:T(8,128)} %pad.59.head, f32[128,128]{1,0:T(8,128)} %pad.60.present, f32[128,128]{1,0:T(8,128)} %pad.61.target, ...), custom_call_target="tpu_custom_call" | custom-call | flops 30000001024 | bytes 5000000 | tf_op jit(solution)/shard_map/readout/pallas_call | solution.py:581
  132.0 54.8 %backward.1 = (bf16[20,3,128,256]{3,2,1,0:T(8,128)(2,1)}, f32[4,320,128]{2,1,0:T(8,128)}) custom-call(s32[2]{0:T(128)} %pad_add_fusion.place, s32[8]{0:T(128)} %get-tuple-element.113.scal, f32[1]{0:T(128)} %bitcast.28.inverse, bf16[16,3200]{1,0:T(8,128)(2,1)} %pad.62.nf_t, bf16[2,384,128]{2,1,0:T(8,128)(2,1)} %bitcast.132, f32[2,384,1]{2,1,0:T(8,128)} %reshape.225.gru_bias, ...), custom_call_target="tpu_custom_call" | custom-call | flops 60000002048 | bytes 20000000 | tf_op jit(solution)/shard_map/backward/pallas_call | solution.py:695
  187.0 5.9 %collective-permute-start.10 = (f32[664,128]{1,0:T(8,128)S(1)}, f32[664,128]{1,0:T(8,128)S(1)}, u32[]{:S(2)}, u32[]{:S(2)}) collective-permute-start(f32[664,128]{1,0:T(8,128)S(1)} %dynamic-slice_bitcast_fusion.2), channel_id=1, source_target_pairs={{0,16},{16,0},{1,17},{17,1},{2,18},{18,2},{3,19},{19,3},{4,20},{20... | collective-permute-start | bytes 1019912 | tf_op jit(solution)/shard_map/ppermute | solution.py:821
  194.9 10.6 %edge_grads.5 = (f32[2048,128]{1,0:T(8,128)}, f32[2048,128]{1,0:T(8,128)}, f32[32,128]{1,0:T(8,128)}) custom-call(s32[2]{0:T(128)} %pad_add_fusion.place, s32[8]{0:T(128)} %get-tuple-element.113.scal, f32[32,128]{1,0:T(8,128)} %broadcast_in_dim.32.first_in, bf16[2352,128]{1,0:T(8,128)(2,1)} %collective-permute-done.1.refs_6_.refs_0_, ...), custom_call_target="tpu_custom_call" | custom-call | flops 8999999488 | bytes 5000000 | tf_op jit(solution)/shard_map/edge_grads/pallas_call | solution.py:794
  208.0 1.7 collective-permute-start.14
  209.7 1.4 collective-permute-start.15
  211.1 1.3 collective-permute-start.16
  212.5 2.1 collective-permute-start.13
  214.6 10.6 %edge_grads.6 = (f32[2048,128]{1,0:T(8,128)}, f32[2048,128]{1,0:T(8,128)}, f32[32,128]{1,0:T(8,128)}) custom-call(s32[2]{0:T(128)} %pad_add_fusion.place, s32[8]{0:T(128)} %get-tuple-element.113.scal, f32[32,128]{1,0:T(8,128)} %get-tuple-element.140.first_in, bf16[2352,128]{1,0:T(8,128)(2,1)} %collective-permute-done.2.refs_4_.refs_0_, ...), custom_call_target="tpu_custom_call" | custom-call | flops 8999999488 | bytes 5000000 | tf_op jit(solution)/shard_map/edge_grads/pallas_call | solution.py:794
  225.3 1.7 collective-permute-done.13
  227.9 2.8 collective-permute-start.20
  230.7 8.0 %collective-permute-start.19 = (f32[320,128]{1,0:T(8,128)S(1)}, f32[320,128]{1,0:T(8,128)S(1)}, u32[]{:S(2)}, u32[]{:S(2)}) collective-permute-start(f32[320,128]{1,0:T(8,128)S(1)} %fusion.6), channel_id=1, source_target_pairs={{0,4},{4,0},{8,12},{12,8},{1,5},{5,1},{9,13},{13,9},{2,6},{6,2},{1... | collective-permute-start | bytes 491528 | tf_op jit(solution)/shard_map/ppermute | solution.py:821
  238.9 10.7 %edge_grads.7 = (f32[2048,128]{1,0:T(8,128)}, f32[2048,128]{1,0:T(8,128)}, f32[32,128]{1,0:T(8,128)}) custom-call(s32[2]{0:T(128)} %pad_add_fusion.place, s32[8]{0:T(128)} %get-tuple-element.113.scal, f32[32,128]{1,0:T(8,128)} %get-tuple-element.145.first_in, bf16[2352,128]{1,0:T(8,128)(2,1)} %collective-permute-done.3.refs_2_.refs_0_, ...), custom_call_target="tpu_custom_call" | custom-call | flops 8999999488 | bytes 5000000 | tf_op jit(solution)/shard_map/edge_grads/pallas_call | solution.py:794
  249.7 2.5 add_convert_fusion.1
  252.6 2.9 collective-permute-start.23
  256.6 7.5 %edge_grads.8 = (f32[2048,128]{1,0:T(8,128)}, f32[32,128]{1,0:T(8,128)}) custom-call(s32[2]{0:T(128)} %pad_add_fusion.place, s32[8]{0:T(128)} %get-tuple-element.113.scal, f32[32,128]{1,0:T(8,128)} %get-tuple-element.154.first_in, bf16[2048,128]{1,0:T(8,128)(2,1)} %get-tuple-element.258.refs_1_.refs_0_, ...), custom_call_target="tpu_custom_call" | custom-call | flops 8999999488 | bytes 5000000 | tf_op jit(solution)/shard_map/edge_grads/pallas_call | solution.py:794
  264.5 2.3 collective-permute-done.24
  268.4 7.4 %edge_grads.9 = (f32[2048,128]{1,0:T(8,128)}, f32[32,128]{1,0:T(8,128)}) custom-call(s32[2]{0:T(128)} %pad_add_fusion.place, s32[8]{0:T(128)} %get-tuple-element.113.scal, f32[32,128]{1,0:T(8,128)} %get-tuple-element.161.first_in, bf16[2352,128]{1,0:T(8,128)(2,1)} %copy-done.8, bf16[20,3,128,256]{3,2,1,0:T(8,128)(2,1)} %get-tuple-element.125.near.refs_2_.refs_1_, ...), custom_call_target="tpu_custom_call" | custom-call | flops 8999999488 | bytes 5000000 | tf_op jit(solution)/shard_map/edge_grads/pallas_call | solution.py:794
  275.8 5.7 %collective-permute-done.26 = bf16[2048,128]{1,0:T(8,128)(2,1)S(1)} collective-permute-done((bf16[2048,128]{1,0:T(8,128)(2,1)}, bf16[2048,128]{1,0:T(8,128)(2,1)S(1)}, u32[]{:S(2)}, u32[]{:S(2)}) %collective-permute-start.26) | collective-permute-done | bytes 524320 | tf_op jit(solution)/shard_map/ppermute | solution.py:821
  281.5 2.3 abs_reduce_fusion
  284.8 3.3 collective-permute-start.28
  288.1 2.4 collective-permute-start.30
  290.6 1.9 multiply_reduce_fusion.1
  292.5 7.5 %collective-permute-done.29 = f16[528,128]{1,0:T(8,128)(2,1)S(1)} collective-permute-done((f16[528,128]{1,0:T(8,128)(2,1)S(1)}, f16[528,128]{1,0:T(8,128)(2,1)S(1)}, u32[]{:S(2)}, u32[]{:S(2)}) %collective-permute-start.29) | collective-permute-done | bytes 135200 | tf_op jit(solution)/shard_map/ppermute | solution.py:821
  301.2 2.4 collective-permute-start.37
  305.3 2.2 collective-permute-start.32
  307.5 2.4 collective-permute-start.34
  312.1 1.2 collective-permute-done.32
  313.3 4.7 %collective-permute-done.33 = f16[528,128]{1,0:T(8,128)(2,1)S(1)} collective-permute-done((f16[528,128]{1,0:T(8,128)(2,1)S(1)}, f16[528,128]{1,0:T(8,128)(2,1)S(1)}, u32[]{:S(2)}, u32[]{:S(2)}) %collective-permute-start.33) | collective-permute-done | bytes 135200 | tf_op jit(solution)/shard_map/ppermute | solution.py:821
  318.3 2.7 collective-permute-start.39
  321.3 1.4 collective-permute-done.39
  322.8 2.0 collective-permute-start.43
  324.9 2.4 convert_multiply_fusion
  328.6 2.4 collective-permute-start.40
  331.0 2.5 collective-permute-start.41
  333.5 2.5 collective-permute-start.42
  336.1 1.8 collective-permute-done.42
  343.2 10.2 %adamw_step.1 = (f32[16,32]{1,0:T(8,128)}, f32[16,32]{1,0:T(8,128)}, f32[16,32]{1,0:T(8,128)}, f32[17,128]{1,0:T(8,128)}, f32[17,128]{1,0:T(8,128)}, /*index=5*/...) custom-call(f32[3]{0:T(128)} %pad_maximum_fusion.4.scale, ...), custom_call_target="tpu_custom_call" | custom-call | tf_op jit(solution)/shard_map/adamw_step/pallas_call | solution.py:915
  (231 shorter events, 35.7 us)
Async XLA Ops:
  5.7 28.9 %collective-permute-start.3 = (bf16[2352,128]{1,0:T(8,128)(2,1)S(1)}, bf16[2352,128]{1,0:T(8,128)(2,1)}, u32[]{:S(2)}, u32[]{:S(2)}) collective-permute-start(bf16[2352,128]{1,0:T(8,128)(2,1)S(1)} %pad_maximum_fusion.refs_0_), channel_id=1, source_target_pairs={{0,1},{1,0},{2,3},{3,2},{4,5},{5,4},{6,7},{7,6},{8,9},{9,8},{10,11... | collective-permute-start | bytes 1806344 | tf_op jit(solution)/shard_map/ppermute | solution.py:821
  8.7 28.1 %collective-permute-start.2 = (bf16[2352,128]{1,0:T(8,128)(2,1)S(1)}, bf16[2352,128]{1,0:T(8,128)(2,1)}, u32[]{:S(2)}, u32[]{:S(2)}) collective-permute-start(bf16[2352,128]{1,0:T(8,128)(2,1)S(1)} %pad_maximum_fusion.refs_0_), channel_id=1, source_target_pairs={{0,2},{1,3},{2,0},{3,1},{4,6},{5,7},{6,4},{7,5},{8,10},{9,11},{10,... | collective-permute-start | bytes 1806344 | tf_op jit(solution)/shard_map/ppermute | solution.py:821
  10.2 28.3 %collective-permute-start.1 = (bf16[2352,128]{1,0:T(8,128)(2,1)S(1)}, bf16[2352,128]{1,0:T(8,128)(2,1)}, u32[]{:S(2)}, u32[]{:S(2)}) collective-permute-start(bf16[2352,128]{1,0:T(8,128)(2,1)S(1)} %pad_maximum_fusion.refs_0_), channel_id=1, source_target_pairs={{0,3},{1,2},{2,1},{3,0},{4,7},{5,6},{6,5},{7,4},{8,11},{9,10},{10,... | collective-permute-start | bytes 1806344 | tf_op jit(solution)/shard_map/ppermute | solution.py:821
  10.9 18.6 %collective-permute-start = (f32[1,1]{1,0:T(1,128)}, f32[1,1]{1,0:T(1,128)}, u32[]{:S(2)}, u32[]{:S(2)}) collective-permute-start(f32[1,1]{1,0:T(1,128)} %bitcast.7), channel_id=1, source_target_pairs={{0,16},{16,0},{1,17},{17,1},{2,18},{18,2},{3,19},{19,3},{4,20},{20... | collective-permute-start | bytes 20 | tf_op jit(solution)/shard_map/ppermute | solution.py:821
  30.8 73.0 %collective-permute-start.7 = (f32[1,1]{1,0:T(1,128)}, f32[1,1]{1,0:T(1,128)}, u32[]{:S(2)}, u32[]{:S(2)}) collective-permute-start(f32[1,1]{1,0:T(1,128)} %add.234), channel_id=1, source_target_pairs={{0,4},{4,0},{8,12},{12,8},{1,5},{5,1},{9,13},{13,9},{2,6},{6,2},{1... | collective-permute-start | bytes 20 | tf_op jit(solution)/shard_map/ppermute | solution.py:821
  34.6 9.3 %collective-permute-start.4 = (bf16[2352,128]{1,0:T(8,128)(2,1)}, bf16[2352,128]{1,0:T(8,128)(2,1)S(1)}, u32[]{:S(2)}, u32[]{:S(2)}) collective-permute-start(bf16[2352,128]{1,0:T(8,128)(2,1)} %collective-permute-done.3.refs_2_.refs_0_), channel_id=1, source_target_pairs={{0,16},{16,0},{1,17},{17,1},{2,18},{18,2},{3,19},{19,3},{4,20},{20... | collective-permute-start | bytes 1806344 | tf_op jit(solution)/shard_map/ppermute | solution.py:821
  36.8 7.1 %collective-permute-start.5 = (bf16[2352,128]{1,0:T(8,128)(2,1)}, bf16[2352,128]{1,0:T(8,128)(2,1)S(1)}, u32[]{:S(2)}, u32[]{:S(2)}) collective-permute-start(bf16[2352,128]{1,0:T(8,128)(2,1)} %collective-permute-done.2.refs_4_.refs_0_), channel_id=1, source_target_pairs={{0,16},{16,0},{1,17},{17,1},{2,18},{18,2},{3,19},{19,3},{4,20},{20... | collective-permute-start | bytes 1806344 | tf_op jit(solution)/shard_map/ppermute | solution.py:821
  38.6 5.3 %collective-permute-start.6 = (bf16[2352,128]{1,0:T(8,128)(2,1)}, bf16[2352,128]{1,0:T(8,128)(2,1)S(1)}, u32[]{:S(2)}, u32[]{:S(2)}) collective-permute-start(bf16[2352,128]{1,0:T(8,128)(2,1)} %collective-permute-done.1.refs_6_.refs_0_), channel_id=1, source_target_pairs={{0,16},{16,0},{1,17},{17,1},{2,18},{18,2},{3,19},{19,3},{4,20},{20... | collective-permute-start | bytes 1806344 | tf_op jit(solution)/shard_map/ppermute | solution.py:821
  104.4 26.9 %collective-permute-start.8 = (f32[1,1]{1,0:T(1,128)}, f32[1,1]{1,0:T(1,128)}, u32[]{:S(2)}, u32[]{:S(2)}) collective-permute-start(f32[1,1]{1,0:T(1,128)} %add.237), channel_id=1, source_target_pairs={{0,8},{4,12},{8,0},{12,4},{1,9},{5,13},{9,1},{13,5},{2,10},{6,14},... | collective-permute-start | bytes 20 | tf_op jit(solution)/shard_map/ppermute | solution.py:821
  130.9 55.9 %collective-permute-start.9 = (f32[1328,128]{1,0:T(8,128)}, f32[1328,128]{1,0:T(8,128)S(1)}, u32[]{:S(2)}, u32[]{:S(2)}) collective-permute-start(f32[1328,128]{1,0:T(8,128)} %get-tuple-element.119), channel_id=1, source_target_pairs={{0,8},{4,12},{8,0},{12,4},{1,9},{5,13},{9,1},{13,5},{2,10},{6,14},... | collective-permute-start | bytes 2039816 | tf_op jit(solution)/shard_map/ppermute | solution.py:821
  132.0 54.9 %copy-start.6 = (f32[1328,128]{1,0:T(8,128)S(1)}, f32[1328,128]{1,0:T(8,128)}, u32[]{:S(2)}) copy-start(f32[1328,128]{1,0:T(8,128)} %get-tuple-element.119) | copy-start | bytes 2039812
  187.0 7.2 %collective-permute-start.10 = (f32[664,128]{1,0:T(8,128)S(1)}, f32[664,128]{1,0:T(8,128)S(1)}, u32[]{:S(2)}, u32[]{:S(2)}) collective-permute-start(f32[664,128]{1,0:T(8,128)S(1)} %dynamic-slice_bitcast_fusion.2), channel_id=1, source_target_pairs={{0,16},{16,0},{1,17},{17,1},{2,18},{18,2},{3,19},{19,3},{4,20},{20... | collective-permute-start | bytes 1019912 | tf_op jit(solution)/shard_map/ppermute | solution.py:821
  193.7 12.3 %collective-permute-start.12 = (f32[4,320,128]{2,1,0:T(8,128)S(1)}, f32[4,320,128]{2,1,0:T(8,128)}, u32[]{:S(2)}, u32[]{:S(2)}) collective-permute-start(f32[4,320,128]{2,1,0:T(8,128)S(1)} %copy-done.7), channel_id=1, source_target_pairs={{0,16},{16,0},{1,17},{17,1},{2,18},{18,2},{3,19},{19,3},{4,20},{20... | collective-permute-start | bytes 1966088 | tf_op jit(solution)/shard_map/ppermute | solution.py:821
  194.2 11.8 %collective-permute-start.11 = (f32[664,128]{1,0:T(8,128)S(1)}, f32[664,128]{1,0:T(8,128)S(1)}, u32[]{:S(2)}, u32[]{:S(2)}) collective-permute-start(f32[664,128]{1,0:T(8,128)S(1)} %bitcast_add_fusion), channel_id=1, source_target_pairs={{0,1},{1,0},{2,3},{3,2},{4,5},{5,4},{6,7},{7,6},{8,9},{9,8},{10,11... | collective-permute-start | bytes 1019912 | tf_op jit(solution)/shard_map/ppermute | solution.py:821
  205.5 21.4 %collective-permute-start.17 = (f32[2048,128]{1,0:T(8,128)}, f32[2048,128]{1,0:T(8,128)S(1)}, u32[]{:S(2)}, u32[]{:S(2)}) collective-permute-start(f32[2048,128]{1,0:T(8,128)} %get-tuple-element.143), channel_id=1, source_target_pairs={{0,16},{16,0},{1,17},{17,1},{2,18},{18,2},{3,19},{19,3},{4,20},{20... | collective-permute-start | bytes 3145736 | tf_op jit(solution)/shard_map/ppermute | solution.py:821
  208.0 17.2 %collective-permute-start.14 = (f32[320,128]{1,0:T(8,128)}, f32[320,128]{1,0:T(8,128)S(1)}, u32[]{:S(2)}, u32[]{:S(2)}) collective-permute-start(f32[320,128]{1,0:T(8,128)} %get-tuple-element.262), channel_id=1, source_target_pairs={{0,1},{1,0},{2,3},{3,2},{4,5},{5,4},{6,7},{7,6},{8,9},{9,8},{10,11... | collective-permute-start | bytes 491528 | tf_op jit(solution)/shard_map/ppermute | solution.py:821
  209.7 15.6 %collective-permute-start.15 = (f32[320,128]{1,0:T(8,128)}, f32[320,128]{1,0:T(8,128)S(1)}, u32[]{:S(2)}, u32[]{:S(2)}) collective-permute-start(f32[320,128]{1,0:T(8,128)} %get-tuple-element.261), channel_id=1, source_target_pairs={{0,2},{1,3},{2,0},{3,1},{4,6},{5,7},{6,4},{7,5},{8,10},{9,11},{10,... | collective-permute-start | bytes 491528 | tf_op jit(solution)/shard_map/ppermute | solution.py:821
  211.1 14.2 %collective-permute-start.16 = (f32[320,128]{1,0:T(8,128)S(1)}, f32[320,128]{1,0:T(8,128)S(1)}, u32[]{:S(2)}, u32[]{:S(2)}) collective-permute-start(f32[320,128]{1,0:T(8,128)S(1)} %get-tuple-element.260), channel_id=1, source_target_pairs={{0,3},{1,2},{2,1},{3,0},{4,7},{5,6},{6,5},{7,4},{8,11},{9,10},{10,... | collective-permute-start | bytes 491528 | tf_op jit(solution)/shard_map/ppermute | solution.py:821
  212.5 14.5 %collective-permute-start.13 = (f32[664,128]{1,0:T(8,128)S(1)}, f32[664,128]{1,0:T(8,128)S(1)}, u32[]{:S(2)}, u32[]{:S(2)}) collective-permute-start(f32[664,128]{1,0:T(8,128)S(1)} %add.241), channel_id=1, source_target_pairs={{0,2},{1,3},{2,0},{3,1},{4,6},{5,7},{6,4},{7,5},{8,10},{9,11},{10,... | collective-permute-start | bytes 1019912 | tf_op jit(solution)/shard_map/ppermute | solution.py:821
  225.2 24.5 %collective-permute-start.21 = (f32[2048,128]{1,0:T(8,128)}, f32[2048,128]{1,0:T(8,128)}, u32[]{:S(2)}, u32[]{:S(2)}) collective-permute-start(f32[2048,128]{1,0:T(8,128)} %get-tuple-element.152), channel_id=1, source_target_pairs={{0,16},{16,0},{1,17},{17,1},{2,18},{18,2},{3,19},{19,3},{4,20},{20... | collective-permute-start | bytes 3145736 | tf_op jit(solution)/shard_map/ppermute | solution.py:821
  227.9 21.8 %collective-permute-start.20 = (bf16[2048,128]{1,0:T(8,128)(2,1)}, bf16[2048,128]{1,0:T(8,128)(2,1)S(1)}, u32[]{:S(2)}, u32[]{:S(2)}) collective-permute-start(bf16[2048,128]{1,0:T(8,128)(2,1)} %add_convert_fusion.2), channel_id=1, source_target_pairs={{0,3},{1,2},{2,1},{3,0},{4,7},{5,6},{6,5},{7,4},{8,11},{9,10},{10,... | collective-permute-start | bytes 1572872 | tf_op jit(solution)/shard_map/ppermute | solution.py:821
  230.7 18.9 %collective-permute-start.19 = (f32[320,128]{1,0:T(8,128)S(1)}, f32[320,128]{1,0:T(8,128)S(1)}, u32[]{:S(2)}, u32[]{:S(2)}) collective-permute-start(f32[320,128]{1,0:T(8,128)S(1)} %fusion.6), channel_id=1, source_target_pairs={{0,4},{4,0},{8,12},{12,8},{1,5},{5,1},{9,13},{13,9},{2,6},{6,2},{1... | collective-permute-start | bytes 491528 | tf_op jit(solution)/shard_map/ppermute | solution.py:821
  238.8 10.9 %collective-permute-start.18 = (f32[664,128]{1,0:T(8,128)S(1)}, f32[664,128]{1,0:T(8,128)S(1)}, u32[]{:S(2)}, u32[]{:S(2)}) collective-permute-start(f32[664,128]{1,0:T(8,128)S(1)} %add.246), channel_id=1, source_target_pairs={{0,4},{4,0},{8,12},{12,8},{1,5},{5,1},{9,13},{13,9},{2,6},{6,2},{1... | collective-permute-start | bytes 1019912 | tf_op jit(solution)/shard_map/ppermute | solution.py:821
  249.5 17.3 %collective-permute-start.25 = (f32[2048,128]{1,0:T(8,128)}, f32[2048,128]{1,0:T(8,128)S(1)}, u32[]{:S(2)}, u32[]{:S(2)}) collective-permute-start(f32[2048,128]{1,0:T(8,128)} %get-tuple-element.159), channel_id=1, source_target_pairs={{0,16},{16,0},{1,17},{17,1},{2,18},{18,2},{3,19},{19,3},{4,20},{20... | collective-permute-start | bytes 3145736 | tf_op jit(solution)/shard_map/ppermute | solution.py:821
  252.2 14.6 %collective-permute-start.24 = (bf16[2048,128]{1,0:T(8,128)(2,1)}, bf16[2048,128]{1,0:T(8,128)(2,1)}, u32[]{:S(2)}, u32[]{:S(2)}) collective-permute-start(bf16[2048,128]{1,0:T(8,128)(2,1)} %add_convert_fusion.1), channel_id=1, source_target_pairs={{0,2},{1,3},{2,0},{3,1},{4,6},{5,7},{6,4},{7,5},{8,10},{9,11},{10,... | collective-permute-start | bytes 1572872 | tf_op jit(solution)/shard_map/ppermute | solution.py:821
  252.6 11.9 %collective-permute-start.23 = (f32[320,128]{1,0:T(8,128)S(1)}, f32[320,128]{1,0:T(8,128)S(1)}, u32[]{:S(2)}, u32[]{:S(2)}) collective-permute-start(f32[320,128]{1,0:T(8,128)S(1)} %add.253), channel_id=1, source_target_pairs={{0,8},{4,12},{8,0},{12,4},{1,9},{5,13},{9,1},{13,5},{2,10},{6,14},... | collective-permute-start | bytes 491528 | tf_op jit(solution)/shard_map/ppermute | solution.py:821
  256.5 8.0 %collective-permute-start.22 = (f32[664,128]{1,0:T(8,128)S(1)}, f32[664,128]{1,0:T(8,128)}, u32[]{:S(2)}, u32[]{:S(2)}) collective-permute-start(f32[664,128]{1,0:T(8,128)S(1)} %add.252), channel_id=1, source_target_pairs={{0,16},{16,0},{1,17},{17,1},{2,18},{18,2},{3,19},{19,3},{4,20},{20... | collective-permute-start | bytes 1019912 | tf_op jit(solution)/shard_map/ppermute | solution.py:821
  264.1 17.4 %collective-permute-start.27 = (f32[2048,128]{1,0:T(8,128)}, f32[2048,128]{1,0:T(8,128)S(1)}, u32[]{:S(2)}, u32[]{:S(2)}) collective-permute-start(f32[2048,128]{1,0:T(8,128)} %get-tuple-element.166), channel_id=1, source_target_pairs={{0,16},{16,0},{1,17},{17,1},{2,18},{18,2},{3,19},{19,3},{4,20},{20... | collective-permute-start | bytes 3145736 | tf_op jit(solution)/shard_map/ppermute | solution.py:821
  267.8 13.7 %collective-permute-start.26 = (bf16[2048,128]{1,0:T(8,128)(2,1)}, bf16[2048,128]{1,0:T(8,128)(2,1)S(1)}, u32[]{:S(2)}, u32[]{:S(2)}) collective-permute-start(bf16[2048,128]{1,0:T(8,128)(2,1)} %add_convert_fusion), channel_id=1, source_target_pairs={{0,1},{1,0},{2,3},{3,2},{4,5},{5,4},{6,7},{7,6},{8,9},{9,8},{10,11... | collective-permute-start | bytes 1572872 | tf_op jit(solution)/shard_map/ppermute | solution.py:821
  284.8 7.7 %collective-permute-start.28 = (f16[528,128]{1,0:T(8,128)(2,1)S(1)}, f16[528,128]{1,0:T(8,128)(2,1)S(1)}, u32[]{:S(2)}, u32[]{:S(2)}) collective-permute-start(f16[528,128]{1,0:T(8,128)(2,1)S(1)} %get-tuple-element.265), channel_id=1, source_target_pairs={{0,4},{4,0},{8,12},{12,8},{1,5},{5,1},{9,13},{13,9},{2,6},{6,2},{1... | collective-permute-start | bytes 405512 | tf_op jit(solution)/shard_map/ppermute | solution.py:821
  288.1 11.9 %collective-permute-start.29 = (f16[528,128]{1,0:T(8,128)(2,1)S(1)}, f16[528,128]{1,0:T(8,128)(2,1)S(1)}, u32[]{:S(2)}, u32[]{:S(2)}) collective-permute-start(f16[528,128]{1,0:T(8,128)(2,1)S(1)} %get-tuple-element.264), channel_id=1, source_target_pairs={{0,8},{4,12},{8,0},{12,4},{1,9},{5,13},{9,1},{13,5},{2,10},{6,14},... | collective-permute-start | bytes 405512 | tf_op jit(solution)/shard_map/ppermute | solution.py:821
  288.1 11.9 %collective-permute-start.30 = (f16[528,128]{1,0:T(8,128)(2,1)S(1)}, f16[528,128]{1,0:T(8,128)(2,1)S(1)}, u32[]{:S(2)}, u32[]{:S(2)}) collective-permute-start(f16[528,128]{1,0:T(8,128)(2,1)S(1)} %get-tuple-element.263), channel_id=1, source_target_pairs={{0,12},{4,8},{8,4},{12,0},{1,13},{5,9},{9,5},{13,1},{2,14},{6,10},... | collective-permute-start | bytes 405512 | tf_op jit(solution)/shard_map/ppermute | solution.py:821
  290.6 2.0 collective-permute-start.31
  292.5 25.6 %copy-start.1 = (f32[1328,128]{1,0:T(8,128)}, f32[1328,128]{1,0:T(8,128)S(1)}, u32[]{:S(2)}) copy-start(f32[1328,128]{1,0:T(8,128)S(1)} %get-tuple-element.248.read) | copy-start | bytes 2039812
  300.0 7.5 %collective-permute-start.35 = (f32[32,128]{1,0:T(8,128)S(1)}, f32[32,128]{1,0:T(8,128)S(1)}, u32[]{:S(2)}, u32[]{:S(2)}) collective-permute-start(f32[32,128]{1,0:T(8,128)S(1)} %add.268), channel_id=1, source_target_pairs={{0,1},{1,0},{2,3},{3,2},{4,5},{5,4},{6,7},{7,6},{8,9},{9,8},{10,11... | collective-permute-start | bytes 49160 | tf_op jit(solution)/shard_map/ppermute | solution.py:821
  300.2 11.9 %collective-permute-start.36 = (f32[32,128]{1,0:T(8,128)S(1)}, f32[32,128]{1,0:T(8,128)S(1)}, u32[]{:S(2)}, u32[]{:S(2)}) collective-permute-start(f32[32,128]{1,0:T(8,128)S(1)} %add.268), channel_id=1, source_target_pairs={{0,2},{1,3},{2,0},{3,1},{4,6},{5,7},{6,4},{7,5},{8,10},{9,11},{10,... | collective-permute-start | bytes 49160 | tf_op jit(solution)/shard_map/ppermute | solution.py:821
  301.2 10.9 %collective-permute-start.37 = (f32[32,128]{1,0:T(8,128)S(1)}, f32[32,128]{1,0:T(8,128)S(1)}, u32[]{:S(2)}, u32[]{:S(2)}) collective-permute-start(f32[32,128]{1,0:T(8,128)S(1)} %add.268), channel_id=1, source_target_pairs={{0,3},{1,2},{2,1},{3,0},{4,7},{5,6},{6,5},{7,4},{8,11},{9,10},{10,... | collective-permute-start | bytes 49160 | tf_op jit(solution)/shard_map/ppermute | solution.py:821
  305.3 8.0 %collective-permute-start.32 = (f16[528,128]{1,0:T(8,128)(2,1)S(1)}, f16[528,128]{1,0:T(8,128)(2,1)S(1)}, u32[]{:S(2)}, u32[]{:S(2)}) collective-permute-start(f16[528,128]{1,0:T(8,128)(2,1)S(1)} %get-tuple-element.266), channel_id=1, source_target_pairs={{0,4},{4,0},{8,12},{12,8},{1,5},{5,1},{9,13},{13,9},{2,6},{6,2},{1... | collective-permute-start | bytes 405512 | tf_op jit(solution)/shard_map/ppermute | solution.py:821
  307.5 10.6 %collective-permute-start.33 = (f16[528,128]{1,0:T(8,128)(2,1)S(1)}, f16[528,128]{1,0:T(8,128)(2,1)S(1)}, u32[]{:S(2)}, u32[]{:S(2)}) collective-permute-start(f16[528,128]{1,0:T(8,128)(2,1)S(1)} %get-tuple-element.266), channel_id=1, source_target_pairs={{0,8},{4,12},{8,0},{12,4},{1,9},{5,13},{9,1},{13,5},{2,10},{6,14},... | collective-permute-start | bytes 405512 | tf_op jit(solution)/shard_map/ppermute | solution.py:821
  307.5 10.6 %collective-permute-start.34 = (f16[528,128]{1,0:T(8,128)(2,1)S(1)}, f16[528,128]{1,0:T(8,128)(2,1)S(1)}, u32[]{:S(2)}, u32[]{:S(2)}) collective-permute-start(f16[528,128]{1,0:T(8,128)(2,1)S(1)} %get-tuple-element.266), channel_id=1, source_target_pairs={{0,12},{4,8},{8,4},{12,0},{1,13},{5,9},{9,5},{13,1},{2,14},{6,10},... | collective-permute-start | bytes 405512 | tf_op jit(solution)/shard_map/ppermute | solution.py:821
  318.2 4.5 %collective-permute-start.38 = (f16[2112,128]{1,0:T(8,128)(2,1)S(1)}, f16[2112,128]{1,0:T(8,128)(2,1)S(1)}, u32[]{:S(2)}, u32[]{:S(2)}) collective-permute-start(f16[2112,128]{1,0:T(8,128)(2,1)S(1)} %constant_dynamic-update-slice_fusion.2), channel_id=1, source_target_pairs={{0,16},{16,0},{1,17},{17,1},{2,18},{18,2},{3,19},{19,3},{4,20},{20... | collective-permute-start | bytes 1622024 | tf_op jit(solution)/shard_map/ppermute | solution.py:821
  318.3 4.4 %collective-permute-start.39 = (f32[32,128]{1,0:T(8,128)S(1)}, f32[32,128]{1,0:T(8,128)S(1)}, u32[]{:S(2)}, u32[]{:S(2)}) collective-permute-start(f32[32,128]{1,0:T(8,128)S(1)} %add_add_fusion), channel_id=1, source_target_pairs={{0,4},{4,0},{8,12},{12,8},{1,5},{5,1},{9,13},{13,9},{2,6},{6,2},{1... | collective-permute-start | bytes 49160 | tf_op jit(solution)/shard_map/ppermute | solution.py:821
  322.7 19.6 %copy-start.10 = (f32[2,129,3,32]{1,3,2,0:T(8,128)S(1)}, f32[2,129,3,32]{1,3,2,0:T(8,128)}, u32[]{:S(2)}) copy-start(f32[2,129,3,32]{1,3,2,0:T(8,128)} %param.38) | copy-start | bytes 297220
  322.7 19.6 %copy-start.14 = (f32[2,129,3,32]{1,3,2,0:T(8,128)S(1)}, f32[2,129,3,32]{1,3,2,0:T(8,128)}, u32[]{:S(2)}) copy-start(f32[2,129,3,32]{1,3,2,0:T(8,128)} %param.50) | copy-start | bytes 297220
  322.8 15.1 %collective-permute-start.43 = (f32[32,128]{1,0:T(8,128)S(1)}, f32[32,128]{1,0:T(8,128)S(1)}, u32[]{:S(2)}, u32[]{:S(2)}) collective-permute-start(f32[32,128]{1,0:T(8,128)S(1)} %add.279), channel_id=1, source_target_pairs={{0,8},{4,12},{8,0},{12,4},{1,9},{5,13},{9,1},{13,5},{2,10},{6,14},... | collective-permute-start | bytes 49160 | tf_op jit(solution)/shard_map/ppermute | solution.py:821
  328.6 7.4 %collective-permute-start.40 = (f32[1,1]{1,0:T(1,128)}, f32[1,1]{1,0:T(1,128)}, u32[]{:S(2)}, u32[]{:S(2)}) collective-permute-start(f32[1,1]{1,0:T(1,128)} %bitcast.48), channel_id=1, source_target_pairs={{0,1},{1,0},{2,3},{3,2},{4,5},{5,4},{6,7},{7,6},{8,9},{9,8},{10,11... | collective-permute-start | bytes 20 | tf_op jit(solution)/shard_map/ppermute | solution.py:821
  331.0 5.1 %collective-permute-start.41 = (f32[1,1]{1,0:T(1,128)}, f32[1,1]{1,0:T(1,128)}, u32[]{:S(2)}, u32[]{:S(2)}) collective-permute-start(f32[1,1]{1,0:T(1,128)} %bitcast.48), channel_id=1, source_target_pairs={{0,2},{1,3},{2,0},{3,1},{4,6},{5,7},{6,4},{7,5},{8,10},{9,11},{10,... | collective-permute-start | bytes 20 | tf_op jit(solution)/shard_map/ppermute | solution.py:821
  333.5 4.4 %collective-permute-start.42 = (f32[1,1]{1,0:T(1,128)}, f32[1,1]{1,0:T(1,128)}, u32[]{:S(2)}, u32[]{:S(2)}) collective-permute-start(f32[1,1]{1,0:T(1,128)} %bitcast.48), channel_id=1, source_target_pairs={{0,3},{1,2},{2,1},{3,0},{4,7},{5,6},{6,5},{7,4},{8,11},{9,10},{10,... | collective-permute-start | bytes 20 | tf_op jit(solution)/shard_map/ppermute | solution.py:821
  (29 other events, 203.2 us)

commit v5 on v4

--- a/solution.py
+++ b/solution.py
@@ -717,13 +717,12 @@
     )(place, scal, inverse, nf_t, gru, gru_bias, idx, hid, msg, state, near, d_final, mats)
 
 
-def final_kernel(place, scal, first_in, *refs, pair, sides, group):
+def final_kernel(place, scal, first_in, narrow, *refs, pair, sides, half, group):
     seconds, refs = refs[: len(sides)], refs[len(sides) :]
     (near, far, eh, pre, feat), refs = refs[:5], refs[5:]
     outs, refs = refs[: len(sides)], refs[len(sides) :]
     first_out, near_s, far_s, eh_s, pre_s, feat_s, sems = refs
     edge_blocks = ceil_blocks(scal[4])
-    half = outs[0].shape[0]
     width = half // H
 
     def copies(block, slot):
@@ -746,8 +745,11 @@
             for copy in copies(jnp.int32(block), block):
                 copy.start()
 
-    for out in outs:
+    share = narrow.shape[1] // 2
+    for side, out in zip(sides, outs):
         out[...] = jnp.zeros(out.shape, F32)
+        begin_row = pl.multiple_of((side ^ place[1]) * share, 8)
+        out[half : half + share, :] = narrow[pair ^ place[0], pl.ds(begin_row, share), :]
     first_out[...] = first_in[...]
 
     def edge_block(block, carry):
@@ -787,15 +789,15 @@
     lax.fori_loop(0, edge_blocks, edge_block, 0)
 
 
-def edge_grads(place, scal, seconds, near, far, eh, pre, feat, first_in, pair, sides, half):
+def edge_grads(place, scal, seconds, near, far, eh, pre, feat, narrow, first_in, pair, sides, half, rows):
     smem = pl.BlockSpec(memory_space=pltpu.SMEM)
     vmem = pl.BlockSpec(memory_space=pltpu.VMEM)
     size = len(sides)
     return pl.pallas_call(
-        functools.partial(final_kernel, pair=pair, sides=sides, group=4),
-        in_specs=[smem] * 2 + [vmem] * (1 + size) + [pl.BlockSpec(memory_space=pl.ANY)] * 5,
+        functools.partial(final_kernel, pair=pair, sides=sides, half=half, group=4),
+        in_specs=[smem] * 2 + [vmem] * (2 + size) + [pl.BlockSpec(memory_space=pl.ANY)] * 5,
         out_specs=[vmem] * (size + 1),
-        out_shape=[jax.ShapeDtypeStruct((half, H), F32)] * size + [jax.ShapeDtypeStruct((FEAT, H), F32)],
+        out_shape=[jax.ShapeDtypeStruct((rows, H), F32)] * size + [jax.ShapeDtypeStruct((FEAT, H), F32)],
         scratch_shapes=[
             pltpu.VMEM((AHEAD, STEPS, H, BLK), BF),
             pltpu.VMEM((AHEAD, STEPS, 2 * half // H, BLK), BF),
@@ -807,7 +809,7 @@
         compiler_params=pltpu.CompilerParams(vmem_limit_bytes=VMEM_LIMIT),
         cost_estimate=pl.CostEstimate(flops=9_000_000_000, transcendentals=0, bytes_accessed=5_000_000),
         name="edge_grads",
-    )(place, scal, first_in, *seconds, near, far, eh, pre, feat)
+    )(place, scal, first_in, narrow, *seconds, near, far, eh, pre, feat)
 
 
 def exact3(value):
@@ -835,6 +837,25 @@
 def unscaled(low):
     power = low[..., -1:, :].astype(F32)
     return low[..., :-16, :].astype(F32) * jnp.exp2(-power)
+
+
+def coded(value):
+    power = jnp.floor(14.0 - jnp.log2(jnp.maximum(jnp.max(jnp.abs(value)), 1e-30)))
+    value = value * jnp.exp2(power)
+    high = lax.reduce_precision(value, 5, 10)
+    terms = [high, value - high, jnp.full((16, H), power, F32)]
+    return jnp.concatenate(terms, axis=0).astype(jnp.float16)
+
+
+def decoded(low):
+    low = low.astype(F32)
+    return (low[:FEAT] + low[FEAT : 2 * FEAT]) * jnp.exp2(-low[-1:])
+
+
+def pair_sum(values):
+    while len(values) > 1:
+        values = [left + right for left, right in zip(values[::2], values[1::2])]
+    return values[0]
 
 
 def flat_rows(array):
@@ -872,7 +893,7 @@
         ins[3 * item : 3 * item + 3] + outs[3 * item : 3 * item + 3] for item in range(5)
     ]
     every = slice(None)
-    update_rows(scale, second, (slice(0, H), every), wide[...].T, RATES[2])
+    update_rows(scale, second, (slice(0, H), every), wide[0].T, RATES[2])
     update_rows(scale, second, (slice(H, H + 1), every), bias[...], RATES[2])
 
     @pl.when(pl.program_id(0) == 0)
@@ -901,6 +922,7 @@
 def adamw_step(scale, wide, bias, read, small, first, groups):
     block = 1024
     columns = groups[2][0].shape[1]
+    each = columns // (block * wide.shape[0])
 
     def whole(array):
         return pl.BlockSpec(array.shape, lambda index: (0, 0))
@@ -917,7 +939,7 @@
         grid=(columns // block,),
         in_specs=[
             pl.BlockSpec(memory_space=pltpu.SMEM),
-            pl.BlockSpec((block, H), lambda index: (index, 0)),
+            pl.BlockSpec((1, block, H), lambda index: (index // each, index % each, 0)),
             pl.BlockSpec((1, block), lambda index: (0, index)),
             whole(read),
             whole(small),
@@ -1048,70 +1070,50 @@
     )
     (small, far), moved = lax.optimization_barrier(((small, far), [arrays for _, _, arrays in chains]))
 
-    def narrow_chain():
-        (got,) = yield [swap(small, "grp", cores, 1)]
-        parts = small + got
-        moved = yield [swap(pick(parts, gate ^ step), "gate", gates, step) for step in range(1, gates)]
-        value = pick(parts, gate)
-        for got in moved:
-            value = value + got
-        step = 1
-        while step < groups:
-            (got,) = yield [swap(value, "edge", groups, step)]
-            value = value + got
-            step *= 2
-        return value
+    share = small.shape[1] // 2
+    rows = up(half + share, 16 * groups)
+    tall = rows // groups + 16
 
     def wide_chain(mine, other, step):
         (got,) = yield [swap(other, "grp", cores, 1)]
         (part,) = yield [swap((mine + got).astype(BF), "gate", gates, step)]
         return part.astype(F32)
+
+    def joined(parts, me, total):
+        out = jnp.zeros((total, H), parts[0].dtype)
+        for step, part in enumerate(parts):
+            out = lax.dynamic_update_slice_in_dim(out, part, (me ^ step) * part.shape[0], 0)
+        return out
 
     def last_chain(other):
         (got,) = yield [swap(other, "grp", cores, 1)]
         total = mine + got
         for step in range(1, gates):
             total = total + results[step]
-        rows = up(half, 16 * groups)
-        total = jnp.pad(total, ((0, rows - half), (0, 0))).reshape(groups, rows // groups, H)
+        total = total.reshape(groups, rows // groups, H)
         parts = scaled(total)
-        moved = yield [swap(pick(parts, group ^ step), "edge", groups, step) for step in range(1, groups)]
+        ends = coded(jnp.where(jnp.arange(FEAT)[:, None] <= EIN, first, 0.0))
+        moved = yield [
+            swap(jnp.concatenate([pick(parts, group ^ step), ends], axis=0), "edge", groups, step)
+            for step in range(1, groups)
+        ]
         shard = pick(total, group)
         for got in moved:
-            shard = shard + unscaled(got)
+            shard = shard + unscaled(got[:tall])
+        ends = coded(pair_sum([decoded(ends)] + [decoded(got[tall:]) for got in moved]))
         shard = scaled(shard)
         moved = yield [swap(shard, "edge", groups, step) for step in range(1, groups)]
-        tall = shard.shape[0]
-
-        def joined(parts, me, total):
-            out = jnp.zeros((total, H), parts[0].dtype)
-            for step, part in enumerate(parts):
-                out = lax.dynamic_update_slice_in_dim(out, part, (me ^ step) * part.shape[0], 0)
-            return out
-
         full = joined([shard] + moved, group, groups * tall)
-        (got,) = yield [swap(full, "grp", cores, 1)]
-        full = joined([full, got], core, cores * groups * tall)
-        grads = unscaled(full.reshape(cores * groups, tall, H)).reshape(cores, rows, H)[:, :half].reshape(-1, H)
-        narrow = results["narrow"]
-        values = [(jnp.sum(grads * grads) + jnp.sum(narrow * narrow)).reshape(1, 1)]
+        (got,) = yield [swap(jnp.concatenate([full, ends], axis=0), "grp", cores, 1)]
+        ends = decoded(ends) + decoded(got[groups * tall :])
+        full = joined([full, got[: groups * tall]], core, cores * groups * tall)
+        full = unscaled(full.reshape(cores * groups, tall, H)).reshape(cores, rows, H)
+        squares = jnp.full((8, H), jnp.sum(full * full), F32)
+        values = [jnp.concatenate([ends, squares], axis=0)]
         values += yield [swap(values[0], "gate", gates, step) for step in range(1, gates)]
-        while len(values) > 1:
-            values = [left + right for left, right in zip(values[::2], values[1::2])]
-        return grads, values[0][0, 0]
-
-    def first_chain(first):
-        (got,) = yield [swap(first, "grp", cores, 1)]
-        values = [first + got]
-        values += yield [swap(values[0], "gate", gates, step) for step in range(1, gates)]
-        while len(values) > 1:
-            values = [left + right for left, right in zip(values[::2], values[1::2])]
-        step = 1
-        while step < groups:
-            (got,) = yield [swap(values[0], "edge", groups, step)]
-            values = [values[0] + got]
-            step *= 2
-        return values[0]
+        ends = pair_sum(values)
+        narrow = full[:, half : half + share].reshape(-1, H)
+        return full, narrow, ends[:FEAT], ends[FEAT, 0]
 
     results = {}
 
@@ -1130,24 +1132,20 @@
         name, chain, arrays = chains[0]
         first, arrays = lax.optimization_barrier((first, arrays))
         chains[0] = (name, chain, chain.send(arrays))
-    fresh = narrow_chain()
-    chains.append(("narrow", fresh, next(fresh)))
     for step in reversed(range(gates)):
         pieces = second[2 * step : 2 * step + 2]
-        edge_args = (near, far, eh, pre, feat)
+        edge_args = (near, far, eh, pre, feat, small)
         if step:
-            mine, other, first = edge_grads(place, scal, pieces, *edge_args, first, step, (0, 1), half)
+            mine, other, first = edge_grads(place, scal, pieces, *edge_args, first, step, (0, 1), half, rows)
         else:
-            other, first = edge_grads(place, scal, pieces[1:], *edge_args, first, step, (1,), half)
+            other, first = edge_grads(place, scal, pieces[1:], *edge_args, first, step, (1,), half, rows)
         first, moved = lax.optimization_barrier((first, [arrays for _, _, arrays in chains]))
         chains = advance(chains, moved)
         fresh = wide_chain(mine, other, step) if step else last_chain(other)
         chains.append((step, fresh, next(fresh)))
-    mine, first = edge_grads(place, scal, second[:1], *edge_args, first, 0, (0,), half)
+    mine, first = edge_grads(place, scal, second[:1], *edge_args, first, 0, (0,), half, rows)
     first, moved = lax.optimization_barrier((first, [arrays for _, _, arrays in chains]))
     chains = advance(chains, moved)
-    fresh = first_chain(first)
-    chains.append(("first", fresh, next(fresh)))
     while chains:
         chains = advance(chains, lax.optimization_barrier([arrays for _, _, arrays in chains]))
     read = results["read"]
@@ -1156,12 +1154,10 @@
     row = jnp.arange(read.shape[0])[:, None]
     within = jnp.where(row < head_begin, row % (2 * H + 8), row - head_begin)
     times = jnp.where(within <= 2 * H, jnp.where((row < head_begin) & (within < H), 2.0, 1.0), 0.0)
-    small = results["narrow"]
+    grads, small, first, squares = results[0]
     tall = H + 16
     grad_gru = small[: 2 * tall, : 3 * width].reshape(2, tall, 3, width)[:, : H + 1]
     grad_bias = small[2 * tall :].reshape(1, width * H)
-    first = results["first"]
-    grads, squares = results[0]
     whole_sq = jnp.sum(read * read * times) + jnp.sum(first[: EIN + 1] * first[: EIN + 1])
 
     norm = jnp.sqrt(squares + whole_sq)

time: 356 us -> 345 us (0.969)
  starting transfers between devices: 67.9 us -> 48 us
  waiting for transfers between devices: 29 us -> 36.9 us
    ppermute x44 -> x32, starting transfers between devices: 67.9 us -> 48 us  [swap(): lax.ppermute(value, axis, [(index, index ^ step) for index in range(size)])]
    ppermute x44 -> x32, waiting for transfers between devices: 29 us -> 36.9 us  [swap(): lax.ppermute(value, axis, [(index, index ^ step) for index in range(size)])]
  transfers between devices with their start and end apart: 44 -> 32, of which waited for: 10 -> 9; matrix products, arithmetic and copies ran while one was open for 9% -> 7% of each run, Pallas kernels for 54% -> 56%
where the time goes in v5:
time: 345 us; the launch traced here: 344 us
  Pallas kernels  202 us (59%)
  starting transfers between devices  48 us (14%)
  waiting for transfers between devices  36.9 us (11%)
  local copies, waits for them, and re-layouts  27.2 us (8%)
  other arithmetic  18.5 us (5%)
  between operations  11 us (3%)
    pallas_call x1, Pallas kernels, forward(): pl.pallas_call(functools.partial(forward_kernel, gates=gates), out_shape=...  58.7 us
    pallas_call x1, Pallas kernels, backward(): pl.pallas_call(backward_kernel, out_shape=(jax.ShapeDtypeStruct((edges //...  54.8 us
    ppermute x32, starting transfers between devices, swap(): lax.ppermute(value, axis, [(index, index ^ step) for index in range(size)])  48 us
    pallas_call x5, Pallas kernels, edge_grads(): pl.pallas_call(functools.partial(final_kernel, pair=pair, sides=sides, ha...  47.9 us
    ppermute x32, waiting for transfers between devices, swap(): lax.ppermute(value, axis, [(index, index ^ step) for index in range(size)])  36.9 us
    pallas_call x1, Pallas kernels, readout(): pl.pallas_call(readout_kernel, out_shape=(jax.ShapeDtypeStruct((H, nodes)...  22.6 us
    pallas_call x1, Pallas kernels, adamw_step(): pl.pallas_call(adamw_kernel, grid=(columns // block,), in_specs=[pl.Block...  10.1 us
    pallas_call x1, Pallas kernels, prep(): pl.pallas_call(functools.partial(prep_kernel, edges=real, gates=gates, eb...  8 us
  transfers between devices with their start and end apart: 32, of which 9 were waited for; matrix products, arithmetic and copies ran while one was open for 7% of the time, Pallas kernels for 56%

profile of v5, /device:TPU:0, one launch (start us, length us, event | category | flops | bytes accessed | tf_op | source)
XLA Modules:
  0.0 343.8 jit_solution(10287099686135463590)
XLA Ops:
  0.7 1.8 fusion
  2.4 0.9 reduce-precision_convert_fusion.5
  4.8 0.9 dynamic-slice_bitcast_fusion
  5.8 3.0 collective-permute-start.3
  8.9 1.5 collective-permute-start.2
  12.8 1.9 concatenate.49
  16.6 1.3 pad.57.data
  19.2 0.9 pad.59.lstm
  21.6 8.0 %prep.1 = (s32[8]{0:T(128)}, f32[20,128,256]{2,1,0:T(8,128)}, bf16[144,5120]{1,0:T(8,128)(2,1)}, bf16[5120,128]{1,0:T(8,128)(2,1)}, bf16[20,32,256]{2,1,0:T(8,128)(2,1)}, /*index=5*/s32[8,5120]{1,0:T(8,128)}) custom-call(s32[2]{0:T(128)} %pad_add_fusion.place, s32[1,3200]{1,0:T(1,128)} %reshape.214.mol, s32[32,256]{1,0:T(8,128)} %pad.56.src2d, ...), custom_call_target="tpu_custom_call" | custom-call | tf_op jit(solution)/shard_map/prep/pallas_call | solution.py:177
  30.9 3.8 %collective-permute-start.7 = (f32[1,1]{1,0:T(1,128)}, f32[1,1]{1,0:T(1,128)}, u32[]{:S(2)}, u32[]{:S(2)}) collective-permute-start(f32[1,1]{1,0:T(1,128)} %add.214), channel_id=1, source_target_pairs={{0,4},{4,0},{8,12},{12,8},{1,5},{5,1},{9,13},{13,9},{2,6},{6,2},{1... | collective-permute-start | bytes 20 | tf_op jit(solution)/shard_map/ppermute | solution.py:823
  34.7 2.2 collective-permute-done.2.refs_4_.refs_0_
  36.9 0.9 slice_bitcast_fusion.1
  38.4 0.9 slice_bitcast_fusion.2
  39.6 1.2 reshape.234.gru_bias
  44.2 58.7 %forward.1 = (bf16[4,128,3200]{2,1,0:T(8,128)(2,1)}, bf16[3,128,3200]{2,1,0:T(8,128)(2,1)}, f32[4,128,3200]{2,1,0:T(8,128)}, bf16[20,3,128,256]{3,2,1,0:T(8,128)(2,1)}, bf16[40,4,4096,128]{3,2,1,0:T(8,128)(2,1)}) custom-call(s32[2]{0:T(128)} %pad_add_fusion.place, s32[8]{0:T(128)} %get-tuple-element.100.scal, bf16[16,3200]{1,0:T(8,128)(2,1)} %pad.63.nf_t, ...), custom_call_target="tpu_custom_call" | custom-call | flops 60000002048 | bytes 20000000 | tf_op jit(solution)/shard_map/forward/pallas_call | solution.py:416
  103.6 10.9 %collective-permute-start.8 = (f32[1,1]{1,0:T(1,128)}, f32[1,1]{1,0:T(1,128)}, u32[]{:S(2)}, u32[]{:S(2)}) collective-permute-start(f32[1,1]{1,0:T(1,128)} %add.217), channel_id=1, source_target_pairs={{0,8},{4,12},{8,0},{12,4},{1,9},{5,13},{9,1},{13,5},{2,10},{6,14},... | collective-permute-start | bytes 20 | tf_op jit(solution)/shard_map/ppermute | solution.py:823
  114.5 22.6 %readout.1 = (f32[128,3200]{1,0:T(8,128)}, f32[1328,128]{1,0:T(8,128)}) custom-call(s32[8]{0:T(128)} %get-tuple-element.100.scal, s32[1,3200]{1,0:T(1,128)} %reshape.214.mol, f32[392,512]{1,0:T(8,128)} %pad.59.lstm, f32[264,128]{1,0:T(8,128)} %pad.60.head, f32[128,128]{1,0:T(8,128)} %pad.61.present, f32[128,128]{1,0:T(8,128)} %pad.62.target, ...), custom_call_target="tpu_custom_call" | custom-call | flops 30000001024 | bytes 5000000 | tf_op jit(solution)/shard_map/readout/pallas_call | solution.py:581
  137.8 54.8 %backward.1 = (bf16[20,3,128,256]{3,2,1,0:T(8,128)(2,1)}, f32[4,320,128]{2,1,0:T(8,128)}) custom-call(s32[2]{0:T(128)} %pad_add_fusion.place, s32[8]{0:T(128)} %get-tuple-element.100.scal, f32[1]{0:T(128)} %bitcast.28.inverse, bf16[16,3200]{1,0:T(8,128)(2,1)} %pad.63.nf_t, bf16[2,384,128]{2,1,0:T(8,128)(2,1)} %bitcast.136, f32[2,384,1]{2,1,0:T(8,128)} %reshape.234.gru_bias, ...), custom_call_target="tpu_custom_call" | custom-call | flops 60000002048 | bytes 20000000 | tf_op jit(solution)/shard_map/backward/pallas_call | solution.py:695
  192.8 1.6 collective-permute-done.10
  195.2 10.9 %edge_grads.5 = (f32[2240,128]{1,0:T(8,128)}, f32[2240,128]{1,0:T(8,128)}, f32[32,128]{1,0:T(8,128)}) custom-call(s32[2]{0:T(128)} %pad_add_fusion.place, s32[8]{0:T(128)} %get-tuple-element.100.scal, f32[32,128]{1,0:T(8,128)} %broadcast_in_dim.50.first_in, f32[4,320,128]{2,1,0:T(8,128)} %get-tuple-element.120.narrow, ...), custom_call_target="tpu_custom_call" | custom-call | flops 8999999488 | bytes 5000000 | tf_op jit(solution)/shard_map/edge_grads/pallas_call | solution.py:796
  207.0 10.9 %edge_grads.6 = (f32[2240,128]{1,0:T(8,128)}, f32[2240,128]{1,0:T(8,128)}, f32[32,128]{1,0:T(8,128)}) custom-call(s32[2]{0:T(128)} %pad_add_fusion.place, s32[8]{0:T(128)} %get-tuple-element.100.scal, f32[32,128]{1,0:T(8,128)} %get-tuple-element.127.first_in, f32[4,320,128]{2,1,0:T(8,128)} %get-tuple-element.120.narrow, ...), custom_call_target="tpu_custom_call" | custom-call | flops 8999999488 | bytes 5000000 | tf_op jit(solution)/shard_map/edge_grads/pallas_call | solution.py:796
  218.2 3.0 collective-permute-start.15
  221.2 7.0 %collective-permute-start.14 = (f32[664,128]{1,0:T(8,128)S(1)}, f32[664,128]{1,0:T(8,128)S(1)}, u32[]{:S(2)}, u32[]{:S(2)}) collective-permute-start(f32[664,128]{1,0:T(8,128)S(1)} %add.222), channel_id=1, source_target_pairs={{0,4},{4,0},{8,12},{12,8},{1,5},{5,1},{9,13},{13,9},{2,6},{6,2},{1... | collective-permute-start | bytes 1019912 | tf_op jit(solution)/shard_map/ppermute | solution.py:823
  228.2 10.9 %edge_grads.7 = (f32[2240,128]{1,0:T(8,128)}, f32[2240,128]{1,0:T(8,128)}, f32[32,128]{1,0:T(8,128)}) custom-call(s32[2]{0:T(128)} %pad_add_fusion.place, s32[8]{0:T(128)} %get-tuple-element.100.scal, f32[32,128]{1,0:T(8,128)} %get-tuple-element.131.first_in, f32[4,320,128]{2,1,0:T(8,128)} %get-tuple-element.120.narrow, bf16[2352,128]{1,0:T(8,128)(2,1)} %copy-done.23, ...), custom_call_target="tpu_custom_call" | custom-call | flops 8999999488 | bytes 5000000 | tf_op jit(solution)/shard_map/edge_grads/pallas_call | solution.py:796
  239.2 2.3 add_convert_fusion.1
  242.2 7.7 %edge_grads.8 = (f32[2240,128]{1,0:T(8,128)}, f32[32,128]{1,0:T(8,128)}) custom-call(s32[2]{0:T(128)} %pad_add_fusion.place, s32[8]{0:T(128)} %get-tuple-element.100.scal, f32[32,128]{1,0:T(8,128)} %get-tuple-element.137.first_in, f32[4,320,128]{2,1,0:T(8,128)} %get-tuple-element.120.narrow, bf16[2048,128]{1,0:T(8,128)(2,1)} %get-tuple-element.232.refs_1_.refs_0_, ...), custom_call_target="tpu_custom_call" | custom-call | flops 8999999488 | bytes 5000000 | tf_op jit(solution)/shard_map/edge_grads/pallas_call | solution.py:796
  250.2 7.0 %collective-permute-done.18 = bf16[2240,128]{1,0:T(8,128)(2,1)} collective-permute-done((bf16[2240,128]{1,0:T(8,128)(2,1)}, bf16[2240,128]{1,0:T(8,128)(2,1)}, u32[]{:S(2)}, u32[]{:S(2)}) %collective-permute-start.18) | collective-permute-done | bytes 573472 | tf_op jit(solution)/shard_map/ppermute | solution.py:823
  257.2 0.9 add_convert_fusion
  258.1 1.4 collective-permute-start.20
  259.5 7.6 %edge_grads.9 = (f32[2240,128]{1,0:T(8,128)}, f32[32,128]{1,0:T(8,128)}) custom-call(s32[2]{0:T(128)} %pad_add_fusion.place, s32[8]{0:T(128)} %get-tuple-element.100.scal, f32[32,128]{1,0:T(8,128)} %get-tuple-element.143.first_in, f32[4,320,128]{2,1,0:T(8,128)} %get-tuple-element.120.narrow, bf16[2352,128]{1,0:T(8,128)(2,1)} %copy-done.8, ...), custom_call_target="tpu_custom_call" | custom-call | flops 8999999488 | bytes 5000000 | tf_op jit(solution)/shard_map/edge_grads/pallas_call | solution.py:796
  267.1 5.8 %collective-permute-done.20 = bf16[2240,128]{1,0:T(8,128)(2,1)S(1)} collective-permute-done((bf16[2240,128]{1,0:T(8,128)(2,1)}, bf16[2240,128]{1,0:T(8,128)(2,1)S(1)}, u32[]{:S(2)}, u32[]{:S(2)}) %collective-permute-start.20) | collective-permute-done | bytes 573472 | tf_op jit(solution)/shard_map/ppermute | solution.py:823
  272.9 2.7 abs_reduce_fusion
  278.3 2.7 collective-permute-start.22
  281.0 1.6 collective-permute-start.23
  282.6 1.4 collective-permute-start.24
  284.0 1.7 collective-permute-done.22
  285.7 9.0 %collective-permute-done.23 = f16[656,128]{1,0:T(8,128)(2,1)S(1)} collective-permute-done((f16[656,128]{1,0:T(8,128)(2,1)S(1)}, f16[656,128]{1,0:T(8,128)(2,1)S(1)}, u32[]{:S(2)}, u32[]{:S(2)}) %collective-permute-start.23) | collective-permute-done | bytes 167968 | tf_op jit(solution)/shard_map/ppermute | solution.py:823
  296.5 2.4 collective-permute-start.25
  298.9 1.6 collective-permute-start.26
  300.5 1.4 collective-permute-start.27
  303.5 8.5 %collective-permute-done.26 = f16[576,128]{1,0:T(8,128)(2,1)S(1)} collective-permute-done((f16[576,128]{1,0:T(8,128)(2,1)S(1)}, f16[576,128]{1,0:T(8,128)(2,1)S(1)}, u32[]{:S(2)}, u32[]{:S(2)}) %collective-permute-start.26) | collective-permute-done | bytes 147488 | tf_op jit(solution)/shard_map/ppermute | solution.py:823
  314.8 1.2 convert_multiply_fusion
  316.0 1.3 concatenate.62
  318.2 2.7 collective-permute-start.31
  323.7 1.1 reshape.232
  324.9 1.4 add_add_fusion
  330.6 1.9 multiply_subtract_fusion
  332.6 10.1 %adamw_step.1 = (f32[16,32]{1,0:T(8,128)}, f32[16,32]{1,0:T(8,128)}, f32[16,32]{1,0:T(8,128)}, f32[17,128]{1,0:T(8,128)}, f32[17,128]{1,0:T(8,128)}, /*index=5*/...) custom-call(f32[3]{0:T(128)} %pad_maximum_fusion.14.scale, ...), custom_call_target="tpu_custom_call" | custom-call | tf_op jit(solution)/shard_map/adamw_step/pallas_call | solution.py:937
  (216 shorter events, 26.9 us)
Async XLA Ops:
  5.7 5.4 %copy-start.20 = (s32[4992]{0:T(1024)S(1)}, s32[4992]{0:T(1024)}, u32[]{:S(2)}) copy-start(s32[4992]{0:T(1024)} %param.31) | copy-start | bytes 59908
  5.7 5.4 %copy-start.21 = (s32[4992]{0:T(1024)S(1)}, s32[4992]{0:T(1024)}, u32[]{:S(2)}) copy-start(s32[4992]{0:T(1024)} %param.29) | copy-start | bytes 59908
  5.7 5.4 %copy-start.18 = (f32[17,128]{1,0:T(8,128)S(1)}, f32[17,128]{1,0:T(8,128)}, u32[]{:S(2)}) copy-start(f32[17,128]{1,0:T(8,128)} %refs_3_.1) | copy-start | bytes 26116
  5.8 7.0 %copy-start.13 = (bf16[4992,12]{0,1:T(8,128)(2,1)S(1)}, bf16[4992,12]{0,1:T(8,128)(2,1)}, u32[]{:S(2)}) copy-start(bf16[4992,12]{0,1:T(8,128)(2,1)} %param.28) | copy-start | bytes 359428
  5.8 9.5 %copy-start.8 = (bf16[2352,128]{1,0:T(8,128)(2,1)}, bf16[2352,128]{1,0:T(8,128)(2,1)S(1)}, u32[]{:S(2)}) copy-start(bf16[2352,128]{1,0:T(8,128)(2,1)S(1)} %pad_maximum_fusion.1.refs_0_) | copy-start | bytes 1806340
  5.8 28.8 %collective-permute-start.3 = (bf16[2352,128]{1,0:T(8,128)(2,1)S(1)}, bf16[2352,128]{1,0:T(8,128)(2,1)S(1)}, u32[]{:S(2)}, u32[]{:S(2)}) collective-permute-start(bf16[2352,128]{1,0:T(8,128)(2,1)S(1)} %pad_maximum_fusion.1.refs_0_), channel_id=1, source_target_pairs={{0,1},{1,0},{2,3},{3,2},{4,5},{5,4},{6,7},{7,6},{8,9},{9,8},{10,11... | collective-permute-start | bytes 1806344 | tf_op jit(solution)/shard_map/ppermute | solution.py:823
  8.9 28.1 %collective-permute-start.2 = (bf16[2352,128]{1,0:T(8,128)(2,1)S(1)}, bf16[2352,128]{1,0:T(8,128)(2,1)}, u32[]{:S(2)}, u32[]{:S(2)}) collective-permute-start(bf16[2352,128]{1,0:T(8,128)(2,1)S(1)} %pad_maximum_fusion.1.refs_0_), channel_id=1, source_target_pairs={{0,2},{1,3},{2,0},{3,1},{4,6},{5,7},{6,4},{7,5},{8,10},{9,11},{10,... | collective-permute-start | bytes 1806344 | tf_op jit(solution)/shard_map/ppermute | solution.py:823
  10.4 27.4 %collective-permute-start.1 = (bf16[2352,128]{1,0:T(8,128)(2,1)S(1)}, bf16[2352,128]{1,0:T(8,128)(2,1)}, u32[]{:S(2)}, u32[]{:S(2)}) collective-permute-start(bf16[2352,128]{1,0:T(8,128)(2,1)S(1)} %pad_maximum_fusion.1.refs_0_), channel_id=1, source_target_pairs={{0,3},{1,2},{2,1},{3,0},{4,7},{5,6},{6,5},{7,4},{8,11},{9,10},{10,... | collective-permute-start | bytes 1806344 | tf_op jit(solution)/shard_map/ppermute | solution.py:823
  11.1 18.6 %collective-permute-start = (f32[1,1]{1,0:T(1,128)}, f32[1,1]{1,0:T(1,128)}, u32[]{:S(2)}, u32[]{:S(2)}) collective-permute-start(f32[1,1]{1,0:T(1,128)} %bitcast.7), channel_id=1, source_target_pairs={{0,16},{16,0},{1,17},{17,1},{2,18},{18,2},{3,19},{19,3},{4,20},{20... | collective-permute-start | bytes 20 | tf_op jit(solution)/shard_map/ppermute | solution.py:823
  30.9 72.0 %collective-permute-start.7 = (f32[1,1]{1,0:T(1,128)}, f32[1,1]{1,0:T(1,128)}, u32[]{:S(2)}, u32[]{:S(2)}) collective-permute-start(f32[1,1]{1,0:T(1,128)} %add.214), channel_id=1, source_target_pairs={{0,4},{4,0},{8,12},{12,8},{1,5},{5,1},{9,13},{13,9},{2,6},{6,2},{1... | collective-permute-start | bytes 20 | tf_op jit(solution)/shard_map/ppermute | solution.py:823
  34.7 6.1 %copy-start.23 = (bf16[2352,128]{1,0:T(8,128)(2,1)}, bf16[2352,128]{1,0:T(8,128)(2,1)S(1)}, u32[]{:S(2)}) copy-start(bf16[2352,128]{1,0:T(8,128)(2,1)S(1)} %collective-permute-done.3.refs_2_.refs_0_) | copy-start | bytes 1806340
  34.7 8.4 %collective-permute-start.4 = (bf16[2352,128]{1,0:T(8,128)(2,1)S(1)}, bf16[2352,128]{1,0:T(8,128)(2,1)S(1)}, u32[]{:S(2)}, u32[]{:S(2)}) collective-permute-start(bf16[2352,128]{1,0:T(8,128)(2,1)S(1)} %collective-permute-done.3.refs_2_.refs_0_), channel_id=1, source_target_pairs={{0,16},{16,0},{1,17},{17,1},{2,18},{18,2},{3,19},{19,3},{4,20},{20... | collective-permute-start | bytes 1806344 | tf_op jit(solution)/shard_map/ppermute | solution.py:823
  36.9 6.2 %collective-permute-start.5 = (bf16[2352,128]{1,0:T(8,128)(2,1)}, bf16[2352,128]{1,0:T(8,128)(2,1)}, u32[]{:S(2)}, u32[]{:S(2)}) collective-permute-start(bf16[2352,128]{1,0:T(8,128)(2,1)} %collective-permute-done.2.refs_4_.refs_0_), channel_id=1, source_target_pairs={{0,16},{16,0},{1,17},{17,1},{2,18},{18,2},{3,19},{19,3},{4,20},{20... | collective-permute-start | bytes 1806344 | tf_op jit(solution)/shard_map/ppermute | solution.py:823
  37.8 5.3 %collective-permute-start.6 = (bf16[2352,128]{1,0:T(8,128)(2,1)}, bf16[2352,128]{1,0:T(8,128)(2,1)S(1)}, u32[]{:S(2)}, u32[]{:S(2)}) collective-permute-start(bf16[2352,128]{1,0:T(8,128)(2,1)} %collective-permute-done.1.refs_6_.refs_0_), channel_id=1, source_target_pairs={{0,16},{16,0},{1,17},{17,1},{2,18},{18,2},{3,19},{19,3},{4,20},{20... | collective-permute-start | bytes 1806344 | tf_op jit(solution)/shard_map/ppermute | solution.py:823
  103.6 33.5 %collective-permute-start.8 = (f32[1,1]{1,0:T(1,128)}, f32[1,1]{1,0:T(1,128)}, u32[]{:S(2)}, u32[]{:S(2)}) collective-permute-start(f32[1,1]{1,0:T(1,128)} %add.217), channel_id=1, source_target_pairs={{0,8},{4,12},{8,0},{12,4},{1,9},{5,13},{9,1},{13,5},{2,10},{6,14},... | collective-permute-start | bytes 20 | tf_op jit(solution)/shard_map/ppermute | solution.py:823
  137.1 55.6 %collective-permute-start.9 = (f32[1328,128]{1,0:T(8,128)}, f32[1328,128]{1,0:T(8,128)S(1)}, u32[]{:S(2)}, u32[]{:S(2)}) collective-permute-start(f32[1328,128]{1,0:T(8,128)} %get-tuple-element.106), channel_id=1, source_target_pairs={{0,8},{4,12},{8,0},{12,4},{1,9},{5,13},{9,1},{13,5},{2,10},{6,14},... | collective-permute-start | bytes 2039816 | tf_op jit(solution)/shard_map/ppermute | solution.py:823
  137.8 54.9 %copy-start.7 = (f32[1328,128]{1,0:T(8,128)S(1)}, f32[1328,128]{1,0:T(8,128)}, u32[]{:S(2)}) copy-start(f32[1328,128]{1,0:T(8,128)} %get-tuple-element.106) | copy-start | bytes 2039812
  192.8 1.7 collective-permute-start.10
  194.5 11.8 %collective-permute-start.11 = (f32[664,128]{1,0:T(8,128)S(1)}, f32[664,128]{1,0:T(8,128)S(1)}, u32[]{:S(2)}, u32[]{:S(2)}) collective-permute-start(f32[664,128]{1,0:T(8,128)S(1)} %bitcast_add_fusion), channel_id=1, source_target_pairs={{0,1},{1,0},{2,3},{3,2},{4,5},{5,4},{6,7},{7,6},{8,9},{9,8},{10,11... | collective-permute-start | bytes 1019912 | tf_op jit(solution)/shard_map/ppermute | solution.py:823
  206.1 11.9 %collective-permute-start.13 = (f32[2240,128]{1,0:T(8,128)}, f32[2240,128]{1,0:T(8,128)S(1)}, u32[]{:S(2)}, u32[]{:S(2)}) collective-permute-start(f32[2240,128]{1,0:T(8,128)} %get-tuple-element.129), channel_id=1, source_target_pairs={{0,16},{16,0},{1,17},{17,1},{2,18},{18,2},{3,19},{19,3},{4,20},{20... | collective-permute-start | bytes 3440648 | tf_op jit(solution)/shard_map/ppermute | solution.py:823
  206.3 11.7 %copy-start.4 = (f32[2240,128]{1,0:T(8,128)S(1)}, f32[2240,128]{1,0:T(8,128)}, u32[]{:S(2)}) copy-start(f32[2240,128]{1,0:T(8,128)} %get-tuple-element.133) | copy-start | bytes 3440644
  206.4 11.7 %collective-permute-start.12 = (f32[664,128]{1,0:T(8,128)S(1)}, f32[664,128]{1,0:T(8,128)S(1)}, u32[]{:S(2)}, u32[]{:S(2)}) collective-permute-start(f32[664,128]{1,0:T(8,128)S(1)} %add.221), channel_id=1, source_target_pairs={{0,2},{1,3},{2,0},{3,1},{4,6},{5,7},{6,4},{7,5},{8,10},{9,11},{10,... | collective-permute-start | bytes 1019912 | tf_op jit(solution)/shard_map/ppermute | solution.py:823
  217.9 21.3 %collective-permute-start.16 = (f32[2240,128]{1,0:T(8,128)}, f32[2240,128]{1,0:T(8,128)}, u32[]{:S(2)}, u32[]{:S(2)}) collective-permute-start(f32[2240,128]{1,0:T(8,128)} %get-tuple-element.135), channel_id=1, source_target_pairs={{0,16},{16,0},{1,17},{17,1},{2,18},{18,2},{3,19},{19,3},{4,20},{20... | collective-permute-start | bytes 3440648 | tf_op jit(solution)/shard_map/ppermute | solution.py:823
  218.2 21.0 %collective-permute-start.15 = (bf16[2240,128]{1,0:T(8,128)(2,1)S(1)}, bf16[2240,128]{1,0:T(8,128)(2,1)S(1)}, u32[]{:S(2)}, u32[]{:S(2)}) collective-permute-start(bf16[2240,128]{1,0:T(8,128)(2,1)S(1)} %add_convert_fusion.2), channel_id=1, source_target_pairs={{0,3},{1,2},{2,1},{3,0},{4,7},{5,6},{6,5},{7,4},{8,11},{9,10},{10,... | collective-permute-start | bytes 1720328 | tf_op jit(solution)/shard_map/ppermute | solution.py:823
  221.2 18.0 %copy-start.6 = (f32[2240,128]{1,0:T(8,128)S(1)}, f32[2240,128]{1,0:T(8,128)}, u32[]{:S(2)}) copy-start(f32[2240,128]{1,0:T(8,128)} %get-tuple-element.139) | copy-start | bytes 3440644
  221.2 18.0 %collective-permute-start.14 = (f32[664,128]{1,0:T(8,128)S(1)}, f32[664,128]{1,0:T(8,128)S(1)}, u32[]{:S(2)}, u32[]{:S(2)}) collective-permute-start(f32[664,128]{1,0:T(8,128)S(1)} %add.222), channel_id=1, source_target_pairs={{0,4},{4,0},{8,12},{12,8},{1,5},{5,1},{9,13},{13,9},{2,6},{6,2},{1... | collective-permute-start | bytes 1019912 | tf_op jit(solution)/shard_map/ppermute | solution.py:823
  239.1 18.1 %collective-permute-start.19 = (f32[2240,128]{1,0:T(8,128)}, f32[2240,128]{1,0:T(8,128)S(1)}, u32[]{:S(2)}, u32[]{:S(2)}) collective-permute-start(f32[2240,128]{1,0:T(8,128)} %get-tuple-element.141), channel_id=1, source_target_pairs={{0,16},{16,0},{1,17},{17,1},{2,18},{18,2},{3,19},{19,3},{4,20},{20... | collective-permute-start | bytes 3440648 | tf_op jit(solution)/shard_map/ppermute | solution.py:823
  241.5 15.7 %collective-permute-start.18 = (bf16[2240,128]{1,0:T(8,128)(2,1)}, bf16[2240,128]{1,0:T(8,128)(2,1)}, u32[]{:S(2)}, u32[]{:S(2)}) collective-permute-start(bf16[2240,128]{1,0:T(8,128)(2,1)} %add_convert_fusion.1), channel_id=1, source_target_pairs={{0,2},{1,3},{2,0},{3,1},{4,6},{5,7},{6,4},{7,5},{8,10},{9,11},{10,... | collective-permute-start | bytes 1720328 | tf_op jit(solution)/shard_map/ppermute | solution.py:823
  241.9 15.3 %copy-start.5 = (f32[2240,128]{1,0:T(8,128)S(1)}, f32[2240,128]{1,0:T(8,128)}, u32[]{:S(2)}) copy-start(f32[2240,128]{1,0:T(8,128)} %get-tuple-element.145) | copy-start | bytes 3440644
  241.9 8.3 %collective-permute-start.17 = (f32[664,128]{1,0:T(8,128)S(1)}, f32[664,128]{1,0:T(8,128)S(1)}, u32[]{:S(2)}, u32[]{:S(2)}) collective-permute-start(f32[664,128]{1,0:T(8,128)S(1)} %add.224), channel_id=1, source_target_pairs={{0,16},{16,0},{1,17},{17,1},{2,18},{18,2},{3,19},{19,3},{4,20},{20... | collective-permute-start | bytes 1019912 | tf_op jit(solution)/shard_map/ppermute | solution.py:823
  249.9 23.0 %collective-permute-start.21 = (f32[2240,128]{1,0:T(8,128)}, f32[2240,128]{1,0:T(8,128)}, u32[]{:S(2)}, u32[]{:S(2)}) collective-permute-start(f32[2240,128]{1,0:T(8,128)} %get-tuple-element.147), channel_id=1, source_target_pairs={{0,16},{16,0},{1,17},{17,1},{2,18},{18,2},{3,19},{19,3},{4,20},{20... | collective-permute-start | bytes 3440648 | tf_op jit(solution)/shard_map/ppermute | solution.py:823
  250.2 7.9 %copy-start.11 = (f32[664,128]{1,0:T(8,128)}, f32[664,128]{1,0:T(8,128)S(1)}, u32[]{:S(2)}) copy-start(f32[664,128]{1,0:T(8,128)S(1)} %collective-permute-done.17) | copy-start | bytes 1019908
  258.1 14.8 %collective-permute-start.20 = (bf16[2240,128]{1,0:T(8,128)(2,1)}, bf16[2240,128]{1,0:T(8,128)(2,1)S(1)}, u32[]{:S(2)}, u32[]{:S(2)}) collective-permute-start(bf16[2240,128]{1,0:T(8,128)(2,1)} %add_convert_fusion), channel_id=1, source_target_pairs={{0,1},{1,0},{2,3},{3,2},{4,5},{5,4},{6,7},{7,6},{8,9},{9,8},{10,11... | collective-permute-start | bytes 1720328 | tf_op jit(solution)/shard_map/ppermute | solution.py:823
  278.3 7.4 %collective-permute-start.22 = (f16[656,128]{1,0:T(8,128)(2,1)S(1)}, f16[656,128]{1,0:T(8,128)(2,1)S(1)}, u32[]{:S(2)}, u32[]{:S(2)}) collective-permute-start(f16[656,128]{1,0:T(8,128)(2,1)S(1)} %get-tuple-element.241), channel_id=1, source_target_pairs={{0,4},{4,0},{8,12},{12,8},{1,5},{5,1},{9,13},{13,9},{2,6},{6,2},{1... | collective-permute-start | bytes 503816 | tf_op jit(solution)/shard_map/ppermute | solution.py:823
  281.0 13.7 %collective-permute-start.23 = (f16[656,128]{1,0:T(8,128)(2,1)S(1)}, f16[656,128]{1,0:T(8,128)(2,1)S(1)}, u32[]{:S(2)}, u32[]{:S(2)}) collective-permute-start(f16[656,128]{1,0:T(8,128)(2,1)S(1)} %get-tuple-element.240), channel_id=1, source_target_pairs={{0,8},{4,12},{8,0},{12,4},{1,9},{5,13},{9,1},{13,5},{2,10},{6,14},... | collective-permute-start | bytes 503816 | tf_op jit(solution)/shard_map/ppermute | solution.py:823
  282.6 12.1 %collective-permute-start.24 = (f16[656,128]{1,0:T(8,128)(2,1)S(1)}, f16[656,128]{1,0:T(8,128)(2,1)S(1)}, u32[]{:S(2)}, u32[]{:S(2)}) collective-permute-start(f16[656,128]{1,0:T(8,128)(2,1)S(1)} %get-tuple-element.239), channel_id=1, source_target_pairs={{0,12},{4,8},{8,4},{12,0},{1,13},{5,9},{9,5},{13,1},{2,14},{6,10},... | collective-permute-start | bytes 503816 | tf_op jit(solution)/shard_map/ppermute | solution.py:823
  296.5 7.1 %collective-permute-start.25 = (f16[576,128]{1,0:T(8,128)(2,1)S(1)}, f16[576,128]{1,0:T(8,128)(2,1)S(1)}, u32[]{:S(2)}, u32[]{:S(2)}) collective-permute-start(f16[576,128]{1,0:T(8,128)(2,1)S(1)} %get-tuple-element.237), channel_id=1, source_target_pairs={{0,4},{4,0},{8,12},{12,8},{1,5},{5,1},{9,13},{13,9},{2,6},{6,2},{1... | collective-permute-start | bytes 442376 | tf_op jit(solution)/shard_map/ppermute | solution.py:823
  298.9 13.1 %collective-permute-start.26 = (f16[576,128]{1,0:T(8,128)(2,1)S(1)}, f16[576,128]{1,0:T(8,128)(2,1)S(1)}, u32[]{:S(2)}, u32[]{:S(2)}) collective-permute-start(f16[576,128]{1,0:T(8,128)(2,1)S(1)} %get-tuple-element.237), channel_id=1, source_target_pairs={{0,8},{4,12},{8,0},{12,4},{1,9},{5,13},{9,1},{13,5},{2,10},{6,14},... | collective-permute-start | bytes 442376 | tf_op jit(solution)/shard_map/ppermute | solution.py:823
  300.5 11.5 %collective-permute-start.27 = (f16[576,128]{1,0:T(8,128)(2,1)S(1)}, f16[576,128]{1,0:T(8,128)(2,1)S(1)}, u32[]{:S(2)}, u32[]{:S(2)}) collective-permute-start(f16[576,128]{1,0:T(8,128)(2,1)S(1)} %get-tuple-element.237), channel_id=1, source_target_pairs={{0,12},{4,8},{8,4},{12,0},{1,13},{5,9},{9,5},{13,1},{2,14},{6,10},... | collective-permute-start | bytes 442376 | tf_op jit(solution)/shard_map/ppermute | solution.py:823
  312.5 2.1 collective-permute-start.28
  314.8 6.1 %copy-start.12 = (f32[664,128]{1,0:T(8,128)S(1)}, f32[664,128]{1,0:T(8,128)}, u32[]{:S(2)}) copy-start(f32[664,128]{1,0:T(8,128)} %copy-done.11) | copy-start | bytes 1019908
  316.0 7.7 %copy-start = (f32[8,560,128]{2,1,0:T(8,128)}, f32[8,560,128]{2,1,0:T(8,128)S(1)}, u32[]{:S(2)}) copy-start(f32[8,560,128]{2,1,0:T(8,128)S(1)} %get-tuple-element.230) | copy-start | bytes 6881284
  317.3 7.5 %collective-permute-start.29 = (f32[40,128]{1,0:T(8,128)}, f32[40,128]{1,0:T(8,128)}, u32[]{:S(2)}, u32[]{:S(2)}) collective-permute-start(f32[40,128]{1,0:T(8,128)} %concatenate.62), channel_id=1, source_target_pairs={{0,1},{1,0},{2,3},{3,2},{4,5},{5,4},{6,7},{7,6},{8,9},{9,8},{10,11... | collective-permute-start | bytes 61448 | tf_op jit(solution)/shard_map/ppermute | solution.py:823
  318.1 6.7 %collective-permute-start.30 = (f32[40,128]{1,0:T(8,128)}, f32[40,128]{1,0:T(8,128)}, u32[]{:S(2)}, u32[]{:S(2)}) collective-permute-start(f32[40,128]{1,0:T(8,128)} %concatenate.62), channel_id=1, source_target_pairs={{0,2},{1,3},{2,0},{3,1},{4,6},{5,7},{6,4},{7,5},{8,10},{9,11},{10,... | collective-permute-start | bytes 61448 | tf_op jit(solution)/shard_map/ppermute | solution.py:823
  318.2 6.7 %collective-permute-start.31 = (f32[40,128]{1,0:T(8,128)}, f32[40,128]{1,0:T(8,128)}, u32[]{:S(2)}, u32[]{:S(2)}) collective-permute-start(f32[40,128]{1,0:T(8,128)} %concatenate.62), channel_id=1, source_target_pairs={{0,3},{1,2},{2,1},{3,0},{4,7},{5,6},{6,5},{7,4},{8,11},{9,10},{10,... | collective-permute-start | bytes 61448 | tf_op jit(solution)/shard_map/ppermute | solution.py:823
  320.8 9.8 %copy-start.10 = (f32[2,129,3,32]{1,3,2,0:T(8,128)S(1)}, f32[2,129,3,32]{1,3,2,0:T(8,128)}, u32[]{:S(2)}) copy-start(f32[2,129,3,32]{1,3,2,0:T(8,128)} %param.38) | copy-start | bytes 297220
  321.7 10.9 %copy-start.2 = (f32[1328,128]{1,0:T(8,128)}, f32[1328,128]{1,0:T(8,128)S(1)}, u32[]{:S(2)}) copy-start(f32[1328,128]{1,0:T(8,128)S(1)} %get-tuple-element.222.read) | copy-start | bytes 2039812
  322.3 10.3 %copy-start.3 = (f32[2,160,128]{2,1,0:T(8,128)}, f32[2,160,128]{2,1,0:T(8,128)S(1)}, u32[]{:S(2)}) copy-start(f32[2,160,128]{2,1,0:T(8,128)S(1)} %slice.250) | copy-start | bytes 491524
  (13 other events, 32.6 us)

commit v6 on v5

--- a/solution.py
+++ b/solution.py
@@ -20,6 +20,7 @@
 WIN = 768
 SLOTS = 14
 AHEAD = 6
+MOLS = 64
 DEEP = H + 16
 
 CLIP = 0.01
@@ -445,73 +446,10 @@
     final = hid.at[STEPS]
     tall = 2 * H + 8
     d_head = read.at[pl.ds(4 * tall, 2 * H + 16)]
-    mols = lax.broadcasted_iota(jnp.int32, (H, 1), 0)
-    owned = jnp.where((mols >= scal[2]) & (mols < scal[3]), 1.0, 0.0)
     by_query = lstm[0:H, :] + lstm[2 * H : 3 * H, :]
     by_summary = lstm[H : 2 * H, :]
     lstm_bias = lstm[3 * H : 3 * H + 1, :]
-    zero = jnp.zeros((H, H), F32)
-
-    def lstm_round(rounds, carry):
-        query, summary, cell = carry
-        gates = lstm_bias + wide(dot, query, by_query) + wide(dot, summary, by_summary)
-        enter = sigmoid(gates[:, 0:H])
-        forget = sigmoid(gates[:, H : 2 * H])
-        fresh = jnp.tanh(gates[:, 2 * H : 3 * H])
-        leave = sigmoid(gates[:, 3 * H : 4 * H])
-        old_cell, old_query, old_summary = cell, query, summary
-        cell = forget * cell + enter * fresh
-        bent = jnp.tanh(cell)
-        query = leave * bent
-        stack = jnp.concatenate(split3(query), axis=0)
-
-        def scores(window, peak):
-            nodes = pl.ds(start_of(scal, window), WIN)
-            three = dot(stack, final[:, nodes])
-            value = three[0:H] + (three[H : 2 * H] + three[2 * H : 3 * H])
-            value = jnp.where(mol[:, nodes] == mols, value, -1e30)
-            score[:, nodes] = value
-            return jnp.maximum(peak, jnp.max(value, axis=1, keepdims=True))
-
-        peak = lax.fori_loop(0, windows, scores, jnp.full((H, 1), -1e30, F32))
-
-        def powers(window, sums):
-            nodes = pl.ds(start_of(scal, window), WIN)
-            value = jnp.where(mol[:, nodes] == mols, jnp.exp(score[:, nodes] - peak), 0.0)
-            score[:, nodes] = value
-            return sums + jnp.sum(value, axis=1, keepdims=True)
-
-        sums = lax.fori_loop(0, windows, powers, jnp.zeros((H, 1), F32))
-        sums = jnp.where(sums > 0.0, sums, 1.0)
-
-        def gather(window, acc):
-            nodes = pl.ds(start_of(scal, window), WIN)
-            value = score[:, nodes] / sums
-            weight[rounds, :, nodes] = value
-            three = dot_nt(jnp.concatenate(split3(value), axis=0), final[:, nodes])
-            return acc + (three[0:H] + (three[H : 2 * H] + three[2 * H : 3 * H]))
-
-        summary = lax.fori_loop(0, windows, gather, zero)
-        for number, value in enumerate((enter, forget, fresh, leave, bent, old_cell, query)):
-            kept[rounds, number] = value
-        columns = pl.ds(pl.multiple_of(rounds * H, H), H)
-        before[0, :, columns] = old_query.T
-        before[1, :, columns] = old_summary.T
-        return query, summary, cell
-
-    query, summary, cell = lax.fori_loop(0, SET_STEPS, lstm_round, (zero, zero, zero))
-    head_query = head[0:H, :]
-    head_summary = head[H : 2 * H, :]
-    guess = wide(dot, query, head_query) + wide(dot, summary, head_summary) + head[2 * H : 2 * H + 1, :]
-    gap = guess - target[...]
-    seen = present[...] * owned
-    d_head[2 * H + 8 : 2 * H + 16, :] = jnp.broadcast_to(jnp.sum(seen * gap * gap), (8, H))
-    d_guess = 2.0 * seen * gap
-    d_head[0:H, :] = wide(dot, query.T, d_guess)
-    d_head[H : 2 * H, :] = wide(dot, summary.T, d_guess)
-    d_head[2 * H : 2 * H + 8, :] = jnp.broadcast_to(jnp.sum(d_guess, axis=0, keepdims=True), (8, H))
-    d_query = wide(dot_nt, d_guess, head_query)
-    d_summary = wide(dot_nt, d_guess, head_summary)
+    read[...] = jnp.zeros(read.shape, F32)
 
     def clear(window, carry):
         nodes = pl.ds(start_of(scal, window), WIN)
@@ -519,61 +457,131 @@
         return carry
 
     lax.fori_loop(0, windows, clear, 0)
-
-    def back_round(number, carry):
-        d_query, d_summary, d_cell, d_bias = carry
-        rounds = SET_STEPS - 1 - number
-        enter, forget, fresh, leave, bent, old_cell, query = [kept[rounds, item] for item in range(7)]
-        stack = jnp.concatenate(split3(d_summary), axis=0)
-
-        def products(window, acc):
-            nodes = pl.ds(start_of(scal, window), WIN)
-            three = dot(stack, final[:, nodes])
-            value = three[0:H] + (three[H : 2 * H] + three[2 * H : 3 * H])
-            score[:, nodes] = value
-            return acc + jnp.sum(value * weight[rounds, :, nodes], axis=1, keepdims=True)
-
-        mean = lax.fori_loop(0, windows, products, jnp.zeros((H, 1), F32))
-        query_t = query.T
-        d_summary_t = d_summary.T
-
-        def spread(window, acc):
-            nodes = pl.ds(start_of(scal, window), WIN)
-            share = weight[rounds, :, nodes]
-            d_score = share * (score[:, nodes] - mean)
-            d_final[:, nodes] += wide(dot, query_t, d_score) + wide(dot, d_summary_t, share)
-            three = dot_nt(jnp.concatenate(split3(d_score), axis=0), final[:, nodes])
-            return acc + (three[0:H] + (three[H : 2 * H] + three[2 * H : 3 * H]))
-
-        d_query = lax.fori_loop(0, windows, spread, d_query)
-        d_leave = d_query * bent
-        d_cell = d_cell + d_query * leave * (1.0 - bent * bent)
-        d_gates = jnp.concatenate(
-            [
-                d_cell * fresh * enter * (1.0 - enter),
-                d_cell * old_cell * forget * (1.0 - forget),
-                d_cell * enter * (1.0 - fresh * fresh),
-                d_leave * leave * (1.0 - leave),
-            ],
-            axis=1,
-        )
-        d_cell = d_cell * forget
-        d_bias = d_bias + jnp.sum(d_gates, axis=0, keepdims=True)
-        slope[rounds] = d_gates
-        d_query = wide(dot_nt, d_gates, by_query)
-        d_summary = wide(dot_nt, d_gates, by_summary)
-        return d_query, d_summary, d_cell, d_bias
-
-    start = (d_query, d_summary, zero, jnp.zeros((1, 4 * H), F32))
-    d_bias = lax.fori_loop(0, SET_STEPS, back_round, start)[3]
-    slopes = slope[...].reshape(SET_STEPS * H, 4 * H)
-    d_by_query = wide(dot, before[0], slopes)
-    d_by_summary = wide(dot, before[1], slopes)
-    for part in range(4):
-        columns = slice(part * H, (part + 1) * H)
-        read[part * tall : part * tall + H, :] = d_by_query[:, columns]
-        read[part * tall + H : part * tall + 2 * H, :] = d_by_summary[:, columns]
-        read[part * tall + 2 * H : (part + 1) * tall, :] = jnp.broadcast_to(d_bias[:, columns], (8, H))
+    base = lax.div(scal[2], 8) * 8
+
+    def readout_rows(begin):
+        mols = lax.broadcasted_iota(jnp.int32, (MOLS, 1), 0) + begin
+        owned = jnp.where((mols >= scal[2]) & (mols < scal[3]), 1.0, 0.0)
+        zero = jnp.zeros((MOLS, H), F32)
+
+        def lstm_round(rounds, carry):
+            query, summary, cell = carry
+            gates = lstm_bias + wide(dot, query, by_query) + wide(dot, summary, by_summary)
+            enter = sigmoid(gates[:, 0:H])
+            forget = sigmoid(gates[:, H : 2 * H])
+            fresh = jnp.tanh(gates[:, 2 * H : 3 * H])
+            leave = sigmoid(gates[:, 3 * H : 4 * H])
+            old_cell, old_query, old_summary = cell, query, summary
+            cell = forget * cell + enter * fresh
+            bent = jnp.tanh(cell)
+            query = leave * bent
+            stack = jnp.concatenate(split3(query), axis=0)
+
+            def scores(window, peak):
+                nodes = pl.ds(start_of(scal, window), WIN)
+                three = dot(stack, final[:, nodes])
+                value = three[0:MOLS] + (three[MOLS : 2 * MOLS] + three[2 * MOLS : 3 * MOLS])
+                value = jnp.where(mol[:, nodes] == mols, value, -1e30)
+                score[:, nodes] = value
+                return jnp.maximum(peak, jnp.max(value, axis=1, keepdims=True))
+
+            peak = lax.fori_loop(0, windows, scores, jnp.full((MOLS, 1), -1e30, F32))
+
+            def powers(window, sums):
+                nodes = pl.ds(start_of(scal, window), WIN)
+                value = jnp.where(mol[:, nodes] == mols, jnp.exp(score[:, nodes] - peak), 0.0)
+                score[:, nodes] = value
+                return sums + jnp.sum(value, axis=1, keepdims=True)
+
+            sums = lax.fori_loop(0, windows, powers, jnp.zeros((MOLS, 1), F32))
+            sums = jnp.where(sums > 0.0, sums, 1.0)
+
+            def gather(window, acc):
+                nodes = pl.ds(start_of(scal, window), WIN)
+                value = score[:, nodes] / sums
+                weight[rounds, :, nodes] = value
+                three = dot_nt(jnp.concatenate(split3(value), axis=0), final[:, nodes])
+                return acc + (three[0:MOLS] + (three[MOLS : 2 * MOLS] + three[2 * MOLS : 3 * MOLS]))
+
+            summary = lax.fori_loop(0, windows, gather, zero)
+            for number, value in enumerate((enter, forget, fresh, leave, bent, old_cell, query)):
+                kept[rounds, number] = value
+            before[0, rounds] = old_query
+            before[1, rounds] = old_summary
+            return query, summary, cell
+
+        query, summary, cell = lax.fori_loop(0, SET_STEPS, lstm_round, (zero, zero, zero))
+        head_query = head[0:H, :]
+        head_summary = head[H : 2 * H, :]
+        guess = wide(dot, query, head_query) + wide(dot, summary, head_summary) + head[2 * H : 2 * H + 1, :]
+        gap = guess - target[pl.ds(begin, MOLS), :]
+        seen = present[pl.ds(begin, MOLS), :] * owned
+        d_head[2 * H + 8 : 2 * H + 16, :] += jnp.broadcast_to(jnp.sum(seen * gap * gap), (8, H))
+        d_guess = 2.0 * seen * gap
+        d_head[0:H, :] += wide(dot_tn, query, d_guess)
+        d_head[H : 2 * H, :] += wide(dot_tn, summary, d_guess)
+        d_head[2 * H : 2 * H + 8, :] += jnp.broadcast_to(jnp.sum(d_guess, axis=0, keepdims=True), (8, H))
+        d_query = wide(dot_nt, d_guess, head_query)
+        d_summary = wide(dot_nt, d_guess, head_summary)
+
+        def back_round(number, carry):
+            d_query, d_summary, d_cell, d_bias = carry
+            rounds = SET_STEPS - 1 - number
+            enter, forget, fresh, leave, bent, old_cell, query = [kept[rounds, item] for item in range(7)]
+            stack = jnp.concatenate(split3(d_summary), axis=0)
+
+            def products(window, acc):
+                nodes = pl.ds(start_of(scal, window), WIN)
+                three = dot(stack, final[:, nodes])
+                value = three[0:MOLS] + (three[MOLS : 2 * MOLS] + three[2 * MOLS : 3 * MOLS])
+                score[:, nodes] = value
+                return acc + jnp.sum(value * weight[rounds, :, nodes], axis=1, keepdims=True)
+
+            mean = lax.fori_loop(0, windows, products, jnp.zeros((MOLS, 1), F32))
+
+            def spread(window, acc):
+                nodes = pl.ds(start_of(scal, window), WIN)
+                share = weight[rounds, :, nodes]
+                d_score = share * (score[:, nodes] - mean)
+                d_final[:, nodes] += wide(dot_tn, query, d_score) + wide(dot_tn, d_summary, share)
+                three = dot_nt(jnp.concatenate(split3(d_score), axis=0), final[:, nodes])
+                return acc + (three[0:MOLS] + (three[MOLS : 2 * MOLS] + three[2 * MOLS : 3 * MOLS]))
+
+            d_query = lax.fori_loop(0, windows, spread, d_query)
+            d_leave = d_query * bent
+            d_cell = d_cell + d_query * leave * (1.0 - bent * bent)
+            d_gates = jnp.concatenate(
+                [
+                    d_cell * fresh * enter * (1.0 - enter),
+                    d_cell * old_cell * forget * (1.0 - forget),
+                    d_cell * enter * (1.0 - fresh * fresh),
+                    d_leave * leave * (1.0 - leave),
+                ],
+                axis=1,
+            )
+            d_cell = d_cell * forget
+            d_bias = d_bias + jnp.sum(d_gates, axis=0, keepdims=True)
+            slope[rounds] = d_gates
+            d_query = wide(dot_nt, d_gates, by_query)
+            d_summary = wide(dot_nt, d_gates, by_summary)
+            return d_query, d_summary, d_cell, d_bias
+
+        start = (d_query, d_summary, zero, jnp.zeros((1, 4 * H), F32))
+        d_bias = lax.fori_loop(0, SET_STEPS, back_round, start)[3]
+        slopes = slope[...].reshape(SET_STEPS * MOLS, 4 * H)
+        d_by_query = wide(dot_tn, before[0].reshape(SET_STEPS * MOLS, H), slopes)
+        d_by_summary = wide(dot_tn, before[1].reshape(SET_STEPS * MOLS, H), slopes)
+        for part in range(4):
+            columns = slice(part * H, (part + 1) * H)
+            read[part * tall : part * tall + H, :] += d_by_query[:, columns]
+            read[part * tall + H : part * tall + 2 * H, :] += d_by_summary[:, columns]
+            read[part * tall + 2 * H : (part + 1) * tall, :] += jnp.broadcast_to(d_bias[:, columns], (8, H))
+
+    def some_molecules(turn, carry):
+        readout_rows(pl.multiple_of(base + turn * MOLS, 8))
+        return carry
+
+    lax.fori_loop(0, lax.div(scal[3] - base + (MOLS - 1), MOLS), some_molecules, 0)
 
 
 def readout(scal, hid, mol, lstm, head, present, target):
@@ -587,11 +595,11 @@
         in_specs=[pl.BlockSpec(memory_space=pltpu.SMEM)] + [pl.BlockSpec(memory_space=pltpu.VMEM)] * 6,
         out_specs=[pl.BlockSpec(memory_space=pltpu.VMEM)] * 2,
         scratch_shapes=[
-            pltpu.VMEM((H, nodes), F32),
-            pltpu.VMEM((SET_STEPS, H, nodes), F32),
-            pltpu.VMEM((SET_STEPS, H, 4 * H), F32),
-            pltpu.VMEM((2, H, SET_STEPS * H), F32),
-            pltpu.VMEM((SET_STEPS, 7, H, H), F32),
+            pltpu.VMEM((MOLS, nodes), F32),
+            pltpu.VMEM((SET_STEPS, MOLS, nodes), F32),
+            pltpu.VMEM((SET_STEPS, MOLS, 4 * H), F32),
+            pltpu.VMEM((2, SET_STEPS, MOLS, H), F32),
+            pltpu.VMEM((SET_STEPS, 7, MOLS, H), F32),
         ],
         compiler_params=pltpu.CompilerParams(vmem_limit_bytes=VMEM_LIMIT),
         cost_estimate=pl.CostEstimate(flops=30_000_000_000, transcendentals=0, bytes_accessed=5_000_000),
@@ -887,7 +895,7 @@
     weight_out[index] = old - rate * (step + DECAY * old)
 
 
-def adamw_kernel(scale, wide, bias, read, small, first, *refs):
+def adamw_kernel(scale, wide, bias, lines, read, small, first, *refs):
     ins, outs = refs[:15], refs[15:]
     embed, edge_first, second, lstm, head = [
         ins[3 * item : 3 * item + 3] + outs[3 * item : 3 * item + 3] for item in range(5)
@@ -895,6 +903,14 @@
     every = slice(None)
     update_rows(scale, second, (slice(0, H), every), wide[0].T, RATES[2])
     update_rows(scale, second, (slice(H, H + 1), every), bias[...], RATES[2])
+    by_query = lines[0:H, :]
+    for begin, value in (
+        (0, by_query),
+        (H, lines[H : 2 * H, :]),
+        (2 * H, by_query),
+        (3 * H, lines[2 * H : 2 * H + 1, :]),
+    ):
+        update_rows(scale, lstm, (slice(begin, begin + value.shape[0]), every), value, RATES[4])
 
     @pl.when(pl.program_id(0) == 0)
     def _():
@@ -902,16 +918,6 @@
         update_rows(scale, embed, (every, every), small[0:16, H - width :], RATES[0])
         update_rows(scale, edge_first, (every, every), first[0 : EIN + 1, :], RATES[1])
         tall = 2 * H + 8
-        for part in range(4):
-            columns = slice(part * H, (part + 1) * H)
-            by_query = read[part * tall : part * tall + H, :]
-            for begin, value in (
-                (0, by_query),
-                (H, read[part * tall + H : part * tall + 2 * H, :]),
-                (2 * H, by_query),
-                (3 * H, read[part * tall + 2 * H : part * tall + 2 * H + 1, :]),
-            ):
-                update_rows(scale, lstm, (slice(begin, begin + value.shape[0]), columns), value, RATES[4])
         for part in range(2):
             value = read[4 * tall + part * H : 4 * tall + (part + 1) * H, :].T[0:NT]
             update_rows(scale, head, (every, slice(part * H, (part + 1) * H)), value, RATES[5])
@@ -930,6 +936,8 @@
     def specs(number, array):
         if number == 2:
             return pl.BlockSpec((array.shape[0], block), lambda index: (0, index))
+        if number == 3:
+            return pl.BlockSpec((array.shape[0], H), lambda index: (0, index))
         return whole(array)
 
     weights = [array for group in groups for array in group]
@@ -941,6 +949,7 @@
             pl.BlockSpec(memory_space=pltpu.SMEM),
             pl.BlockSpec((1, block, H), lambda index: (index // each, index % each, 0)),
             pl.BlockSpec((1, block), lambda index: (0, index)),
+            pl.BlockSpec((2 * H + 8, H), lambda index: (index, 0)),
             whole(read),
             whole(small),
             whole(first),
@@ -950,7 +959,7 @@
         out_shape=[jax.ShapeDtypeStruct(array.shape, F32) for array in weights],
         compiler_params=pltpu.CompilerParams(vmem_limit_bytes=VMEM_LIMIT),
         name="adamw_step",
-    )(scale, wide, bias, read, small, first, *weights)
+    )(scale, wide, bias, read, read, small, first, *weights)
 
 
 def on_device(
@@ -1037,7 +1046,7 @@
         moved = [swap(count, "edge", groups, step)]
     d_final, read = readout(
         scal, hid, mol, lstm, head,
-        jnp.pad(present, ((0, H - mols), (0, H - NT))), jnp.pad(target, ((0, H - mols), (0, H - NT))),
+        jnp.pad(present, ((0, MOLS), (0, H - NT))), jnp.pad(target, ((0, MOLS), (0, H - NT))),
     )
     d_final, moved = lax.optimization_barrier((d_final, moved))
     while step < groups:

time: 345 us -> 341 us (0.988)
  Pallas kernels: 202 us -> 198 us
    pallas_call x1, Pallas kernels: 22.6 us -> 19 us  [readout(): pl.pallas_call(readout_kernel, out_shape=(jax.ShapeDtypeStruct((H, nodes)...]
  transfers between devices with their start and end apart: 32 -> 32, of which waited for: 9 -> 10; matrix products, arithmetic and copies ran while one was open for 7% -> 8% of each run, Pallas kernels for 56% -> 55%
where the time goes in v6:
time: 341 us; the launch traced here: 339 us
  Pallas kernels  198 us (58%)
  starting transfers between devices  48.2 us (14%)
  waiting for transfers between devices  36.1 us (11%)
  local copies, waits for them, and re-layouts  27.2 us (8%)
  other arithmetic  18.5 us (5%)
  between operations  11 us (3%)
    pallas_call x1, Pallas kernels, forward(): pl.pallas_call(functools.partial(forward_kernel, gates=gates), out_shape=...  58.6 us
    pallas_call x1, Pallas kernels, backward(): pl.pallas_call(backward_kernel, out_shape=(jax.ShapeDtypeStruct((edges //...  54.8 us
    ppermute x32, starting transfers between devices, swap(): lax.ppermute(value, axis, [(index, index ^ step) for index in range(size)])  48.2 us
    pallas_call x5, Pallas kernels, edge_grads(): pl.pallas_call(functools.partial(final_kernel, pair=pair, sides=sides, ha...  47.9 us
    ppermute x32, waiting for transfers between devices, swap(): lax.ppermute(value, axis, [(index, index ^ step) for index in range(size)])  36.1 us
    pallas_call x1, Pallas kernels, readout(): pl.pallas_call(readout_kernel, out_shape=(jax.ShapeDtypeStruct((H, nodes)...  19 us
    pallas_call x1, Pallas kernels, adamw_step(): pl.pallas_call(adamw_kernel, grid=(columns // block,), in_specs=[pl.Block...  10.2 us
    pallas_call x1, Pallas kernels, prep(): pl.pallas_call(functools.partial(prep_kernel, edges=real, gates=gates, eb...  7.97 us
  transfers between devices with their start and end apart: 32, of which 10 were waited for; matrix products, arithmetic and copies ran while one was open for 8% of the time, Pallas kernels for 55%

profile of v6, /device:TPU:0, one launch (start us, length us, event | category | flops | bytes accessed | tf_op | source)
XLA Modules:
  0.0 339.4 jit_solution(6689763822044579475)
XLA Ops:
  0.7 1.8 fusion
  2.4 0.9 reduce-precision_convert_fusion.5
  4.8 0.9 dynamic-slice_bitcast_fusion
  5.8 3.0 collective-permute-start.3
  8.9 1.5 collective-permute-start.2
  12.8 1.9 concatenate.49
  16.6 1.3 pad.57.data
  19.2 0.9 pad.59.lstm
  21.7 8.0 %prep.1 = (s32[8]{0:T(128)}, f32[20,128,256]{2,1,0:T(8,128)}, bf16[144,5120]{1,0:T(8,128)(2,1)}, bf16[5120,128]{1,0:T(8,128)(2,1)}, bf16[20,32,256]{2,1,0:T(8,128)(2,1)}, /*index=5*/s32[8,5120]{1,0:T(8,128)}) custom-call(s32[2]{0:T(128)} %pad_add_fusion.place, s32[1,3200]{1,0:T(1,128)} %reshape.214.mol, s32[32,256]{1,0:T(8,128)} %pad.56.src2d, ...), custom_call_target="tpu_custom_call" | custom-call | tf_op jit(solution)/shard_map/prep/pallas_call | solution.py:178
  30.9 3.8 %collective-permute-start.7 = (f32[1,1]{1,0:T(1,128)}, f32[1,1]{1,0:T(1,128)}, u32[]{:S(2)}, u32[]{:S(2)}) collective-permute-start(f32[1,1]{1,0:T(1,128)} %add.214), channel_id=1, source_target_pairs={{0,4},{4,0},{8,12},{12,8},{1,5},{5,1},{9,13},{13,9},{2,6},{6,2},{1... | collective-permute-start | bytes 20 | tf_op jit(solution)/shard_map/ppermute | solution.py:831
  34.7 2.2 collective-permute-done.2.refs_4_.refs_0_
  36.9 0.9 slice_bitcast_fusion.1
  38.4 0.9 slice_bitcast_fusion.2
  39.6 1.2 reshape.234.gru_bias
  44.2 58.6 %forward.1 = (bf16[4,128,3200]{2,1,0:T(8,128)(2,1)}, bf16[3,128,3200]{2,1,0:T(8,128)(2,1)}, f32[4,128,3200]{2,1,0:T(8,128)}, bf16[20,3,128,256]{3,2,1,0:T(8,128)(2,1)}, bf16[40,4,4096,128]{3,2,1,0:T(8,128)(2,1)}) custom-call(s32[2]{0:T(128)} %pad_add_fusion.place, s32[8]{0:T(128)} %get-tuple-element.100.scal, bf16[16,3200]{1,0:T(8,128)(2,1)} %pad.63.nf_t, ...), custom_call_target="tpu_custom_call" | custom-call | flops 60000002048 | bytes 20000000 | tf_op jit(solution)/shard_map/forward/pallas_call | solution.py:417
  103.4 4.0 %collective-permute-start.8 = (f32[1,1]{1,0:T(1,128)}, f32[1,1]{1,0:T(1,128)}, u32[]{:S(2)}, u32[]{:S(2)}) collective-permute-start(f32[1,1]{1,0:T(1,128)} %add.217), channel_id=1, source_target_pairs={{0,8},{4,12},{8,0},{12,4},{1,9},{5,13},{9,1},{13,5},{2,10},{6,14},... | collective-permute-start | bytes 20 | tf_op jit(solution)/shard_map/ppermute | solution.py:831
  107.4 19.0 %readout.1 = (f32[128,3200]{1,0:T(8,128)}, f32[1328,128]{1,0:T(8,128)}) custom-call(s32[8]{0:T(128)} %get-tuple-element.100.scal, s32[1,3200]{1,0:T(1,128)} %reshape.214.mol, f32[392,512]{1,0:T(8,128)} %pad.59.lstm, f32[264,128]{1,0:T(8,128)} %pad.60.head, f32[192,128]{1,0:T(8,128)} %pad.61.present, f32[192,128]{1,0:T(8,128)} %pad.62.target, ...), custom_call_target="tpu_custom_call" | custom-call | flops 30000001024 | bytes 5000000 | tf_op jit(solution)/shard_map/readout/pallas_call | solution.py:589
  127.4 54.8 %backward.1 = (bf16[20,3,128,256]{3,2,1,0:T(8,128)(2,1)}, f32[4,320,128]{2,1,0:T(8,128)}) custom-call(s32[2]{0:T(128)} %pad_add_fusion.place, s32[8]{0:T(128)} %get-tuple-element.100.scal, f32[1]{0:T(128)} %bitcast.28.inverse, bf16[16,3200]{1,0:T(8,128)(2,1)} %pad.63.nf_t, bf16[2,384,128]{2,1,0:T(8,128)(2,1)} %bitcast.136, f32[2,384,1]{2,1,0:T(8,128)} %reshape.234.gru_bias, ...), custom_call_target="tpu_custom_call" | custom-call | flops 60000002048 | bytes 20000000 | tf_op jit(solution)/shard_map/backward/pallas_call | solution.py:703
  182.4 1.6 collective-permute-done.10
  184.1 5.8 %collective-permute-start.11 = (f32[664,128]{1,0:T(8,128)S(1)}, f32[664,128]{1,0:T(8,128)S(1)}, u32[]{:S(2)}, u32[]{:S(2)}) collective-permute-start(f32[664,128]{1,0:T(8,128)S(1)} %bitcast_add_fusion), channel_id=1, source_target_pairs={{0,1},{1,0},{2,3},{3,2},{4,5},{5,4},{6,7},{7,6},{8,9},{9,8},{10,11... | collective-permute-start | bytes 1019912 | tf_op jit(solution)/shard_map/ppermute | solution.py:831
  190.6 10.9 %edge_grads.5 = (f32[2240,128]{1,0:T(8,128)}, f32[2240,128]{1,0:T(8,128)}, f32[32,128]{1,0:T(8,128)}) custom-call(s32[2]{0:T(128)} %pad_add_fusion.place, s32[8]{0:T(128)} %get-tuple-element.100.scal, f32[32,128]{1,0:T(8,128)} %broadcast_in_dim.50.first_in, f32[4,320,128]{2,1,0:T(8,128)} %get-tuple-element.120.narrow, ...), custom_call_target="tpu_custom_call" | custom-call | flops 8999999488 | bytes 5000000 | tf_op jit(solution)/shard_map/edge_grads/pallas_call | solution.py:804
  201.6 7.1 %collective-permute-start.12 = (f32[664,128]{1,0:T(8,128)S(1)}, f32[664,128]{1,0:T(8,128)S(1)}, u32[]{:S(2)}, u32[]{:S(2)}) collective-permute-start(f32[664,128]{1,0:T(8,128)S(1)} %add.221), channel_id=1, source_target_pairs={{0,2},{1,3},{2,0},{3,1},{4,6},{5,7},{6,4},{7,5},{8,10},{9,11},{10,... | collective-permute-start | bytes 1019912 | tf_op jit(solution)/shard_map/ppermute | solution.py:831
  208.8 10.9 %edge_grads.6 = (f32[2240,128]{1,0:T(8,128)}, f32[2240,128]{1,0:T(8,128)}, f32[32,128]{1,0:T(8,128)}) custom-call(s32[2]{0:T(128)} %pad_add_fusion.place, s32[8]{0:T(128)} %get-tuple-element.100.scal, f32[32,128]{1,0:T(8,128)} %get-tuple-element.127.first_in, f32[4,320,128]{2,1,0:T(8,128)} %get-tuple-element.120.narrow, ...), custom_call_target="tpu_custom_call" | custom-call | flops 8999999488 | bytes 5000000 | tf_op jit(solution)/shard_map/edge_grads/pallas_call | solution.py:804
  220.0 2.5 collective-permute-start.15
  222.5 2.1 collective-permute-start.14
  224.6 10.9 %edge_grads.7 = (f32[2240,128]{1,0:T(8,128)}, f32[2240,128]{1,0:T(8,128)}, f32[32,128]{1,0:T(8,128)}) custom-call(s32[2]{0:T(128)} %pad_add_fusion.place, s32[8]{0:T(128)} %get-tuple-element.100.scal, f32[32,128]{1,0:T(8,128)} %get-tuple-element.131.first_in, f32[4,320,128]{2,1,0:T(8,128)} %get-tuple-element.120.narrow, bf16[2352,128]{1,0:T(8,128)(2,1)} %copy-done.23, ...), custom_call_target="tpu_custom_call" | custom-call | flops 8999999488 | bytes 5000000 | tf_op jit(solution)/shard_map/edge_grads/pallas_call | solution.py:804
  236.2 2.3 add_convert_fusion.1
  239.1 7.7 %edge_grads.8 = (f32[2240,128]{1,0:T(8,128)}, f32[32,128]{1,0:T(8,128)}) custom-call(s32[2]{0:T(128)} %pad_add_fusion.place, s32[8]{0:T(128)} %get-tuple-element.100.scal, f32[32,128]{1,0:T(8,128)} %get-tuple-element.137.first_in, f32[4,320,128]{2,1,0:T(8,128)} %get-tuple-element.120.narrow, bf16[2048,128]{1,0:T(8,128)(2,1)} %get-tuple-element.232.refs_1_.refs_0_, ...), custom_call_target="tpu_custom_call" | custom-call | flops 8999999488 | bytes 5000000 | tf_op jit(solution)/shard_map/edge_grads/pallas_call | solution.py:804
  247.3 6.3 %collective-permute-done.18 = bf16[2240,128]{1,0:T(8,128)(2,1)} collective-permute-done((bf16[2240,128]{1,0:T(8,128)(2,1)}, bf16[2240,128]{1,0:T(8,128)(2,1)}, u32[]{:S(2)}, u32[]{:S(2)}) %collective-permute-start.18) | collective-permute-done | bytes 573472 | tf_op jit(solution)/shard_map/ppermute | solution.py:831
  253.6 0.9 add_convert_fusion
  254.5 1.7 collective-permute-start.20
  256.2 7.6 %edge_grads.9 = (f32[2240,128]{1,0:T(8,128)}, f32[32,128]{1,0:T(8,128)}) custom-call(s32[2]{0:T(128)} %pad_add_fusion.place, s32[8]{0:T(128)} %get-tuple-element.100.scal, f32[32,128]{1,0:T(8,128)} %get-tuple-element.143.first_in, f32[4,320,128]{2,1,0:T(8,128)} %get-tuple-element.120.narrow, bf16[2352,128]{1,0:T(8,128)(2,1)} %copy-done.8, ...), custom_call_target="tpu_custom_call" | custom-call | flops 8999999488 | bytes 5000000 | tf_op jit(solution)/shard_map/edge_grads/pallas_call | solution.py:804
  263.8 4.8 %collective-permute-done.20 = bf16[2240,128]{1,0:T(8,128)(2,1)S(1)} collective-permute-done((bf16[2240,128]{1,0:T(8,128)(2,1)}, bf16[2240,128]{1,0:T(8,128)(2,1)S(1)}, u32[]{:S(2)}, u32[]{:S(2)}) %collective-permute-start.20) | collective-permute-done | bytes 573472 | tf_op jit(solution)/shard_map/ppermute | solution.py:831
  268.7 2.7 abs_reduce_fusion
  274.1 3.4 collective-permute-start.22
  278.1 1.8 collective-permute-start.24
  279.9 2.3 collective-permute-done.22
  282.2 8.9 %collective-permute-done.23 = f16[656,128]{1,0:T(8,128)(2,1)S(1)} collective-permute-done((f16[656,128]{1,0:T(8,128)(2,1)S(1)}, f16[656,128]{1,0:T(8,128)(2,1)S(1)}, u32[]{:S(2)}, u32[]{:S(2)}) %collective-permute-start.23) | collective-permute-done | bytes 167968 | tf_op jit(solution)/shard_map/ppermute | solution.py:831
  292.8 2.5 collective-permute-start.25
  295.4 2.4 collective-permute-start.27
  299.6 8.0 %collective-permute-done.26 = f16[576,128]{1,0:T(8,128)(2,1)S(1)} collective-permute-done((f16[576,128]{1,0:T(8,128)(2,1)S(1)}, f16[576,128]{1,0:T(8,128)(2,1)S(1)}, u32[]{:S(2)}, u32[]{:S(2)}) %collective-permute-start.26) | collective-permute-done | bytes 147488 | tf_op jit(solution)/shard_map/ppermute | solution.py:831
  310.3 1.2 convert_multiply_fusion
  311.5 1.3 concatenate.62
  313.8 2.6 collective-permute-start.31
  319.3 1.1 reshape.232
  320.4 1.4 add_add_fusion
  326.2 1.9 multiply_subtract_fusion
  328.1 10.2 %adamw_step.1 = (f32[16,32]{1,0:T(8,128)}, f32[16,32]{1,0:T(8,128)}, f32[16,32]{1,0:T(8,128)}, f32[17,128]{1,0:T(8,128)}, f32[17,128]{1,0:T(8,128)}, /*index=5*/...) custom-call(f32[3]{0:T(128)} %pad_maximum_fusion.14.scale, ...), custom_call_target="tpu_custom_call" | custom-call | tf_op jit(solution)/shard_map/adamw_step/pallas_call | solution.py:945
  (216 shorter events, 28.3 us)
Async XLA Ops:
  5.7 5.4 %copy-start.20 = (s32[4992]{0:T(1024)S(1)}, s32[4992]{0:T(1024)}, u32[]{:S(2)}) copy-start(s32[4992]{0:T(1024)} %param.31) | copy-start | bytes 59908
  5.7 5.4 %copy-start.21 = (s32[4992]{0:T(1024)S(1)}, s32[4992]{0:T(1024)}, u32[]{:S(2)}) copy-start(s32[4992]{0:T(1024)} %param.29) | copy-start | bytes 59908
  5.7 5.4 %copy-start.18 = (f32[17,128]{1,0:T(8,128)S(1)}, f32[17,128]{1,0:T(8,128)}, u32[]{:S(2)}) copy-start(f32[17,128]{1,0:T(8,128)} %refs_3_.1) | copy-start | bytes 26116
  5.8 7.0 %copy-start.13 = (bf16[4992,12]{0,1:T(8,128)(2,1)S(1)}, bf16[4992,12]{0,1:T(8,128)(2,1)}, u32[]{:S(2)}) copy-start(bf16[4992,12]{0,1:T(8,128)(2,1)} %param.28) | copy-start | bytes 359428
  5.8 9.5 %copy-start.8 = (bf16[2352,128]{1,0:T(8,128)(2,1)}, bf16[2352,128]{1,0:T(8,128)(2,1)S(1)}, u32[]{:S(2)}) copy-start(bf16[2352,128]{1,0:T(8,128)(2,1)S(1)} %pad_maximum_fusion.1.refs_0_) | copy-start | bytes 1806340
  5.8 28.9 %collective-permute-start.3 = (bf16[2352,128]{1,0:T(8,128)(2,1)S(1)}, bf16[2352,128]{1,0:T(8,128)(2,1)S(1)}, u32[]{:S(2)}, u32[]{:S(2)}) collective-permute-start(bf16[2352,128]{1,0:T(8,128)(2,1)S(1)} %pad_maximum_fusion.1.refs_0_), channel_id=1, source_target_pairs={{0,1},{1,0},{2,3},{3,2},{4,5},{5,4},{6,7},{7,6},{8,9},{9,8},{10,11... | collective-permute-start | bytes 1806344 | tf_op jit(solution)/shard_map/ppermute | solution.py:831
  8.9 28.1 %collective-permute-start.2 = (bf16[2352,128]{1,0:T(8,128)(2,1)S(1)}, bf16[2352,128]{1,0:T(8,128)(2,1)}, u32[]{:S(2)}, u32[]{:S(2)}) collective-permute-start(bf16[2352,128]{1,0:T(8,128)(2,1)S(1)} %pad_maximum_fusion.1.refs_0_), channel_id=1, source_target_pairs={{0,2},{1,3},{2,0},{3,1},{4,6},{5,7},{6,4},{7,5},{8,10},{9,11},{10,... | collective-permute-start | bytes 1806344 | tf_op jit(solution)/shard_map/ppermute | solution.py:831
  10.4 27.4 %collective-permute-start.1 = (bf16[2352,128]{1,0:T(8,128)(2,1)S(1)}, bf16[2352,128]{1,0:T(8,128)(2,1)}, u32[]{:S(2)}, u32[]{:S(2)}) collective-permute-start(bf16[2352,128]{1,0:T(8,128)(2,1)S(1)} %pad_maximum_fusion.1.refs_0_), channel_id=1, source_target_pairs={{0,3},{1,2},{2,1},{3,0},{4,7},{5,6},{6,5},{7,4},{8,11},{9,10},{10,... | collective-permute-start | bytes 1806344 | tf_op jit(solution)/shard_map/ppermute | solution.py:831
  11.1 18.6 %collective-permute-start = (f32[1,1]{1,0:T(1,128)}, f32[1,1]{1,0:T(1,128)}, u32[]{:S(2)}, u32[]{:S(2)}) collective-permute-start(f32[1,1]{1,0:T(1,128)} %bitcast.7), channel_id=1, source_target_pairs={{0,16},{16,0},{1,17},{17,1},{2,18},{18,2},{3,19},{19,3},{4,20},{20... | collective-permute-start | bytes 20 | tf_op jit(solution)/shard_map/ppermute | solution.py:831
  30.9 71.8 %collective-permute-start.7 = (f32[1,1]{1,0:T(1,128)}, f32[1,1]{1,0:T(1,128)}, u32[]{:S(2)}, u32[]{:S(2)}) collective-permute-start(f32[1,1]{1,0:T(1,128)} %add.214), channel_id=1, source_target_pairs={{0,4},{4,0},{8,12},{12,8},{1,5},{5,1},{9,13},{13,9},{2,6},{6,2},{1... | collective-permute-start | bytes 20 | tf_op jit(solution)/shard_map/ppermute | solution.py:831
  34.7 6.1 %copy-start.23 = (bf16[2352,128]{1,0:T(8,128)(2,1)}, bf16[2352,128]{1,0:T(8,128)(2,1)S(1)}, u32[]{:S(2)}) copy-start(bf16[2352,128]{1,0:T(8,128)(2,1)S(1)} %collective-permute-done.3.refs_2_.refs_0_) | copy-start | bytes 1806340
  34.7 8.4 %collective-permute-start.4 = (bf16[2352,128]{1,0:T(8,128)(2,1)S(1)}, bf16[2352,128]{1,0:T(8,128)(2,1)S(1)}, u32[]{:S(2)}, u32[]{:S(2)}) collective-permute-start(bf16[2352,128]{1,0:T(8,128)(2,1)S(1)} %collective-permute-done.3.refs_2_.refs_0_), channel_id=1, source_target_pairs={{0,16},{16,0},{1,17},{17,1},{2,18},{18,2},{3,19},{19,3},{4,20},{20... | collective-permute-start | bytes 1806344 | tf_op jit(solution)/shard_map/ppermute | solution.py:831
  36.9 6.2 %collective-permute-start.5 = (bf16[2352,128]{1,0:T(8,128)(2,1)}, bf16[2352,128]{1,0:T(8,128)(2,1)}, u32[]{:S(2)}, u32[]{:S(2)}) collective-permute-start(bf16[2352,128]{1,0:T(8,128)(2,1)} %collective-permute-done.2.refs_4_.refs_0_), channel_id=1, source_target_pairs={{0,16},{16,0},{1,17},{17,1},{2,18},{18,2},{3,19},{19,3},{4,20},{20... | collective-permute-start | bytes 1806344 | tf_op jit(solution)/shard_map/ppermute | solution.py:831
  37.8 5.3 %collective-permute-start.6 = (bf16[2352,128]{1,0:T(8,128)(2,1)}, bf16[2352,128]{1,0:T(8,128)(2,1)S(1)}, u32[]{:S(2)}, u32[]{:S(2)}) collective-permute-start(bf16[2352,128]{1,0:T(8,128)(2,1)} %collective-permute-done.1.refs_6_.refs_0_), channel_id=1, source_target_pairs={{0,16},{16,0},{1,17},{17,1},{2,18},{18,2},{3,19},{19,3},{4,20},{20... | collective-permute-start | bytes 1806344 | tf_op jit(solution)/shard_map/ppermute | solution.py:831
  103.4 23.3 %collective-permute-start.8 = (f32[1,1]{1,0:T(1,128)}, f32[1,1]{1,0:T(1,128)}, u32[]{:S(2)}, u32[]{:S(2)}) collective-permute-start(f32[1,1]{1,0:T(1,128)} %add.217), channel_id=1, source_target_pairs={{0,8},{4,12},{8,0},{12,4},{1,9},{5,13},{9,1},{13,5},{2,10},{6,14},... | collective-permute-start | bytes 20 | tf_op jit(solution)/shard_map/ppermute | solution.py:831
  126.3 55.8 %collective-permute-start.9 = (f32[1328,128]{1,0:T(8,128)}, f32[1328,128]{1,0:T(8,128)S(1)}, u32[]{:S(2)}, u32[]{:S(2)}) collective-permute-start(f32[1328,128]{1,0:T(8,128)} %get-tuple-element.106), channel_id=1, source_target_pairs={{0,8},{4,12},{8,0},{12,4},{1,9},{5,13},{9,1},{13,5},{2,10},{6,14},... | collective-permute-start | bytes 2039816 | tf_op jit(solution)/shard_map/ppermute | solution.py:831
  127.3 54.9 %copy-start.7 = (f32[1328,128]{1,0:T(8,128)S(1)}, f32[1328,128]{1,0:T(8,128)}, u32[]{:S(2)}) copy-start(f32[1328,128]{1,0:T(8,128)} %get-tuple-element.106) | copy-start | bytes 2039812
  182.3 1.7 collective-permute-start.10
  184.1 17.5 %collective-permute-start.11 = (f32[664,128]{1,0:T(8,128)S(1)}, f32[664,128]{1,0:T(8,128)S(1)}, u32[]{:S(2)}, u32[]{:S(2)}) collective-permute-start(f32[664,128]{1,0:T(8,128)S(1)} %bitcast_add_fusion), channel_id=1, source_target_pairs={{0,1},{1,0},{2,3},{3,2},{4,5},{5,4},{6,7},{7,6},{8,9},{9,8},{10,11... | collective-permute-start | bytes 1019912 | tf_op jit(solution)/shard_map/ppermute | solution.py:831
  201.4 18.5 %collective-permute-start.13 = (f32[2240,128]{1,0:T(8,128)}, f32[2240,128]{1,0:T(8,128)S(1)}, u32[]{:S(2)}, u32[]{:S(2)}) collective-permute-start(f32[2240,128]{1,0:T(8,128)} %get-tuple-element.129), channel_id=1, source_target_pairs={{0,16},{16,0},{1,17},{17,1},{2,18},{18,2},{3,19},{19,3},{4,20},{20... | collective-permute-start | bytes 3440648 | tf_op jit(solution)/shard_map/ppermute | solution.py:831
  201.6 18.3 %copy-start.4 = (f32[2240,128]{1,0:T(8,128)S(1)}, f32[2240,128]{1,0:T(8,128)}, u32[]{:S(2)}) copy-start(f32[2240,128]{1,0:T(8,128)} %get-tuple-element.133) | copy-start | bytes 3440644
  201.6 18.2 %collective-permute-start.12 = (f32[664,128]{1,0:T(8,128)S(1)}, f32[664,128]{1,0:T(8,128)S(1)}, u32[]{:S(2)}, u32[]{:S(2)}) collective-permute-start(f32[664,128]{1,0:T(8,128)S(1)} %add.221), channel_id=1, source_target_pairs={{0,2},{1,3},{2,0},{3,1},{4,6},{5,7},{6,4},{7,5},{8,10},{9,11},{10,... | collective-permute-start | bytes 1019912 | tf_op jit(solution)/shard_map/ppermute | solution.py:831
  219.7 15.9 %collective-permute-start.16 = (f32[2240,128]{1,0:T(8,128)}, f32[2240,128]{1,0:T(8,128)}, u32[]{:S(2)}, u32[]{:S(2)}) collective-permute-start(f32[2240,128]{1,0:T(8,128)} %get-tuple-element.135), channel_id=1, source_target_pairs={{0,16},{16,0},{1,17},{17,1},{2,18},{18,2},{3,19},{19,3},{4,20},{20... | collective-permute-start | bytes 3440648 | tf_op jit(solution)/shard_map/ppermute | solution.py:831
  220.0 16.2 %collective-permute-start.15 = (bf16[2240,128]{1,0:T(8,128)(2,1)S(1)}, bf16[2240,128]{1,0:T(8,128)(2,1)S(1)}, u32[]{:S(2)}, u32[]{:S(2)}) collective-permute-start(bf16[2240,128]{1,0:T(8,128)(2,1)S(1)} %add_convert_fusion.2), channel_id=1, source_target_pairs={{0,3},{1,2},{2,1},{3,0},{4,7},{5,6},{6,5},{7,4},{8,11},{9,10},{10,... | collective-permute-start | bytes 1720328 | tf_op jit(solution)/shard_map/ppermute | solution.py:831
  222.5 13.7 %copy-start.6 = (f32[2240,128]{1,0:T(8,128)S(1)}, f32[2240,128]{1,0:T(8,128)}, u32[]{:S(2)}) copy-start(f32[2240,128]{1,0:T(8,128)} %get-tuple-element.139) | copy-start | bytes 3440644
  222.5 13.0 %collective-permute-start.14 = (f32[664,128]{1,0:T(8,128)S(1)}, f32[664,128]{1,0:T(8,128)S(1)}, u32[]{:S(2)}, u32[]{:S(2)}) collective-permute-start(f32[664,128]{1,0:T(8,128)S(1)} %add.222), channel_id=1, source_target_pairs={{0,4},{4,0},{8,12},{12,8},{1,5},{5,1},{9,13},{13,9},{2,6},{6,2},{1... | collective-permute-start | bytes 1019912 | tf_op jit(solution)/shard_map/ppermute | solution.py:831
  235.5 18.1 %collective-permute-start.19 = (f32[2240,128]{1,0:T(8,128)}, f32[2240,128]{1,0:T(8,128)S(1)}, u32[]{:S(2)}, u32[]{:S(2)}) collective-permute-start(f32[2240,128]{1,0:T(8,128)} %get-tuple-element.141), channel_id=1, source_target_pairs={{0,16},{16,0},{1,17},{17,1},{2,18},{18,2},{3,19},{19,3},{4,20},{20... | collective-permute-start | bytes 3440648 | tf_op jit(solution)/shard_map/ppermute | solution.py:831
  238.5 15.1 %collective-permute-start.18 = (bf16[2240,128]{1,0:T(8,128)(2,1)}, bf16[2240,128]{1,0:T(8,128)(2,1)}, u32[]{:S(2)}, u32[]{:S(2)}) collective-permute-start(bf16[2240,128]{1,0:T(8,128)(2,1)} %add_convert_fusion.1), channel_id=1, source_target_pairs={{0,2},{1,3},{2,0},{3,1},{4,6},{5,7},{6,4},{7,5},{8,10},{9,11},{10,... | collective-permute-start | bytes 1720328 | tf_op jit(solution)/shard_map/ppermute | solution.py:831
  239.0 14.6 %copy-start.5 = (f32[2240,128]{1,0:T(8,128)S(1)}, f32[2240,128]{1,0:T(8,128)}, u32[]{:S(2)}) copy-start(f32[2240,128]{1,0:T(8,128)} %get-tuple-element.145) | copy-start | bytes 3440644
  239.0 8.3 %collective-permute-start.17 = (f32[664,128]{1,0:T(8,128)S(1)}, f32[664,128]{1,0:T(8,128)S(1)}, u32[]{:S(2)}, u32[]{:S(2)}) collective-permute-start(f32[664,128]{1,0:T(8,128)S(1)} %add.224), channel_id=1, source_target_pairs={{0,16},{16,0},{1,17},{17,1},{2,18},{18,2},{3,19},{19,3},{4,20},{20... | collective-permute-start | bytes 1019912 | tf_op jit(solution)/shard_map/ppermute | solution.py:831
  246.8 21.8 %collective-permute-start.21 = (f32[2240,128]{1,0:T(8,128)}, f32[2240,128]{1,0:T(8,128)}, u32[]{:S(2)}, u32[]{:S(2)}) collective-permute-start(f32[2240,128]{1,0:T(8,128)} %get-tuple-element.147), channel_id=1, source_target_pairs={{0,16},{16,0},{1,17},{17,1},{2,18},{18,2},{3,19},{19,3},{4,20},{20... | collective-permute-start | bytes 3440648 | tf_op jit(solution)/shard_map/ppermute | solution.py:831
  247.3 7.2 %copy-start.11 = (f32[664,128]{1,0:T(8,128)}, f32[664,128]{1,0:T(8,128)S(1)}, u32[]{:S(2)}) copy-start(f32[664,128]{1,0:T(8,128)S(1)} %collective-permute-done.17) | copy-start | bytes 1019908
  254.5 14.1 %collective-permute-start.20 = (bf16[2240,128]{1,0:T(8,128)(2,1)}, bf16[2240,128]{1,0:T(8,128)(2,1)S(1)}, u32[]{:S(2)}, u32[]{:S(2)}) collective-permute-start(bf16[2240,128]{1,0:T(8,128)(2,1)} %add_convert_fusion), channel_id=1, source_target_pairs={{0,1},{1,0},{2,3},{3,2},{4,5},{5,4},{6,7},{7,6},{8,9},{9,8},{10,11... | collective-permute-start | bytes 1720328 | tf_op jit(solution)/shard_map/ppermute | solution.py:831
  274.1 8.1 %collective-permute-start.22 = (f16[656,128]{1,0:T(8,128)(2,1)S(1)}, f16[656,128]{1,0:T(8,128)(2,1)S(1)}, u32[]{:S(2)}, u32[]{:S(2)}) collective-permute-start(f16[656,128]{1,0:T(8,128)(2,1)S(1)} %get-tuple-element.241), channel_id=1, source_target_pairs={{0,4},{4,0},{8,12},{12,8},{1,5},{5,1},{9,13},{13,9},{2,6},{6,2},{1... | collective-permute-start | bytes 503816 | tf_op jit(solution)/shard_map/ppermute | solution.py:831
  277.4 13.7 %collective-permute-start.23 = (f16[656,128]{1,0:T(8,128)(2,1)S(1)}, f16[656,128]{1,0:T(8,128)(2,1)S(1)}, u32[]{:S(2)}, u32[]{:S(2)}) collective-permute-start(f16[656,128]{1,0:T(8,128)(2,1)S(1)} %get-tuple-element.240), channel_id=1, source_target_pairs={{0,8},{4,12},{8,0},{12,4},{1,9},{5,13},{9,1},{13,5},{2,10},{6,14},... | collective-permute-start | bytes 503816 | tf_op jit(solution)/shard_map/ppermute | solution.py:831
  278.1 13.0 %collective-permute-start.24 = (f16[656,128]{1,0:T(8,128)(2,1)S(1)}, f16[656,128]{1,0:T(8,128)(2,1)S(1)}, u32[]{:S(2)}, u32[]{:S(2)}) collective-permute-start(f16[656,128]{1,0:T(8,128)(2,1)S(1)} %get-tuple-element.239), channel_id=1, source_target_pairs={{0,12},{4,8},{8,4},{12,0},{1,13},{5,9},{9,5},{13,1},{2,14},{6,10},... | collective-permute-start | bytes 503816 | tf_op jit(solution)/shard_map/ppermute | solution.py:831
  292.8 6.8 %collective-permute-start.25 = (f16[576,128]{1,0:T(8,128)(2,1)S(1)}, f16[576,128]{1,0:T(8,128)(2,1)S(1)}, u32[]{:S(2)}, u32[]{:S(2)}) collective-permute-start(f16[576,128]{1,0:T(8,128)(2,1)S(1)} %get-tuple-element.237), channel_id=1, source_target_pairs={{0,4},{4,0},{8,12},{12,8},{1,5},{5,1},{9,13},{13,9},{2,6},{6,2},{1... | collective-permute-start | bytes 442376 | tf_op jit(solution)/shard_map/ppermute | solution.py:831
  295.3 12.3 %collective-permute-start.26 = (f16[576,128]{1,0:T(8,128)(2,1)S(1)}, f16[576,128]{1,0:T(8,128)(2,1)S(1)}, u32[]{:S(2)}, u32[]{:S(2)}) collective-permute-start(f16[576,128]{1,0:T(8,128)(2,1)S(1)} %get-tuple-element.237), channel_id=1, source_target_pairs={{0,8},{4,12},{8,0},{12,4},{1,9},{5,13},{9,1},{13,5},{2,10},{6,14},... | collective-permute-start | bytes 442376 | tf_op jit(solution)/shard_map/ppermute | solution.py:831
  295.4 12.2 %collective-permute-start.27 = (f16[576,128]{1,0:T(8,128)(2,1)S(1)}, f16[576,128]{1,0:T(8,128)(2,1)S(1)}, u32[]{:S(2)}, u32[]{:S(2)}) collective-permute-start(f16[576,128]{1,0:T(8,128)(2,1)S(1)} %get-tuple-element.237), channel_id=1, source_target_pairs={{0,12},{4,8},{8,4},{12,0},{1,13},{5,9},{9,5},{13,1},{2,14},{6,10},... | collective-permute-start | bytes 442376 | tf_op jit(solution)/shard_map/ppermute | solution.py:831
  308.0 2.1 collective-permute-start.28
  310.3 6.1 %copy-start.12 = (f32[664,128]{1,0:T(8,128)S(1)}, f32[664,128]{1,0:T(8,128)}, u32[]{:S(2)}) copy-start(f32[664,128]{1,0:T(8,128)} %copy-done.11) | copy-start | bytes 1019908
  311.5 7.7 %copy-start = (f32[8,560,128]{2,1,0:T(8,128)}, f32[8,560,128]{2,1,0:T(8,128)S(1)}, u32[]{:S(2)}) copy-start(f32[8,560,128]{2,1,0:T(8,128)S(1)} %get-tuple-element.230) | copy-start | bytes 6881284
  312.9 7.5 %collective-permute-start.29 = (f32[40,128]{1,0:T(8,128)}, f32[40,128]{1,0:T(8,128)}, u32[]{:S(2)}, u32[]{:S(2)}) collective-permute-start(f32[40,128]{1,0:T(8,128)} %concatenate.62), channel_id=1, source_target_pairs={{0,1},{1,0},{2,3},{3,2},{4,5},{5,4},{6,7},{7,6},{8,9},{9,8},{10,11... | collective-permute-start | bytes 61448 | tf_op jit(solution)/shard_map/ppermute | solution.py:831
  313.6 6.8 %collective-permute-start.30 = (f32[40,128]{1,0:T(8,128)}, f32[40,128]{1,0:T(8,128)}, u32[]{:S(2)}, u32[]{:S(2)}) collective-permute-start(f32[40,128]{1,0:T(8,128)} %concatenate.62), channel_id=1, source_target_pairs={{0,2},{1,3},{2,0},{3,1},{4,6},{5,7},{6,4},{7,5},{8,10},{9,11},{10,... | collective-permute-start | bytes 61448 | tf_op jit(solution)/shard_map/ppermute | solution.py:831
  313.8 6.6 %collective-permute-start.31 = (f32[40,128]{1,0:T(8,128)}, f32[40,128]{1,0:T(8,128)}, u32[]{:S(2)}, u32[]{:S(2)}) collective-permute-start(f32[40,128]{1,0:T(8,128)} %concatenate.62), channel_id=1, source_target_pairs={{0,3},{1,2},{2,1},{3,0},{4,7},{5,6},{6,5},{7,4},{8,11},{9,10},{10,... | collective-permute-start | bytes 61448 | tf_op jit(solution)/shard_map/ppermute | solution.py:831
  316.4 9.8 %copy-start.10 = (f32[2,129,3,32]{1,3,2,0:T(8,128)S(1)}, f32[2,129,3,32]{1,3,2,0:T(8,128)}, u32[]{:S(2)}) copy-start(f32[2,129,3,32]{1,3,2,0:T(8,128)} %param.38) | copy-start | bytes 297220
  317.2 10.9 %copy-start.1 = (f32[1328,128]{1,0:T(8,128)}, f32[1328,128]{1,0:T(8,128)S(1)}, u32[]{:S(2)}) copy-start(f32[1328,128]{1,0:T(8,128)S(1)} %get-tuple-element.222.lines.read) | copy-start | bytes 2039812
  317.8 10.3 %copy-start.3 = (f32[2,160,128]{2,1,0:T(8,128)}, f32[2,160,128]{2,1,0:T(8,128)S(1)}, u32[]{:S(2)}) copy-start(f32[2,160,128]{2,1,0:T(8,128)S(1)} %slice.250) | copy-start | bytes 491524
  (13 other events, 32.7 us)
